TPU v7x, 32 devices: a whole 2x2x4 slice. The times are simulated.
32 devices in a mesh: dp: 8 (over y, x, core), fsdp: 4 (over z).
Axes of the slice: x: 2, y: 2, z: 4, core: 2. Of those that a mesh axis runs over, the one named last changes fastest.
Arguments:
- tokens: bfloat16 [32, 1024, 2048], P(('dp', 'fsdp')), may hold values from -6 to 6
- cotangent: bfloat16 [32, 1024, 2048], P(('dp', 'fsdp')), may hold values from -6 to 6
- doc_starts: int32 [32, 4], P(('dp', 'fsdp')), may hold values from 0 to 896, as said below
- active_len: int32 [32, 4], P(('dp', 'fsdp')), may hold values from 0 to 128, as said below
- ln1_gain: bfloat16 [2048], P(('dp', 'fsdp')), may hold values from 0.5 to 1.5
- ln1_bias: bfloat16 [2048], P(('dp', 'fsdp')), may hold values from -1 to 1
- q_weight: bfloat16 [2048, 2048], P(('dp', 'fsdp')), may hold values from -0.125 to 0.125
- q_bias: bfloat16 [2048], P(('dp', 'fsdp')), may hold values from -1.5 to 1.5
- k_weight: bfloat16 [2048, 2048], P(('dp', 'fsdp')), may hold values from -0.125 to 0.125
- v_weight: bfloat16 [2048, 2048], P(('dp', 'fsdp')), may hold values from -0.125 to 0.125
- v_bias: bfloat16 [2048], P(('dp', 'fsdp')), may hold values from -1.5 to 1.5
- o_weight: bfloat16 [2048, 2048], P(('dp', 'fsdp')), may hold values from -0.5 to 0.5
- o_bias: bfloat16 [2048], P(('dp', 'fsdp')), may hold values from -1.5 to 1.5
- ln2_gain: bfloat16 [2048], P(('dp', 'fsdp')), may hold values from 0.5 to 1.5
- ln2_bias: bfloat16 [2048], P(('dp', 'fsdp')), may hold values from -1 to 1
- up_weight: bfloat16 [2048, 8192], P(('dp', 'fsdp')), may hold values from -0.125 to 0.125
- up_bias: bfloat16 [8192], P(('dp', 'fsdp')), may hold values from -1.5 to 1.5
- down_weight: bfloat16 [8192, 2048], P(('dp', 'fsdp')), may hold values from -0.09375 to 0.09375
- down_bias: bfloat16 [2048], P(('dp', 'fsdp')), may hold values from -1.5 to 1.5
Outputs:
- layer_out: bfloat16 [32, 1024, 2048], P(('dp', 'fsdp'))
- input_grad: bfloat16 [32, 1024, 2048], P(('dp', 'fsdp'))
- grad_ln1_gain: float32 [2048], P(('dp', 'fsdp'))
- grad_ln1_bias: float32 [2048], P(('dp', 'fsdp'))
- grad_q_weight: float32 [2048, 2048], P(('dp', 'fsdp'))
- grad_q_bias: float32 [2048], P(('dp', 'fsdp'))
- grad_k_weight: float32 [2048, 2048], P(('dp', 'fsdp'))
- grad_v_weight: float32 [2048, 2048], P(('dp', 'fsdp'))
- grad_v_bias: float32 [2048], P(('dp', 'fsdp'))
- grad_o_weight: float32 [2048, 2048], P(('dp', 'fsdp'))
- grad_o_bias: float32 [2048], P(('dp', 'fsdp'))
- grad_ln2_gain: float32 [2048], P(('dp', 'fsdp'))
- grad_ln2_bias: float32 [2048], P(('dp', 'fsdp'))
- grad_up_weight: float32 [2048, 8192], P(('dp', 'fsdp'))
- grad_up_bias: float32 [8192], P(('dp', 'fsdp'))
- grad_down_weight: float32 [8192, 2048], P(('dp', 'fsdp'))
- grad_down_bias: float32 [2048], P(('dp', 'fsdp'))
Inputs may be any that keep to these rules, and one draw needn't show every extreme that they name: `doc_starts`: each row holds 4 documents; starts rise from 0 at the first, every document spans 128 tokens or more, and the last ends at 1024; some row's last document starts at 896. `active_len`: 0 marks a document that exited before this layer; an active document has 64 or more active tokens, never more than its length. Over the rows with the same row index on the devices of one fsdp group, exactly 3 * 4 of the 4 * 4 documents are active.
All inputs are finite; a program needn't handle non-finite values.
Results may differ from a plain program's by a relative error of at most 0.013.
Values may be sent and summed in bfloat16 or wider, within the bound.
No kernel may reach another device: no remote copies, remote signals or barrier semaphores. Data moves between devices by JAX's collectives and lax.ppermute only.
A program may use at most 448 MiB of HBM per device.

v0:
```python
import jax
import jax.numpy as jnp
from jax import lax
from jax.sharding import PartitionSpec as P

HEADS = 32
HD = 64
SLOT = 128
RECV = 3
KPEER = 2


EPSILON = 1e-05
MASKED = -1e30
ROOT_HALF = 0.7071067811865476
DENSITY_SCALE = 0.3989422804014327


def product(einsum_form, factor_one, factor_two):
    return jnp.einsum(einsum_form, factor_one, factor_two, preferred_element_type=jnp.float32)


def smooth_gate(values):
    return values * (0.5 + 0.5 * lax.erf(values * ROOT_HALF))


def smooth_slope(values):
    return (
        0.5
        + 0.5 * lax.erf(values * ROOT_HALF)
        + values * DENSITY_SCALE * jnp.exp(-0.5 * values * values)
    )


def norm_parts(row_block, norm_gain, norm_shift):
    centred = row_block - jnp.mean(row_block, axis=-1, keepdims=True)
    inverse = lax.rsqrt(jnp.mean(centred * centred, axis=-1, keepdims=True) + EPSILON)
    normal = centred * inverse
    return (
        normal,
        inverse,
        normal * norm_gain.astype(jnp.float32) + norm_shift.astype(jnp.float32),
    )


def norm_back(grad_out, normal, inverse, norm_gain):
    scaled = grad_out * norm_gain.astype(jnp.float32)
    centre = jnp.mean(scaled, axis=-1, keepdims=True)
    projected = jnp.mean(scaled * normal, axis=-1, keepdims=True)
    return inverse * (scaled - centre - normal * projected)


def assign_targets(length_table, peer_count, group_count):
    doc_count = length_table.shape[1]
    length_grid = jnp.transpose(length_table.reshape(peer_count, group_count, doc_count), (1, 0, 2))
    active = length_grid > 0
    counts = jnp.sum(active.astype(jnp.int32), axis=-1)
    priority = counts * 64 + jnp.arange(peer_count, dtype=jnp.int32)[None, :]
    sender_rank = jnp.sum((priority[:, None, :] > priority[:, :, None]).astype(jnp.int32), axis=-1)
    order_key = (
        sender_rank[:, :, None] * doc_count + jnp.arange(doc_count, dtype=jnp.int32)[None, None, :]
    )
    flat_key = order_key.reshape(group_count, peer_count * doc_count)
    flat_live = active.reshape(group_count, peer_count * doc_count)
    before = flat_live[:, None, :] & (flat_key[:, None, :] < flat_key[:, :, None])
    position = jnp.sum(before.astype(jnp.int32), axis=-1)
    target = jnp.where(position < 2 * peer_count, position // 2, position - 2 * peer_count)
    return jnp.where(flat_live, target, 0).reshape(group_count, peer_count, doc_count)


def slot_ranks(target, live_docs):
    doc_count = target.shape[1]
    same_peer = (target[:, :, None] == target[:, None, :]) & live_docs[:, None, :]
    earlier = jnp.arange(doc_count)[None, :] < jnp.arange(doc_count)[:, None]
    return jnp.sum((same_peer & earlier[None]).astype(jnp.int32), axis=-1)


def send_tables(doc_starts, active_len, target, slot_rank, live_docs, peer_count):
    peer_ids = jnp.arange(peer_count, dtype=jnp.int32)[:, None, None, None]
    slot_ids = jnp.arange(KPEER, dtype=jnp.int32)[None, None, :, None]
    chosen = (
        live_docs[None, :, None, :]
        & (target[None, :, None, :] == peer_ids)
        & (slot_rank[None, :, None, :] == slot_ids)
    )
    send_start = jnp.sum(jnp.where(chosen, doc_starts[None, :, None, :], 0), axis=-1)
    send_len = jnp.sum(jnp.where(chosen, active_len[None, :, None, :], 0), axis=-1)
    return (send_start, send_len)


def pack(source, send_start, send_len):
    group_count, row_len, feature_count = source.shape
    offsets = jnp.arange(SLOT, dtype=jnp.int32)
    row_base = jnp.arange(group_count, dtype=jnp.int32)[None, :, None] * row_len + send_start
    picked = jnp.take(
        source.reshape(group_count * row_len, feature_count), row_base[..., None] + offsets, axis=0
    )
    keep_rows = offsets < send_len[..., None]
    return jnp.where(keep_rows[..., None], picked, jnp.zeros((), source.dtype))


def compact_tables(arrived_len):
    peer_count, group_count, slot_room = arrived_len.shape
    live_flat = jnp.transpose(arrived_len > 0, (1, 0, 2)).reshape(
        group_count, peer_count * slot_room
    )
    live_order = jnp.cumsum(live_flat.astype(jnp.int32), axis=1) - 1
    matched = live_flat[:, None, :] & (
        live_order[:, None, :] == jnp.arange(RECV, dtype=jnp.int32)[None, :, None]
    )
    located = jnp.sum(
        jnp.where(matched, jnp.arange(peer_count * slot_room, dtype=jnp.int32), 0), axis=-1
    )
    group_ids = jnp.arange(group_count, dtype=jnp.int32)
    take_index = (
        located // slot_room * group_count + group_ids[:, None]
    ) * slot_room + located % slot_room
    back_order = jnp.transpose(
        jnp.clip(live_order, 0, RECV - 1).reshape(group_count, peer_count, slot_room), (1, 0, 2)
    )
    put_index = group_ids[None, :, None] * RECV + back_order
    return (take_index.reshape(-1), put_index, arrived_len > 0)


def spread(result_rows, put_index, put_live):
    slot_block = result_rows.reshape(-1, SLOT, result_rows.shape[-1])
    picked = jnp.take(slot_block, put_index, axis=0)
    return jnp.where(put_live[..., None, None], picked, jnp.zeros((), result_rows.dtype))


def unpack(returned, doc_starts, active_len, target, slot_rank, fallback):
    peer_count, group_count, slot_room, slot_len, feature_count = returned.shape
    row_len = fallback.shape[1]
    position = jnp.arange(row_len, dtype=jnp.int32)
    member = (
        jnp.sum((position[None, :, None] >= doc_starts[:, None, :]).astype(jnp.int32), axis=-1) - 1
    )
    offset = position[None, :] - jnp.take_along_axis(doc_starts, member, axis=1)
    inside = offset < jnp.take_along_axis(active_len, member, axis=1)
    holder = jnp.take_along_axis(target, member, axis=1)
    placed_rank = jnp.take_along_axis(slot_rank, member, axis=1)
    group_ids = jnp.arange(group_count, dtype=jnp.int32)[:, None]
    flat_index = (
        (holder * group_count + group_ids) * slot_room + placed_rank
    ) * slot_len + jnp.minimum(offset, slot_len - 1)
    picked = jnp.take(returned.reshape(-1, feature_count), flat_index, axis=0)
    return jnp.where(inside[..., None], picked, fallback)


def score_block(query_heads, key_heads):
    scores = product("sqhd,skhd->shqk", query_heads, key_heads) * 0.125
    causal = jnp.arange(SLOT)[:, None] >= jnp.arange(SLOT)[None, :]
    return (jnp.where(causal, scores, MASKED), causal)


def layer_forward(slot_rows, attn_params, ffn_params, slot_count):
    ln1_gain, ln1_bias, q_weight, q_bias, k_weight, v_weight, v_bias, o_weight, o_bias = attn_params
    ln2_gain, ln2_bias, up_weight, up_bias, down_weight, down_bias = ffn_params
    residual = slot_rows.astype(jnp.float32)
    normal_one, inverse_one, normed_one = norm_parts(residual, ln1_gain, ln1_bias)
    normed_one = normed_one.astype(jnp.bfloat16)
    query = (product("nd,dc->nc", normed_one, q_weight) + q_bias.astype(jnp.float32)).astype(
        jnp.bfloat16
    )
    key_rows = product("nd,dc->nc", normed_one, k_weight).astype(jnp.bfloat16)
    value_rows = (product("nd,dc->nc", normed_one, v_weight) + v_bias.astype(jnp.float32)).astype(
        jnp.bfloat16
    )
    head_shape = (slot_count, SLOT, HEADS, HD)
    scores, causal = score_block(query.reshape(head_shape), key_rows.reshape(head_shape))
    row_max = jnp.max(scores, axis=-1, keepdims=True)
    exponent = jnp.exp(scores - row_max)
    row_total = jnp.sum(exponent, axis=-1, keepdims=True)
    probs = (exponent / row_total).astype(jnp.bfloat16)
    log_total = row_max + jnp.log(row_total)
    context = (
        product("shqk,skhd->sqhd", probs, value_rows.reshape(head_shape))
        .reshape(slot_rows.shape)
        .astype(jnp.bfloat16)
    )
    hidden = residual + product("nc,cd->nd", context, o_weight) + o_bias.astype(jnp.float32)
    normal_two, inverse_two, normed_two = norm_parts(hidden, ln2_gain, ln2_bias)
    normed_two = normed_two.astype(jnp.bfloat16)
    inner = product("nd,df->nf", normed_two, up_weight) + up_bias.astype(jnp.float32)
    activated = smooth_gate(inner).astype(jnp.bfloat16)
    output = hidden + product("nf,fd->nd", activated, down_weight) + down_bias.astype(jnp.float32)
    saved = (
        normal_one,
        inverse_one,
        normed_one,
        query,
        key_rows,
        value_rows,
        log_total,
        context,
        normal_two,
        inverse_two,
        normed_two,
        inner,
        activated,
    )
    return (output.astype(jnp.bfloat16), saved)


def ffn_backward(grad_rows, saved, ffn_params):
    normal_two, inverse_two, inner = (saved[8], saved[9], saved[11])
    ln2_gain, up_weight, down_weight = (ffn_params[0], ffn_params[2], ffn_params[4])
    grad_float = grad_rows.astype(jnp.float32)
    grad_down_bias = jnp.sum(grad_float, axis=0)
    grad_active = product("nd,fd->nf", grad_rows, down_weight)
    grad_inner = (grad_active * smooth_slope(inner)).astype(jnp.bfloat16)
    grad_up_bias = jnp.sum(grad_inner, axis=0, dtype=jnp.float32)
    grad_normed = product("nf,df->nd", grad_inner, up_weight)
    grad_gain = jnp.sum(grad_normed * normal_two, axis=0)
    grad_shift = jnp.sum(grad_normed, axis=0)
    grad_hidden = grad_float + norm_back(grad_normed, normal_two, inverse_two, ln2_gain)
    return (grad_gain, grad_shift, grad_inner, grad_up_bias, grad_down_bias, grad_hidden)


def attn_backward(grad_hidden, saved, attn_params, slot_count):
    normal_one, inverse_one, normed_one, query, key_rows, value_rows, log_total, context = saved[:8]
    ln1_gain, q_weight, k_weight, v_weight, o_weight = (
        attn_params[0],
        attn_params[2],
        attn_params[4],
        attn_params[5],
        attn_params[7],
    )
    grad_out = grad_hidden.astype(jnp.bfloat16)
    grad_o_weight = product("nc,nd->cd", context, grad_out)
    grad_o_bias = jnp.sum(grad_out, axis=0, dtype=jnp.float32)
    grad_context = product("nd,cd->nc", grad_out, o_weight).astype(jnp.bfloat16)
    head_shape = (slot_count, SLOT, HEADS, HD)
    query_heads = query.reshape(head_shape)
    key_heads = key_rows.reshape(head_shape)
    value_heads = value_rows.reshape(head_shape)
    grad_heads = grad_context.reshape(head_shape)
    scores, causal = score_block(query_heads, key_heads)
    probs = jnp.where(causal, jnp.exp(scores - log_total), 0.0)
    grad_probs = product("sqhd,skhd->shqk", grad_heads, value_heads)
    row_dot = jnp.sum(probs * grad_probs, axis=-1, keepdims=True)
    grad_scores = (probs * (grad_probs - row_dot)).astype(jnp.bfloat16)
    grad_query = (
        (product("shqk,skhd->sqhd", grad_scores, key_heads) * 0.125)
        .reshape(grad_hidden.shape)
        .astype(jnp.bfloat16)
    )
    grad_key = (
        (product("shqk,sqhd->skhd", grad_scores, query_heads) * 0.125)
        .reshape(grad_hidden.shape)
        .astype(jnp.bfloat16)
    )
    grad_value = (
        product("shqk,sqhd->skhd", probs.astype(jnp.bfloat16), grad_heads)
        .reshape(grad_hidden.shape)
        .astype(jnp.bfloat16)
    )
    grad_q_weight = product("nd,nc->dc", normed_one, grad_query)
    grad_q_bias = jnp.sum(grad_query, axis=0, dtype=jnp.float32)
    grad_k_weight = product("nd,nc->dc", normed_one, grad_key)
    grad_v_weight = product("nd,nc->dc", normed_one, grad_value)
    grad_v_bias = jnp.sum(grad_value, axis=0, dtype=jnp.float32)
    grad_normed = (
        product("nc,dc->nd", grad_query, q_weight)
        + product("nc,dc->nd", grad_key, k_weight)
        + product("nc,dc->nd", grad_value, v_weight)
    )
    grad_gain = jnp.sum(grad_normed * normal_one, axis=0)
    grad_shift = jnp.sum(grad_normed, axis=0)
    grad_input_rows = (
        grad_hidden + norm_back(grad_normed, normal_one, inverse_one, ln1_gain)
    ).astype(jnp.bfloat16)
    return (
        grad_gain,
        grad_shift,
        grad_q_weight,
        grad_q_bias,
        grad_k_weight,
        grad_v_weight,
        grad_v_bias,
        grad_o_weight,
        grad_o_bias,
        grad_input_rows,
    )


def body(
    tokens,
    cotangent,
    doc_starts,
    active_len,
    ln1_gain,
    ln1_bias,
    q_weight,
    q_bias,
    k_weight,
    v_weight,
    v_bias,
    o_weight,
    o_bias,
    ln2_gain,
    ln2_bias,
    up_weight,
    up_bias,
    down_weight,
    down_bias,
):
    peer_count = lax.axis_size("fsdp")
    group_count = tokens.shape[0]
    feature_count = tokens.shape[2]
    slot_count = group_count * RECV
    length_table = lax.all_gather(active_len, "fsdp", axis=0, tiled=True)
    target_grid = assign_targets(length_table, peer_count, group_count)
    target = jnp.take(target_grid, lax.axis_index("fsdp"), axis=1)
    live_docs = active_len > 0
    slot_rank = slot_ranks(target, live_docs)
    send_start, send_len = send_tables(
        doc_starts, active_len, target, slot_rank, live_docs, peer_count
    )
    outgoing = pack(tokens, send_start, send_len)
    arrived, arrived_len = (
        lax.all_to_all(outgoing, "fsdp", split_axis=0, concat_axis=0, tiled=True),
        lax.all_to_all(send_len, "fsdp", split_axis=0, concat_axis=0, tiled=True),
    )
    take_index, put_index, put_live = compact_tables(arrived_len)
    work_rows = jnp.take(arrived.reshape(-1, SLOT, feature_count), take_index, axis=0).reshape(
        slot_count * SLOT, feature_count
    )
    attn_params = (
        lax.all_gather(ln1_gain, ("dp", "fsdp"), axis=0, tiled=True),
        lax.all_gather(ln1_bias, ("dp", "fsdp"), axis=0, tiled=True),
        lax.all_gather(q_weight, ("dp", "fsdp"), axis=0, tiled=True),
        lax.all_gather(q_bias, ("dp", "fsdp"), axis=0, tiled=True),
        lax.all_gather(k_weight, ("dp", "fsdp"), axis=0, tiled=True),
        lax.all_gather(v_weight, ("dp", "fsdp"), axis=0, tiled=True),
        lax.all_gather(v_bias, ("dp", "fsdp"), axis=0, tiled=True),
        lax.all_gather(o_weight, ("dp", "fsdp"), axis=0, tiled=True),
        lax.all_gather(o_bias, ("dp", "fsdp"), axis=0, tiled=True),
    )
    ffn_params = (
        lax.all_gather(ln2_gain, ("dp", "fsdp"), axis=0, tiled=True),
        lax.all_gather(ln2_bias, ("dp", "fsdp"), axis=0, tiled=True),
        lax.all_gather(up_weight, ("dp", "fsdp"), axis=0, tiled=True),
        lax.all_gather(up_bias, ("dp", "fsdp"), axis=0, tiled=True),
        lax.all_gather(down_weight, ("dp", "fsdp"), axis=0, tiled=True),
        lax.all_gather(down_bias, ("dp", "fsdp"), axis=0, tiled=True),
    )
    out_rows, saved = layer_forward(work_rows, attn_params, ffn_params, slot_count)
    returned = lax.all_to_all(
        spread(out_rows, put_index, put_live), "fsdp", split_axis=0, concat_axis=0, tiled=True
    )
    layer_out = unpack(returned, doc_starts, active_len, target, slot_rank, tokens)
    grad_arrived = lax.all_to_all(
        pack(cotangent, send_start, send_len), "fsdp", split_axis=0, concat_axis=0, tiled=True
    )
    grad_rows = jnp.take(grad_arrived.reshape(-1, SLOT, feature_count), take_index, axis=0).reshape(
        slot_count * SLOT, feature_count
    )
    attn_params = (
        lax.all_gather(ln1_gain, ("dp", "fsdp"), axis=0, tiled=True),
        lax.all_gather(ln1_bias, ("dp", "fsdp"), axis=0, tiled=True),
        lax.all_gather(q_weight, ("dp", "fsdp"), axis=0, tiled=True),
        lax.all_gather(q_bias, ("dp", "fsdp"), axis=0, tiled=True),
        lax.all_gather(k_weight, ("dp", "fsdp"), axis=0, tiled=True),
        lax.all_gather(v_weight, ("dp", "fsdp"), axis=0, tiled=True),
        lax.all_gather(v_bias, ("dp", "fsdp"), axis=0, tiled=True),
        lax.all_gather(o_weight, ("dp", "fsdp"), axis=0, tiled=True),
        lax.all_gather(o_bias, ("dp", "fsdp"), axis=0, tiled=True),
    )
    ffn_params = (
        lax.all_gather(ln2_gain, ("dp", "fsdp"), axis=0, tiled=True),
        lax.all_gather(ln2_bias, ("dp", "fsdp"), axis=0, tiled=True),
        lax.all_gather(up_weight, ("dp", "fsdp"), axis=0, tiled=True),
        lax.all_gather(up_bias, ("dp", "fsdp"), axis=0, tiled=True),
        lax.all_gather(down_weight, ("dp", "fsdp"), axis=0, tiled=True),
        lax.all_gather(down_bias, ("dp", "fsdp"), axis=0, tiled=True),
    )
    gain_two, shift_two, grad_inner, up_bias_term, down_bias_term, grad_hidden = ffn_backward(
        grad_rows, saved, ffn_params
    )
    normed_two, activated = (saved[10], saved[12])
    (
        gain_one,
        shift_one,
        query_term,
        query_bias_term,
        key_term,
        value_term,
        value_bias_term,
        out_term,
        out_bias_term,
        grad_input_rows,
    ) = attn_backward(grad_hidden, saved, attn_params, slot_count)
    up_term = product("nd,nf->df", normed_two, grad_inner)
    down_term = product("nf,nd->fd", activated, grad_rows)
    ffn_grads = (
        lax.psum_scatter(gain_two, ("dp", "fsdp"), scatter_dimension=0, tiled=True),
        lax.psum_scatter(shift_two, ("dp", "fsdp"), scatter_dimension=0, tiled=True),
        lax.psum_scatter(up_term, ("dp", "fsdp"), scatter_dimension=0, tiled=True),
        lax.psum_scatter(up_bias_term, ("dp", "fsdp"), scatter_dimension=0, tiled=True),
        lax.psum_scatter(down_term, ("dp", "fsdp"), scatter_dimension=0, tiled=True),
        lax.psum_scatter(down_bias_term, ("dp", "fsdp"), scatter_dimension=0, tiled=True),
    )
    attn_grads = (
        lax.psum_scatter(gain_one, ("dp", "fsdp"), scatter_dimension=0, tiled=True),
        lax.psum_scatter(shift_one, ("dp", "fsdp"), scatter_dimension=0, tiled=True),
        lax.psum_scatter(query_term, ("dp", "fsdp"), scatter_dimension=0, tiled=True),
        lax.psum_scatter(query_bias_term, ("dp", "fsdp"), scatter_dimension=0, tiled=True),
        lax.psum_scatter(key_term, ("dp", "fsdp"), scatter_dimension=0, tiled=True),
        lax.psum_scatter(value_term, ("dp", "fsdp"), scatter_dimension=0, tiled=True),
        lax.psum_scatter(value_bias_term, ("dp", "fsdp"), scatter_dimension=0, tiled=True),
        lax.psum_scatter(out_term, ("dp", "fsdp"), scatter_dimension=0, tiled=True),
        lax.psum_scatter(out_bias_term, ("dp", "fsdp"), scatter_dimension=0, tiled=True),
    )
    grad_returned = lax.all_to_all(
        spread(grad_input_rows, put_index, put_live),
        "fsdp",
        split_axis=0,
        concat_axis=0,
        tiled=True,
    )
    input_grad = unpack(grad_returned, doc_starts, active_len, target, slot_rank, cotangent)
    return (layer_out, input_grad) + tuple(attn_grads) + tuple(ffn_grads)


def solution(mesh):
    in_specs = (
        P(("dp", "fsdp"), None, None),
        P(("dp", "fsdp"), None, None),
        P(("dp", "fsdp"), None),
        P(("dp", "fsdp"), None),
        P(("dp", "fsdp")),
        P(("dp", "fsdp")),
        P(("dp", "fsdp"), None),
        P(("dp", "fsdp")),
        P(("dp", "fsdp"), None),
        P(("dp", "fsdp"), None),
        P(("dp", "fsdp")),
        P(("dp", "fsdp"), None),
        P(("dp", "fsdp")),
        P(("dp", "fsdp")),
        P(("dp", "fsdp")),
        P(("dp", "fsdp"), None),
        P(("dp", "fsdp")),
        P(("dp", "fsdp"), None),
        P(("dp", "fsdp")),
    )
    out_specs = (
        P(("dp", "fsdp"), None, None),
        P(("dp", "fsdp"), None, None),
        P(("dp", "fsdp")),
        P(("dp", "fsdp")),
        P(("dp", "fsdp"), None),
        P(("dp", "fsdp")),
        P(("dp", "fsdp"), None),
        P(("dp", "fsdp"), None),
        P(("dp", "fsdp")),
        P(("dp", "fsdp"), None),
        P(("dp", "fsdp")),
        P(("dp", "fsdp")),
        P(("dp", "fsdp")),
        P(("dp", "fsdp"), None),
        P(("dp", "fsdp")),
        P(("dp", "fsdp"), None),
        P(("dp", "fsdp")),
    )
    return jax.shard_map(body, mesh=mesh, in_specs=in_specs, out_specs=out_specs, check_vma=False)
```

profile of v0, /device:TPU:0, one launch (start us, length us, event | category | flops | bytes accessed | tf_op | source)
XLA Modules:
  0.0 5539.2 jit_solution(5266568608176709535)
XLA Ops:
  11.2 12.6 all-gather
  30.1 11.6 gather_fusion.4
  41.7 11.5 gather_fusion
  53.4 6.1 select_select_fusion.1
  59.5 156.4 %all_to_all.25 = bf16[4,1,2,128,2048]{4,3,2,1,0:T(8,128)(2,1)} all-to-all(bf16[4,1,2,128,2048]{4,3,2,1,0:T(8,128)(2,1)} %get-tuple-element.72), channel_id=1, replica_groups=mesh['dp'=8,'fsdp'=4] {'fsdp'}, dimensions={0} | all-to-all | bytes 8388608 | tf_op jit(solution)/shard_map/all_to_all | solution.py:353
  223.2 150.4 %all-reduce.18 = (bf16[2048]{0:T(1024)(128)(2,1)S(1)}, bf16[2048]{0:T(1024)(128)(2,1)S(1)}, bf16[2048]{0:T(1024)(128)(2,1)S(1)}, bf16[2048]{0:T(1024)(128)(2,1)S...) all-reduce(bf16[2048]{0:T(1024)(128)(2,1)S(1)} %dynamic-update-slic, ...), channel_id=1, replica_groups=mesh['dp'=8,'fsdp'=4] {'dp','fsdp'}, use_global_device_ids=true, to_apply=%add.4 | all-reduce | flops 16384 | bytes 65536
  373.6 65.7 %all-gather.1 = bf16[32,1,256]{2,1,0:T(2,128)(2,1)S(1)} all-gather(bf16[1,1,256]{2,1,0:T(2,128)(2,1)S(1)} %reshape.1344), channel_id=1, replica_groups=mesh['dp'=8,'fsdp'=4] {'dp','fsdp'}, dimensions={0}, use_global_device_ids=true | all-gather | bytes 16896 | tf_op jit(solution)/shard_map/all_gather | solution.py:344
  454.9 8.4 convolution_convert_fusion.1
  463.4 5.7 reshape.1408
  473.6 9.7 add_convert_fusion.3
  483.3 5.7 reshape.1406
  489.0 5.4 copy.133
  494.4 8.5 add_convert_fusion.2
  502.9 5.7 reshape.1407
  508.6 5.6 copy.131
  524.5 6.7 fusion.94
  533.8 97.5 %all-gather.17.cloned.1.call-done = bf16[2048,8192]{1,0:T(8,128)(2,1)} async-done(((bf16[64,8192]{1,0:T(8,128)(2,1)}), bf16[2048,8192]{1,0:T(8,128)(2,1)}) %all-gather.17.cloned.1.call-update) | async-done | bytes 33554448 | tf_op jit(solution)/shard_map/all_gather | solution.py:343
  631.3 23.4 convolution_add_fusion
  654.7 172.4 %all-gather.19.cloned.1.call-done = bf16[8192,2048]{1,0:T(8,128)(2,1)} async-done(((bf16[256,2048]{1,0:T(8,128)(2,1)}), bf16[8192,2048]{1,0:T(8,128)(2,1)}) %all-gather.19.cloned.1.call-update) | async-done | bytes 33554448 | tf_op jit(solution)/shard_map/all_gather | solution.py:345
  827.1 23.8 convert_reduce_fusion
  850.9 20.8 multiply_reduce_fusion.1
  875.4 6.9 convolution_convert_fusion
  886.5 5.6 copy.138
  892.1 6.8 convert_reduce_fusion.4
  915.6 9.4 fusion.42
  925.1 9.1 fusion.46
  934.3 8.4 fusion.27
  942.8 12.9 fusion.48
  957.4 8.2 fusion.37
  965.7 9.9 fusion.44
  975.7 9.9 fusion.40
  987.0 31.5 fusion.89
  1020.3 29.0 fusion.88
  1050.2 20.7 add_convert_fusion
  1082.4 5.4 select_select_fusion
  1087.8 197.2 %all_to_all.26 = bf16[4,1,2,128,2048]{4,3,2,1,0:T(8,128)(2,1)} all-to-all(bf16[4,1,2,128,2048]{4,3,2,1,0:T(8,128)(2,1)S(1)} %get-tuple-element.85), channel_id=1, replica_groups=mesh['dp'=8,'fsdp'=4] {'fsdp'}, dimensions={0} | all-to-all | bytes 8388608 | tf_op jit(solution)/shard_map/all_to_all | solution.py:415
  1285.0 5.2 all-to-all-start.2
  1293.6 10.3 and_reduce_fusion
  1315.3 11.5 gather_fusion.7
  1326.9 136.2 %all-to-all-done.2 = bf16[4,1,2,128,2048]{4,3,2,1,0:T(8,128)(2,1)} async-done(((bf16[4,1,2,128,2048]{4,3,2,1,0:T(8,128)(2,1)}), bf16[4,1,2,128,2048]{4,3,2,1,0:T(8,128)(2,1)}, u32[]{:S(2)}, u32[]{:S(2)}) %all-to-all-start.2) | async-done | bytes 4194336 | tf_op jit(solution)/shard_map/all_to_all | solution.py:349
  1463.0 11.6 gather_fusion.3
  1474.6 10.1 fusion.6
  1484.7 123.2 %reduce-scatter.13.cloned.1.call-done = f32[64,2048]{1,0:T(8,128)} async-done(((f32[2048,2048]{1,0:T(8,128)}), f32[64,2048]{1,0:T(8,128)}) %reduce-scatter.13.cloned.1.call-update) | async-done | bytes 524304 | tf_op jit(solution)/shard_map/reduce_scatter | solution.py:412
  1607.9 368.9 %reduce-scatter.11.cloned.1.call-done = f32[64,2048]{1,0:T(8,128)} async-done(((f32[2048,2048]{1,0:T(8,128)}), f32[64,2048]{1,0:T(8,128)}) %reduce-scatter.11.cloned.1.call-update) | async-done | bytes 524304 | tf_op jit(solution)/shard_map/reduce_scatter | solution.py:410
  1976.9 365.0 %reduce-scatter.7.cloned.1.call-done = f32[64,2048]{1,0:T(8,128)} async-done(((f32[2048,2048]{1,0:T(8,128)}), f32[64,2048]{1,0:T(8,128)}) %reduce-scatter.7.cloned.1.call-update) | async-done | bytes 524304 | tf_op jit(solution)/shard_map/reduce_scatter | solution.py:407
  2341.9 365.2 %reduce-scatter.9.cloned.1.call-done = f32[64,2048]{1,0:T(8,128)} async-done(((f32[2048,2048]{1,0:T(8,128)}), f32[64,2048]{1,0:T(8,128)}) %reduce-scatter.9.cloned.1.call-update) | async-done | bytes 524304 | tf_op jit(solution)/shard_map/reduce_scatter | solution.py:409
  2707.0 1411.5 %reduce-scatter.17.cloned.1.call-done = f32[256,2048]{1,0:T(8,128)} async-done(((f32[8192,2048]{1,0:T(8,128)}), f32[256,2048]{1,0:T(8,128)}) %reduce-scatter.17.cloned.1.call-update) | async-done | bytes 2097168 | tf_op jit(solution)/shard_map/reduce_scatter | solution.py:401
  4118.5 1413.7 %reduce-scatter.15.cloned.1.call-done = f32[64,8192]{1,0:T(8,128)} async-done(((f32[2048,8192]{1,0:T(8,128)}), f32[64,8192]{1,0:T(8,128)}) %reduce-scatter.15.cloned.1.call-update) | async-done | bytes 2097168 | tf_op jit(solution)/shard_map/reduce_scatter | solution.py:399
  (280 shorter events, 107.3 us)
Async XLA Ops:
  7.2 18.3 copy-start.38
  7.2 447.7 %all-gather.13.cloned.1.call-start = ((), (), s32[]{:S(2)}) async-start(), calls=%async_computation.13 | async-start | bytes 8650752 | tf_op jit(solution)/shard_map/all_gather | solution.py:334
  7.9 465.7 %all-gather.9.cloned.1.call-start = ((), (), s32[]{:S(2)}) async-start(), calls=%async_computation.11 | async-start | bytes 8650752 | tf_op jit(solution)/shard_map/all_gather | solution.py:335
  8.7 485.7 %all-gather.11.cloned.1.call-start = ((), (), s32[]{:S(2)}) async-start(), calls=%async_computation.12 | async-start | bytes 8650752 | tf_op jit(solution)/shard_map/all_gather | solution.py:332
  9.4 515.1 %all-gather.15.cloned.1.call-start = ((), (), s32[]{:S(2)}) async-start(), calls=%async_computation.14 | async-start | bytes 8650752 | tf_op jit(solution)/shard_map/all_gather | solution.py:337
  10.0 621.3 %all-gather.17.cloned.1.call-start = ((), (), s32[]{:S(2)}) async-start(), calls=%async_computation.15 | async-start | bytes 34603008 | tf_op jit(solution)/shard_map/all_gather | solution.py:343
  10.6 816.5 %all-gather.19.cloned.1.call-start = ((), (), s32[]{:S(2)}) async-start(), calls=%async_computation.16 | async-start | bytes 34603008 | tf_op jit(solution)/shard_map/all_gather | solution.py:345
  26.6 32.9 all-to-all-start
  216.0 5.9 copy-start.53
  216.0 6.2 copy-start.54
  216.0 6.4 copy-start.55
  216.0 6.7 copy-start.56
  216.0 6.9 copy-start.57
  216.0 227.9 %all-to-all-start.1 = ((bf16[4,1,2,128,2048]{4,3,2,1,0:T(8,128)(2,1)}), bf16[4,1,2,128,2048]{4,3,2,1,0:T(8,128)(2,1)}, u32[]{:S(2)}, u32[]{:S(2)}) async-start(bf16[4,1,2,128,2048]{4,3,2,1,0:T(8,128)(2,1)} %get-tuple-element.73), calls=%async_computation.1 | async-start | bytes 8388608 | tf_op jit(solution)/shard_map/all_to_all | solution.py:322
  221.1 1082.8 %all-reduce.21.cloned.1.call-start = ((), (), s32[]{:S(2)}) async-start(), calls=%async_computation.23 | async-start | bytes 196608
  373.5 80.7 %copy-start.23 = (f32[2048]{0:T(1024)}, f32[2048]{0:T(1024)S(1)}, u32[]{:S(2)}) copy-start(f32[2048]{0:T(1024)S(1)} %convert_element_type.228) | copy-start | bytes 24580
  373.6 80.7 %copy-start.26 = (f32[2048]{0:T(1024)}, f32[2048]{0:T(1024)S(1)}, u32[]{:S(2)}) copy-start(f32[2048]{0:T(1024)S(1)} %convert_element_type.229) | copy-start | bytes 24580
  373.6 257.7 %copy-start.21 = (f32[2048]{0:T(1024)}, f32[2048]{0:T(1024)S(1)}, u32[]{:S(2)}) copy-start(f32[2048]{0:T(1024)S(1)} %convert_element_type.242) | copy-start | bytes 24580
  452.5 72.1 %copy-start.1 = (bf16[3,128,2048]{2,1,0:T(8,128)(2,1)}, bf16[3,128,2048]{2,1,0:T(8,128)(2,1)S(1)}, u32[]{:S(2)}) copy-start(bf16[3,128,2048]{2,1,0:T(8,128)(2,1)S(1)} %get-tuple-element.88) | copy-start | bytes 4718596
  452.5 10.9 copy-start.28
  454.2 9.2 copy-start.31
  454.9 8.5 copy-start.20
  473.6 40.6 copy-start.8
  631.3 195.8 %copy-start.11 = (bf16[3,128,2048]{2,1,0:T(8,128)(2,1)S(1)}, bf16[3,128,2048]{2,1,0:T(8,128)(2,1)}, u32[]{:S(2)}) copy-start(bf16[3,128,2048]{2,1,0:T(8,128)(2,1)} %get-tuple-element.61) | copy-start | bytes 4718596
  827.1 23.8 copy-start.5
  886.5 12.4 slice-start
  892.1 6.8 slice-start.1
  892.1 6.8 copy-start.18
  892.1 6.8 copy-start.19
  914.1 10.9 copy-start.13
  915.6 9.4 copy-start.14
  915.6 18.6 slice-start.2
  925.1 9.2 copy-start.2
  925.1 9.2 copy-start.15
  925.1 9.2 copy-start.24
  925.1 9.2 copy-start.29
  925.1 9.2 copy-start.32
  925.1 9.2 slice-start.3
  942.8 665.2 %reduce-scatter.13.cloned.1.call-start = ((), (), s32[]{:S(2)}) async-start(), calls=%async_computation.20 | async-start | bytes 17301504 | tf_op jit(solution)/shard_map/reduce_scatter | solution.py:412
  955.7 1021.2 %reduce-scatter.11.cloned.1.call-start = ((), (), s32[]{:S(2)}) async-start(), calls=%async_computation.19 | async-start | bytes 17301504 | tf_op jit(solution)/shard_map/reduce_scatter | solution.py:410
  965.6 1376.2 %reduce-scatter.7.cloned.1.call-start = ((), (), s32[]{:S(2)}) async-start(), calls=%async_computation.17 | async-start | bytes 17301504 | tf_op jit(solution)/shard_map/reduce_scatter | solution.py:407
  975.6 1731.4 %reduce-scatter.9.cloned.1.call-start = ((), (), s32[]{:S(2)}) async-start(), calls=%async_computation.18 | async-start | bytes 17301504 | tf_op jit(solution)/shard_map/reduce_scatter | solution.py:409
  985.6 3133.0 %reduce-scatter.17.cloned.1.call-start = ((), (), s32[]{:S(2)}) async-start(), calls=%async_computation.22 | async-start | bytes 69206016 | tf_op jit(solution)/shard_map/reduce_scatter | solution.py:401
  1018.5 4513.8 %reduce-scatter.15.cloned.1.call-start = ((), (), s32[]{:S(2)}) async-start(), calls=%async_computation.21 | async-start | bytes 69206016 | tf_op jit(solution)/shard_map/reduce_scatter | solution.py:399
  1285.0 5.9 copy-start.39
  1285.0 6.5 copy-start.37
  1285.0 7.8 copy-start.41
  1285.0 178.0 %all-to-all-start.2 = ((bf16[4,1,2,128,2048]{4,3,2,1,0:T(8,128)(2,1)}), bf16[4,1,2,128,2048]{4,3,2,1,0:T(8,128)(2,1)}, u32[]{:S(2)}, u32[]{:S(2)}) async-start(bf16[4,1,2,128,2048]{4,3,2,1,0:T(8,128)(2,1)} %get-tuple-element.86), calls=%async_computation.2 | async-start | bytes 8388608 | tf_op jit(solution)/shard_map/all_to_all | solution.py:349
  (30 other events, 78.6 us)
Sparse Core Ops, SparseCore 0:
  11.0 104.1 all-gather.12
  118.1 100.1 all-gather.8
  221.3 134.1 all-gather.10
  358.3 76.7 all-gather.14
  437.9 193.4 all-gather.16
  634.1 192.9 all-gather.18
  942.9 123.3 all-reduce.20
  1069.2 538.6 reduce-scatter.12
  1610.9 365.9 reduce-scatter.10
  1979.7 362.1 reduce-scatter.6
  2344.9 362.1 reduce-scatter.8
  2709.9 1408.5 reduce-scatter.16
  4121.6 1410.5 reduce-scatter.14
where the time goes:
time: 5550 us; the launch traced here: 5540 us
  waiting for transfers between devices  4460 us (80%)
  blocking collectives  582 us (10%)
  matrix products  274 us (5%)
  local copies, waits for them, and re-layouts  143 us (3%)
    reduce_scatter x1, waiting for transfers between devices, body(): lax.psum_scatter(up_term, ('dp', 'fsdp'), scatter_dimension=0, tiled=True)  1410 us
    reduce_scatter x1, waiting for transfers between devices, body(): lax.psum_scatter(down_term, ('dp', 'fsdp'), scatter_dimension=0, tiled=True)  1410 us
    reduce_scatter x1, waiting for transfers between devices, body(): lax.psum_scatter(value_term, ('dp', 'fsdp'), scatter_dimension=0, tiled=T...  369 us
    reduce_scatter x1, waiting for transfers between devices, body(): lax.psum_scatter(key_term, ('dp', 'fsdp'), scatter_dimension=0, tiled=True)  365 us
    reduce_scatter x1, waiting for transfers between devices, body(): lax.psum_scatter(query_term, ('dp', 'fsdp'), scatter_dimension=0, tiled=T...  365 us
    dot_general x24, matrix products, product(): jnp.einsum(einsum_form, factor_one, factor_two, preferred_element_type=jn...  274 us
    all_to_all x1, blocking collectives, body(): lax.all_to_all(spread(grad_input_rows, put_index, put_live), 'fsdp', spli...  197 us
    all_gather x1, waiting for transfers between devices, body(): lax.all_gather(down_weight, ('dp', 'fsdp'), axis=0, tiled=True)  172 us
  transfers between devices with their start and end apart: 16, of which 9 were waited for; matrix products, arithmetic and copies ran while one was open for 6% of the time, Pallas kernels for 0%

commit v1 on v0

v1 whole, which is shorter than its diff:
```python
import jax
import jax.numpy as jnp
from jax import lax
from jax.sharding import PartitionSpec as P

HEADS = 32
HD = 64
SLOT = 128
TEAM = 4

EPSILON = 1e-05
MASKED = -1e30
ROOT_HALF = 0.7071067811865476
DENSITY_SCALE = 0.3989422804014327
BF = jnp.bfloat16
F32 = jnp.float32
BOTH = ("dp", "fsdp")


def dot(a, b, ca, cb):
    return lax.dot_general(a, b, (((ca,), (cb,)), ((), ())), preferred_element_type=F32)


def smooth_gate(values):
    return values * (0.5 + 0.5 * lax.erf(values * ROOT_HALF))


def smooth_slope(values):
    return (
        0.5
        + 0.5 * lax.erf(values * ROOT_HALF)
        + values * DENSITY_SCALE * jnp.exp(-0.5 * values * values)
    )


def norm_parts(row_block, gain, shift):
    centred = row_block - jnp.mean(row_block, axis=-1, keepdims=True)
    inverse = lax.rsqrt(jnp.mean(centred * centred, axis=-1, keepdims=True) + EPSILON)
    normal = centred * inverse
    return normal, inverse, (normal * gain + shift).astype(BF)


def norm_back(grad_out, normal, inverse, gain):
    scaled = grad_out * gain
    centre = jnp.mean(scaled, axis=-1, keepdims=True)
    projected = jnp.mean(scaled * normal, axis=-1, keepdims=True)
    return inverse * (scaled - centre - normal * projected)


def team_swap(a, flip):
    size = lax.axis_size("dp")
    return lax.ppermute(a, "dp", [(i, i ^ flip) for i in range(size)])


def team_gather(own):
    two = jnp.concatenate([own, team_swap(own, 2)], axis=0)
    return jnp.concatenate([two, team_swap(two, 1)], axis=0)


def team_scatter(partial):
    half = partial.shape[0] // 2
    other = team_swap(partial[half:].astype(BF), 1)
    two = partial[:half] + other.astype(F32)
    quarter = half // 2
    last = team_swap(two[quarter:].astype(BF), 2)
    return two[:quarter] + last.astype(F32)


def by_team(stacked, member):
    odd = (member & 1) == 1
    high = (member & 2) == 2
    a = [jnp.where(odd, stacked[i ^ 1], stacked[i]) for i in range(4)]
    return [jnp.where(high, a[i ^ 2], a[i]) for i in range(4)]


def ring_order(size):
    return list(range(0, size, 2)) + list(range(1, size, 2))[::-1]


def outer_pass(a):
    outer = lax.axis_size("dp") // TEAM
    order = ring_order(outer)
    pairs = []
    for p, o in enumerate(order):
        nxt = order[(p + 1) % outer]
        pairs += [(o * TEAM + t, nxt * TEAM + t) for t in range(TEAM)]
    return lax.ppermute(a, "dp", pairs)


def outer_place(me):
    outer = lax.axis_size("dp") // TEAM
    order = ring_order(outer)
    place = [0] * outer
    for p, o in enumerate(order):
        place[o] = p
    return jnp.asarray(order, jnp.int32), jnp.asarray(place, jnp.int32)[me]


def outer_gather(a, me):
    outer = lax.axis_size("dp") // TEAM
    if outer == 1:
        return a[None]
    if outer == 2:
        b = outer_pass(a)
        first = me == 0
        return jnp.stack([jnp.where(first, a, b), jnp.where(first, b, a)])
    order, place = outer_place(me)
    whole = jnp.zeros((outer,) + a.shape, a.dtype)
    whole = lax.dynamic_update_index_in_dim(whole, a, me, 0)
    moving = a
    for step in range(1, outer):
        moving = outer_pass(moving)
        source = order[(place - step) % outer]
        whole = lax.dynamic_update_index_in_dim(whole, moving, source, 0)
    return whole


def outer_scatter(blocks, me):
    outer = lax.axis_size("dp") // TEAM
    if outer == 1:
        return blocks[0]
    order, place = outer_place(me)
    moving = lax.dynamic_index_in_dim(blocks, order[(place - 1) % outer], 0, False)
    for step in range(1, outer):
        moving = outer_pass(moving)
        mine = lax.dynamic_index_in_dim(blocks, order[(place - 1 - step) % outer], 0, False)
        moving = (moving.astype(F32) + mine.astype(F32)).astype(BF)
    return moving


def deal_columns(shard, member, outer, depth):
    r = shard.shape[0]
    parts = shard.reshape(r, outer, TEAM, depth, -1)
    got = []
    for flip in range(TEAM):
        piece = lax.dynamic_index_in_dim(parts, member ^ flip, 2, False).reshape(r, -1)
        got.append(piece if flip == 0 else team_swap(piece, flip))
    return jnp.concatenate(by_team(got, member), axis=0)


def return_columns(block, member, outer, depth):
    r, c = block.shape[0] // TEAM, block.shape[1]
    parts = block.reshape(TEAM, r, c)
    got = []
    for flip in range(TEAM):
        piece = lax.dynamic_index_in_dim(parts, member ^ flip, 0, False)
        got.append(piece if flip == 0 else team_swap(piece, flip))
    cols = jnp.stack([g.reshape(r, outer, depth, -1) for g in by_team(got, member)], axis=2)
    return cols.reshape(r, -1).astype(F32)


def score_block(query_heads, key_heads):
    scores = jnp.einsum("sqhd,skhd->shqk", query_heads, key_heads, preferred_element_type=F32) * 0.125
    causal = jnp.arange(SLOT)[:, None] >= jnp.arange(SLOT)[None, :]
    return jnp.where(causal, scores, MASKED), causal


def body(
    tokens,
    cotangent,
    doc_starts,
    active_len,
    ln1_gain,
    ln1_bias,
    q_weight,
    q_bias,
    k_weight,
    v_weight,
    v_bias,
    o_weight,
    o_bias,
    ln2_gain,
    ln2_bias,
    up_weight,
    up_bias,
    down_weight,
    down_bias,
):
    depth = lax.axis_size("fsdp")
    devices = lax.axis_size("dp") * depth
    outer = lax.axis_size("dp") // TEAM
    dp = lax.axis_index("dp")
    member, me = dp % TEAM, dp // TEAM
    groups, row_len, width = tokens.shape
    docs = doc_starts.shape[1]
    r = q_weight.shape[0]
    hidden_block = down_weight.shape[0]
    part_width = width // TEAM

    vectors = (ln1_gain, ln1_bias, o_bias, ln2_gain, ln2_bias, down_bias, q_bias, v_bias, up_bias)
    packed = lax.all_gather(jnp.concatenate(vectors), BOTH, axis=0, tiled=False)
    edges = [0]
    for v in vectors:
        edges.append(edges[-1] + v.shape[0])
    pieces = [packed[:, edges[i] : edges[i + 1]] for i in range(len(vectors))]
    gain1, shift1, bias_o, gain2, shift2, bias_down = [p.reshape(-1).astype(F32) for p in pieces[:6]]

    def member_part(p):
        whole = p.reshape(outer, TEAM, depth, -1)
        return lax.dynamic_index_in_dim(whole, member, 1, False).reshape(-1).astype(F32)

    bias_q, bias_v, bias_up = [member_part(p) for p in pieces[6:]]

    position = jnp.arange(row_len, dtype=jnp.int32)
    offset = jnp.arange(SLOT, dtype=jnp.int32)
    wanted = doc_starts[:, :, None] + offset
    live = offset < active_len[:, :, None]
    chosen = (wanted[..., None] == position) & live[..., None]
    chosen = chosen.reshape(groups, docs * SLOT, row_len)
    select = chosen.astype(BF)
    covered = jnp.any(chosen, axis=1)

    def pack(source):
        picked = jnp.einsum("gst,gtd->gsd", select, source, preferred_element_type=F32)
        return picked.reshape(groups * docs * SLOT, width).astype(BF)

    def unpack(slot_rows, fallback):
        blocks = slot_rows.astype(BF).reshape(groups, docs * SLOT, width)
        placed = jnp.einsum("gst,gsd->gtd", select, blocks, preferred_element_type=F32).astype(BF)
        return jnp.where(covered[..., None], placed, fallback)

    x_rows = pack(tokens)
    residual = x_rows.astype(F32)
    normal1, inverse1, a_own = norm_parts(residual, gain1, shift1)
    a_all = team_gather(a_own)

    qkv_deal = jnp.concatenate(
        [deal_columns(w, member, outer, depth) for w in (q_weight, k_weight, v_weight)], axis=1
    )
    up_deal = deal_columns(up_weight, member, outer, depth)

    def depth_gather(a):
        return lax.all_gather(a, "fsdp", axis=0, tiled=True)

    def natural(stacked):
        c = stacked.shape[-1]
        return stacked.reshape(outer, depth, TEAM, r, c).transpose(0, 2, 1, 3, 4).reshape(width, c)

    w_qkv = natural(outer_gather(depth_gather(qkv_deal), me))
    w_o = outer_gather(depth_gather(o_weight), me).reshape(part_width, width)
    w_up = natural(outer_gather(depth_gather(up_deal), me))
    w_down = outer_gather(depth_gather(down_weight), me).reshape(-1, width)

    g_rows = pack(cotangent)
    g_all = team_gather(g_rows)

    rows = a_all.shape[0]
    slots = rows // SLOT
    heads = part_width // HD
    zero = jnp.zeros_like(bias_q)
    qkv = (dot(a_all, w_qkv, 1, 0) + jnp.concatenate([bias_q, zero, bias_v])).astype(BF)
    shape = (slots, SLOT, heads, HD)
    q, k, v = [qkv[:, i * part_width : (i + 1) * part_width].reshape(shape) for i in range(3)]
    scores, causal = score_block(q, k)
    row_max = jnp.max(scores, axis=-1, keepdims=True)
    exponent = jnp.exp(scores - row_max)
    total = jnp.sum(exponent, axis=-1, keepdims=True)
    probs = exponent / total
    probs_low = probs.astype(BF)
    context = jnp.einsum("shqk,skhd->sqhd", probs_low, v, preferred_element_type=F32)
    context = context.reshape(rows, part_width).astype(BF)
    hidden = residual + team_scatter(dot(context, w_o, 1, 0)) + bias_o
    normal2, inverse2, b_own = norm_parts(hidden, gain2, shift2)
    b_all = team_gather(b_own)
    inner = dot(b_all, w_up, 1, 0) + bias_up
    activated = smooth_gate(inner).astype(BF)
    y_rows = hidden + team_scatter(dot(activated, w_down, 1, 0)) + bias_down
    layer_out = unpack(y_rows, tokens)

    def depth_scatter(a):
        return lax.psum_scatter(a, "fsdp", scatter_dimension=0, tiled=True)

    def reduce_rows(grad):
        blocks = grad.astype(BF).reshape(outer, -1, grad.shape[1])
        return depth_scatter(outer_scatter(blocks, me))

    def reduce_natural(grad):
        c = grad.shape[1]
        blocks = grad.astype(BF).reshape(outer, TEAM, depth, r, c).transpose(0, 2, 1, 3, 4)
        return depth_scatter(outer_scatter(blocks.reshape(outer, -1, c), me))

    grad_down = reduce_rows(dot(activated, g_all, 0, 0)).astype(F32)
    d_inner_float = dot(g_all, w_down, 1, 1) * smooth_slope(inner)
    d_inner = d_inner_float.astype(BF)
    d_normed2 = team_scatter(dot(d_inner, w_up, 1, 1))
    grad_up = reduce_natural(dot(b_all, d_inner, 0, 0))
    grad_up = return_columns(grad_up, member, outer, depth)
    g_float = g_rows.astype(F32)
    d_hidden = g_float + norm_back(d_normed2, normal2, inverse2, gain2)
    d_out = d_hidden.astype(BF)
    d_out_all = team_gather(d_out)

    d_context = dot(d_out_all, w_o, 1, 1).astype(BF).reshape(shape)
    grad_o = reduce_rows(dot(context, d_out_all, 0, 0)).astype(F32)
    d_probs = jnp.einsum("sqhd,skhd->shqk", d_context, v, preferred_element_type=F32)
    row_dot = jnp.sum(probs * d_probs, axis=-1, keepdims=True)
    d_scores = (probs * (d_probs - row_dot)).astype(BF)
    d_q = (jnp.einsum("shqk,skhd->sqhd", d_scores, k, preferred_element_type=F32) * 0.125).astype(BF)
    d_k = (jnp.einsum("shqk,sqhd->skhd", d_scores, q, preferred_element_type=F32) * 0.125).astype(BF)
    d_v = jnp.einsum("shqk,sqhd->skhd", probs_low, d_context, preferred_element_type=F32).astype(BF)
    d_qkv = jnp.concatenate([d.reshape(rows, part_width) for d in (d_q, d_k, d_v)], axis=1)
    grad_qkv = reduce_natural(dot(a_all, d_qkv, 0, 0))
    grad_q, grad_k, grad_v = [
        return_columns(grad_qkv[:, i * part_width : (i + 1) * part_width], member, outer, depth)
        for i in range(3)
    ]
    d_normed1 = team_scatter(dot(d_qkv, w_qkv, 1, 1))
    d_input = d_hidden + norm_back(d_normed1, normal1, inverse1, gain1)
    input_grad = unpack(d_input, cotangent)

    qkv_sum = jnp.sum(d_qkv, axis=0, dtype=F32)
    whole_sums = [
        jnp.sum(d_normed1 * normal1, axis=0),
        jnp.sum(d_normed1, axis=0),
        jnp.sum(d_out, axis=0, dtype=F32),
        jnp.sum(d_normed2 * normal2, axis=0),
        jnp.sum(d_normed2, axis=0),
        jnp.sum(g_float, axis=0),
    ]
    part_sums = [
        qkv_sum[:part_width],
        qkv_sum[2 * part_width :],
        jnp.sum(d_inner, axis=0, dtype=F32),
    ]
    is_mine = (jnp.arange(TEAM) == member)[None, :, None, None]

    def widen(s):
        blocks = s.reshape(outer, 1, depth, -1)
        return jnp.where(is_mine, blocks, 0.0).reshape(devices, -1)

    table = jnp.concatenate([s.reshape(devices, -1) for s in whole_sums] + [widen(s) for s in part_sums], axis=1)
    small = lax.psum_scatter(table, BOTH, scatter_dimension=0, tiled=True)[0]
    cuts = [small[edges[i] : edges[i + 1]] for i in range(len(vectors))]
    g_gain1, g_shift1, g_bias_o, g_gain2, g_shift2, g_bias_down, g_bias_q, g_bias_v, g_bias_up = cuts
    return (
        layer_out,
        input_grad,
        g_gain1,
        g_shift1,
        grad_q,
        g_bias_q,
        grad_k,
        grad_v,
        g_bias_v,
        grad_o,
        g_bias_o,
        g_gain2,
        g_shift2,
        grad_up,
        g_bias_up,
        grad_down,
        g_bias_down,
    )


def solution(mesh):
    rows2 = P(BOTH, None)
    rows1 = P(BOTH)
    rows3 = P(BOTH, None, None)
    in_specs = (
        rows3,
        rows3,
        rows2,
        rows2,
        rows1,
        rows1,
        rows2,
        rows1,
        rows2,
        rows2,
        rows1,
        rows2,
        rows1,
        rows1,
        rows1,
        rows2,
        rows1,
        rows2,
        rows1,
    )
    out_specs = (rows3, rows3) + tuple(
        rows2 if kind == "w" else rows1 for kind in "vvwvwwvwvvvwvwv"
    )
    return jax.shard_map(body, mesh=mesh, in_specs=in_specs, out_specs=out_specs, check_vma=False)
```

time: 5550 us -> 1270 us (0.23)
  waiting for transfers between devices: 4460 us -> 545 us
  blocking collectives: 582 us -> 70.7 us
  other arithmetic: 53.2 us -> 132 us
    reduce_scatter x6 -> x4, waiting for transfers between devices: 4050 us -> 60.8 us  [depth_scatter(): return lax.psum_scatter(a, 'fsdp', scatter_dimension=0, tiled=True)]
    ppermute x0 -> x48, waiting for transfers between devices: none -> 455 us  [the longest x40 267 us: team_swap(): return lax.ppermute(a, 'dp', [(i, i ^ flip) for i in range(size)])]
    all_to_all x2 -> x0, blocking collectives: 354 us -> none  [the longest x1 197 us: body(): lax.all_to_all(spread(grad_input_rows, put_index, put_live), 'fsdp', spli...]
    all_gather x6 -> x4, waiting for transfers between devices: 270 us -> 14.6 us  [depth_gather(): return lax.all_gather(a, 'fsdp', axis=0, tiled=True)]
    unnamed x1 -> x0, blocking collectives: 150 us -> none
    all_to_all x3 -> x0, waiting for transfers between devices: 136 us -> none  [the longest x1 136 us: body(): lax.all_to_all(spread(out_rows, put_index, put_live), 'fsdp', split_axis=...]
    gather x12 -> x0, local copies, waits for them, and re-layouts: 63.3 us -> none  [the longest x2 23.1 us: unpack(): picked = jnp.take(returned.reshape(-1, feature_count), flat_index, axis=0)]
    dot_general x24 -> x21, matrix products: 274 us -> 281 us  [the longest x12 228 us: dot(): lax.dot_general(a, b, (((ca,), (cb,)), ((), ())), preferred_element_type=...]
  transfers between devices with their start and end apart: 16 -> 57, of which waited for: 9 -> 22; matrix products, arithmetic and copies ran while one was open for 6% -> 40% of each run, Pallas kernels for 0% -> 0%
where the time goes in v1:
time: 1270 us
  waiting for transfers between devices  545 us (43%)
  matrix products  289 us (23%)
  local copies, waits for them, and re-layouts  179 us (14%)
  other arithmetic  132 us (10%)
  blocking collectives  70.7 us (6%)
  starting transfers between devices  33.8 us (3%)
  between operations  15.6 us (1%)
    ppermute x40, waiting for transfers between devices, team_swap(): return lax.ppermute(a, 'dp', [(i, i ^ flip) for i in range(size)])  267 us
    dot_general x12, matrix products, dot(): lax.dot_general(a, b, (((ca,), (cb,)), ((), ())), preferred_element_type=...  228 us
    ppermute x8, waiting for transfers between devices, outer_pass(): return lax.ppermute(a, 'dp', pairs)  188 us
    all_gather x1, blocking collectives, body(): packed = lax.all_gather(jnp.concatenate(vectors), BOTH, axis=0, tiled=False)  70.7 us
    reduce_scatter x4, waiting for transfers between devices, depth_scatter(): return lax.psum_scatter(a, 'fsdp', scatter_dimension=0, tiled=True)  60.8 us
    unnamed x161, local copies, waits for them, and re-layouts  36.7 us
    reshape x6, local copies, waits for them, and re-layouts, body(): qkv[:, i * part_width:(i + 1) * part_width].reshape(shape)  34 us
    ppermute x40, starting transfers between devices, team_swap(): return lax.ppermute(a, 'dp', [(i, i ^ flip) for i in range(size)])  26.6 us
  transfers between devices with their start and end apart: 57, of which 22 were waited for; matrix products, arithmetic and copies ran while one was open for 40% of the time, Pallas kernels for 0%

profile of v1, /device:TPU:0, one launch (start us, length us, event | category | flops | bytes accessed | tf_op | source)
XLA Modules:
  0.0 1265.1 jit_solution(17803274027509188730)
XLA Ops:
  26.3 70.7 %all-gather.1 = bf16[32,1,768]{2,1,0:T(2,128)(2,1)S(1)} all-gather(bf16[1,1,768]{2,1,0:T(2,128)(2,1)S(1)} %reshape.621), channel_id=2, replica_groups=mesh['dp'=8,'fsdp'=4] {'dp','fsdp'}, dimensions={0}, use_global_device_ids=true | all-gather | bytes 50688 | tf_op jit(solution)/shard_map/all_gather | solution.py:191
  106.3 42.2 %collective-permute-done = bf16[512,2048]{1,0:T(8,128)(2,1)} collective-permute-done((bf16[512,2048]{1,0:T(8,128)(2,1)}, bf16[512,2048]{1,0:T(8,128)(2,1)}, u32[]{:S(2)}, u32[]{:S(2)}) %collective-permute-start) | collective-permute-done | bytes 2097184 | tf_op jit(solution)/shard_map/ppermute | solution.py:52
  154.6 39.0 %collective-permute-done.12 = bf16[256,2048]{1,0:T(8,128)(2,1)S(1)} collective-permute-done((bf16[256,2048]{1,0:T(8,128)(2,1)}, bf16[256,2048]{1,0:T(8,128)(2,1)S(1)}, u32[]{:S(2)}, u32[]{:S(2)}) %collective-permute-start.12) | collective-permute-done | bytes 1048608 | tf_op jit(solution)/shard_map/ppermute | solution.py:87
  200.0 20.5 %add_convert_fusion = bf16[2048,1536]{1,0:T(8,128)(2,1)} fusion(bf16[2048,1536]{1,0:T(8,128)(2,1)S(1)} %bitcast.316, f32[1536]{0:T(1024)S(1)} %pad_maximum_fusion.23, bf16[1024,2048]{1,0:T(8,128)(2,1)} %collective-permute-done.1, bf16[512,2048]{1,0:T(8,128)(2,1)} %collective-permute-done, bf16[512,2048]{1,0:T(8,128)(2,1)} %fusion.17), kind=kOutput, calls=%fused_computation.11 | convolution fusion | flops 12916359168 | bytes 20977664 | tf_op jit(solution)/shard_map/dot_general | solution.py:21
  226.3 6.1 reshape.625
  237.5 6.1 reshape.626
  248.7 6.1 reshape.624
  260.3 8.5 fusion.108
  303.1 5.9 collective-permute-done.18
  311.4 5.9 slice_add_fusion.3
  324.8 45.1 %collective-permute-done.14 = bf16[512,2048]{1,0:T(8,128)(2,1)} collective-permute-done((bf16[512,2048]{1,0:T(8,128)(2,1)}, bf16[512,2048]{1,0:T(8,128)(2,1)}, u32[]{:S(2)}, u32[]{:S(2)}) %collective-permute-start.14) | collective-permute-done | bytes 2097184 | tf_op jit(solution)/shard_map/ppermute | solution.py:52
  377.8 14.6 %all-gather.11.cloned.1.call-done = bf16[1024,2048]{1,0:T(8,128)(2,1)} async-done(((bf16[256,2048]{1,0:T(8,128)(2,1)}), bf16[1024,2048]{1,0:T(8,128)(2,1)}) %all-gather.11.cloned.1.call-update) | async-done | bytes 4194320 | tf_op jit(solution)/shard_map/all_gather | solution.py:233
  400.1 25.2 %collective-permute-done.15 = bf16[512,2048]{1,0:T(8,128)(2,1)} collective-permute-done((bf16[512,2048]{1,0:T(8,128)(2,1)}, bf16[512,2048]{1,0:T(8,128)(2,1)}, u32[]{:S(2)}, u32[]{:S(2)}) %collective-permute-start.15) | collective-permute-done | bytes 2097184 | tf_op jit(solution)/shard_map/ppermute | solution.py:52
  430.1 37.7 %collective-permute-done.24 = bf16[512,2048]{1,0:T(8,128)(2,1)} collective-permute-done((bf16[512,2048]{1,0:T(8,128)(2,1)S(1)}, bf16[512,2048]{1,0:T(8,128)(2,1)}, u32[]{:S(2)}, u32[]{:S(2)}) %collective-permute-start.24) | collective-permute-done | bytes 2097184 | tf_op jit(solution)/shard_map/ppermute | solution.py:52
  476.0 6.2 pad_maximum_fusion.2
  482.2 24.0 %collective-permute-done.20 = bf16[1024,2048]{1,0:T(8,128)(2,1)} collective-permute-done((bf16[1024,2048]{1,0:T(8,128)(2,1)}, bf16[1024,2048]{1,0:T(8,128)(2,1)}, u32[]{:S(2)}, u32[]{:S(2)}) %collective-permute-start.20) | collective-permute-done | bytes 4194336 | tf_op jit(solution)/shard_map/ppermute | solution.py:87
  511.2 6.3 maximum_bitcast_fusion
  517.5 8.3 copy.291
  525.8 28.2 %multiply_convert_fusion = (bf16[2048,2048]{1,0:T(8,128)(2,1)}, f32[2048,2048]{1,0:T(8,128)}) fusion(f32[2048]{0:T(1024)S(1)} %bitcast.341, bf16[2048,2048]{1,0:T(8,128)(2,1)} %bitcast.310, bf16[1024,2048]{1,0:T(8,128)(2,1)} %collective-permute-done.16, bf16[512,2048]{1,0:T(8,128)(2,1)} %collective-permute-done.15, bf16[512,2048]{1,0:T(8,128)(2,1)} %add_convert_fusion.1), kind=kOutput, calls=%fused_computation.8 | convolution fusion | flops 17230200832 | bytes 41951232 | tf_op jit(solution)/shard_map/dot_general | solution.py:21
  554.0 32.9 %convert_reduce_fusion = (f32[2048]{0:T(1024)}, bf16[2048,2048]{1,0:T(8,128)(2,1)}) fusion(f32[2048,2048]{1,0:T(8,128)} %get-tuple-element.130, f32[2048]{0:T(1024)S(1)} %bitcast.342, bf16[2048,2048]{1,0:T(8,128)(2,1)} %bitcast.306, bf16[1024,2048]{1,0:T(8,128)(2,1)} %collective-permute-done.25, bf16[512,2048]{1,0:T(8,128)(2,1)} %collective-permute-done.24, ...), kind=kOutput, calls=%fused_computation.7 | convolution fusion | flops 17259558912 | bytes 41959424 | tf_op jit(solution)/shard_map/dot_general | solution.py:21
  586.8 21.6 %fusion.110 = f32[2048,2048]{1,0:T(8,128)S(1)} fusion(bf16[2048,2048]{1,0:T(8,128)(2,1)} %get-tuple-element.134, bf16[2048,2048]{1,0:T(8,128)(2,1)} %bitcast.311), kind=kOutput, calls=%fused_computation.309 | convolution fusion | flops 17179869184 | bytes 33554432 | tf_op jit(solution)/shard_map/dot_general | solution.py:21
  611.5 27.8 %convolution_convert_fusion.1 = bf16[2048,2048]{1,0:T(8,128)(2,1)} fusion(bf16[2048,2048]{1,0:T(8,128)(2,1)} %get-tuple-element.134, bf16[1024,2048]{1,0:T(8,128)(2,1)} %collective-permute-done.16, bf16[512,2048]{1,0:T(8,128)(2,1)} %collective-permute-done.15, bf16[512,2048]{1,0:T(8,128)(2,1)} %add_convert_fusion.1), kind=kOutput, calls=%fused_computation.35 | convolution fusion | flops 17209229312 | bytes 25165824 | tf_op jit(solution)/shard_map/dot_general | solution.py:21
  639.3 8.3 copy.320
  663.2 79.9 %collective-permute-done.43 = bf16[1024,2048]{1,0:T(8,128)(2,1)} collective-permute-done((bf16[1024,2048]{1,0:T(8,128)(2,1)}, bf16[1024,2048]{1,0:T(8,128)(2,1)}, u32[]{:S(2)}, u32[]{:S(2)}) %collective-permute-start.43) | collective-permute-done | bytes 4194336 | tf_op jit(solution)/shard_map/ppermute | solution.py:87
  743.1 7.7 fusion.7
  757.3 6.7 convert_reduce_fusion.4
  765.2 20.6 %convolution_convert_fusion = bf16[2048,2048]{1,0:T(8,128)(2,1)S(1)} fusion(bf16[2048,2048]{1,0:T(8,128)(2,1)S(1)} %bitcast.347, bf16[1024,2048]{1,0:T(8,128)(2,1)} %collective-permute-done.25, bf16[512,2048]{1,0:T(8,128)(2,1)} %collective-permute-done.24, bf16[512,2048]{1,0:T(8,128)(2,1)S(1)} %copy-done.17), kind=kOutput, calls=%fused_computation.34 | convolution fusion | flops 17209229312 | bytes 25165824 | tf_op jit(solution)/shard_map/dot_general | solution.py:21
  791.0 17.4 %collective-permute-done.28 = bf16[512,2048]{1,0:T(8,128)(2,1)S(1)} collective-permute-done((bf16[512,2048]{1,0:T(8,128)(2,1)S(1)}, bf16[512,2048]{1,0:T(8,128)(2,1)S(1)}, u32[]{:S(2)}, u32[]{:S(2)}) %collective-permute-start.28) | collective-permute-done | bytes 2097184 | tf_op jit(solution)/shard_map/ppermute | solution.py:52
  811.1 21.7 %fusion.109 = f32[2048,2048]{1,0:T(8,128)S(1)} fusion(bf16[2048,2048]{1,0:T(8,128)(2,1)} %get-tuple-element.129, bf16[2048,2048]{1,0:T(8,128)(2,1)} %bitcast.307), kind=kOutput, calls=%fused_computation.308 | convolution fusion | flops 17179869184 | bytes 33554432 | tf_op jit(solution)/shard_map/dot_general | solution.py:21
  832.8 5.8 copy-done.10
  841.8 37.8 %collective-permute-done.47 = bf16[1024,2048]{1,0:T(8,128)(2,1)S(1)} collective-permute-done((bf16[1024,2048]{1,0:T(8,128)(2,1)}, bf16[1024,2048]{1,0:T(8,128)(2,1)S(1)}, u32[]{:S(2)}, u32[]{:S(2)}) %collective-permute-start.47) | collective-permute-done | bytes 4194336 | tf_op jit(solution)/shard_map/ppermute | solution.py:87
  879.6 6.2 fusion.6
  887.4 9.4 fusion.45
  896.8 6.2 reshape.627
  907.2 7.9 convert_bitcast_fusion
  935.6 16.7 %fusion.111 = f32[2048,2048]{1,0:T(8,128)} fusion(bf16[2048,1536]{0,1:T(8,128)(2,1)S(1)} %bitcast_dynamic-update-slice_fusion, bf16[2048,1536]{1,0:T(8,128)(2,1)S(1)} %bitcast.319), kind=kOutput, calls=%fused_computation.310 | convolution fusion | flops 12884901888 | bytes 29360128 | tf_op jit(solution)/shard_map/dot_general | solution.py:21
  952.3 6.3 slice.313
  958.6 6.3 fusion.46
  968.0 17.7 %convolution_convert_fusion.2 = bf16[2048,1536]{1,0:T(8,128)(2,1)} fusion(bf16[2048,1536]{0,1:T(8,128)(2,1)S(1)} %bitcast_dynamic-update-slice_fusion, bf16[1024,2048]{1,0:T(8,128)(2,1)} %collective-permute-done.1, bf16[512,2048]{1,0:T(8,128)(2,1)} %collective-permute-done, bf16[512,2048]{1,0:T(8,128)(2,1)} %fusion.17), kind=kOutput, calls=%fused_computation.36 | convolution fusion | flops 12913213440 | bytes 20971520 | tf_op jit(solution)/shard_map/dot_general | solution.py:21
  992.9 5.8 slice_add_fusion
  1010.2 38.3 %collective-permute-done.31 = bf16[512,2048]{1,0:T(8,128)(2,1)} collective-permute-done((bf16[512,2048]{1,0:T(8,128)(2,1)}, bf16[512,2048]{1,0:T(8,128)(2,1)}, u32[]{:S(2)}, u32[]{:S(2)}) %collective-permute-start.31) | collective-permute-done | bytes 2097184 | tf_op jit(solution)/shard_map/ppermute | solution.py:52
  1054.0 7.7 collective-permute-done.32
  1067.1 5.9 slice_add_fusion.2
  1082.5 44.8 %collective-permute-done.23 = bf16[512,2048]{1,0:T(8,128)(2,1)} collective-permute-done((bf16[512,2048]{1,0:T(8,128)(2,1)}, bf16[512,2048]{1,0:T(8,128)(2,1)}, u32[]{:S(2)}, u32[]{:S(2)}) %collective-permute-start.23) | collective-permute-done | bytes 2097184 | tf_op jit(solution)/shard_map/ppermute | solution.py:52
  1127.3 9.8 bitcast_select_fusion.1
  1150.9 10.7 bitcast_select_fusion
  1161.7 14.0 %all-reduce.3.cloned.1.call-done = f32[32,768]{1,0:T(8,128)} async-done(((f32[32,768]{1,0:T(8,128)}), f32[32,768]{1,0:T(8,128)}) %all-reduce.3.cloned.1.call-update) | async-done | bytes 98320
  1178.4 60.7 %reduce-scatter.5.cloned.1.call-done = bf16[256,1536]{1,0:T(8,128)(2,1)} async-done(((bf16[1024,1536]{1,0:T(8,128)(2,1)}), bf16[256,1536]{1,0:T(8,128)(2,1)}) %reduce-scatter.5.cloned.1.call-update) | async-done | bytes 786448 | tf_op jit(solution)/shard_map/reduce_scatter | solution.py:271
  (452 shorter events, 280.2 us)
Async XLA Ops:
  7.2 98.5 %all-gather.7.cloned.1.call-start = ((), (), s32[]{:S(2)}) async-start(), calls=%async_computation.4 | async-start | bytes 3932160 | tf_op jit(solution)/shard_map/all_gather | solution.py:233
  9.1 9.5 collective-permute-start.5
  11.7 7.0 collective-permute-start.6
  12.5 6.8 collective-permute-start.7
  14.6 5.9 collective-permute-start.2
  26.0 127.3 %all-gather.9.cloned.1.call-start = ((), (), s32[]{:S(2)}) async-start(), calls=%async_computation.5 | async-start | bytes 1310720 | tf_op jit(solution)/shard_map/all_gather | solution.py:233
  105.6 42.9 %collective-permute-start = (bf16[512,2048]{1,0:T(8,128)(2,1)}, bf16[512,2048]{1,0:T(8,128)(2,1)}, u32[]{:S(2)}, u32[]{:S(2)}) collective-permute-start(bf16[512,2048]{1,0:T(8,128)(2,1)} %fusion.17), channel_id=1, source_target_pairs={{0,8},{4,12},{8,0},{12,4},{16,24},{20,28},{24,16},{28,20},{1,9},{5... | collective-permute-start | bytes 6291464 | tf_op jit(solution)/shard_map/ppermute | solution.py:52
  105.6 218.7 %all-gather.13.cloned.1.call-start = ((), (), s32[]{:S(2)}) async-start(), calls=%async_computation.7 | async-start | bytes 5242880 | tf_op jit(solution)/shard_map/all_gather | solution.py:233
  105.7 90.7 %collective-permute-start.11 = (bf16[1024,1536]{1,0:T(8,128)(2,1)}, bf16[1024,1536]{1,0:T(8,128)(2,1)}, u32[]{:S(2)}, u32[]{:S(2)}) collective-permute-start(bf16[1024,1536]{1,0:T(8,128)(2,1)} %all-gather.7.cloned.1.call-done), channel_id=1, source_target_pairs={{0,16},{4,20},{8,24},{12,28},{16,0},{20,4},{24,8},{28,12},{1,17},{... | collective-permute-start | bytes 9437192 | tf_op jit(solution)/shard_map/ppermute | solution.py:87
  153.3 46.6 %collective-permute-start.1 = (bf16[1024,2048]{1,0:T(8,128)(2,1)}, bf16[1024,2048]{1,0:T(8,128)(2,1)}, u32[]{:S(2)}, u32[]{:S(2)}) collective-permute-start(bf16[1024,2048]{1,0:T(8,128)(2,1)} %pad_maximum_fusion.5), channel_id=1, source_target_pairs={{0,4},{4,0},{8,12},{12,8},{16,20},{20,16},{24,28},{28,24},{1,5},{5... | collective-permute-start | bytes 12582920 | tf_op jit(solution)/shard_map/ppermute | solution.py:52
  153.4 40.1 %collective-permute-start.12 = (bf16[256,2048]{1,0:T(8,128)(2,1)}, bf16[256,2048]{1,0:T(8,128)(2,1)S(1)}, u32[]{:S(2)}, u32[]{:S(2)}) collective-permute-start(bf16[256,2048]{1,0:T(8,128)(2,1)} %all-gather.9.cloned.1.call-done), channel_id=1, source_target_pairs={{0,16},{4,20},{8,24},{12,28},{16,0},{20,4},{24,8},{28,12},{1,17},{... | collective-permute-start | bytes 3145736 | tf_op jit(solution)/shard_map/ppermute | solution.py:87
  154.1 238.3 %all-gather.11.cloned.1.call-start = ((), (), s32[]{:S(2)}) async-start(), calls=%async_computation.6 | async-start | bytes 5242880 | tf_op jit(solution)/shard_map/all_gather | solution.py:233
  290.1 21.3 %collective-permute-start.13 = (bf16[1024,2048]{1,0:T(8,128)(2,1)}, bf16[1024,2048]{1,0:T(8,128)(2,1)}, u32[]{:S(2)}, u32[]{:S(2)}) collective-permute-start(bf16[1024,2048]{1,0:T(8,128)(2,1)} %slice.316), channel_id=1, source_target_pairs={{0,4},{4,0},{8,12},{12,8},{16,20},{20,16},{24,28},{28,24},{1,5},{5... | collective-permute-start | bytes 12582920 | tf_op jit(solution)/shard_map/ppermute | solution.py:52
  294.5 8.6 collective-permute-start.17
  297.6 11.5 collective-permute-start.18
  299.1 10.0 collective-permute-start.19
  311.3 768.1 %reduce-scatter.9.cloned.1.call-start = ((), (), s32[]{:S(2)}) async-start(), calls=%async_computation.10 | async-start | bytes 5242880 | tf_op jit(solution)/shard_map/reduce_scatter | solution.py:271
  322.5 47.4 %collective-permute-start.14 = (bf16[512,2048]{1,0:T(8,128)(2,1)}, bf16[512,2048]{1,0:T(8,128)(2,1)}, u32[]{:S(2)}, u32[]{:S(2)}) collective-permute-start(bf16[512,2048]{1,0:T(8,128)(2,1)} %slice.320), channel_id=1, source_target_pairs={{0,8},{4,12},{8,0},{12,4},{16,24},{20,28},{24,16},{28,20},{1,9},{5... | collective-permute-start | bytes 6291464 | tf_op jit(solution)/shard_map/ppermute | solution.py:52
  324.3 147.5 %collective-permute-start.21 = (bf16[1024,2048]{1,0:T(8,128)(2,1)}, bf16[1024,2048]{1,0:T(8,128)(2,1)}, u32[]{:S(2)}, u32[]{:S(2)}) collective-permute-start(bf16[1024,2048]{1,0:T(8,128)(2,1)} %all-gather.13.cloned.1.call-done), channel_id=1, source_target_pairs={{0,16},{4,20},{8,24},{12,28},{16,0},{20,4},{24,8},{28,12},{1,17},{... | collective-permute-start | bytes 12582920 | tf_op jit(solution)/shard_map/ppermute | solution.py:87
  376.4 48.9 %collective-permute-start.15 = (bf16[512,2048]{1,0:T(8,128)(2,1)}, bf16[512,2048]{1,0:T(8,128)(2,1)}, u32[]{:S(2)}, u32[]{:S(2)}) collective-permute-start(bf16[512,2048]{1,0:T(8,128)(2,1)} %add_convert_fusion.1), channel_id=1, source_target_pairs={{0,8},{4,12},{8,0},{12,4},{16,24},{20,28},{24,16},{28,20},{1,9},{5... | collective-permute-start | bytes 6291464 | tf_op jit(solution)/shard_map/ppermute | solution.py:52
  392.4 113.7 %collective-permute-start.20 = (bf16[1024,2048]{1,0:T(8,128)(2,1)}, bf16[1024,2048]{1,0:T(8,128)(2,1)}, u32[]{:S(2)}, u32[]{:S(2)}) collective-permute-start(bf16[1024,2048]{1,0:T(8,128)(2,1)} %all-gather.11.cloned.1.call-done), channel_id=1, source_target_pairs={{0,16},{4,20},{8,24},{12,28},{16,0},{20,4},{24,8},{28,12},{1,17},{... | collective-permute-start | bytes 12582920 | tf_op jit(solution)/shard_map/ppermute | solution.py:87
  398.5 69.2 %collective-permute-start.24 = (bf16[512,2048]{1,0:T(8,128)(2,1)S(1)}, bf16[512,2048]{1,0:T(8,128)(2,1)}, u32[]{:S(2)}, u32[]{:S(2)}) collective-permute-start(bf16[512,2048]{1,0:T(8,128)(2,1)S(1)} %fusion.42), channel_id=1, source_target_pairs={{0,8},{4,12},{8,0},{12,4},{16,24},{20,28},{24,16},{28,20},{1,9},{5... | collective-permute-start | bytes 6291464 | tf_op jit(solution)/shard_map/ppermute | solution.py:52
  430.0 95.8 %collective-permute-start.16 = (bf16[1024,2048]{1,0:T(8,128)(2,1)}, bf16[1024,2048]{1,0:T(8,128)(2,1)}, u32[]{:S(2)}, u32[]{:S(2)}) collective-permute-start(bf16[1024,2048]{1,0:T(8,128)(2,1)} %pad_maximum_fusion.6), channel_id=1, source_target_pairs={{0,4},{4,0},{8,12},{12,8},{16,20},{20,16},{24,28},{28,24},{1,5},{5... | collective-permute-start | bytes 12582920 | tf_op jit(solution)/shard_map/ppermute | solution.py:52
  471.9 82.1 %collective-permute-start.25 = (bf16[1024,2048]{1,0:T(8,128)(2,1)}, bf16[1024,2048]{1,0:T(8,128)(2,1)}, u32[]{:S(2)}, u32[]{:S(2)}) collective-permute-start(bf16[1024,2048]{1,0:T(8,128)(2,1)} %pad_maximum_fusion.7), channel_id=1, source_target_pairs={{0,4},{4,0},{8,12},{12,8},{16,20},{20,16},{24,28},{28,24},{1,5},{5... | collective-permute-start | bytes 12582920 | tf_op jit(solution)/shard_map/ppermute | solution.py:52
  611.5 41.3 %collective-permute-start.26 = (bf16[1024,2048]{1,0:T(8,128)(2,1)}, bf16[1024,2048]{1,0:T(8,128)(2,1)S(1)}, u32[]{:S(2)}, u32[]{:S(2)}) collective-permute-start(bf16[1024,2048]{1,0:T(8,128)(2,1)} %slice.314), channel_id=1, source_target_pairs={{0,4},{4,0},{8,12},{12,8},{16,20},{20,16},{24,28},{28,24},{1,5},{5... | collective-permute-start | bytes 12582920 | tf_op jit(solution)/shard_map/ppermute | solution.py:52
  652.4 90.7 %collective-permute-start.43 = (bf16[1024,2048]{1,0:T(8,128)(2,1)}, bf16[1024,2048]{1,0:T(8,128)(2,1)}, u32[]{:S(2)}, u32[]{:S(2)}) collective-permute-start(bf16[1024,2048]{1,0:T(8,128)(2,1)} %dynamic-slice_bitcast_fusion.1), channel_id=1, source_target_pairs={{0,16},{4,20},{8,24},{12,28},{16,0},{20,4},{24,8},{28,12},{1,17},{... | collective-permute-start | bytes 12582920 | tf_op jit(solution)/shard_map/ppermute | solution.py:87
  662.7 88.3 %collective-permute-start.27 = (bf16[512,2048]{1,0:T(8,128)(2,1)}, bf16[512,2048]{1,0:T(8,128)(2,1)S(1)}, u32[]{:S(2)}, u32[]{:S(2)}) collective-permute-start(bf16[512,2048]{1,0:T(8,128)(2,1)} %slice.318), channel_id=1, source_target_pairs={{0,8},{4,12},{8,0},{12,4},{16,24},{20,28},{24,16},{28,20},{1,9},{5... | collective-permute-start | bytes 6291464 | tf_op jit(solution)/shard_map/ppermute | solution.py:52
  750.9 386.3 %reduce-scatter.11.cloned.1.call-start = ((), (), s32[]{:S(2)}) async-start(), calls=%async_computation.11 | async-start | bytes 5242880 | tf_op jit(solution)/shard_map/reduce_scatter | solution.py:271
  764.0 44.4 %collective-permute-start.28 = (bf16[512,2048]{1,0:T(8,128)(2,1)S(1)}, bf16[512,2048]{1,0:T(8,128)(2,1)S(1)}, u32[]{:S(2)}, u32[]{:S(2)}) collective-permute-start(bf16[512,2048]{1,0:T(8,128)(2,1)S(1)} %get-tuple-element.26), channel_id=1, source_target_pairs={{0,8},{4,12},{8,0},{12,4},{16,24},{20,28},{24,16},{28,20},{1,9},{5... | collective-permute-start | bytes 6291464 | tf_op jit(solution)/shard_map/ppermute | solution.py:52
  790.6 89.1 %collective-permute-start.47 = (bf16[1024,2048]{1,0:T(8,128)(2,1)}, bf16[1024,2048]{1,0:T(8,128)(2,1)S(1)}, u32[]{:S(2)}, u32[]{:S(2)}) collective-permute-start(bf16[1024,2048]{1,0:T(8,128)(2,1)} %dynamic-slice_bitcast_fusion), channel_id=1, source_target_pairs={{0,16},{4,20},{8,24},{12,28},{16,0},{20,4},{24,8},{28,12},{1,17},{... | collective-permute-start | bytes 12582920 | tf_op jit(solution)/shard_map/ppermute | solution.py:87
  811.1 74.8 %collective-permute-start.29 = (bf16[1024,2048]{1,0:T(8,128)(2,1)}, bf16[1024,2048]{1,0:T(8,128)(2,1)}, u32[]{:S(2)}, u32[]{:S(2)}) collective-permute-start(bf16[1024,2048]{1,0:T(8,128)(2,1)} %pad_maximum_fusion.8), channel_id=1, source_target_pairs={{0,4},{4,0},{8,12},{12,8},{16,20},{20,16},{24,28},{28,24},{1,5},{5... | collective-permute-start | bytes 12582920 | tf_op jit(solution)/shard_map/ppermute | solution.py:52
  841.3 225.8 %collective-permute-start.22 = (bf16[1024,2048]{1,0:T(8,128)(2,1)}, bf16[1024,2048]{1,0:T(8,128)(2,1)}, u32[]{:S(2)}, u32[]{:S(2)}) collective-permute-start(bf16[1024,2048]{1,0:T(8,128)(2,1)} %slice.315), channel_id=1, source_target_pairs={{0,4},{4,0},{8,12},{12,8},{16,20},{20,16},{24,28},{28,24},{1,5},{5... | collective-permute-start | bytes 12582920 | tf_op jit(solution)/shard_map/ppermute | solution.py:52
  885.8 263.3 %reduce-scatter.7.cloned.1.call-start = ((), (), s32[]{:S(2)}) async-start(), calls=%async_computation.9 | async-start | bytes 1310720 | tf_op jit(solution)/shard_map/reduce_scatter | solution.py:271
  958.6 34.3 %collective-permute-start.30 = (bf16[1024,2048]{1,0:T(8,128)(2,1)}, bf16[1024,2048]{1,0:T(8,128)(2,1)}, u32[]{:S(2)}, u32[]{:S(2)}) collective-permute-start(bf16[1024,2048]{1,0:T(8,128)(2,1)} %slice.313), channel_id=1, source_target_pairs={{0,4},{4,0},{8,12},{12,8},{16,20},{20,16},{24,28},{28,24},{1,5},{5... | collective-permute-start | bytes 12582920 | tf_op jit(solution)/shard_map/ppermute | solution.py:52
  967.4 34.0 %collective-permute-start.42 = (bf16[256,2048]{1,0:T(8,128)(2,1)}, bf16[256,2048]{1,0:T(8,128)(2,1)}, u32[]{:S(2)}, u32[]{:S(2)}) collective-permute-start(bf16[256,2048]{1,0:T(8,128)(2,1)} %dynamic-slice_bitcast_fusion.3), channel_id=1, source_target_pairs={{0,16},{4,20},{8,24},{12,28},{16,0},{20,4},{24,8},{28,12},{1,17},{... | collective-permute-start | bytes 3145736 | tf_op jit(solution)/shard_map/ppermute | solution.py:87
  991.2 70.5 %collective-permute-start.32 = (bf16[1024,1536]{1,0:T(8,128)(2,1)}, bf16[1024,1536]{1,0:T(8,128)(2,1)}, u32[]{:S(2)}, u32[]{:S(2)}) collective-permute-start(bf16[1024,1536]{1,0:T(8,128)(2,1)} %dynamic-slice_bitcast_fusion.2), channel_id=1, source_target_pairs={{0,16},{4,20},{8,24},{12,28},{16,0},{20,4},{24,8},{28,12},{1,17},{... | collective-permute-start | bytes 9437192 | tf_op jit(solution)/shard_map/ppermute | solution.py:87
  1000.4 48.0 %collective-permute-start.31 = (bf16[512,2048]{1,0:T(8,128)(2,1)}, bf16[512,2048]{1,0:T(8,128)(2,1)}, u32[]{:S(2)}, u32[]{:S(2)}) collective-permute-start(bf16[512,2048]{1,0:T(8,128)(2,1)} %slice.317), channel_id=1, source_target_pairs={{0,8},{4,12},{8,0},{12,4},{16,24},{20,28},{24,16},{28,20},{1,9},{5... | collective-permute-start | bytes 6291464 | tf_op jit(solution)/shard_map/ppermute | solution.py:52
  1005.6 170.0 %all-reduce.3.cloned.1.call-start = ((), (), s32[]{:S(2)}) async-start(), calls=%async_computation.12 | async-start | bytes 196608
  1053.6 185.6 %reduce-scatter.5.cloned.1.call-start = ((), (), s32[]{:S(2)}) async-start(), calls=%async_computation.8 | async-start | bytes 3932160 | tf_op jit(solution)/shard_map/reduce_scatter | solution.py:271
  1078.0 49.3 %collective-permute-start.23 = (bf16[512,2048]{1,0:T(8,128)(2,1)}, bf16[512,2048]{1,0:T(8,128)(2,1)}, u32[]{:S(2)}, u32[]{:S(2)}) collective-permute-start(bf16[512,2048]{1,0:T(8,128)(2,1)} %slice.319), channel_id=1, source_target_pairs={{0,8},{4,12},{8,0},{12,4},{16,24},{20,28},{24,16},{28,20},{1,9},{5... | collective-permute-start | bytes 6291464 | tf_op jit(solution)/shard_map/ppermute | solution.py:52
  1080.6 59.3 %collective-permute-start.44 = (bf16[64,2048]{1,0:T(8,128)(2,1)S(1)}, bf16[64,2048]{1,0:T(8,128)(2,1)S(1)}, u32[]{:S(2)}, u32[]{:S(2)}) collective-permute-start(bf16[64,2048]{1,0:T(8,128)(2,1)S(1)} %get-tuple-element.48), channel_id=1, source_target_pairs={{0,12},{4,8},{8,4},{12,0},{16,28},{20,24},{24,20},{28,16},{1,13},{... | collective-permute-start | bytes 786440 | tf_op jit(solution)/shard_map/ppermute | solution.py:52
  1080.7 59.3 %collective-permute-start.45 = (bf16[64,2048]{1,0:T(8,128)(2,1)S(1)}, bf16[64,2048]{1,0:T(8,128)(2,1)S(1)}, u32[]{:S(2)}, u32[]{:S(2)}) collective-permute-start(bf16[64,2048]{1,0:T(8,128)(2,1)S(1)} %get-tuple-element.47), channel_id=1, source_target_pairs={{0,8},{4,12},{8,0},{12,4},{16,24},{20,28},{24,16},{28,20},{1,9},{5... | collective-permute-start | bytes 786440 | tf_op jit(solution)/shard_map/ppermute | solution.py:52
  1081.8 58.8 %collective-permute-start.46 = (bf16[64,2048]{1,0:T(8,128)(2,1)S(1)}, bf16[64,2048]{1,0:T(8,128)(2,1)}, u32[]{:S(2)}, u32[]{:S(2)}) collective-permute-start(bf16[64,2048]{1,0:T(8,128)(2,1)S(1)} %get-tuple-element.46), channel_id=1, source_target_pairs={{0,4},{4,0},{8,12},{12,8},{16,20},{20,16},{24,28},{28,24},{1,5},{5... | collective-permute-start | bytes 786440 | tf_op jit(solution)/shard_map/ppermute | solution.py:52
  1242.3 5.6 collective-permute-start.39
  1243.4 5.6 collective-permute-start.40
  1246.2 9.0 collective-permute-start.33
  1247.1 8.1 collective-permute-start.34
  1247.9 7.3 collective-permute-start.35
  (85 other events, 2097.2 us)
Sparse Core Ops, SparseCore 0:
  26.2 65.9 all-gather.6
  105.7 25.7 all-gather.8
  154.2 79.5 all-gather.12
  311.4 80.9 all-gather.10
  751.0 76.8 reduce-scatter.8
  886.0 77.7 reduce-scatter.10
  1005.7 28.0 reduce-scatter.6
  1053.7 121.8 all-reduce.2
  1178.0 61.0 reduce-scatter.4

commit v2 on v1

v2 whole, which is shorter than its diff:
```python
import functools

import jax
import jax.numpy as jnp
from jax import lax
from jax.experimental import pallas as pl
from jax.experimental.pallas import tpu as pltpu
from jax.sharding import Mesh
from jax.sharding import PartitionSpec as P

HD = 64
SLOT = 128
TEAM = 4
TILE = 256
HASTE = 1000
VMEM = 48 * 2**20

EPSILON = 1e-05
MASKED = -1e30
ROOT_HALF = 0.7071067811865476
DENSITY_SCALE = 0.3989422804014327
BF = jnp.bfloat16
F32 = jnp.float32
ALL = ("outer", "team", "fsdp")
SPREAD = ("outer", "fsdp")


def dot(a, b, ca, cb):
    return lax.dot_general(a, b, (((ca,), (cb,)), ((), ())), preferred_element_type=F32)


def team_swap(a, flip):
    return lax.ppermute(a, "team", [(i, i ^ flip) for i in range(TEAM)])


def ring_order(size):
    return list(range(0, size, 2)) + list(range(1, size, 2))[::-1]


def outer_pass(a):
    outer = lax.axis_size("outer")
    order = ring_order(outer)
    return lax.ppermute(a, "outer", [(o, order[(p + 1) % outer]) for p, o in enumerate(order)])


def outer_place(me):
    outer = lax.axis_size("outer")
    order = ring_order(outer)
    place = [0] * outer
    for p, o in enumerate(order):
        place[o] = p
    return jnp.asarray(order, jnp.int32), jnp.asarray(place, jnp.int32)[me]


def outer_halves(a, me):
    outer = lax.axis_size("outer")
    if outer == 2:
        return [a, outer_pass(a)]
    order, place = outer_place(me)
    whole = jnp.zeros((outer,) + a.shape[1:], a.dtype)
    whole = lax.dynamic_update_slice_in_dim(whole, a, me, 0)
    moving = a
    for step in range(1, outer):
        moving = outer_pass(moving)
        whole = lax.dynamic_update_slice_in_dim(whole, moving, order[(place - step) % outer], 0)
    return [whole[: outer // 2], whole[outer // 2 :]]


def outer_scatter(blocks, me):
    outer = lax.axis_size("outer")
    order, place = outer_place(me)
    moving = lax.dynamic_slice_in_dim(blocks, order[(place - 1) % outer], 1, 0)
    for step in range(1, outer):
        moving = outer_pass(moving)
        mine = lax.dynamic_slice_in_dim(blocks, order[(place - 1 - step) % outer], 1, 0)
        moving = (moving.astype(F32) + mine.astype(F32)).astype(BF)
    return moving


def by_team(stacked, member):
    odd = (member & 1) == 1
    high = (member & 2) == 2
    a = [jnp.where(odd, stacked[i ^ 1], stacked[i]) for i in range(4)]
    return [jnp.where(high, a[i ^ 2], a[i]) for i in range(4)]


def deal_columns(shards, member, outer, depth):
    r = shards[0].shape[0]
    parts = [w.reshape(r, outer, TEAM, depth, -1) for w in shards]
    got = []
    for flip in range(TEAM):
        piece = jnp.concatenate(
            [lax.dynamic_index_in_dim(w, member ^ flip, 2, False).reshape(r, -1) for w in parts], axis=1
        )
        got.append(piece if flip == 0 else team_swap(piece, flip))
    return jnp.concatenate(by_team(got, member), axis=0)


def return_columns(block, member, outer, depth, shares):
    r, c = block.shape[0] // TEAM, block.shape[1] // shares
    parts = block.reshape(TEAM, r, shares * c)
    got = []
    for flip in range(TEAM):
        piece = lax.dynamic_index_in_dim(parts, member ^ flip, 0, False)
        got.append(piece if flip == 0 else team_swap(piece, flip))
    got = by_team(got, member)
    result = []
    for i in range(shares):
        cols = jnp.stack([g[:, i * c : (i + 1) * c].reshape(r, outer, depth, -1) for g in got], axis=2)
        result.append(cols.reshape(r, -1).astype(F32))
    return result


def shift_pass(a, axis, step):
    size = lax.axis_size(axis)
    return lax.ppermute(a, axis, [(i, (i + step) % size) for i in range(size)])


def gather_small(vector, member, me, layer):
    depth = lax.axis_size("fsdp")
    outer = lax.axis_size("outer")
    a = vector[None]
    a = jnp.concatenate([a if s == 0 else shift_pass(a, "fsdp", s) for s in range(depth)])
    a = jnp.concatenate([a if s == 0 else shift_pass(a, "outer", s) for s in range(outer)])
    a = jnp.concatenate([a if f == 0 else team_swap(a, f) for f in range(TEAM)])
    index = jnp.arange(TEAM * outer * depth, dtype=jnp.int32)
    flip, step, drop = index // (outer * depth), index // depth % outer, index % depth
    source = ((me - step) % outer * TEAM + (member ^ flip)) * depth + (layer - drop) % depth
    place = (index[:, None] == source[None, :]).astype(BF)
    return dot(place, a, 1, 0)


def reduce_small(table, member, me, layer):
    depth = lax.axis_size("fsdp")
    outer = lax.axis_size("outer")
    blocks = table.reshape(outer, TEAM, depth, -1)
    total = lax.dynamic_index_in_dim(blocks, member, 1, False)
    for flip in range(1, TEAM):
        total = total + team_swap(lax.dynamic_index_in_dim(blocks, member ^ flip, 1, False), flip)
    blocks = total
    total = lax.dynamic_index_in_dim(blocks, me, 0, False)
    for step in range(1, outer):
        total = total + shift_pass(
            lax.dynamic_index_in_dim(blocks, (me + step) % outer, 0, False), "outer", step
        )
    blocks = total
    total = lax.dynamic_index_in_dim(blocks, layer, 0, False)
    for step in range(1, depth):
        total = total + shift_pass(
            lax.dynamic_index_in_dim(blocks, (layer + step) % depth, 0, False), "fsdp", step
        )
    return total


def params():
    return pltpu.CompilerParams(vmem_limit_bytes=VMEM)


def cost(flops, nbytes, exps=0):
    return pl.CostEstimate(
        flops=flops // HASTE, bytes_accessed=nbytes // HASTE, transcendentals=exps // HASTE
    )


def kernel_call(kernel, prefetch, grid, specs, args, out_specs, out_shape, estimate, hold=()):
    count = len(prefetch) + len(args)

    def run(*refs):
        kernel(*refs[:count], *refs[count + len(hold) :])

    return pl.pallas_call(
        run,
        grid_spec=pltpu.PrefetchScalarGridSpec(
            num_scalar_prefetch=len(prefetch),
            grid=grid,
            in_specs=list(specs) + [pl.BlockSpec(memory_space=pl.ANY)] * len(hold),
            out_specs=out_specs,
        ),
        out_shape=out_shape,
        compiler_params=params(),
        cost_estimate=estimate,
    )(*prefetch, *args, *hold)


def pin(value, *hold):
    def run(*refs):
        del refs

    anywhere = pl.BlockSpec(memory_space=pl.ANY)
    return pl.pallas_call(
        run,
        in_specs=[anywhere] * (1 + len(hold)),
        out_specs=anywhere,
        out_shape=jax.ShapeDtypeStruct(value.shape, value.dtype),
        input_output_aliases={0: 0},
        compiler_params=params(),
        cost_estimate=cost(0, 0),
    )(value, *hold)


def still(shape, first=0):
    return pl.BlockSpec(shape, lambda *_: (first,) + (0,) * (len(shape) - 1))


def in_order(block):
    h, z, t, r, n = block.shape
    rows = [block[o, :, i].reshape(z * r, n) for o in range(h) for i in range(t)]
    return jnp.concatenate(rows, axis=0) if len(rows) > 1 else rows[0]


def half_of(start, which, size):
    at = start if which == 0 else 1 - start
    return pl.ds(pl.multiple_of(at * size, size), size)


def forward_kernel(style, count, spread, cuts, per_cut, start_ref, *refs):
    pieces, weights, rest = refs[:count], refs[count : count + 2 * cuts], refs[count + 2 * cuts :]
    start = start_ref[0]
    load = in_order if spread else (lambda b: b.reshape(-1, b.shape[-1]))
    firsts, seconds = load(weights[0][...]), load(weights[1][...])
    for i in range(1, cuts):
        late = pl.program_id(0) >= i * per_cut
        firsts = jnp.where(late, load(weights[2 * i][...]), firsts)
        seconds = jnp.where(late, load(weights[2 * i + 1][...]), seconds)
    size = firsts.shape[0]
    if style == "bare":
        outs = rest
    else:
        bias, outs = rest[0][...], rest[1:]
    at = 0
    for ref in pieces:
        views = [ref] if len(ref.shape) == 2 else [ref.at[i] for i in range(ref.shape[0])]
        for view in views:
            value = dot(view[:, half_of(start, 0, size)], firsts, 1, 0)
            value = value + dot(view[:, half_of(start, 1, size)], seconds, 1, 0)
            if style == "bare":
                outs[at][...] = value.astype(BF)
            elif style == "plain":
                outs[0][at] = (value + bias).astype(BF)
            else:
                value = value + bias
                phi = 0.5 + 0.5 * lax.erf(value * ROOT_HALF)
                outs[0][at] = (value * phi).astype(BF)
                outs[1][at] = (phi + value * DENSITY_SCALE * jnp.exp(-0.5 * value * value)).astype(BF)
            at += 1


def forward_product(pieces, weights, start, bias=None, style="plain", pick=None, rows=512, hold=()):
    whole = len(weights[0]) == 1
    sample = weights[0][0]
    spread = sample.ndim == 5
    paired = sample.ndim == 4
    cuts = len(weights)
    n = sample.shape[-1] * cuts
    tile = min(n // cuts, TILE)
    per_cut = n // cuts // tile
    stack = pieces[0].ndim == 3
    if stack:
        total = pick[1] if pick else pieces[0].shape[0]
        specs = [still((total,) + pieces[0].shape[1:], pick[0] if pick else 0)]
        k = pieces[0].shape[2]
    else:
        total, k = len(pieces), pieces[0].shape[1]
        specs = [still(p.shape) for p in pieces]
    lead = sample.shape[:-1]
    args = list(pieces)
    for i, pair in enumerate(weights):

        def at(j, s, i=i):
            return (0,) * len(lead) + (jnp.clip(j - i * per_cut, 0, per_cut - 1),)

        if paired:
            z, _, b, _ = sample.shape
            specs += [pl.BlockSpec((z, 1, b, tile), lambda j, s, h=h: (0, h, 0, j)) for h in range(2)]
            args += [pair[0], pair[0]]
        elif whole:
            specs += [pl.BlockSpec((lead[0] // 2, tile), lambda j, s, h=h: (h, j)) for h in range(2)]
            args += [pair[0], pair[0]]
        else:
            specs += [pl.BlockSpec(lead + (tile,), at)] * 2
            args += list(pair)
    if style != "bare":
        specs.append(pl.BlockSpec((1, tile), lambda j, s: (0, j)))
        args.append(bias.reshape(1, n))
    if style == "bare":
        out_specs = [pl.BlockSpec((rows, tile), lambda j, s: (0, j))] * total
        out_shape = [jax.ShapeDtypeStruct((rows, n), BF)] * total
    else:
        copies = 2 if style == "gate" else 1
        out_specs = [pl.BlockSpec((total, rows, tile), lambda j, s: (0, 0, j))] * copies
        out_shape = [jax.ShapeDtypeStruct((total, rows, n), BF)] * copies
    return kernel_call(
        functools.partial(forward_kernel, style, len(pieces), spread, cuts, per_cut),
        [start],
        (n // tile,),
        specs,
        args,
        out_specs,
        out_shape,
        cost(2 * total * rows * k * n, 2 * (total * rows * (k + n) + k * n)),
        hold,
    )


def back_kernel(style, count, shares, per_half, start_ref, *refs):
    pieces, weights, rest = refs[:count], refs[count : count + 2 * shares], refs[count + 2 * shares :]
    late = pl.program_id(0) >= per_half
    chosen = []
    for i in range(shares):
        w0, w1 = weights[2 * i][...], weights[2 * i + 1][...]
        if len(w0.shape) == 5:
            w0, w1 = in_order(w0), in_order(w1)
        elif len(w0.shape) == 4:
            w0, w1 = w0[0, 0], w1[0, 0]
        chosen.append(jnp.where(late, w1, w0))
    views = []
    for ref in pieces:
        views += [ref] if len(ref.shape) == 2 else [ref.at[i] for i in range(ref.shape[0])]
    width = chosen[0].shape[1]
    total = None
    for at, view in enumerate(views):
        value = dot(view[:, :width], chosen[0], 1, 1)
        for i in range(1, shares):
            value = value + dot(view[:, i * width : (i + 1) * width], chosen[i], 1, 1)
        if style == "slope":
            low = (value * rest[0][at].astype(F32)).astype(BF)
            rest[1][at] = low
            part = jnp.sum(low.astype(F32), axis=0, keepdims=True)
            total = part if total is None else total + part
        elif style == "plain":
            rest[0][at] = value.astype(BF)
        else:
            rest[at][...] = value.astype(BF)
    if style == "slope":
        rest[2][...] = total


def back_product(pieces, weights, start, style="plain", slope=None, pick=None, rows=512, hold=()):
    shares = len(weights)
    sample = weights[0][0]
    k = sample.shape[-1]
    half_rows = 1
    for d in sample.shape[:-1]:
        half_rows *= d
    whole = len(weights[0]) == 1
    if whole:
        half_rows //= 2
    n = 2 * half_rows
    tile = min(half_rows, TILE)
    per_half = half_rows // tile
    stack = pieces[0].ndim == 3
    if stack:
        total = pick[1] if pick else pieces[0].shape[0]
        specs = [still((total,) + pieces[0].shape[1:], pick[0] if pick else 0)]
    else:
        total = len(pieces)
        specs = [still(p.shape) for p in pieces]
    if sample.ndim == 4:
        tile = sample.shape[2]
        per_half = sample.shape[0]
        block = (1, 1, tile, k)
    elif sample.ndim == 5:
        h, z, t, r, _ = sample.shape
        group = max(1, tile // (z * r))
        tile = group * z * r
        per_half = half_rows // tile
        each = t // group
        block = (1, z, group, r, k)

        def at(j):
            return (j // each, 0, j % each, 0, 0)
    else:
        block = (tile, k)

        def at(j):
            return (j, 0)

    if sample.ndim == 4:
        first = pl.BlockSpec(block, lambda j, s: (jnp.minimum(j, per_half - 1), 0, 0, 0))
        second = pl.BlockSpec(block, lambda j, s: (jnp.maximum(j - per_half, 0), 1, 0, 0))
    else:
        first = pl.BlockSpec(block, lambda j, s: at(jnp.minimum(j, per_half - 1)))
        second = pl.BlockSpec(block, lambda j, s: at(jnp.maximum(j - per_half, 0) + (per_half if whole else 0)))
    args = list(pieces)
    for w in weights:
        specs += [first, second]
        args += [w[0], w[-1]]

    def column(j, s):
        return lax.rem(s[0] * per_half + j, 2 * per_half)

    stacked = pl.BlockSpec((total, rows, tile), lambda j, s: (0, 0, column(j, s)))
    stack_shape = jax.ShapeDtypeStruct((total, rows, n), BF)
    if style == "slope":
        specs.append(stacked)
        args.append(slope)
        out_specs = [stacked, pl.BlockSpec((1, tile), lambda j, s: (0, column(j, s)))]
        out_shape = [stack_shape, jax.ShapeDtypeStruct((1, n), F32)]
    elif style == "plain":
        out_specs, out_shape = [stacked], [stack_shape]
    else:
        out_specs = [pl.BlockSpec((rows, tile), lambda j, s: (0, column(j, s)))] * total
        out_shape = [jax.ShapeDtypeStruct((rows, n), BF)] * total
    return kernel_call(
        functools.partial(back_kernel, style, len(pieces), shares, per_half),
        [start],
        (2 * per_half,),
        specs,
        args,
        out_specs,
        out_shape,
        cost(2 * total * rows * k * n * shares, 2 * (total * rows * (k * shares + n) + k * n)),
        hold,
    )


def weight_kernel(left_count, right_count, start_ref, *refs):
    lefts, rights, out = refs[:left_count], refs[left_count : left_count + right_count], refs[-1]

    def views(group):
        found = []
        for ref in group:
            found += [ref] if len(ref.shape) == 2 else [ref.at[i] for i in range(ref.shape[0])]
        return found

    total = None
    for a, b in zip(views(lefts), views(rights)):
        part = dot(a[...], b[...], 0, 0)
        total = part if total is None else total + part
    low = total.astype(BF)
    if len(out.shape) == 2:
        out[...] = low
    else:
        h, z, t, r, n = out.shape
        for o in range(h):
            for i in range(t):
                base = (o * t + i) * z * r
                out[o, :, i] = low[base : base + z * r].reshape(z, r, n)


def weight_product(left, right, start, which, spread=None, cut=(0, 1, 1), tile=512, hold=()):
    def spec(group, width, index):
        found = []
        for a in group:
            if a.ndim == 2:
                found.append(pl.BlockSpec((a.shape[0], width), lambda j, s: (0, index(j, s))))
            else:
                found.append(pl.BlockSpec(a.shape[:2] + (width,), lambda j, s: (0, 0, index(j, s))))
        return found

    half = left[0].shape[-1] // (1 if which is None else 2)
    share = right[0].shape[-1] // cut[2]
    n = share * (cut[1] - cut[0])
    tile = min(tile, share)
    skip = cut[0] * (share // tile)
    rows = sum(a.shape[0] if a.ndim == 2 else a.shape[0] * a.shape[1] for a in left)
    specs = spec(left, half, lambda j, s: 0 if which is None else s[0] if which == 0 else 1 - s[0])
    specs += spec(right, tile, lambda j, s: j + skip)
    shape = (half, n) if spread is None else spread + (n,)
    block = shape[:-1] + (tile,)
    return kernel_call(
        functools.partial(weight_kernel, len(left), len(right)),
        [start],
        (n // tile,),
        specs,
        [*left, *right],
        pl.BlockSpec(block, lambda j, s: (0,) * (len(block) - 1) + (j,)),
        jax.ShapeDtypeStruct(shape, BF),
        cost(2 * rows * half * n, 2 * (rows * (half + n) + half * n)),
        hold,
    )


def pair_masks():
    lane = lax.broadcasted_iota(jnp.int32, (1, 2 * HD), 1)
    low = jnp.where(lane < HD, 1.0, 0.0).astype(BF)
    high = jnp.where(lane < HD, 0.0, 1.0).astype(BF)
    return low, high


def pair_probs(q_two, k):
    scores = dot(q_two, k, 1, 1) * 0.125
    row = lax.broadcasted_iota(jnp.int32, scores.shape, 0) & (SLOT - 1)
    column = lax.broadcasted_iota(jnp.int32, scores.shape, 1)
    scores = jnp.where(row >= column, scores, MASKED)
    exponent = jnp.exp(scores - jnp.max(scores, axis=-1, keepdims=True))
    return exponent / jnp.sum(exponent, axis=-1, keepdims=True)


def attend_kernel(q_ref, k_ref, v_ref, context_ref):
    low, high = pair_masks()
    for at in range(0, context_ref.shape[1], 2 * HD):
        q, k, v = [ref[:, at : at + 2 * HD] for ref in (q_ref, k_ref, v_ref)]
        probs = pair_probs(jnp.concatenate([q * low, q * high], axis=0), k).astype(BF)
        context = dot(probs[:SLOT], v * low, 1, 0) + dot(probs[SLOT:], v * high, 1, 0)
        context_ref[:, at : at + 2 * HD] = context.astype(BF)


def attend_back_kernel(q_ref, k_ref, v_ref, grad_ref, out_ref, sum_ref):
    part = grad_ref.shape[1]
    low, high = pair_masks()

    @pl.when(pl.program_id(0) == 0)
    def _():
        sum_ref[...] = jnp.zeros_like(sum_ref)

    for at in range(0, part, 2 * HD):
        q, k, v, grad = [ref[:, at : at + 2 * HD] for ref in (q_ref, k_ref, v_ref, grad_ref)]
        q_two = jnp.concatenate([q * low, q * high], axis=0)
        g_two = jnp.concatenate([grad * low, grad * high], axis=0)
        probs = pair_probs(q_two, k)
        d_probs = dot(g_two, v, 1, 1)
        row_dot = jnp.sum(probs * d_probs, axis=-1, keepdims=True)
        d_scores = (probs * (d_probs - row_dot)).astype(BF)
        d_q = dot(d_scores[:SLOT], k * low, 1, 0) + dot(d_scores[SLOT:], k * high, 1, 0)
        d_k = dot(d_scores, q_two, 0, 0)
        d_v = dot(probs.astype(BF), g_two, 0, 0)
        for i, value in enumerate((d_q * 0.125, d_k * 0.125, d_v)):
            where = slice(i * part + at, i * part + at + 2 * HD)
            value = value.astype(BF)
            out_ref[:, where] = value
            sum_ref[:, where] += jnp.sum(value.astype(F32), axis=0, keepdims=True)


def attend(q, k, v, hold=()):
    rows, part = q.shape
    one = pl.BlockSpec((SLOT, part), lambda i: (i, 0))
    return kernel_call(
        attend_kernel,
        [],
        (rows // SLOT,),
        [one] * 3,
        [q, k, v],
        one,
        jax.ShapeDtypeStruct((rows, part), BF),
        cost(32 * rows * SLOT * part, 8 * rows * part, rows * SLOT * part // HD),
        hold,
    )


def attend_back(q, k, v, grad, first, hold=()):
    rows, part = grad.shape
    one = pl.BlockSpec((SLOT, part), lambda i: (i, 0))
    shifted = pl.BlockSpec((SLOT, part), lambda i: (i + first, 0))
    return kernel_call(
        attend_back_kernel,
        [],
        (rows // SLOT,),
        [shifted] * 3 + [one],
        [q, k, v, grad],
        [pl.BlockSpec((SLOT, 3 * part), lambda i: (i, 0)), still((1, 3 * part))],
        [jax.ShapeDtypeStruct((rows, 3 * part), BF), jax.ShapeDtypeStruct((1, 3 * part), F32)],
        cost(80 * rows * SLOT * part, 14 * rows * part, rows * SLOT * part // HD),
        hold,
    )


def normal_of(values):
    centred = values - jnp.mean(values, axis=-1, keepdims=True)
    inverse = lax.rsqrt(jnp.mean(centred * centred, axis=-1, keepdims=True) + EPSILON)
    return centred * inverse, inverse


def rows_of(refs):
    total = refs[0][...].astype(F32)
    for ref in refs[1:]:
        total = total + ref[...].astype(F32)
    return total


def norm_kernel(x_ref, gain_ref, shift_ref, out_ref):
    normal, _ = normal_of(x_ref[...].astype(F32))
    out_ref[...] = (normal * gain_ref[...] + shift_ref[...]).astype(BF)


def join_norm_kernel(count, *refs):
    bias, gain, shift, hidden_ref, out_ref = refs[count:]
    hidden = rows_of(refs[:count]) + bias[...]
    hidden_ref[...] = hidden
    normal, _ = normal_of(hidden)
    out_ref[...] = (normal * gain[...] + shift[...]).astype(BF)


def join_kernel(count, *refs):
    refs[count + 1][...] = (rows_of(refs[:count]) + refs[count][...]).astype(BF)


def norm_back_kernel(count, *refs):
    source, carry, gain, grad_ref, low_ref, sums = refs[count:]
    grad = rows_of(refs[:count])
    normal, inverse = normal_of(source[...].astype(F32))
    scaled = grad * gain[...]
    centre = jnp.mean(scaled, axis=-1, keepdims=True)
    projected = jnp.mean(scaled * normal, axis=-1, keepdims=True)
    carried = carry[...].astype(F32)
    result = carried + inverse * (scaled - centre - normal * projected)
    grad_ref[...] = result.astype(grad_ref.dtype)
    low = result.astype(BF)
    low_ref[...] = low

    @pl.when(pl.program_id(0) == 0)
    def _():
        sums[...] = jnp.zeros_like(sums)

    for i, value in enumerate((grad * normal, grad, low.astype(F32), carried)):
        sums[i : i + 1] += jnp.sum(value, axis=0, keepdims=True)


def add_kernel(a_ref, b_ref, out_ref):
    out_ref[...] = (a_ref[...].astype(F32) + b_ref[...].astype(F32)).astype(BF)


def add_low(a, b, hold=()):
    width = a.shape[-1]
    flat = [x.reshape(-1, width) for x in (a, b)]
    rows = flat[0].shape[0]
    step = min(rows, 256)
    one = pl.BlockSpec((step, width), lambda i: (i, 0))
    result = kernel_call(
        add_kernel,
        [],
        (rows // step,),
        [one, one],
        flat,
        one,
        jax.ShapeDtypeStruct((rows, width), BF),
        cost(rows * width, 6 * rows * width),
        hold,
    )
    return result.reshape(a.shape)


def row_call(kernel, blocks, vectors, outs, sums=0, step=128, hold=()):
    rows, width = blocks[0].shape
    one = pl.BlockSpec((step, width), lambda i: (i, 0))
    out_specs = [one] * len(outs)
    out_shape = [jax.ShapeDtypeStruct((rows, width), d) for d in outs]
    if sums:
        out_specs.append(still((sums, width)))
        out_shape.append(jax.ShapeDtypeStruct((sums, width), F32))
    return kernel_call(
        kernel,
        [],
        (rows // step,),
        [one] * len(blocks) + [still((1, width))] * len(vectors),
        [*blocks, *[v.reshape(1, width) for v in vectors]],
        out_specs,
        out_shape,
        cost(20 * rows * width, 16 * rows * width),
        hold,
    )


def body(
    tokens,
    cotangent,
    doc_starts,
    active_len,
    ln1_gain,
    ln1_bias,
    q_weight,
    q_bias,
    k_weight,
    v_weight,
    v_bias,
    o_weight,
    o_bias,
    ln2_gain,
    ln2_bias,
    up_weight,
    up_bias,
    down_weight,
    down_bias,
):
    depth = lax.axis_size("fsdp")
    outer = lax.axis_size("outer")
    devices = outer * TEAM * depth
    member, me = lax.axis_index("team"), lax.axis_index("outer")
    layer = lax.axis_index("fsdp")
    start = (me if outer == 2 else jnp.zeros_like(me)).reshape(1)
    groups, row_len, width = tokens.shape
    docs = doc_starts.shape[1]
    r = q_weight.shape[0]
    part_width = width // TEAM
    rows = groups * docs * SLOT

    zero_bias = jnp.zeros((part_width,), F32)

    def depth_gather(a):
        return lax.all_gather(a, "fsdp", axis=0, tiled=True)

    def columns(a, i, n):
        c = a.shape[1] // n
        return a[:, i * c : (i + 1) * c]

    def stored(block):
        return block.reshape(1, depth, TEAM, r, block.shape[1])

    def flat(block):
        return block[None]

    def both_halves(block, *hold):
        return outer_halves(pin(block, *hold) if hold else block, me)

    def flatten(halves):
        return [h.reshape(-1, h.shape[-1]) for h in halves]

    qkv_deal = deal_columns((q_weight, k_weight, v_weight), member, outer, depth)
    block_q, block_k, block_v = [stored(depth_gather(columns(qkv_deal, i, 3))) for i in range(3)]
    w_q, w_k = [both_halves(b) for b in (block_q, block_k)]
    block_o = flat(depth_gather(o_weight))

    vectors = (ln1_gain, ln1_bias, o_bias, ln2_gain, ln2_bias, down_bias, q_bias, v_bias, up_bias)
    packed = gather_small(jnp.concatenate(vectors), member, me, layer)
    edges = [0]
    for v in vectors:
        edges.append(edges[-1] + v.shape[0])
    pieces = [packed[:, edges[i] : edges[i + 1]] for i in range(len(vectors))]
    gain1, shift1, bias_o, gain2, shift2, bias_down = [p.reshape(-1) for p in pieces[:6]]

    def member_part(p):
        whole = p.reshape(outer, TEAM, depth, -1)
        return lax.dynamic_index_in_dim(whole, member, 1, False).reshape(-1)

    bias_q, bias_v, bias_up = [member_part(p) for p in pieces[6:]]

    position = jnp.arange(row_len, dtype=jnp.int32)
    offset = jnp.arange(SLOT, dtype=jnp.int32)
    wanted = doc_starts[:, :, None] + offset
    live = offset < active_len[:, :, None]
    chosen = (wanted[..., None] == position) & live[..., None]
    chosen = chosen.reshape(groups, docs * SLOT, row_len)
    select = chosen.astype(BF)
    covered = jnp.any(chosen, axis=1)

    def pack(source):
        picked = jnp.einsum("gst,gtd->gsd", select, source, preferred_element_type=F32)
        return picked.reshape(rows, width).astype(BF)

    def unpack(slot_rows, fallback):
        blocks = slot_rows.reshape(groups, docs * SLOT, width)
        placed = jnp.einsum("gst,gsd->gtd", select, blocks, preferred_element_type=F32).astype(BF)
        return jnp.where(covered[..., None], placed, fallback)

    class Order:
        last = ()

        def step(self, kernel, *args, hold=(), **kw):
            result = kernel(*args, hold=self.last + tuple(hold), **kw)
            self.last = (jax.tree.leaves(result)[-1],)
            return result

    order = Order()

    def begin(weights):
        return jnp.zeros_like(start) if len(weights[0]) == 1 and outer != 2 else start

    def forward(pieces, weights, *rest, **kw):
        return order.step(forward_product, pieces, weights, begin(weights), *rest, rows=rows, **kw)

    def back(pieces, weights, **kw):
        return order.step(back_product, pieces, weights, begin(weights), rows=rows, **kw)

    def weight_grad(left, right, which, **kw):
        return order.step(weight_product, left, right, start, which, **kw)

    def by_rows(kernel, blocks, *args, **kw):
        return order.step(row_call, kernel, blocks, *args, **kw)

    def add(a, b, **kw):
        return order.step(add_low, a, b, **kw)

    def team_gather(own, *hold):
        across = team_swap(own, 2)
        if hold:
            across = pin(across, *hold)
        return [own, across, team_swap(own, 1), team_swap(across, 1)]

    def send_far(parts):
        return [team_swap(p, 1) for p in parts]

    def join_near(near, far, **kw):
        across = add(near[1], far[1], **kw)
        return [near[0], far[0], team_swap(across, 2), across]

    x_rows = pack(tokens)
    down_pair = jnp.stack([down_weight, outer_pass(down_weight)])[None]
    (a_own,) = by_rows(norm_kernel, [x_rows], [gain1, shift1], [BF], hold=[down_pair])
    up_deal = deal_columns((pin(up_weight, a_own),), member, outer, depth)
    a_all = team_gather(pin(a_own, block_o), w_q[1], w_k[1], up_deal)
    block_up = [stored(depth_gather(columns(up_deal, i, 2))) for i in range(2)]
    if outer == 2:
        w_down = [[depth_gather(down_pair)]]
    else:
        w_down = [[lax.all_gather(down_weight, SPREAD, axis=0, tiled=True)]]
    g_rows = pack(cotangent)
    g_all = team_gather(pin(g_rows, a_all[1]))

    wide = TEAM * rows
    q = forward(a_all, [w_q], bias_q)[0]
    k = forward(a_all, [w_k], zero_bias)[0]
    w_v = both_halves(block_v)
    v = forward(a_all, [w_v], bias_v)[0]
    w_o = flatten(both_halves(block_o))
    q, k, v = [s.reshape(wide, part_width) for s in (q, k, v)]
    context = order.step(attend, q, k, v).reshape(TEAM, rows, part_width)
    o_far = send_far(forward([context], [w_o], style="bare", pick=(1, 2), hold=[g_all[1]]))
    o_near = forward([context], [w_o], style="bare", pick=(0, 2))
    w_up = [both_halves(block_up[0], context)]
    *o_parts, o_across = join_near(o_near, o_far)
    hidden, b_own = by_rows(
        functools.partial(join_norm_kernel, 4),
        [x_rows] + o_parts,
        [bias_o, gain2, shift2],
        [F32, BF],
        hold=[w_up[0][1]],
    )
    w_up.append(both_halves(block_up[1], b_own))
    b_all = team_gather(b_own, w_up[1][1])

    active, slope = forward(b_all, w_up, bias_up, style="gate")

    def depth_scatter(a):
        return lax.psum_scatter(a, "fsdp", scatter_dimension=0, tiled=True)

    def send_away(away, *hold):
        if outer != 2:
            return away
        return outer_pass(pin(away, *hold) if hold else away)

    def settle(sent, mine, **kw):
        c = mine.shape[-1]
        if outer == 2:
            total = add(sent, mine, **kw)
        else:
            both = jnp.concatenate([mine.reshape(outer // 2, -1, c), sent.reshape(outer // 2, -1, c)])
            total = outer_scatter(both, me)
        return depth_scatter(total.reshape(-1, c))

    spread = (outer // 2, depth, TEAM, r)

    def settle_whole(grad):
        return lax.psum_scatter(grad, SPREAD, scatter_dimension=0, tiled=True)

    grad_down = [settle_whole(weight_grad([active], g_all, None, cut=(0, 1, 2)))]
    d_inner, sum_inner = back(g_all, w_down, style="slope", slope=slope)
    n_far = send_far(back([d_inner], w_up, style="bare", pick=(1, 2)))
    n_near = back([d_inner], w_up, style="bare", pick=(0, 2))
    n_parts = join_near(n_near, n_far)[:3]
    up_sent = [send_away(weight_grad(b_all, [d_inner], 1, spread=spread, cut=(0, 1, 2)))]
    grad_down.append(settle_whole(weight_grad([active], g_all, None, cut=(1, 2, 2))))
    up_sent.append(send_away(weight_grad(b_all, [d_inner], 1, spread=spread, cut=(1, 2, 2))))
    up_mine = [weight_grad(b_all, [d_inner], 0, spread=spread, cut=(0, 1, 2))]
    d_hidden, d_out, sums2 = by_rows(
        functools.partial(norm_back_kernel, 3), n_parts + [hidden, g_rows], [gain2], [F32, BF], sums=4
    )
    y_far = send_far(forward([active], w_down, style="bare", pick=(1, 2), hold=[grad_down[0]]))
    y_near = forward([active], w_down, style="bare", pick=(0, 2))
    up_mine.append(weight_grad(b_all, [d_inner], 0, spread=spread, cut=(1, 2, 2)))
    d_out_all = team_gather(d_out, up_sent[0], up_mine[1])

    (d_near,) = back(d_out_all[:2], [w_o])
    grad_up = [settle(up_sent[0], up_mine[0])]
    *y_parts, y_across = join_near(y_near, y_far)
    (d_far,) = back(d_out_all[2:], [w_o], hold=[grad_down[1]])
    q_far, sum_far = order.step(attend_back, q, k, v, d_far.reshape(2 * rows, -1), 2 * rows // SLOT)
    q_far = q_far.reshape(2, rows, -1)
    a_far = send_far(back([q_far], [w_q, w_k, w_v], style="bare"))
    grad_up.append(settle(up_sent[1], up_mine[1]))
    o_sent = send_away(weight_grad([context], d_out_all, 1))
    o_mine = weight_grad([context], d_out_all, 0)
    q_near, sum_near = order.step(attend_back, q, k, v, d_near.reshape(2 * rows, -1), 0, hold=[grad_up[0]])
    q_near = q_near.reshape(2, rows, -1)
    grad_o = settle(o_sent, o_mine)
    a_near = back([q_near], [w_q, w_k, w_v], style="bare")
    a_parts = join_near(a_near, a_far, hold=[y_parts[2]])[:3]
    parts = ((0, 1, 3), (1, 3, 3))
    d_both = [q_near, q_far]
    qkv_sent = [
        send_away(weight_grad(a_all, d_both, 1, spread=spread, cut=parts[0], hold=[grad_up[1]])),
        send_away(weight_grad(a_all, d_both, 1, spread=spread, cut=parts[1], hold=[grad_o])),
    ]
    grad_q = settle(qkv_sent[0], weight_grad(a_all, d_both, 0, spread=spread, cut=parts[0]))
    (y_rows,) = by_rows(functools.partial(join_kernel, 4), [hidden] + y_parts, [bias_down], [BF])
    layer_out = unpack(y_rows, tokens)
    (grad_up,) = return_columns(jnp.concatenate(grad_up, axis=1), member, outer, depth, 1)
    held = [a_parts[2], layer_out, grad_up]
    kv_mine = weight_grad(a_all, d_both, 0, spread=spread, cut=parts[1], hold=held)
    grad_kv = settle(qkv_sent[1], kv_mine)
    _, d_input, sums1 = by_rows(
        functools.partial(norm_back_kernel, 3), a_parts + [x_rows, d_hidden], [gain1], [BF, BF], sums=4
    )
    sum_qkv = sum_far + sum_near
    grad_o = grad_o.astype(F32)
    input_grad = unpack(d_input, cotangent)
    grad_down = jnp.concatenate([g.astype(F32) for g in grad_down], axis=1)
    (grad_q,) = return_columns(grad_q, member, outer, depth, 1)
    grad_k, grad_v = return_columns(grad_kv, member, outer, depth, 2)

    whole_sums = [sums1[0], sums1[1], sums2[2], sums2[0], sums2[1], sums2[3]]
    part_sums = [sum_qkv[0, :part_width], sum_qkv[0, 2 * part_width :], sum_inner[0]]
    is_mine = (jnp.arange(TEAM) == member)[None, :, None, None]

    def widen(s):
        blocks = s.reshape(outer, 1, depth, -1)
        return jnp.where(is_mine, blocks, 0.0).reshape(devices, -1)

    table = jnp.concatenate([s.reshape(devices, -1) for s in whole_sums] + [widen(s) for s in part_sums], axis=1)
    small = reduce_small(table, member, me, layer)
    cuts = [small[edges[i] : edges[i + 1]] for i in range(len(vectors))]
    g_gain1, g_shift1, g_bias_o, g_gain2, g_shift2, g_bias_down, g_bias_q, g_bias_v, g_bias_up = cuts
    return (
        layer_out,
        input_grad,
        g_gain1,
        g_shift1,
        grad_q,
        g_bias_q,
        grad_k,
        grad_v,
        g_bias_v,
        grad_o,
        g_bias_o,
        g_gain2,
        g_shift2,
        grad_up,
        g_bias_up,
        grad_down,
        g_bias_down,
    )


def solution(mesh):
    outer = mesh.shape["dp"] // TEAM
    devices = mesh.devices.reshape(outer, TEAM, mesh.shape["fsdp"])
    fine = Mesh(devices, ALL)
    kinds = {"t": P(ALL, None, None), "w": P(ALL, None), "v": P(ALL)}
    vectors = "vvwvwwvwvvvwvwv"
    in_specs = tuple(kinds[c] for c in "ttww" + vectors)
    out_specs = tuple(kinds[c] for c in "tt" + vectors)
    return jax.shard_map(body, mesh=fine, in_specs=in_specs, out_specs=out_specs, check_vma=False)
```

time: 1270 us -> 886 us (0.70)
  Pallas kernels: 0 us -> 403 us
  matrix products: 289 us -> 18.6 us
  waiting for transfers between devices: 545 us -> 275 us
  other arithmetic: 132 us -> 14.8 us
  local copies, waits for them, and re-layouts: 179 us -> 104 us
  blocking collectives: 70.7 us -> 0 us
    pallas_call x0 -> x52, Pallas kernels: none -> 403 us  [the longest x44 403 us: kernel_call(): pl.pallas_call(run, grid_spec=pltpu.PrefetchScalarGridSpec(num_scalar_pre...]
    dot_general x12 -> x1, matrix products: 228 us -> 0.13 us  [dot(): lax.dot_general(a, b, (((ca,), (cb,)), ((), ())), preferred_element_type=...]
    ppermute x48 -> x65, waiting for transfers between devices: 455 us -> 265 us  [the longest x45 123 us: team_swap(): return lax.ppermute(a, 'team', [(i, i ^ flip) for i in range(TEAM)])]
    all_gather x1 -> x0, blocking collectives: 70.7 us -> none  [body(): packed = lax.all_gather(jnp.concatenate(vectors), BOTH, axis=0, tiled=False)]
    reshape x36 -> x21, local copies, waits for them, and re-layouts: 67.3 us -> 5.67 us  [the longest x16 3.35 us: deal_columns(): lax.dynamic_index_in_dim(w, member ^ flip, 2, False).reshape(r, -1)]
    reduce_scatter x4 -> x5, waiting for transfers between devices: 60.8 us -> 0.05 us  [depth_scatter(): return lax.psum_scatter(a, 'fsdp', scatter_dimension=0, tiled=True)]
    unnamed x161 -> x239, local copies, waits for them, and re-layouts: 36.7 us -> 73.5 us
    convert_element_type x16 -> x5, other arithmetic: 35.2 us -> 4.31 us  [the longest x4 3.48 us: return_columns(): result.append(cols.reshape(r, -1).astype(F32))]
  transfers between devices with their start and end apart: 57 -> 79, of which waited for: 22 -> 31; matrix products, arithmetic and copies ran while one was open for 40% -> 6% of each run, Pallas kernels for 0% -> 46%
where the time goes in v2:
time: 886 us; the launch traced here: 876 us
  Pallas kernels  403 us (45%)
  waiting for transfers between devices  275 us (31%)
  local copies, waits for them, and re-layouts  104 us (12%)
  starting transfers between devices  44.5 us (5%)
  matrix products  18.6 us (2%)
  between operations  15.9 us (2%)
  other arithmetic  14.8 us (2%)
    pallas_call x44, Pallas kernels, kernel_call(): pl.pallas_call(run, grid_spec=pltpu.PrefetchScalarGridSpec(num_scalar_pre...  403 us
    ppermute x45, waiting for transfers between devices, team_swap(): return lax.ppermute(a, 'team', [(i, i ^ flip) for i in range(TEAM)])  123 us
    ppermute x12, waiting for transfers between devices, outer_pass(): lax.ppermute(a, 'outer', [(o, order[(p + 1) % outer]) for p, o in enumera...  123 us
    unnamed x239, local copies, waits for them, and re-layouts  73.5 us
    ppermute x45, starting transfers between devices, team_swap(): return lax.ppermute(a, 'team', [(i, i ^ flip) for i in range(TEAM)])  20.7 us
    ppermute x8, waiting for transfers between devices, shift_pass(): return lax.ppermute(a, axis, [(i, (i + step) % size) for i in range(size)])  18.4 us
  transfers between devices with their start and end apart: 79, of which 31 were waited for; matrix products, arithmetic and copies ran while one was open for 6% of the time, Pallas kernels for 46%

profile of v2, /device:TPU:0, one launch (start us, length us, event | category | flops | bytes accessed | tf_op | source)
XLA Modules:
  0.0 875.6 jit_solution(15676292396412957263)
XLA Ops:
  35.1 4.6 fusion.4.refs_0_.refs_3_
  39.7 16.8 %collective-permute-done.3 = bf16[4,768]{1,0:T(4,128)(2,1)S(1)} collective-permute-done((bf16[4,768]{1,0:T(4,128)(2,1)S(1)}, bf16[4,768]{1,0:T(4,128)(2,1)S(1)}, u32[]{:S(2)}, u32[]{:S(2)}) %collective-permute-start.3) | collective-permute-done | bytes 6176 | tf_op jit(solution)/shard_map/ppermute | solution.py:116
  73.7 5.0 collective-permute-done.14
  78.7 6.3 collective-permute-done.15
  94.7 9.0 %all-gather.13.cloned.1.call-done = bf16[1024,512]{1,0:T(8,128)(2,1)} async-done(((bf16[256,512]{1,0:T(8,128)(2,1)}), bf16[1024,512]{1,0:T(8,128)(2,1)}) %all-gather.13.cloned.1.call-update) | async-done | bytes 1048592 | tf_op jit(solution)/shard_map/all_gather | solution.py:690
  105.2 14.3 %collective-permute-done.12.refs_1_.refs_6_.refs_3_ = bf16[1,4,4,64,512]{4,3,2,1,0:T(8,128)(2,1)S(1)} collective-permute-done((bf16[1,4,4,64,512]{4,3,2,1,0:T(8,128)(2,1)}, bf16[1,4,4,64,512]{4,3,2,1,0:T(8,128)(2,1)S(1)}, u32[]{:S(2)}, u32[]{:S(2)}) %collective-permute-start.12) | collective-permute-done | bytes 1048608 | tf_op jit(solution)/shard_map/ppermute | solution.py:43
  119.5 20.7 %collective-permute-done.13.refs_2_.refs_6_.refs_5_ = bf16[1,4,4,64,512]{4,3,2,1,0:T(8,128)(2,1)S(1)} collective-permute-done((bf16[1,4,4,64,512]{4,3,2,1,0:T(8,128)(2,1)}, bf16[1,4,4,64,512]{4,3,2,1,0:T(8,128)(2,1)S(1)}, u32[]{:S(2)}, u32[]{:S(2)}) %collective-permute-start.13) | collective-permute-done | bytes 1048608 | tf_op jit(solution)/shard_map/ppermute | solution.py:43
  156.0 8.6 shard_map.324.refs_8_
  165.9 8.6 shard_map.325.refs_8_
  177.7 8.5 shard_map.326.refs_3_
  187.6 13.9 %shard_map.327.refs_4_ = bf16[2048,512]{1,0:T(8,128)(2,1)S(1)} custom-call(bf16[2048,512]{1,0:T(8,128)(2,1)S(1)} %bitcast.165, bf16[2048,512]{1,0:T(8,128)(2,1)} %bitcast.168, bf16[2048,512]{1,0:T(8,128)(2,1)} %bitcast.171, bf16[4,512,512]{2,1,0:T(8,128)(2,1)} %copy-done.17), custom_call_target="tpu_custom_call" | custom-call | flops 4294967 | bytes 8388 | tf_op jit(solution)/shard_map/pallas_call | solution.py:171
  202.9 8.0 shard_map.329
  212.6 7.7 shard_map.330
  226.0 33.2 %collective-permute-done.25.refs_8_.refs_6_.refs_3_ = bf16[1,4,4,64,1024]{4,3,2,1,0:T(8,128)(2,1)} collective-permute-done((bf16[1,4,4,64,1024]{4,3,2,1,0:T(8,128)(2,1)}, bf16[1,4,4,64,1024]{4,3,2,1,0:T(8,128)(2,1)}, u32[]{:S(2)}, u32[]{:S(2)}) %collective-permute-start.25) | collective-permute-done | bytes 2097184 | tf_op jit(solution)/shard_map/ppermute | solution.py:43
  259.2 13.8 %collective-permute-done.24.refs_3_ = bf16[512,2048]{1,0:T(8,128)(2,1)} collective-permute-done((bf16[512,2048]{1,0:T(8,128)(2,1)S(1)}, bf16[512,2048]{1,0:T(8,128)(2,1)}, u32[]{:S(2)}, u32[]{:S(2)}) %collective-permute-start.24) | collective-permute-done | bytes 2097184 | tf_op jit(solution)/shard_map/ppermute | solution.py:33
  274.7 6.1 shard_map.333
  284.4 45.1 %collective-permute-done.27.refs_1_.refs_8_.refs_5_ = bf16[1,4,4,64,1024]{4,3,2,1,0:T(8,128)(2,1)S(1)} collective-permute-done((bf16[1,4,4,64,1024]{4,3,2,1,0:T(8,128)(2,1)S(1)}, bf16[1,4,4,64,1024]{4,3,2,1,0:T(8,128)(2,1)S(1)}, u32[]{:S(2)}, u32[]{:S(2)}) %collective-permute-start.27) | collective-permute-done | bytes 2097184 | tf_op jit(solution)/shard_map/ppermute | solution.py:43
  335.5 30.0 %shard_map.336 = (bf16[4,512,2048]{2,1,0:T(8,128)(2,1)}, bf16[4,512,2048]{2,1,0:T(8,128)(2,1)}) custom-call(s32[1]{0:T(128)} %bitcast.5.refs_0_, bf16[512,2048]{1,0:T(8,128)(2,1)S(1)} %get-tuple-element.53.refs_1_.refs_10_, bf16[512,2048]{1,0:T(8,128)(2,1)} %shard_map.335.refs_2_, bf16[512,2048]{1,0:T(8,128)(2,1)} %collective-permute-done.28.refs_3_, ...), custom_call_target="tpu_custom_call" | custom-call | flops 17179868 | bytes 25165 | tf_op jit(solution)/shard_map/pallas_call | solution.py:171
  365.5 25.2 %shard_map.337.refs_8_ = bf16[2048,1024]{1,0:T(8,128)(2,1)} custom-call(s32[1]{0:T(128)} %bitcast.5.refs_0_, bf16[4,512,2048]{2,1,0:T(8,128)(2,1)} %get-tuple-element.54.refs_1_, bf16[512,2048]{1,0:T(8,128)(2,1)} %shard_map.328.refs_2_.refs_1_, bf16[512,2048]{1,0:T(8,128)(2,1)} %collective-permute-done.21.refs_5_.refs_3_.refs_2_, ...), custom_call_target="tpu_custom_call" | custom-call | flops 8589934 | bytes 16777 | tf_op jit(solution)/shard_map/pallas_call | solution.py:171
  390.8 26.0 %shard_map.338 = (bf16[4,512,2048]{2,1,0:T(8,128)(2,1)}, f32[1,2048]{1,0:T(1,128)S(1)}) custom-call(s32[1]{0:T(128)} %bitcast.5.refs_0_, bf16[512,2048]{1,0:T(8,128)(2,1)} %shard_map.328.refs_2_.refs_1_, bf16[512,2048]{1,0:T(8,128)(2,1)} %collective-permute-done.21.refs_5_.refs_3_.refs_2_, bf16[512,2048]{1,0:T(8,128)(2,1)} %collective-permute-done.30.refs_4_.refs_3_, ...), custom_call_target="tpu_custom_call" | custom-call | flops 17179868 | bytes 25165 | tf_op jit(solution)/shard_map/pallas_call | solution.py:171
  416.8 14.5 %shard_map.339 = (bf16[512,2048]{1,0:T(8,128)(2,1)S(1)}, bf16[512,2048]{1,0:T(8,128)(2,1)S(1)}) custom-call(s32[1]{0:T(128)} %bitcast.5.refs_0_, bf16[4,512,2048]{2,1,0:T(8,128)(2,1)} %get-tuple-element.56.refs_1_.refs_5_, bf16[1,4,4,64,1024]{4,3,2,1,0:T(8,128)(2,1)} %shard_map.332.refs_5_.refs_2_, ...), custom_call_target="tpu_custom_call" | custom-call | flops 8589934 | bytes 12582 | tf_op jit(solution)/shard_map/pallas_call | solution.py:171
  434.0 14.4 %shard_map.340 = (bf16[512,2048]{1,0:T(8,128)(2,1)S(1)}, bf16[512,2048]{1,0:T(8,128)(2,1)S(1)}) custom-call(s32[1]{0:T(128)} %bitcast.5.refs_0_, bf16[4,512,2048]{2,1,0:T(8,128)(2,1)} %get-tuple-element.56.refs_1_.refs_5_, bf16[1,4,4,64,1024]{4,3,2,1,0:T(8,128)(2,1)} %shard_map.332.refs_5_.refs_2_, ...), custom_call_target="tpu_custom_call" | custom-call | flops 8589934 | bytes 12582 | tf_op jit(solution)/shard_map/pallas_call | solution.py:171
  454.3 7.8 shard_map.342.refs_6_
  463.4 15.1 %shard_map.343.refs_6_ = bf16[2048,1024]{1,0:T(8,128)(2,1)} custom-call(s32[1]{0:T(128)} %bitcast.5.refs_0_, bf16[4,512,2048]{2,1,0:T(8,128)(2,1)} %get-tuple-element.54.refs_1_, bf16[512,2048]{1,0:T(8,128)(2,1)} %shard_map.328.refs_2_.refs_1_, bf16[512,2048]{1,0:T(8,128)(2,1)} %collective-permute-done.21.refs_5_.refs_3_.refs_2_, ...), custom_call_target="tpu_custom_call" | custom-call | flops 8589934 | bytes 16777 | tf_op jit(solution)/shard_map/pallas_call | solution.py:171
  479.2 8.5 shard_map.344.refs_6_
  487.7 7.6 shard_map.345.refs_6_
  496.6 30.3 %collective-permute-done.34.refs_2_ = bf16[512,2048]{1,0:T(8,128)(2,1)S(1)} collective-permute-done((bf16[512,2048]{1,0:T(8,128)(2,1)}, bf16[512,2048]{1,0:T(8,128)(2,1)S(1)}, u32[]{:S(2)}, u32[]{:S(2)}) %collective-permute-start.34) | collective-permute-done | bytes 2097184 | tf_op jit(solution)/shard_map/ppermute | solution.py:33
  528.3 8.5 shard_map.346
  538.1 13.7 %shard_map.347 = (bf16[512,2048]{1,0:T(8,128)(2,1)}, bf16[512,2048]{1,0:T(8,128)(2,1)S(1)}) custom-call(s32[1]{0:T(128)} %bitcast.5.refs_0_, bf16[4,512,2048]{2,1,0:T(8,128)(2,1)} %get-tuple-element.54.refs_1_, bf16[4,2,256,2048]{3,2,1,0:T(8,128)(2,1)} %bitcast.198, bf16[4,2,256,2048]{3,2,1,0:T(8,128)(2,1)} %bitcast.199, ...), custom_call_target="tpu_custom_call" | custom-call | flops 8589934 | bytes 16777 | tf_op jit(solution)/shard_map/pallas_call | solution.py:171
  553.2 13.2 %shard_map.348 = (bf16[512,2048]{1,0:T(8,128)(2,1)S(1)}, bf16[512,2048]{1,0:T(8,128)(2,1)S(1)}) custom-call(s32[1]{0:T(128)} %bitcast.5.refs_0_, bf16[4,512,2048]{2,1,0:T(8,128)(2,1)} %get-tuple-element.54.refs_1_, bf16[4,2,256,2048]{3,2,1,0:T(8,128)(2,1)} %bitcast.200, bf16[4,2,256,2048]{3,2,1,0:T(8,128)(2,1)} %bitcast.201, bf16[512,2048]{1,0:T(8,128)(2,1)} %copy-done.67), custom_call_target="tpu_custom_call" | custom-call | flops 8589934 | bytes 16777 | tf_op jit(solution)/shard_map/pallas_call | solution.py:171
  569.0 7.5 shard_map.349.refs_2_.refs_5_
  577.8 6.6 collective-permute-done.38.refs_0_
  584.4 5.3 shard_map.351.refs_2_
  609.7 4.7 shard_map.354.refs_4_
  614.5 18.8 %shard_map.355 = (bf16[1024,1536]{1,0:T(8,128)(2,1)}, f32[1,1536]{1,0:T(1,128)S(1)}) custom-call(bf16[2048,512]{1,0:T(8,128)(2,1)S(1)} %bitcast.166, bf16[2048,512]{1,0:T(8,128)(2,1)S(1)} %bitcast.170, bf16[2048,512]{1,0:T(8,128)(2,1)} %bitcast.172, bf16[1024,512]{1,0:T(8,128)(2,1)S(1)} %bitcast.195, bf16[2,512,512]{2,1,0:T(8,128)(2,1)S(1)} %shard_map.354.refs_4_), custom_call_target="tpu_custom_call" | custom-call | flops 5368709 | bytes 7340 | tf_op jit(solution)/shard_map/pallas_call | solution.py:171
  633.3 11.9 %shard_map.356 = (bf16[512,2048]{1,0:T(8,128)(2,1)}, bf16[512,2048]{1,0:T(8,128)(2,1)}) custom-call(s32[1]{0:T(128)} %bitcast.5.refs_0_, bf16[2,512,1536]{2,1,0:T(8,128)(2,1)} %bitcast.202, bf16[1,4,4,64,512]{4,3,2,1,0:T(8,128)(2,1)S(1)} %bitcast.184, bf16[1,4,4,64,512]{4,3,2,1,0:T(8,128)(2,1)S(1)} %copy-done.34, bf16[1,4,4,64,512]{4,3,2,1,0:T(8,128)(2,1)S(1)} %bitcast.188, ...), custom_call_target="tpu_custom_call" | custom-call | flops 6442450 | bytes 9437 | tf_op jit(solution)/shard_map/pallas_call | solution.py:171
  651.2 6.6 shard_map.358.refs_6_
  658.2 5.6 shard_map.359.refs_4_.refs_1_
  668.6 18.8 %shard_map.360 = (bf16[1024,1536]{1,0:T(8,128)(2,1)}, f32[1,1536]{1,0:T(1,128)S(1)}) custom-call(bf16[2048,512]{1,0:T(8,128)(2,1)S(1)} %bitcast.167, bf16[2048,512]{1,0:T(8,128)(2,1)} %bitcast.169, bf16[2048,512]{1,0:T(8,128)(2,1)} %bitcast.173, bf16[1024,512]{1,0:T(8,128)(2,1)S(1)} %bitcast.181, bf16[256,2048]{1,0:T(8,128)(2,1)S(1)} %copy-done.43, ...), custom_call_target="tpu_custom_call" | custom-call | flops 5368709 | bytes 7340 | tf_op jit(solution)/shard_map/pallas_call | solution.py:171
  692.6 12.0 %shard_map.362 = (bf16[512,2048]{1,0:T(8,128)(2,1)}, bf16[512,2048]{1,0:T(8,128)(2,1)}) custom-call(s32[1]{0:T(128)} %bitcast.5.refs_0_, bf16[2,512,1536]{2,1,0:T(8,128)(2,1)} %bitcast.207, bf16[1,4,4,64,512]{4,3,2,1,0:T(8,128)(2,1)S(1)} %bitcast.185, bf16[1,4,4,64,512]{4,3,2,1,0:T(8,128)(2,1)S(1)} %copy-done.35, bf16[1,4,4,64,512]{4,3,2,1,0:T(8,128)(2,1)S(1)} %bitcast.189, ...), custom_call_target="tpu_custom_call" | custom-call | flops 6442450 | bytes 9437 | tf_op jit(solution)/shard_map/pallas_call | solution.py:171
  713.4 4.7 shard_map.364.refs_7_
  723.1 8.4 shard_map.365.refs_7_
  736.3 8.0 collective-permute-done.45
  748.6 25.0 %collective-permute-done.49 = bf16[64,2048]{1,0:T(8,128)(2,1)S(1)} collective-permute-done((bf16[64,2048]{1,0:T(8,128)(2,1)S(1)}, bf16[64,2048]{1,0:T(8,128)(2,1)S(1)}, u32[]{:S(2)}, u32[]{:S(2)}) %collective-permute-start.49) | collective-permute-done | bytes 262176 | tf_op jit(solution)/shard_map/ppermute | solution.py:33
  790.9 4.7 bitcast_select_fusion.1.refs_9_
  795.6 7.5 shard_map.369.refs_2_
  813.2 8.3 shard_map.371
  837.7 6.7 bitcast_select_fusion
  (539 shorter events, 243.6 us)
Async XLA Ops:
  7.2 82.3 %all-gather.9.cloned.1.call-start = ((), (), s32[]{:S(2)}) async-start(), calls=%async_computation.7 | async-start | bytes 1310720 | tf_op jit(solution)/shard_map/all_gather | solution.py:690
  16.3 76.8 %all-gather.11.cloned.1.call-start = ((), (), s32[]{:S(2)}) async-start(), calls=%async_computation.8 | async-start | bytes 1310720 | tf_op jit(solution)/shard_map/all_gather | solution.py:690
  25.3 78.4 %all-gather.13.cloned.1.call-start = ((), (), s32[]{:S(2)}) async-start(), calls=%async_computation.9 | async-start | bytes 1310720 | tf_op jit(solution)/shard_map/all_gather | solution.py:690
  31.1 31.3 %collective-permute-start.7 = (bf16[256,2048]{1,0:T(8,128)(2,1)}, bf16[256,2048]{1,0:T(8,128)(2,1)}, u32[]{:S(2)}, u32[]{:S(2)}) collective-permute-start(bf16[256,2048]{1,0:T(8,128)(2,1)} %param.36), channel_id=1, source_target_pairs={{0,16},{16,0},{1,17},{17,1},{2,18},{18,2},{3,19},{19,3},{4,20},{20... | collective-permute-start | bytes 3145736 | tf_op jit(solution)/shard_map/ppermute | solution.py:43
  32.7 118.6 %all-gather.15.cloned.1.call-start = ((), (), s32[]{:S(2)}) async-start(), calls=%async_computation.10 | async-start | bytes 1310720 | tf_op jit(solution)/shard_map/all_gather | solution.py:690
  33.5 23.0 %collective-permute-start.3 = (bf16[4,768]{1,0:T(4,128)(2,1)S(1)}, bf16[4,768]{1,0:T(4,128)(2,1)S(1)}, u32[]{:S(2)}, u32[]{:S(2)}) collective-permute-start(bf16[4,768]{1,0:T(4,128)(2,1)S(1)} %pad_maximum_fusion.7), channel_id=1, source_target_pairs={{0,16},{16,0},{1,17},{17,1},{2,18},{18,2},{3,19},{19,3},{4,20},{20... | collective-permute-start | bytes 18440 | tf_op jit(solution)/shard_map/ppermute | solution.py:116
  62.4 148.5 %all-gather.17.cloned.1.call-start = ((), (), s32[]{:S(2)}) async-start(), calls=%async_computation.11 | async-start | bytes 2621440 | tf_op jit(solution)/shard_map/all_gather | solution.py:690
  71.7 13.3 %collective-permute-start.15 = (bf16[64,2048]{1,0:T(8,128)(2,1)S(1)}, bf16[64,2048]{1,0:T(8,128)(2,1)S(1)}, u32[]{:S(2)}, u32[]{:S(2)}) collective-permute-start(bf16[64,2048]{1,0:T(8,128)(2,1)S(1)} %reshape.501), channel_id=1, source_target_pairs={{0,8},{4,12},{8,0},{12,4},{1,9},{5,13},{9,1},{13,5},{2,10},{6,14},... | collective-permute-start | bytes 786440 | tf_op jit(solution)/shard_map/ppermute | solution.py:33
  87.3 193.5 %all-gather.19.cloned.1.call-start = ((), (), s32[]{:S(2)}) async-start(), calls=%async_computation.12 | async-start | bytes 2621440 | tf_op jit(solution)/shard_map/all_gather | solution.py:690
  87.9 302.9 %all-gather.21.cloned.1.call-start = ((), (), s32[]{:S(2)}) async-start(), calls=%async_computation.20 | async-start | bytes 10485760 | tf_op jit(solution)/shard_map/all_gather | solution.py:690
  92.1 48.1 %collective-permute-start.8 = (bf16[512,2048]{1,0:T(8,128)(2,1)}, bf16[512,2048]{1,0:T(8,128)(2,1)S(1)}, u32[]{:S(2)}, u32[]{:S(2)}) collective-permute-start(bf16[512,2048]{1,0:T(8,128)(2,1)} %copy-done.3), channel_id=1, source_target_pairs={{0,8},{4,12},{8,0},{12,4},{1,9},{5,13},{9,1},{13,5},{2,10},{6,14},... | collective-permute-start | bytes 6291464 | tf_op jit(solution)/shard_map/ppermute | solution.py:33
  92.8 444.3 %reduce-scatter.8.cloned.1.call-start = ((), (), s32[]{:S(2)}) async-start(), calls=%async_computation.13 | async-start | bytes 4718592 | tf_op jit(solution)/shard_map/reduce_scatter | solution.py:843
  93.1 26.4 %collective-permute-start.12 = (bf16[1,4,4,64,512]{4,3,2,1,0:T(8,128)(2,1)}, bf16[1,4,4,64,512]{4,3,2,1,0:T(8,128)(2,1)S(1)}, u32[]{:S(2)}, u32[]{:S(2)}) collective-permute-start(bf16[1,4,4,64,512]{4,3,2,1,0:T(8,128)(2,1)} %bitcast.182), channel_id=1, source_target_pairs={{0,16},{16,0},{1,17},{17,1},{2,18},{18,2},{3,19},{19,3},{4,20},{20... | collective-permute-start | bytes 3145736 | tf_op jit(solution)/shard_map/ppermute | solution.py:43
  103.7 36.5 %collective-permute-start.13 = (bf16[1,4,4,64,512]{4,3,2,1,0:T(8,128)(2,1)}, bf16[1,4,4,64,512]{4,3,2,1,0:T(8,128)(2,1)S(1)}, u32[]{:S(2)}, u32[]{:S(2)}) collective-permute-start(bf16[1,4,4,64,512]{4,3,2,1,0:T(8,128)(2,1)} %bitcast.186), channel_id=1, source_target_pairs={{0,16},{16,0},{1,17},{17,1},{2,18},{18,2},{3,19},{19,3},{4,20},{20... | collective-permute-start | bytes 3145736 | tf_op jit(solution)/shard_map/ppermute | solution.py:43
  105.2 48.4 %collective-permute-start.17 = (bf16[512,2048]{1,0:T(8,128)(2,1)}, bf16[512,2048]{1,0:T(8,128)(2,1)}, u32[]{:S(2)}, u32[]{:S(2)}) collective-permute-start(bf16[512,2048]{1,0:T(8,128)(2,1)} %copy-done.3), channel_id=1, source_target_pairs={{0,4},{4,0},{8,12},{12,8},{1,5},{5,1},{9,13},{13,9},{2,6},{6,2},{1... | collective-permute-start | bytes 6291464 | tf_op jit(solution)/shard_map/ppermute | solution.py:33
  150.0 52.9 %collective-permute-start.21 = (bf16[512,2048]{1,0:T(8,128)(2,1)}, bf16[512,2048]{1,0:T(8,128)(2,1)}, u32[]{:S(2)}, u32[]{:S(2)}) collective-permute-start(bf16[512,2048]{1,0:T(8,128)(2,1)} %shard_map.328.refs_2_.refs_1_), channel_id=1, source_target_pairs={{0,8},{4,12},{8,0},{12,4},{1,9},{5,13},{9,1},{13,5},{2,10},{6,14},... | collective-permute-start | bytes 6291464 | tf_op jit(solution)/shard_map/ppermute | solution.py:33
  151.3 26.4 %collective-permute-start.19 = (bf16[1,4,4,64,512]{4,3,2,1,0:T(8,128)(2,1)}, bf16[1,4,4,64,512]{4,3,2,1,0:T(8,128)(2,1)}, u32[]{:S(2)}, u32[]{:S(2)}) collective-permute-start(bf16[1,4,4,64,512]{4,3,2,1,0:T(8,128)(2,1)} %bitcast.190), channel_id=1, source_target_pairs={{0,16},{16,0},{1,17},{17,1},{2,18},{18,2},{3,19},{19,3},{4,20},{20... | collective-permute-start | bytes 3145736 | tf_op jit(solution)/shard_map/ppermute | solution.py:43
  152.8 50.0 %collective-permute-start.20 = (bf16[1,256,2048]{2,1,0:T(8,128)(2,1)S(1)}, bf16[1,256,2048]{2,1,0:T(8,128)(2,1)}, u32[]{:S(2)}, u32[]{:S(2)}) collective-permute-start(bf16[1,256,2048]{2,1,0:T(8,128)(2,1)S(1)} %bitcast.177), channel_id=1, source_target_pairs={{0,16},{16,0},{1,17},{17,1},{2,18},{18,2},{3,19},{19,3},{4,20},{20... | collective-permute-start | bytes 3145736 | tf_op jit(solution)/shard_map/ppermute | solution.py:43
  210.9 48.4 %collective-permute-start.25 = (bf16[1,4,4,64,1024]{4,3,2,1,0:T(8,128)(2,1)}, bf16[1,4,4,64,1024]{4,3,2,1,0:T(8,128)(2,1)}, u32[]{:S(2)}, u32[]{:S(2)}) collective-permute-start(bf16[1,4,4,64,1024]{4,3,2,1,0:T(8,128)(2,1)} %shard_map.332.refs_5_.refs_2_), channel_id=1, source_target_pairs={{0,16},{16,0},{1,17},{17,1},{2,18},{18,2},{3,19},{19,3},{4,20},{20... | collective-permute-start | bytes 6291464 | tf_op jit(solution)/shard_map/ppermute | solution.py:43
  212.5 46.8 %collective-permute-start.22 = (bf16[512,2048]{1,0:T(8,128)(2,1)}, bf16[512,2048]{1,0:T(8,128)(2,1)}, u32[]{:S(2)}, u32[]{:S(2)}) collective-permute-start(bf16[512,2048]{1,0:T(8,128)(2,1)} %get-tuple-element.50), channel_id=1, source_target_pairs={{0,4},{4,0},{8,12},{12,8},{1,5},{5,1},{9,13},{13,9},{2,6},{6,2},{1... | collective-permute-start | bytes 6291464 | tf_op jit(solution)/shard_map/ppermute | solution.py:33
  225.0 48.1 %collective-permute-start.24 = (bf16[512,2048]{1,0:T(8,128)(2,1)S(1)}, bf16[512,2048]{1,0:T(8,128)(2,1)}, u32[]{:S(2)}, u32[]{:S(2)}) collective-permute-start(bf16[512,2048]{1,0:T(8,128)(2,1)S(1)} %shard_map.331.refs_7_), channel_id=1, source_target_pairs={{0,8},{4,12},{8,0},{12,4},{1,9},{5,13},{9,1},{13,5},{2,10},{6,14},... | collective-permute-start | bytes 6291464 | tf_op jit(solution)/shard_map/ppermute | solution.py:33
  282.4 47.1 %collective-permute-start.27 = (bf16[1,4,4,64,1024]{4,3,2,1,0:T(8,128)(2,1)S(1)}, bf16[1,4,4,64,1024]{4,3,2,1,0:T(8,128)(2,1)S(1)}, u32[]{:S(2)}, u32[]{:S(2)}) collective-permute-start(bf16[1,4,4,64,1024]{4,3,2,1,0:T(8,128)(2,1)S(1)} %shard_map.334.refs_7_.refs_4_), channel_id=1, source_target_pairs={{0,16},{16,0},{1,17},{17,1},{2,18},{18,2},{3,19},{19,3},{4,20},{20... | collective-permute-start | bytes 6291464 | tf_op jit(solution)/shard_map/ppermute | solution.py:43
  283.8 47.2 %collective-permute-start.26 = (bf16[512,2048]{1,0:T(8,128)(2,1)S(1)}, bf16[512,2048]{1,0:T(8,128)(2,1)}, u32[]{:S(2)}, u32[]{:S(2)}) collective-permute-start(bf16[512,2048]{1,0:T(8,128)(2,1)S(1)} %get-tuple-element.53.refs_1_.refs_10_), channel_id=1, source_target_pairs={{0,8},{4,12},{8,0},{12,4},{1,9},{5,13},{9,1},{13,5},{2,10},{6,14},... | collective-permute-start | bytes 6291464 | tf_op jit(solution)/shard_map/ppermute | solution.py:33
  284.4 47.1 %collective-permute-start.28 = (bf16[512,2048]{1,0:T(8,128)(2,1)S(1)}, bf16[512,2048]{1,0:T(8,128)(2,1)}, u32[]{:S(2)}, u32[]{:S(2)}) collective-permute-start(bf16[512,2048]{1,0:T(8,128)(2,1)S(1)} %get-tuple-element.53.refs_1_.refs_10_), channel_id=1, source_target_pairs={{0,4},{4,0},{8,12},{12,8},{1,5},{5,1},{9,13},{13,9},{2,6},{6,2},{1... | collective-permute-start | bytes 6291464 | tf_op jit(solution)/shard_map/ppermute | solution.py:33
  331.0 34.5 %collective-permute-start.30 = (bf16[512,2048]{1,0:T(8,128)(2,1)}, bf16[512,2048]{1,0:T(8,128)(2,1)}, u32[]{:S(2)}, u32[]{:S(2)}) collective-permute-start(bf16[512,2048]{1,0:T(8,128)(2,1)} %shard_map.328.refs_2_.refs_1_), channel_id=1, source_target_pairs={{0,4},{4,0},{8,12},{12,8},{1,5},{5,1},{9,13},{13,9},{2,6},{6,2},{1... | collective-permute-start | bytes 6291464 | tf_op jit(solution)/shard_map/ppermute | solution.py:33
  331.5 34.0 %collective-permute-start.31 = (bf16[512,2048]{1,0:T(8,128)(2,1)}, bf16[512,2048]{1,0:T(8,128)(2,1)}, u32[]{:S(2)}, u32[]{:S(2)}) collective-permute-start(bf16[512,2048]{1,0:T(8,128)(2,1)} %collective-permute-done.21.refs_5_.refs_3_.refs_2_), channel_id=1, source_target_pairs={{0,4},{4,0},{8,12},{12,8},{1,5},{5,1},{9,13},{13,9},{2,6},{6,2},{1... | collective-permute-start | bytes 6291464 | tf_op jit(solution)/shard_map/ppermute | solution.py:33
  390.7 216.3 %reduce-scatter.10.cloned.1.call-start = ((), (), s32[]{:S(2)}) async-start(), calls=%async_computation.14 | async-start | bytes 4718592 | tf_op jit(solution)/shard_map/reduce_scatter | solution.py:843
  432.7 17.1 %collective-permute-start.33 = (bf16[512,2048]{1,0:T(8,128)(2,1)S(1)}, bf16[512,2048]{1,0:T(8,128)(2,1)S(1)}, u32[]{:S(2)}, u32[]{:S(2)}) collective-permute-start(bf16[512,2048]{1,0:T(8,128)(2,1)S(1)} %get-tuple-element.58.refs_6_), channel_id=1, source_target_pairs={{0,4},{4,0},{8,12},{12,8},{1,5},{5,1},{9,13},{13,9},{2,6},{6,2},{1... | collective-permute-start | bytes 6291464 | tf_op jit(solution)/shard_map/ppermute | solution.py:33
  478.6 186.2 %reduce-scatter.12.cloned.1.call-start = ((), (), s32[]{:S(2)}) async-start(), calls=%async_computation.15 | async-start | bytes 2621440 | tf_op jit(solution)/shard_map/reduce_scatter | solution.py:824
  478.6 18.0 %collective-permute-start.32 = (bf16[512,2048]{1,0:T(8,128)(2,1)}, bf16[512,2048]{1,0:T(8,128)(2,1)S(1)}, u32[]{:S(2)}, u32[]{:S(2)}) collective-permute-start(bf16[512,2048]{1,0:T(8,128)(2,1)} %copy-done.84), channel_id=1, source_target_pairs={{0,4},{4,0},{8,12},{12,8},{1,5},{5,1},{9,13},{13,9},{2,6},{6,2},{1... | collective-permute-start | bytes 6291464 | tf_op jit(solution)/shard_map/ppermute | solution.py:33
  478.7 48.2 %collective-permute-start.34 = (bf16[512,2048]{1,0:T(8,128)(2,1)}, bf16[512,2048]{1,0:T(8,128)(2,1)S(1)}, u32[]{:S(2)}, u32[]{:S(2)}) collective-permute-start(bf16[512,2048]{1,0:T(8,128)(2,1)} %copy-done.61), channel_id=1, source_target_pairs={{0,8},{4,12},{8,0},{12,4},{1,9},{5,13},{9,1},{13,5},{2,10},{6,14},... | collective-permute-start | bytes 6291464 | tf_op jit(solution)/shard_map/ppermute | solution.py:33
  478.8 99.0 %collective-permute-start.37 = (bf16[1,4,4,64,1024]{4,3,2,1,0:T(8,128)(2,1)}, bf16[1,4,4,64,1024]{4,3,2,1,0:T(8,128)(2,1)}, u32[]{:S(2)}, u32[]{:S(2)}) collective-permute-start(bf16[1,4,4,64,1024]{4,3,2,1,0:T(8,128)(2,1)} %copy-done.57), channel_id=1, source_target_pairs={{0,16},{16,0},{1,17},{17,1},{2,18},{18,2},{3,19},{19,3},{4,20},{20... | collective-permute-start | bytes 6291464 | tf_op jit(solution)/shard_map/ppermute | solution.py:43
  536.8 47.6 %collective-permute-start.38 = (bf16[512,2048]{1,0:T(8,128)(2,1)}, bf16[512,2048]{1,0:T(8,128)(2,1)}, u32[]{:S(2)}, u32[]{:S(2)}) collective-permute-start(bf16[512,2048]{1,0:T(8,128)(2,1)} %get-tuple-element.67.refs_1_.refs_2_), channel_id=1, source_target_pairs={{0,8},{4,12},{8,0},{12,4},{1,9},{5,13},{9,1},{13,5},{2,10},{6,14},... | collective-permute-start | bytes 6291464 | tf_op jit(solution)/shard_map/ppermute | solution.py:33
  595.1 115.6 %reduce-scatter.14.cloned.1.call-start = ((), (), s32[]{:S(2)}) async-start(), calls=%async_computation.16 | async-start | bytes 2621440 | tf_op jit(solution)/shard_map/reduce_scatter | solution.py:824
  595.8 49.4 %collective-permute-start.42 = (bf16[1,4,4,64,1024]{4,3,2,1,0:T(8,128)(2,1)}, bf16[1,4,4,64,1024]{4,3,2,1,0:T(8,128)(2,1)}, u32[]{:S(2)}, u32[]{:S(2)}) collective-permute-start(bf16[1,4,4,64,1024]{4,3,2,1,0:T(8,128)(2,1)} %shard_map.344.refs_6_), channel_id=1, source_target_pairs={{0,16},{16,0},{1,17},{17,1},{2,18},{18,2},{3,19},{19,3},{4,20},{20... | collective-permute-start | bytes 6291464 | tf_op jit(solution)/shard_map/ppermute | solution.py:43
  649.6 70.8 %reduce-scatter.16.cloned.1.call-start = ((), (), s32[]{:S(2)}) async-start(), calls=%async_computation.17 | async-start | bytes 1310720 | tf_op jit(solution)/shard_map/reduce_scatter | solution.py:824
  657.8 29.6 %collective-permute-start.43 = (bf16[256,2048]{1,0:T(8,128)(2,1)}, bf16[256,2048]{1,0:T(8,128)(2,1)}, u32[]{:S(2)}, u32[]{:S(2)}) collective-permute-start(bf16[256,2048]{1,0:T(8,128)(2,1)} %shard_map.358.refs_6_), channel_id=1, source_target_pairs={{0,16},{16,0},{1,17},{17,1},{2,18},{18,2},{3,19},{19,3},{4,20},{20... | collective-permute-start | bytes 3145736 | tf_op jit(solution)/shard_map/ppermute | solution.py:43
  657.8 46.9 %collective-permute-start.44 = (bf16[512,2048]{1,0:T(8,128)(2,1)}, bf16[512,2048]{1,0:T(8,128)(2,1)}, u32[]{:S(2)}, u32[]{:S(2)}) collective-permute-start(bf16[512,2048]{1,0:T(8,128)(2,1)} %get-tuple-element.70.refs_2_), channel_id=1, source_target_pairs={{0,4},{4,0},{8,12},{12,8},{1,5},{5,1},{9,13},{13,9},{2,6},{6,2},{1... | collective-permute-start | bytes 6291464 | tf_op jit(solution)/shard_map/ppermute | solution.py:33
  658.0 48.1 %collective-permute-start.39 = (bf16[512,2048]{1,0:T(8,128)(2,1)}, bf16[512,2048]{1,0:T(8,128)(2,1)}, u32[]{:S(2)}, u32[]{:S(2)}) collective-permute-start(bf16[512,2048]{1,0:T(8,128)(2,1)} %shard_map.353.refs_5_), channel_id=1, source_target_pairs={{0,8},{4,12},{8,0},{12,4},{1,9},{5,13},{9,1},{13,5},{2,10},{6,14},... | collective-permute-start | bytes 6291464 | tf_op jit(solution)/shard_map/ppermute | solution.py:33
  690.1 154.3 %reduce-scatter.18.cloned.1.call-start = ((), (), s32[]{:S(2)}) async-start(), calls=%async_computation.18 | async-start | bytes 1310720 | tf_op jit(solution)/shard_map/reduce_scatter | solution.py:824
  718.1 26.2 %collective-permute-start.45 = (bf16[1,4,4,64,512]{4,3,2,1,0:T(8,128)(2,1)S(1)}, bf16[1,4,4,64,512]{4,3,2,1,0:T(8,128)(2,1)}, u32[]{:S(2)}, u32[]{:S(2)}) collective-permute-start(bf16[1,4,4,64,512]{4,3,2,1,0:T(8,128)(2,1)S(1)} %shard_map.364.refs_7_), channel_id=1, source_target_pairs={{0,16},{16,0},{1,17},{17,1},{2,18},{18,2},{3,19},{19,3},{4,20},{20... | collective-permute-start | bytes 3145736 | tf_op jit(solution)/shard_map/ppermute | solution.py:43
  720.1 66.0 %collective-permute-start.35 = (bf16[512,2048]{1,0:T(8,128)(2,1)}, bf16[512,2048]{1,0:T(8,128)(2,1)}, u32[]{:S(2)}, u32[]{:S(2)}) collective-permute-start(bf16[512,2048]{1,0:T(8,128)(2,1)} %get-tuple-element.65), channel_id=1, source_target_pairs={{0,4},{4,0},{8,12},{12,8},{1,5},{5,1},{9,13},{13,9},{2,6},{6,2},{1... | collective-permute-start | bytes 6291464 | tf_op jit(solution)/shard_map/ppermute | solution.py:33
  720.1 75.5 %collective-permute-start.47 = (bf16[512,2048]{1,0:T(8,128)(2,1)}, bf16[512,2048]{1,0:T(8,128)(2,1)}, u32[]{:S(2)}, u32[]{:S(2)}) collective-permute-start(bf16[512,2048]{1,0:T(8,128)(2,1)} %shard_map.363.refs_7_), channel_id=1, source_target_pairs={{0,8},{4,12},{8,0},{12,4},{1,9},{5,13},{9,1},{13,5},{2,10},{6,14},... | collective-permute-start | bytes 6291464 | tf_op jit(solution)/shard_map/ppermute | solution.py:33
  731.5 72.9 %collective-permute-start.48 = (bf16[1,4,4,64,1024]{4,3,2,1,0:T(8,128)(2,1)}, bf16[1,4,4,64,1024]{4,3,2,1,0:T(8,128)(2,1)}, u32[]{:S(2)}, u32[]{:S(2)}) collective-permute-start(bf16[1,4,4,64,1024]{4,3,2,1,0:T(8,128)(2,1)} %shard_map.365.refs_7_), channel_id=1, source_target_pairs={{0,16},{16,0},{1,17},{17,1},{2,18},{18,2},{3,19},{19,3},{4,20},{20... | collective-permute-start | bytes 6291464 | tf_op jit(solution)/shard_map/ppermute | solution.py:43
  747.9 104.7 %reduce-scatter.20.cloned.1.call-start = ((), (), s32[]{:S(2)}) async-start(), calls=%async_computation.19 | async-start | bytes 2621440 | tf_op jit(solution)/shard_map/reduce_scatter | solution.py:824
  748.2 25.5 %collective-permute-start.49 = (bf16[64,2048]{1,0:T(8,128)(2,1)S(1)}, bf16[64,2048]{1,0:T(8,128)(2,1)S(1)}, u32[]{:S(2)}, u32[]{:S(2)}) collective-permute-start(bf16[64,2048]{1,0:T(8,128)(2,1)S(1)} %get-tuple-element.99), channel_id=1, source_target_pairs={{0,12},{4,8},{8,4},{12,0},{1,13},{5,9},{9,5},{13,1},{2,14},{6,10},... | collective-permute-start | bytes 786440 | tf_op jit(solution)/shard_map/ppermute | solution.py:33
  748.2 31.4 %collective-permute-start.50 = (bf16[64,2048]{1,0:T(8,128)(2,1)S(1)}, bf16[64,2048]{1,0:T(8,128)(2,1)S(1)}, u32[]{:S(2)}, u32[]{:S(2)}) collective-permute-start(bf16[64,2048]{1,0:T(8,128)(2,1)S(1)} %get-tuple-element.98), channel_id=1, source_target_pairs={{0,8},{4,12},{8,0},{12,4},{1,9},{5,13},{9,1},{13,5},{2,10},{6,14},... | collective-permute-start | bytes 786440 | tf_op jit(solution)/shard_map/ppermute | solution.py:33
  779.6 33.5 %collective-permute-start.46 = (bf16[512,2048]{1,0:T(8,128)(2,1)}, bf16[512,2048]{1,0:T(8,128)(2,1)}, u32[]{:S(2)}, u32[]{:S(2)}) collective-permute-start(bf16[512,2048]{1,0:T(8,128)(2,1)} %get-tuple-element.75), channel_id=1, source_target_pairs={{0,4},{4,0},{8,12},{12,8},{1,5},{5,1},{9,13},{13,9},{2,6},{6,2},{1... | collective-permute-start | bytes 6291464 | tf_op jit(solution)/shard_map/ppermute | solution.py:33
  (146 other events, 1141.2 us)
Sparse Core Ops, SparseCore 0:
  16.4 28.7 all-gather.8
  46.8 27.2 all-gather.10
  76.2 27.4 all-gather.12
  105.7 27.4 all-gather.14
  135.1 45.4 all-gather.16
  182.6 44.6 all-gather.18
  229.4 148.3 all-gather.20
  390.8 84.5 reduce-scatter.7
  479.5 98.6 reduce-scatter.9
  595.3 40.0 reduce-scatter.11
  649.7 40.0 reduce-scatter.13
  692.0 26.4 reduce-scatter.15
  748.0 24.8 reduce-scatter.17
  808.9 40.3 reduce-scatter.19

commit v3 on v2

--- a/solution.py
+++ b/solution.py
@@ -705,7 +705,9 @@
     def flatten(halves):
         return [h.reshape(-1, h.shape[-1]) for h in halves]
 
-    qkv_deal = deal_columns((q_weight, k_weight, v_weight), member, outer, depth)
+    down_other = outer_pass(down_weight)
+    deal = deal_columns((q_weight, k_weight, v_weight, up_weight), member, outer, depth)
+    qkv_deal, up_deal = deal[:, : 3 * part_width], deal[:, 3 * part_width :]
     block_q, block_k, block_v = [stored(depth_gather(columns(qkv_deal, i, 3))) for i in range(3)]
     w_q, w_k = [both_halves(b) for b in (block_q, block_k)]
     block_o = flat(depth_gather(o_weight))
@@ -784,10 +786,13 @@
         return [near[0], far[0], team_swap(across, 2), across]
 
     x_rows = pack(tokens)
-    down_pair = jnp.stack([down_weight, outer_pass(down_weight)])[None]
-    (a_own,) = by_rows(norm_kernel, [x_rows], [gain1, shift1], [BF], hold=[down_pair])
-    up_deal = deal_columns((pin(up_weight, a_own),), member, outer, depth)
-    a_all = team_gather(pin(a_own, block_o), w_q[1], w_k[1], up_deal)
+    (a_own,) = by_rows(norm_kernel, [x_rows], [gain1, shift1], [BF], hold=[down_other])
+    a_own = pin(a_own, block_o)
+    a_across = team_swap(a_own, 2)
+    w_o = flatten(both_halves(block_o))
+    a_across = pin(a_across, w_q[1], w_o[1])
+    a_all = [a_own, a_across, team_swap(a_own, 1), team_swap(a_across, 1)]
+    down_pair = jnp.stack([down_weight, down_other])[None]
     block_up = [stored(depth_gather(columns(up_deal, i, 2))) for i in range(2)]
     if outer == 2:
         w_down = [[depth_gather(down_pair)]]
@@ -799,9 +804,8 @@
     wide = TEAM * rows
     q = forward(a_all, [w_q], bias_q)[0]
     k = forward(a_all, [w_k], zero_bias)[0]
-    w_v = both_halves(block_v)
+    w_v = both_halves(block_v, q)
     v = forward(a_all, [w_v], bias_v)[0]
-    w_o = flatten(both_halves(block_o))
     q, k, v = [s.reshape(wide, part_width) for s in (q, k, v)]
     context = order.step(attend, q, k, v).reshape(TEAM, rows, part_width)
     o_far = send_far(forward([context], [w_o], style="bare", pick=(1, 2), hold=[g_all[1]]))
@@ -843,26 +847,26 @@
         return lax.psum_scatter(grad, SPREAD, scatter_dimension=0, tiled=True)
 
     grad_down = [settle_whole(weight_grad([active], g_all, None, cut=(0, 1, 2)))]
+    grad_down.append(settle_whole(weight_grad([active], g_all, None, cut=(1, 2, 2))))
     d_inner, sum_inner = back(g_all, w_down, style="slope", slope=slope)
     n_far = send_far(back([d_inner], w_up, style="bare", pick=(1, 2)))
     n_near = back([d_inner], w_up, style="bare", pick=(0, 2))
     n_parts = join_near(n_near, n_far)[:3]
-    up_sent = [send_away(weight_grad(b_all, [d_inner], 1, spread=spread, cut=(0, 1, 2)))]
-    grad_down.append(settle_whole(weight_grad([active], g_all, None, cut=(1, 2, 2))))
-    up_sent.append(send_away(weight_grad(b_all, [d_inner], 1, spread=spread, cut=(1, 2, 2))))
-    up_mine = [weight_grad(b_all, [d_inner], 0, spread=spread, cut=(0, 1, 2))]
+    up_sent = [
+        send_away(weight_grad(b_all, [d_inner], 1, spread=spread, cut=(i, i + 1, 2))) for i in range(2)
+    ]
+    up_mine = [weight_grad(b_all, [d_inner], 0, spread=spread, cut=(i, i + 1, 2)) for i in range(2)]
     d_hidden, d_out, sums2 = by_rows(
         functools.partial(norm_back_kernel, 3), n_parts + [hidden, g_rows], [gain2], [F32, BF], sums=4
     )
     y_far = send_far(forward([active], w_down, style="bare", pick=(1, 2), hold=[grad_down[0]]))
     y_near = forward([active], w_down, style="bare", pick=(0, 2))
-    up_mine.append(weight_grad(b_all, [d_inner], 0, spread=spread, cut=(1, 2, 2)))
-    d_out_all = team_gather(d_out, up_sent[0], up_mine[1])
+    d_out_all = team_gather(d_out, up_sent[0], y_near[1])
 
     (d_near,) = back(d_out_all[:2], [w_o])
-    grad_up = [settle(up_sent[0], up_mine[0])]
+    (d_far,) = back(d_out_all[2:], [w_o])
+    grad_up = [settle(up_sent[0], up_mine[0], hold=[grad_down[1]])]
     *y_parts, y_across = join_near(y_near, y_far)
-    (d_far,) = back(d_out_all[2:], [w_o], hold=[grad_down[1]])
     q_far, sum_far = order.step(attend_back, q, k, v, d_far.reshape(2 * rows, -1), 2 * rows // SLOT)
     q_far = q_far.reshape(2, rows, -1)
     a_far = send_far(back([q_far], [w_q, w_k, w_v], style="bare"))
@@ -881,19 +885,23 @@
         send_away(weight_grad(a_all, d_both, 1, spread=spread, cut=parts[1], hold=[grad_o])),
     ]
     grad_q = settle(qkv_sent[0], weight_grad(a_all, d_both, 0, spread=spread, cut=parts[0]))
+    kv_mine = weight_grad(a_all, d_both, 0, spread=spread, cut=parts[1])
     (y_rows,) = by_rows(functools.partial(join_kernel, 4), [hidden] + y_parts, [bias_down], [BF])
     layer_out = unpack(y_rows, tokens)
-    (grad_up,) = return_columns(jnp.concatenate(grad_up, axis=1), member, outer, depth, 1)
-    held = [a_parts[2], layer_out, grad_up]
-    kv_mine = weight_grad(a_all, d_both, 0, spread=spread, cut=parts[1], hold=held)
+    _, d_input, sums1 = by_rows(
+        functools.partial(norm_back_kernel, 3),
+        a_parts + [x_rows, d_hidden],
+        [gain1],
+        [BF, BF],
+        sums=4,
+        hold=[layer_out],
+    )
     grad_kv = settle(qkv_sent[1], kv_mine)
-    _, d_input, sums1 = by_rows(
-        functools.partial(norm_back_kernel, 3), a_parts + [x_rows, d_hidden], [gain1], [BF, BF], sums=4
-    )
     sum_qkv = sum_far + sum_near
     grad_o = grad_o.astype(F32)
     input_grad = unpack(d_input, cotangent)
     grad_down = jnp.concatenate([g.astype(F32) for g in grad_down], axis=1)
+    (grad_up,) = return_columns(jnp.concatenate(grad_up, axis=1), member, outer, depth, 1)
     (grad_q,) = return_columns(grad_q, member, outer, depth, 1)
     grad_k, grad_v = return_columns(grad_kv, member, outer, depth, 2)
 

time: 886 us -> 863 us (0.974)
  local copies, waits for them, and re-layouts: 104 us -> 87.3 us
    ppermute x12, waiting for transfers between devices: 123 us -> 164 us  [outer_pass(): lax.ppermute(a, 'outer', [(o, order[(p + 1) % outer]) for p, o in enumera...]
    ppermute x45 -> x42, waiting for transfers between devices: 123 us -> 87.7 us  [team_swap(): return lax.ppermute(a, 'team', [(i, i ^ flip) for i in range(TEAM)])]
    unnamed x239 -> x200, local copies, waits for them, and re-layouts: 73.5 us -> 63 us
    all_gather x7, waiting for transfers between devices: 9.02 us -> 0.05 us  [depth_gather(): return lax.all_gather(a, 'fsdp', axis=0, tiled=True)]
    ppermute x45 -> x42, starting transfers between devices: 20.7 us -> 22 us  [team_swap(): return lax.ppermute(a, 'team', [(i, i ^ flip) for i in range(TEAM)])]
  transfers between devices with their start and end apart: 79 -> 76, of which waited for: 31 -> 31; matrix products, arithmetic and copies ran while one was open for 6% -> 6% of each run, Pallas kernels for 46% -> 46%
where the time goes in v3:
time: 863 us; the launch traced here: 853 us
  Pallas kernels  395 us (46%)
  waiting for transfers between devices  273 us (32%)
  local copies, waits for them, and re-layouts  87.3 us (10%)
  starting transfers between devices  48 us (6%)
  matrix products  18.5 us (2%)
  other arithmetic  15.9 us (2%)
  between operations  15.7 us (2%)
    pallas_call x44, Pallas kernels, kernel_call(): pl.pallas_call(run, grid_spec=pltpu.PrefetchScalarGridSpec(num_scalar_pre...  395 us
    ppermute x12, waiting for transfers between devices, outer_pass(): lax.ppermute(a, 'outer', [(o, order[(p + 1) % outer]) for p, o in enumera...  164 us
    ppermute x42, waiting for transfers between devices, team_swap(): return lax.ppermute(a, 'team', [(i, i ^ flip) for i in range(TEAM)])  87.7 us
    unnamed x200, local copies, waits for them, and re-layouts  63 us
    ppermute x42, starting transfers between devices, team_swap(): return lax.ppermute(a, 'team', [(i, i ^ flip) for i in range(TEAM)])  22 us
  transfers between devices with their start and end apart: 76, of which 31 were waited for; matrix products, arithmetic and copies ran while one was open for 6% of the time, Pallas kernels for 46%

profile of v3, /device:TPU:0, one launch (start us, length us, event | category | flops | bytes accessed | tf_op | source)
XLA Modules:
  0.0 853.0 jit_solution(17711958583920086093)
XLA Ops:
  19.1 8.1 collective-permute-done.9
  27.2 10.1 %collective-permute-done.10 = bf16[64,3584]{1,0:T(8,128)(2,1)} collective-permute-done((bf16[64,3584]{1,0:T(8,128)(2,1)S(1)}, bf16[64,3584]{1,0:T(8,128)(2,1)}, u32[]{:S(2)}, u32[]{:S(2)}) %collective-permute-start.10) | collective-permute-done | bytes 458784 | tf_op jit(solution)/shard_map/ppermute | solution.py:33
  59.2 13.9 %collective-permute-done.3 = bf16[4,768]{1,0:T(4,128)(2,1)S(1)} collective-permute-done((bf16[4,768]{1,0:T(4,128)(2,1)S(1)}, bf16[4,768]{1,0:T(4,128)(2,1)S(1)}, u32[]{:S(2)}, u32[]{:S(2)}) %collective-permute-start.3) | collective-permute-done | bytes 6176 | tf_op jit(solution)/shard_map/ppermute | solution.py:116
  90.8 20.8 %collective-permute-done.13 = bf16[1,256,2048]{2,1,0:T(8,128)(2,1)S(1)} collective-permute-done((bf16[1,256,2048]{2,1,0:T(8,128)(2,1)}, bf16[1,256,2048]{2,1,0:T(8,128)(2,1)S(1)}, u32[]{:S(2)}, u32[]{:S(2)}) %collective-permute-start.13) | collective-permute-done | bytes 1048608 | tf_op jit(solution)/shard_map/ppermute | solution.py:43
  111.6 20.7 %collective-permute-done.12.refs_1_.refs_6_.refs_3_ = bf16[1,4,4,64,512]{4,3,2,1,0:T(8,128)(2,1)} collective-permute-done((bf16[1,4,4,64,512]{4,3,2,1,0:T(8,128)(2,1)}, bf16[1,4,4,64,512]{4,3,2,1,0:T(8,128)(2,1)}, u32[]{:S(2)}, u32[]{:S(2)}) %collective-permute-start.12) | collective-permute-done | bytes 1048608 | tf_op jit(solution)/shard_map/ppermute | solution.py:43
  144.8 8.6 %shard_map.323.refs_8_.refs_1_ = bf16[4,512,512]{2,1,0:T(8,128)(2,1)S(1)} custom-call(s32[1]{0:T(128)} %bitcast.5.refs_0_, bf16[512,2048]{1,0:T(8,128)(2,1)} %copy-done.3, bf16[512,2048]{1,0:T(8,128)(2,1)} %copy-done, bf16[512,2048]{1,0:T(8,128)(2,1)} %collective-permute-done.14.refs_3_, bf16[512,2048]{1,0:T(8,128)(2,1)} %collective-permute-done.15.refs_4_, ...), custom_call_target="tpu_custom_call" | custom-call | flops 4294967 | bytes 12582 | tf_op jit(solution)/shard_map/pallas_call | solution.py:171
  155.4 13.1 %collective-permute-done.16.refs_6_.refs_5_ = bf16[1,4,4,64,512]{4,3,2,1,0:T(8,128)(2,1)} collective-permute-done((bf16[1,4,4,64,512]{4,3,2,1,0:T(8,128)(2,1)}, bf16[1,4,4,64,512]{4,3,2,1,0:T(8,128)(2,1)}, u32[]{:S(2)}, u32[]{:S(2)}) %collective-permute-start.16) | collective-permute-done | bytes 1048608 | tf_op jit(solution)/shard_map/ppermute | solution.py:43
  169.7 8.5 %shard_map.324.refs_8_ = bf16[4,512,512]{2,1,0:T(8,128)(2,1)S(1)} custom-call(s32[1]{0:T(128)} %bitcast.5.refs_0_, bf16[512,2048]{1,0:T(8,128)(2,1)} %copy-done.3, bf16[512,2048]{1,0:T(8,128)(2,1)} %copy-done, bf16[512,2048]{1,0:T(8,128)(2,1)} %collective-permute-done.14.refs_3_, bf16[512,2048]{1,0:T(8,128)(2,1)} %collective-permute-done.15.refs_4_, ...), custom_call_target="tpu_custom_call" | custom-call | flops 4294967 | bytes 12582 | tf_op jit(solution)/shard_map/pallas_call | solution.py:171
  179.6 9.3 %collective-permute-done.17.refs_6_.refs_7_ = bf16[1,4,4,64,512]{4,3,2,1,0:T(8,128)(2,1)} collective-permute-done((bf16[1,4,4,64,512]{4,3,2,1,0:T(8,128)(2,1)}, bf16[1,4,4,64,512]{4,3,2,1,0:T(8,128)(2,1)}, u32[]{:S(2)}, u32[]{:S(2)}) %collective-permute-start.17) | collective-permute-done | bytes 1048608 | tf_op jit(solution)/shard_map/ppermute | solution.py:43
  189.0 8.7 %shard_map.326.refs_3_ = bf16[4,512,512]{2,1,0:T(8,128)(2,1)S(1)} custom-call(s32[1]{0:T(128)} %bitcast.5.refs_0_, bf16[512,2048]{1,0:T(8,128)(2,1)} %copy-done.3, bf16[512,2048]{1,0:T(8,128)(2,1)} %copy-done, bf16[512,2048]{1,0:T(8,128)(2,1)} %collective-permute-done.14.refs_3_, bf16[512,2048]{1,0:T(8,128)(2,1)} %collective-permute-done.15.refs_4_, ...), custom_call_target="tpu_custom_call" | custom-call | flops 4294967 | bytes 12582 | tf_op jit(solution)/shard_map/pallas_call | solution.py:171
  199.0 13.9 %shard_map.327.refs_4_ = bf16[2048,512]{1,0:T(8,128)(2,1)S(1)} custom-call(bf16[2048,512]{1,0:T(8,128)(2,1)S(1)} %bitcast.142, bf16[2048,512]{1,0:T(8,128)(2,1)} %bitcast.145, bf16[2048,512]{1,0:T(8,128)(2,1)} %bitcast.148, bf16[4,512,512]{2,1,0:T(8,128)(2,1)} %copy-done.17), custom_call_target="tpu_custom_call" | custom-call | flops 4294967 | bytes 8388 | tf_op jit(solution)/shard_map/pallas_call | solution.py:171
  214.3 7.9 shard_map.329
  223.9 7.6 shard_map.330
  237.6 33.0 %collective-permute-done.22.refs_8_.refs_6_.refs_3_ = bf16[1,4,4,64,1024]{4,3,2,1,0:T(8,128)(2,1)} collective-permute-done((bf16[1,4,4,64,1024]{4,3,2,1,0:T(8,128)(2,1)}, bf16[1,4,4,64,1024]{4,3,2,1,0:T(8,128)(2,1)}, u32[]{:S(2)}, u32[]{:S(2)}) %collective-permute-start.22) | collective-permute-done | bytes 2097184 | tf_op jit(solution)/shard_map/ppermute | solution.py:43
  270.6 14.1 %collective-permute-done.21.refs_3_ = bf16[512,2048]{1,0:T(8,128)(2,1)} collective-permute-done((bf16[512,2048]{1,0:T(8,128)(2,1)S(1)}, bf16[512,2048]{1,0:T(8,128)(2,1)}, u32[]{:S(2)}, u32[]{:S(2)}) %collective-permute-start.21) | collective-permute-done | bytes 2097184 | tf_op jit(solution)/shard_map/ppermute | solution.py:33
  286.3 6.2 shard_map.333
  296.1 45.1 %collective-permute-done.24.refs_1_.refs_8_.refs_5_ = bf16[1,4,4,64,1024]{4,3,2,1,0:T(8,128)(2,1)S(1)} collective-permute-done((bf16[1,4,4,64,1024]{4,3,2,1,0:T(8,128)(2,1)S(1)}, bf16[1,4,4,64,1024]{4,3,2,1,0:T(8,128)(2,1)S(1)}, u32[]{:S(2)}, u32[]{:S(2)}) %collective-permute-start.24) | collective-permute-done | bytes 2097184 | tf_op jit(solution)/shard_map/ppermute | solution.py:43
  347.1 30.1 %shard_map.336 = (bf16[4,512,2048]{2,1,0:T(8,128)(2,1)}, bf16[4,512,2048]{2,1,0:T(8,128)(2,1)}) custom-call(s32[1]{0:T(128)} %bitcast.5.refs_0_, bf16[512,2048]{1,0:T(8,128)(2,1)S(1)} %get-tuple-element.53.refs_1_.refs_10_, bf16[512,2048]{1,0:T(8,128)(2,1)} %shard_map.335.refs_2_, bf16[512,2048]{1,0:T(8,128)(2,1)} %collective-permute-done.25.refs_3_, ...), custom_call_target="tpu_custom_call" | custom-call | flops 17179868 | bytes 25165 | tf_op jit(solution)/shard_map/pallas_call | solution.py:171
  377.2 15.3 %shard_map.337.refs_6_ = bf16[2048,1024]{1,0:T(8,128)(2,1)} custom-call(s32[1]{0:T(128)} %bitcast.5.refs_0_, bf16[4,512,2048]{2,1,0:T(8,128)(2,1)} %get-tuple-element.54.refs_1_, bf16[512,2048]{1,0:T(8,128)(2,1)} %shard_map.328.refs_2_.refs_1_, bf16[512,2048]{1,0:T(8,128)(2,1)} %collective-permute-done.18.refs_5_.refs_3_.refs_2_, ...), custom_call_target="tpu_custom_call" | custom-call | flops 8589934 | bytes 16777 | tf_op jit(solution)/shard_map/pallas_call | solution.py:171
  392.6 15.0 %shard_map.338.refs_8_ = bf16[2048,1024]{1,0:T(8,128)(2,1)} custom-call(s32[1]{0:T(128)} %bitcast.5.refs_0_, bf16[4,512,2048]{2,1,0:T(8,128)(2,1)} %get-tuple-element.54.refs_1_, bf16[512,2048]{1,0:T(8,128)(2,1)} %shard_map.328.refs_2_.refs_1_, bf16[512,2048]{1,0:T(8,128)(2,1)} %collective-permute-done.18.refs_5_.refs_3_.refs_2_, ...), custom_call_target="tpu_custom_call" | custom-call | flops 8589934 | bytes 16777 | tf_op jit(solution)/shard_map/pallas_call | solution.py:171
  407.6 25.8 %shard_map.339 = (bf16[4,512,2048]{2,1,0:T(8,128)(2,1)}, f32[1,2048]{1,0:T(1,128)S(1)}) custom-call(s32[1]{0:T(128)} %bitcast.5.refs_0_, bf16[512,2048]{1,0:T(8,128)(2,1)} %shard_map.328.refs_2_.refs_1_, bf16[512,2048]{1,0:T(8,128)(2,1)} %collective-permute-done.18.refs_5_.refs_3_.refs_2_, bf16[512,2048]{1,0:T(8,128)(2,1)} %collective-permute-done.27.refs_4_.refs_3_, ...), custom_call_target="tpu_custom_call" | custom-call | flops 17179868 | bytes 25165 | tf_op jit(solution)/shard_map/pallas_call | solution.py:171
  433.4 15.0 %shard_map.340 = (bf16[512,2048]{1,0:T(8,128)(2,1)S(1)}, bf16[512,2048]{1,0:T(8,128)(2,1)}) custom-call(s32[1]{0:T(128)} %bitcast.5.refs_0_, bf16[4,512,2048]{2,1,0:T(8,128)(2,1)} %get-tuple-element.56.refs_1_.refs_5_, bf16[1,4,4,64,1024]{4,3,2,1,0:T(8,128)(2,1)} %shard_map.332.refs_5_.refs_2_, ...), custom_call_target="tpu_custom_call" | custom-call | flops 8589934 | bytes 12582 | tf_op jit(solution)/shard_map/pallas_call | solution.py:171
  450.5 14.7 %shard_map.341 = (bf16[512,2048]{1,0:T(8,128)(2,1)S(1)}, bf16[512,2048]{1,0:T(8,128)(2,1)S(1)}) custom-call(s32[1]{0:T(128)} %bitcast.5.refs_0_, bf16[4,512,2048]{2,1,0:T(8,128)(2,1)} %get-tuple-element.56.refs_1_.refs_5_, bf16[1,4,4,64,1024]{4,3,2,1,0:T(8,128)(2,1)} %shard_map.332.refs_5_.refs_2_, ...), custom_call_target="tpu_custom_call" | custom-call | flops 8589934 | bytes 12582 | tf_op jit(solution)/shard_map/pallas_call | solution.py:171
  468.4 8.3 shard_map.343.refs_6_
  477.2 7.5 shard_map.344.refs_6_
  486.0 7.4 shard_map.345.refs_6_
  494.8 7.4 shard_map.346.refs_6_
  503.6 11.2 %collective-permute-done.31.refs_2_ = bf16[512,2048]{1,0:T(8,128)(2,1)S(1)} collective-permute-done((bf16[512,2048]{1,0:T(8,128)(2,1)S(1)}, bf16[512,2048]{1,0:T(8,128)(2,1)S(1)}, u32[]{:S(2)}, u32[]{:S(2)}) %collective-permute-start.31) | collective-permute-done | bytes 2097184 | tf_op jit(solution)/shard_map/ppermute | solution.py:33
  516.1 8.5 shard_map.347
  526.2 13.8 %shard_map.348 = (bf16[512,2048]{1,0:T(8,128)(2,1)}, bf16[512,2048]{1,0:T(8,128)(2,1)S(1)}) custom-call(s32[1]{0:T(128)} %bitcast.5.refs_0_, bf16[4,512,2048]{2,1,0:T(8,128)(2,1)} %get-tuple-element.54.refs_1_, bf16[4,2,256,2048]{3,2,1,0:T(8,128)(2,1)} %bitcast.177, bf16[4,2,256,2048]{3,2,1,0:T(8,128)(2,1)} %bitcast.178, ...), custom_call_target="tpu_custom_call" | custom-call | flops 8589934 | bytes 16777 | tf_op jit(solution)/shard_map/pallas_call | solution.py:171
  541.3 13.4 %shard_map.349 = (bf16[512,2048]{1,0:T(8,128)(2,1)S(1)}, bf16[512,2048]{1,0:T(8,128)(2,1)S(1)}) custom-call(s32[1]{0:T(128)} %bitcast.5.refs_0_, bf16[4,512,2048]{2,1,0:T(8,128)(2,1)} %get-tuple-element.54.refs_1_, bf16[4,2,256,2048]{3,2,1,0:T(8,128)(2,1)} %bitcast.179, bf16[4,2,256,2048]{3,2,1,0:T(8,128)(2,1)} %bitcast.180, bf16[512,2048]{1,0:T(8,128)(2,1)} %copy-done.52), custom_call_target="tpu_custom_call" | custom-call | flops 8589934 | bytes 16777 | tf_op jit(solution)/shard_map/pallas_call | solution.py:171
  557.4 14.2 %collective-permute-done.36.refs_0_ = bf16[512,2048]{1,0:T(8,128)(2,1)S(1)} collective-permute-done((bf16[512,2048]{1,0:T(8,128)(2,1)}, bf16[512,2048]{1,0:T(8,128)(2,1)S(1)}, u32[]{:S(2)}, u32[]{:S(2)}) %collective-permute-start.36) | collective-permute-done | bytes 2097184 | tf_op jit(solution)/shard_map/ppermute | solution.py:33
  573.0 5.4 shard_map.351.refs_5_
  579.8 5.3 shard_map.352.refs_2_
  600.8 18.7 %shard_map.355 = (bf16[1024,1536]{1,0:T(8,128)(2,1)}, f32[1,1536]{1,0:T(1,128)S(1)}) custom-call(bf16[2048,512]{1,0:T(8,128)(2,1)S(1)} %bitcast.143, bf16[2048,512]{1,0:T(8,128)(2,1)S(1)} %bitcast.147, bf16[2048,512]{1,0:T(8,128)(2,1)} %bitcast.149, bf16[1024,512]{1,0:T(8,128)(2,1)S(1)} %bitcast.163, bf16[512,2048]{1,0:T(8,128)(2,1)} %shard_map.354.refs_4_), custom_call_target="tpu_custom_call" | custom-call | flops 5368709 | bytes 7340 | tf_op jit(solution)/shard_map/pallas_call | solution.py:171
  619.6 12.4 %shard_map.356 = (bf16[512,2048]{1,0:T(8,128)(2,1)}, bf16[512,2048]{1,0:T(8,128)(2,1)}) custom-call(s32[1]{0:T(128)} %bitcast.5.refs_0_, bf16[2,512,1536]{2,1,0:T(8,128)(2,1)} %bitcast.181, bf16[1,4,4,64,512]{4,3,2,1,0:T(8,128)(2,1)S(1)} %bitcast.166, bf16[1,4,4,64,512]{4,3,2,1,0:T(8,128)(2,1)} %collective-permute-done.12.refs_1_.refs_6_.refs_3_, ...), custom_call_target="tpu_custom_call" | custom-call | flops 6442450 | bytes 9437 | tf_op jit(solution)/shard_map/pallas_call | solution.py:171
  632.0 7.9 collective-permute-done.39
  645.4 6.6 shard_map.358.refs_6_
  653.2 5.5 shard_map.359.refs_4_.refs_1_
  663.6 18.7 %shard_map.360 = (bf16[1024,1536]{1,0:T(8,128)(2,1)}, f32[1,1536]{1,0:T(1,128)S(1)}) custom-call(bf16[2048,512]{1,0:T(8,128)(2,1)S(1)} %bitcast.144, bf16[2048,512]{1,0:T(8,128)(2,1)} %bitcast.146, bf16[2048,512]{1,0:T(8,128)(2,1)} %bitcast.150, bf16[1024,512]{1,0:T(8,128)(2,1)S(1)} %bitcast.162, bf16[256,2048]{1,0:T(8,128)(2,1)S(1)} %copy-done.35, ...), custom_call_target="tpu_custom_call" | custom-call | flops 5368709 | bytes 7340 | tf_op jit(solution)/shard_map/pallas_call | solution.py:171
  685.0 12.8 %shard_map.362 = (bf16[512,2048]{1,0:T(8,128)(2,1)}, bf16[512,2048]{1,0:T(8,128)(2,1)}) custom-call(s32[1]{0:T(128)} %bitcast.5.refs_0_, bf16[2,512,1536]{2,1,0:T(8,128)(2,1)} %bitcast.186, bf16[1,4,4,64,512]{4,3,2,1,0:T(8,128)(2,1)S(1)} %bitcast.167, bf16[1,4,4,64,512]{4,3,2,1,0:T(8,128)(2,1)} %collective-permute-done.12.refs_1_.refs_6_.refs_3_, ...), custom_call_target="tpu_custom_call" | custom-call | flops 6442450 | bytes 9437 | tf_op jit(solution)/shard_map/pallas_call | solution.py:171
  718.2 8.5 shard_map.365.refs_7_
  732.7 5.2 collective-permute-done.42
  743.3 7.7 shard_map.368.refs_5_
  761.8 8.3 shard_map.370
  771.4 9.1 %collective-permute-done.55 = bf16[1,4,4,64,1024]{4,3,2,1,0:T(8,128)(2,1)} collective-permute-done((bf16[1,4,4,64,1024]{4,3,2,1,0:T(8,128)(2,1)}, bf16[1,4,4,64,1024]{4,3,2,1,0:T(8,128)(2,1)}, u32[]{:S(2)}, u32[]{:S(2)}) %collective-permute-start.55) | collective-permute-done | bytes 2097184 | tf_op jit(solution)/shard_map/ppermute | solution.py:43
  797.2 4.7 collective-permute-done.59
  814.8 6.8 bitcast_select_fusion
  (492 shorter events, 236.4 us)
Async XLA Ops:
  7.2 75.3 %all-gather.9.cloned.1.call-start = ((), (), s32[]{:S(2)}) async-start(), calls=%async_computation.7 | async-start | bytes 1310720 | tf_op jit(solution)/shard_map/all_gather | solution.py:690
  7.9 78.9 %all-gather.11.cloned.1.call-start = ((), (), s32[]{:S(2)}) async-start(), calls=%async_computation.8 | async-start | bytes 1310720 | tf_op jit(solution)/shard_map/all_gather | solution.py:690
  16.9 20.4 %collective-permute-start.10 = (bf16[64,3584]{1,0:T(8,128)(2,1)S(1)}, bf16[64,3584]{1,0:T(8,128)(2,1)}, u32[]{:S(2)}, u32[]{:S(2)}) collective-permute-start(bf16[64,3584]{1,0:T(8,128)(2,1)S(1)} %pad_maximum_fusion.7), channel_id=1, source_target_pairs={{0,8},{4,12},{8,0},{12,4},{1,9},{5,13},{9,1},{13,5},{2,10},{6,14},... | collective-permute-start | bytes 1376264 | tf_op jit(solution)/shard_map/ppermute | solution.py:33
  18.3 19.0 %collective-permute-start.11 = (bf16[64,3584]{1,0:T(8,128)(2,1)S(1)}, bf16[64,3584]{1,0:T(8,128)(2,1)}, u32[]{:S(2)}, u32[]{:S(2)}) collective-permute-start(bf16[64,3584]{1,0:T(8,128)(2,1)S(1)} %pad_maximum_fusion.8), channel_id=1, source_target_pairs={{0,4},{4,0},{8,12},{12,8},{1,5},{5,1},{9,13},{13,9},{2,6},{6,2},{1... | collective-permute-start | bytes 1376264 | tf_op jit(solution)/shard_map/ppermute | solution.py:33
  39.6 102.4 %all-gather.13.cloned.1.call-start = ((), (), s32[]{:S(2)}) async-start(), calls=%async_computation.9 | async-start | bytes 1310720 | tf_op jit(solution)/shard_map/all_gather | solution.py:690
  40.4 113.1 %all-gather.15.cloned.1.call-start = ((), (), s32[]{:S(2)}) async-start(), calls=%async_computation.10 | async-start | bytes 1310720 | tf_op jit(solution)/shard_map/all_gather | solution.py:690
  40.9 181.2 %all-gather.17.cloned.1.call-start = ((), (), s32[]{:S(2)}) async-start(), calls=%async_computation.11 | async-start | bytes 2621440 | tf_op jit(solution)/shard_map/all_gather | solution.py:690
  42.1 250.4 %all-gather.19.cloned.1.call-start = ((), (), s32[]{:S(2)}) async-start(), calls=%async_computation.12 | async-start | bytes 2621440 | tf_op jit(solution)/shard_map/all_gather | solution.py:690
  42.7 364.9 %all-gather.21.cloned.1.call-start = ((), (), s32[]{:S(2)}) async-start(), calls=%async_computation.20 | async-start | bytes 10485760 | tf_op jit(solution)/shard_map/all_gather | solution.py:690
  48.4 29.5 %collective-permute-start.7 = (bf16[256,2048]{1,0:T(8,128)(2,1)}, bf16[256,2048]{1,0:T(8,128)(2,1)S(1)}, u32[]{:S(2)}, u32[]{:S(2)}) collective-permute-start(bf16[256,2048]{1,0:T(8,128)(2,1)} %param.36), channel_id=1, source_target_pairs={{0,16},{16,0},{1,17},{17,1},{2,18},{18,2},{3,19},{19,3},{4,20},{20... | collective-permute-start | bytes 3145736 | tf_op jit(solution)/shard_map/ppermute | solution.py:43
  52.9 20.1 %collective-permute-start.3 = (bf16[4,768]{1,0:T(4,128)(2,1)S(1)}, bf16[4,768]{1,0:T(4,128)(2,1)S(1)}, u32[]{:S(2)}, u32[]{:S(2)}) collective-permute-start(bf16[4,768]{1,0:T(4,128)(2,1)S(1)} %pad_maximum_fusion.12), channel_id=1, source_target_pairs={{0,16},{16,0},{1,17},{17,1},{2,18},{18,2},{3,19},{19,3},{4,20},{20... | collective-permute-start | bytes 18440 | tf_op jit(solution)/shard_map/ppermute | solution.py:116
  83.8 48.6 %collective-permute-start.8 = (bf16[512,2048]{1,0:T(8,128)(2,1)}, bf16[512,2048]{1,0:T(8,128)(2,1)S(1)}, u32[]{:S(2)}, u32[]{:S(2)}) collective-permute-start(bf16[512,2048]{1,0:T(8,128)(2,1)} %copy-done.3), channel_id=1, source_target_pairs={{0,8},{4,12},{8,0},{12,4},{1,9},{5,13},{9,1},{13,5},{2,10},{6,14},... | collective-permute-start | bytes 6291464 | tf_op jit(solution)/shard_map/ppermute | solution.py:33
  85.3 26.3 %collective-permute-start.13 = (bf16[1,256,2048]{2,1,0:T(8,128)(2,1)}, bf16[1,256,2048]{2,1,0:T(8,128)(2,1)S(1)}, u32[]{:S(2)}, u32[]{:S(2)}) collective-permute-start(bf16[1,256,2048]{2,1,0:T(8,128)(2,1)} %bitcast.6.refs_1_), channel_id=1, source_target_pairs={{0,16},{16,0},{1,17},{17,1},{2,18},{18,2},{3,19},{19,3},{4,20},{20... | collective-permute-start | bytes 3145736 | tf_op jit(solution)/shard_map/ppermute | solution.py:43
  86.9 45.5 %collective-permute-start.12 = (bf16[1,4,4,64,512]{4,3,2,1,0:T(8,128)(2,1)}, bf16[1,4,4,64,512]{4,3,2,1,0:T(8,128)(2,1)}, u32[]{:S(2)}, u32[]{:S(2)}) collective-permute-start(bf16[1,4,4,64,512]{4,3,2,1,0:T(8,128)(2,1)} %bitcast.164), channel_id=1, source_target_pairs={{0,16},{16,0},{1,17},{17,1},{2,18},{18,2},{3,19},{19,3},{4,20},{20... | collective-permute-start | bytes 3145736 | tf_op jit(solution)/shard_map/ppermute | solution.py:43
  90.5 434.7 %reduce-scatter.8.cloned.1.call-start = ((), (), s32[]{:S(2)}) async-start(), calls=%async_computation.13 | async-start | bytes 4718592 | tf_op jit(solution)/shard_map/reduce_scatter | solution.py:847
  90.7 52.9 %collective-permute-start.14 = (bf16[512,2048]{1,0:T(8,128)(2,1)}, bf16[512,2048]{1,0:T(8,128)(2,1)}, u32[]{:S(2)}, u32[]{:S(2)}) collective-permute-start(bf16[512,2048]{1,0:T(8,128)(2,1)} %copy-done.3), channel_id=1, source_target_pairs={{0,4},{4,0},{8,12},{12,8},{1,5},{5,1},{9,13},{13,9},{2,6},{6,2},{1... | collective-permute-start | bytes 6291464 | tf_op jit(solution)/shard_map/ppermute | solution.py:33
  140.5 73.7 %collective-permute-start.18 = (bf16[512,2048]{1,0:T(8,128)(2,1)}, bf16[512,2048]{1,0:T(8,128)(2,1)}, u32[]{:S(2)}, u32[]{:S(2)}) collective-permute-start(bf16[512,2048]{1,0:T(8,128)(2,1)} %shard_map.328.refs_2_.refs_1_), channel_id=1, source_target_pairs={{0,8},{4,12},{8,0},{12,4},{1,9},{5,13},{9,1},{13,5},{2,10},{6,14},... | collective-permute-start | bytes 6291464 | tf_op jit(solution)/shard_map/ppermute | solution.py:33
  142.1 26.4 %collective-permute-start.16 = (bf16[1,4,4,64,512]{4,3,2,1,0:T(8,128)(2,1)}, bf16[1,4,4,64,512]{4,3,2,1,0:T(8,128)(2,1)}, u32[]{:S(2)}, u32[]{:S(2)}) collective-permute-start(bf16[1,4,4,64,512]{4,3,2,1,0:T(8,128)(2,1)} %bitcast.168), channel_id=1, source_target_pairs={{0,16},{16,0},{1,17},{17,1},{2,18},{18,2},{3,19},{19,3},{4,20},{20... | collective-permute-start | bytes 3145736 | tf_op jit(solution)/shard_map/ppermute | solution.py:43
  154.8 34.1 %collective-permute-start.17 = (bf16[1,4,4,64,512]{4,3,2,1,0:T(8,128)(2,1)}, bf16[1,4,4,64,512]{4,3,2,1,0:T(8,128)(2,1)}, u32[]{:S(2)}, u32[]{:S(2)}) collective-permute-start(bf16[1,4,4,64,512]{4,3,2,1,0:T(8,128)(2,1)} %shard_map.325.refs_5_.refs_6_), channel_id=1, source_target_pairs={{0,16},{16,0},{1,17},{17,1},{2,18},{18,2},{3,19},{19,3},{4,20},{20... | collective-permute-start | bytes 3145736 | tf_op jit(solution)/shard_map/ppermute | solution.py:43
  222.2 48.4 %collective-permute-start.22 = (bf16[1,4,4,64,1024]{4,3,2,1,0:T(8,128)(2,1)}, bf16[1,4,4,64,1024]{4,3,2,1,0:T(8,128)(2,1)}, u32[]{:S(2)}, u32[]{:S(2)}) collective-permute-start(bf16[1,4,4,64,1024]{4,3,2,1,0:T(8,128)(2,1)} %shard_map.332.refs_5_.refs_2_), channel_id=1, source_target_pairs={{0,16},{16,0},{1,17},{17,1},{2,18},{18,2},{3,19},{19,3},{4,20},{20... | collective-permute-start | bytes 6291464 | tf_op jit(solution)/shard_map/ppermute | solution.py:43
  223.8 46.8 %collective-permute-start.19 = (bf16[512,2048]{1,0:T(8,128)(2,1)}, bf16[512,2048]{1,0:T(8,128)(2,1)}, u32[]{:S(2)}, u32[]{:S(2)}) collective-permute-start(bf16[512,2048]{1,0:T(8,128)(2,1)} %get-tuple-element.50), channel_id=1, source_target_pairs={{0,4},{4,0},{8,12},{12,8},{1,5},{5,1},{9,13},{13,9},{2,6},{6,2},{1... | collective-permute-start | bytes 6291464 | tf_op jit(solution)/shard_map/ppermute | solution.py:33
  236.7 48.0 %collective-permute-start.21 = (bf16[512,2048]{1,0:T(8,128)(2,1)S(1)}, bf16[512,2048]{1,0:T(8,128)(2,1)}, u32[]{:S(2)}, u32[]{:S(2)}) collective-permute-start(bf16[512,2048]{1,0:T(8,128)(2,1)S(1)} %shard_map.331.refs_7_), channel_id=1, source_target_pairs={{0,8},{4,12},{8,0},{12,4},{1,9},{5,13},{9,1},{13,5},{2,10},{6,14},... | collective-permute-start | bytes 6291464 | tf_op jit(solution)/shard_map/ppermute | solution.py:33
  294.1 47.1 %collective-permute-start.24 = (bf16[1,4,4,64,1024]{4,3,2,1,0:T(8,128)(2,1)S(1)}, bf16[1,4,4,64,1024]{4,3,2,1,0:T(8,128)(2,1)S(1)}, u32[]{:S(2)}, u32[]{:S(2)}) collective-permute-start(bf16[1,4,4,64,1024]{4,3,2,1,0:T(8,128)(2,1)S(1)} %shard_map.334.refs_7_.refs_4_), channel_id=1, source_target_pairs={{0,16},{16,0},{1,17},{17,1},{2,18},{18,2},{3,19},{19,3},{4,20},{20... | collective-permute-start | bytes 6291464 | tf_op jit(solution)/shard_map/ppermute | solution.py:43
  295.4 47.2 %collective-permute-start.23 = (bf16[512,2048]{1,0:T(8,128)(2,1)S(1)}, bf16[512,2048]{1,0:T(8,128)(2,1)}, u32[]{:S(2)}, u32[]{:S(2)}) collective-permute-start(bf16[512,2048]{1,0:T(8,128)(2,1)S(1)} %get-tuple-element.53.refs_1_.refs_10_), channel_id=1, source_target_pairs={{0,8},{4,12},{8,0},{12,4},{1,9},{5,13},{9,1},{13,5},{2,10},{6,14},... | collective-permute-start | bytes 6291464 | tf_op jit(solution)/shard_map/ppermute | solution.py:33
  296.1 47.1 %collective-permute-start.25 = (bf16[512,2048]{1,0:T(8,128)(2,1)S(1)}, bf16[512,2048]{1,0:T(8,128)(2,1)}, u32[]{:S(2)}, u32[]{:S(2)}) collective-permute-start(bf16[512,2048]{1,0:T(8,128)(2,1)S(1)} %get-tuple-element.53.refs_1_.refs_10_), channel_id=1, source_target_pairs={{0,4},{4,0},{8,12},{12,8},{1,5},{5,1},{9,13},{13,9},{2,6},{6,2},{1... | collective-permute-start | bytes 6291464 | tf_op jit(solution)/shard_map/ppermute | solution.py:33
  342.6 34.6 %collective-permute-start.27 = (bf16[512,2048]{1,0:T(8,128)(2,1)}, bf16[512,2048]{1,0:T(8,128)(2,1)}, u32[]{:S(2)}, u32[]{:S(2)}) collective-permute-start(bf16[512,2048]{1,0:T(8,128)(2,1)} %shard_map.328.refs_2_.refs_1_), channel_id=1, source_target_pairs={{0,4},{4,0},{8,12},{12,8},{1,5},{5,1},{9,13},{13,9},{2,6},{6,2},{1... | collective-permute-start | bytes 6291464 | tf_op jit(solution)/shard_map/ppermute | solution.py:33
  343.1 34.1 %collective-permute-start.28 = (bf16[512,2048]{1,0:T(8,128)(2,1)}, bf16[512,2048]{1,0:T(8,128)(2,1)}, u32[]{:S(2)}, u32[]{:S(2)}) collective-permute-start(bf16[512,2048]{1,0:T(8,128)(2,1)} %collective-permute-done.18.refs_5_.refs_3_.refs_2_), channel_id=1, source_target_pairs={{0,4},{4,0},{8,12},{12,8},{1,5},{5,1},{9,13},{13,9},{2,6},{6,2},{1... | collective-permute-start | bytes 6291464 | tf_op jit(solution)/shard_map/ppermute | solution.py:33
  392.5 193.5 %reduce-scatter.10.cloned.1.call-start = ((), (), s32[]{:S(2)}) async-start(), calls=%async_computation.14 | async-start | bytes 4718592 | tf_op jit(solution)/shard_map/reduce_scatter | solution.py:847
  449.9 15.4 %collective-permute-start.30 = (bf16[512,2048]{1,0:T(8,128)(2,1)}, bf16[512,2048]{1,0:T(8,128)(2,1)}, u32[]{:S(2)}, u32[]{:S(2)}) collective-permute-start(bf16[512,2048]{1,0:T(8,128)(2,1)} %get-tuple-element.58.refs_6_), channel_id=1, source_target_pairs={{0,4},{4,0},{8,12},{12,8},{1,5},{5,1},{9,13},{13,9},{2,6},{6,2},{1... | collective-permute-start | bytes 6291464 | tf_op jit(solution)/shard_map/ppermute | solution.py:33
  450.0 209.7 %reduce-scatter.12.cloned.1.call-start = ((), (), s32[]{:S(2)}) async-start(), calls=%async_computation.15 | async-start | bytes 2621440 | tf_op jit(solution)/shard_map/reduce_scatter | solution.py:828
  450.1 53.5 %collective-permute-start.29 = (bf16[512,2048]{1,0:T(8,128)(2,1)}, bf16[512,2048]{1,0:T(8,128)(2,1)S(1)}, u32[]{:S(2)}, u32[]{:S(2)}) collective-permute-start(bf16[512,2048]{1,0:T(8,128)(2,1)} %copy-done.68), channel_id=1, source_target_pairs={{0,4},{4,0},{8,12},{12,8},{1,5},{5,1},{9,13},{13,9},{2,6},{6,2},{1... | collective-permute-start | bytes 6291464 | tf_op jit(solution)/shard_map/ppermute | solution.py:33
  467.1 47.7 %collective-permute-start.31 = (bf16[512,2048]{1,0:T(8,128)(2,1)S(1)}, bf16[512,2048]{1,0:T(8,128)(2,1)S(1)}, u32[]{:S(2)}, u32[]{:S(2)}) collective-permute-start(bf16[512,2048]{1,0:T(8,128)(2,1)S(1)} %shard_map.342.refs_6_), channel_id=1, source_target_pairs={{0,8},{4,12},{8,0},{12,4},{1,9},{5,13},{9,1},{13,5},{2,10},{6,14},... | collective-permute-start | bytes 6291464 | tf_op jit(solution)/shard_map/ppermute | solution.py:33
  476.7 80.7 %collective-permute-start.34 = (bf16[1,4,4,64,1024]{4,3,2,1,0:T(8,128)(2,1)}, bf16[1,4,4,64,1024]{4,3,2,1,0:T(8,128)(2,1)}, u32[]{:S(2)}, u32[]{:S(2)}) collective-permute-start(bf16[1,4,4,64,1024]{4,3,2,1,0:T(8,128)(2,1)} %shard_map.343.refs_6_), channel_id=1, source_target_pairs={{0,16},{16,0},{1,17},{17,1},{2,18},{18,2},{3,19},{19,3},{4,20},{20... | collective-permute-start | bytes 6291464 | tf_op jit(solution)/shard_map/ppermute | solution.py:43
  524.6 47.1 %collective-permute-start.36 = (bf16[512,2048]{1,0:T(8,128)(2,1)}, bf16[512,2048]{1,0:T(8,128)(2,1)S(1)}, u32[]{:S(2)}, u32[]{:S(2)}) collective-permute-start(bf16[512,2048]{1,0:T(8,128)(2,1)} %get-tuple-element.67.refs_1_.refs_2_), channel_id=1, source_target_pairs={{0,8},{4,12},{8,0},{12,4},{1,9},{5,13},{9,1},{13,5},{2,10},{6,14},... | collective-permute-start | bytes 6291464 | tf_op jit(solution)/shard_map/ppermute | solution.py:33
  525.2 53.2 %collective-permute-start.35 = (bf16[512,2048]{1,0:T(8,128)(2,1)}, bf16[512,2048]{1,0:T(8,128)(2,1)}, u32[]{:S(2)}, u32[]{:S(2)}) collective-permute-start(bf16[512,2048]{1,0:T(8,128)(2,1)} %get-tuple-element.67.refs_1_.refs_2_), channel_id=1, source_target_pairs={{0,4},{4,0},{8,12},{12,8},{1,5},{5,1},{9,13},{13,9},{2,6},{6,2},{1... | collective-permute-start | bytes 6291464 | tf_op jit(solution)/shard_map/ppermute | solution.py:33
  591.5 112.7 %reduce-scatter.14.cloned.1.call-start = ((), (), s32[]{:S(2)}) async-start(), calls=%async_computation.16 | async-start | bytes 2621440 | tf_op jit(solution)/shard_map/reduce_scatter | solution.py:828
  591.6 48.3 %collective-permute-start.39 = (bf16[1,4,4,64,1024]{4,3,2,1,0:T(8,128)(2,1)}, bf16[1,4,4,64,1024]{4,3,2,1,0:T(8,128)(2,1)S(1)}, u32[]{:S(2)}, u32[]{:S(2)}) collective-permute-start(bf16[1,4,4,64,1024]{4,3,2,1,0:T(8,128)(2,1)} %copy-done.43), channel_id=1, source_target_pairs={{0,16},{16,0},{1,17},{17,1},{2,18},{18,2},{3,19},{19,3},{4,20},{20... | collective-permute-start | bytes 6291464 | tf_op jit(solution)/shard_map/ppermute | solution.py:43
  643.9 71.8 %reduce-scatter.16.cloned.1.call-start = ((), (), s32[]{:S(2)}) async-start(), calls=%async_computation.17 | async-start | bytes 1310720 | tf_op jit(solution)/shard_map/reduce_scatter | solution.py:828
  652.0 30.3 %collective-permute-start.40 = (bf16[256,2048]{1,0:T(8,128)(2,1)}, bf16[256,2048]{1,0:T(8,128)(2,1)}, u32[]{:S(2)}, u32[]{:S(2)}) collective-permute-start(bf16[256,2048]{1,0:T(8,128)(2,1)} %shard_map.358.refs_6_), channel_id=1, source_target_pairs={{0,16},{16,0},{1,17},{17,1},{2,18},{18,2},{3,19},{19,3},{4,20},{20... | collective-permute-start | bytes 3145736 | tf_op jit(solution)/shard_map/ppermute | solution.py:43
  652.3 47.3 %collective-permute-start.38 = (bf16[512,2048]{1,0:T(8,128)(2,1)}, bf16[512,2048]{1,0:T(8,128)(2,1)}, u32[]{:S(2)}, u32[]{:S(2)}) collective-permute-start(bf16[512,2048]{1,0:T(8,128)(2,1)} %shard_map.354.refs_4_), channel_id=1, source_target_pairs={{0,8},{4,12},{8,0},{12,4},{1,9},{5,13},{9,1},{13,5},{2,10},{6,14},... | collective-permute-start | bytes 6291464 | tf_op jit(solution)/shard_map/ppermute | solution.py:33
  653.2 46.4 %collective-permute-start.41 = (bf16[512,2048]{1,0:T(8,128)(2,1)}, bf16[512,2048]{1,0:T(8,128)(2,1)}, u32[]{:S(2)}, u32[]{:S(2)}) collective-permute-start(bf16[512,2048]{1,0:T(8,128)(2,1)} %get-tuple-element.70.refs_2_), channel_id=1, source_target_pairs={{0,4},{4,0},{8,12},{12,8},{1,5},{5,1},{9,13},{13,9},{2,6},{6,2},{1... | collective-permute-start | bytes 6291464 | tf_op jit(solution)/shard_map/ppermute | solution.py:33
  685.0 137.5 %reduce-scatter.18.cloned.1.call-start = ((), (), s32[]{:S(2)}) async-start(), calls=%async_computation.18 | async-start | bytes 1310720 | tf_op jit(solution)/shard_map/reduce_scatter | solution.py:828
  711.6 26.3 %collective-permute-start.42 = (bf16[1,4,4,64,512]{4,3,2,1,0:T(8,128)(2,1)S(1)}, bf16[1,4,4,64,512]{4,3,2,1,0:T(8,128)(2,1)}, u32[]{:S(2)}, u32[]{:S(2)}) collective-permute-start(bf16[1,4,4,64,512]{4,3,2,1,0:T(8,128)(2,1)S(1)} %shard_map.364.refs_7_), channel_id=1, source_target_pairs={{0,16},{16,0},{1,17},{17,1},{2,18},{18,2},{3,19},{19,3},{4,20},{20... | collective-permute-start | bytes 3145736 | tf_op jit(solution)/shard_map/ppermute | solution.py:43
  713.3 39.1 %collective-permute-start.32 = (bf16[512,2048]{1,0:T(8,128)(2,1)}, bf16[512,2048]{1,0:T(8,128)(2,1)}, u32[]{:S(2)}, u32[]{:S(2)}) collective-permute-start(bf16[512,2048]{1,0:T(8,128)(2,1)} %get-tuple-element.65), channel_id=1, source_target_pairs={{0,4},{4,0},{8,12},{12,8},{1,5},{5,1},{9,13},{13,9},{2,6},{6,2},{1... | collective-permute-start | bytes 6291464 | tf_op jit(solution)/shard_map/ppermute | solution.py:33
  713.3 48.5 %collective-permute-start.43 = (bf16[512,2048]{1,0:T(8,128)(2,1)}, bf16[512,2048]{1,0:T(8,128)(2,1)}, u32[]{:S(2)}, u32[]{:S(2)}) collective-permute-start(bf16[512,2048]{1,0:T(8,128)(2,1)} %get-tuple-element.75), channel_id=1, source_target_pairs={{0,4},{4,0},{8,12},{12,8},{1,5},{5,1},{9,13},{13,9},{2,6},{6,2},{1... | collective-permute-start | bytes 6291464 | tf_op jit(solution)/shard_map/ppermute | solution.py:33
  713.8 48.0 %collective-permute-start.44 = (bf16[512,2048]{1,0:T(8,128)(2,1)}, bf16[512,2048]{1,0:T(8,128)(2,1)}, u32[]{:S(2)}, u32[]{:S(2)}) collective-permute-start(bf16[512,2048]{1,0:T(8,128)(2,1)} %shard_map.363.refs_7_), channel_id=1, source_target_pairs={{0,8},{4,12},{8,0},{12,4},{1,9},{5,13},{9,1},{13,5},{2,10},{6,14},... | collective-permute-start | bytes 6291464 | tf_op jit(solution)/shard_map/ppermute | solution.py:33
  726.6 53.8 %collective-permute-start.55 = (bf16[1,4,4,64,1024]{4,3,2,1,0:T(8,128)(2,1)}, bf16[1,4,4,64,1024]{4,3,2,1,0:T(8,128)(2,1)}, u32[]{:S(2)}, u32[]{:S(2)}) collective-permute-start(bf16[1,4,4,64,1024]{4,3,2,1,0:T(8,128)(2,1)} %shard_map.365.refs_7_), channel_id=1, source_target_pairs={{0,16},{16,0},{1,17},{17,1},{2,18},{18,2},{3,19},{19,3},{4,20},{20... | collective-permute-start | bytes 6291464 | tf_op jit(solution)/shard_map/ppermute | solution.py:43
  741.5 89.2 %reduce-scatter.20.cloned.1.call-start = ((), (), s32[]{:S(2)}) async-start(), calls=%async_computation.19 | async-start | bytes 2621440 | tf_op jit(solution)/shard_map/reduce_scatter | solution.py:828
  (124 other events, 754.2 us)
Sparse Core Ops, SparseCore 0:
  9.6 30.5 all-gather.8
  41.8 27.9 all-gather.10
  72.0 27.4 all-gather.12
  101.4 27.4 all-gather.14
  130.9 45.4 all-gather.16
  178.4 44.6 all-gather.18
  224.6 148.3 all-gather.20
  392.7 87.0 reduce-scatter.7
  483.8 96.6 reduce-scatter.9
  591.6 42.8 reduce-scatter.11
  644.0 42.8 reduce-scatter.13
  689.0 26.5 reduce-scatter.15
  741.7 26.8 reduce-scatter.17
  784.9 44.6 reduce-scatter.19

commit v4 on v3

--- a/solution.py
+++ b/solution.py
@@ -705,7 +705,6 @@
     def flatten(halves):
         return [h.reshape(-1, h.shape[-1]) for h in halves]
 
-    down_other = outer_pass(down_weight)
     deal = deal_columns((q_weight, k_weight, v_weight, up_weight), member, outer, depth)
     qkv_deal, up_deal = deal[:, : 3 * part_width], deal[:, 3 * part_width :]
     block_q, block_k, block_v = [stored(depth_gather(columns(qkv_deal, i, 3))) for i in range(3)]
@@ -786,18 +785,13 @@
         return [near[0], far[0], team_swap(across, 2), across]
 
     x_rows = pack(tokens)
-    (a_own,) = by_rows(norm_kernel, [x_rows], [gain1, shift1], [BF], hold=[down_other])
+    (a_own,) = by_rows(norm_kernel, [x_rows], [gain1, shift1], [BF])
     a_own = pin(a_own, block_o)
     a_across = team_swap(a_own, 2)
     w_o = flatten(both_halves(block_o))
     a_across = pin(a_across, w_q[1], w_o[1])
     a_all = [a_own, a_across, team_swap(a_own, 1), team_swap(a_across, 1)]
-    down_pair = jnp.stack([down_weight, down_other])[None]
     block_up = [stored(depth_gather(columns(up_deal, i, 2))) for i in range(2)]
-    if outer == 2:
-        w_down = [[depth_gather(down_pair)]]
-    else:
-        w_down = [[lax.all_gather(down_weight, SPREAD, axis=0, tiled=True)]]
     g_rows = pack(cotangent)
     g_all = team_gather(pin(g_rows, a_all[1]))
 
@@ -807,8 +801,13 @@
     w_v = both_halves(block_v, q)
     v = forward(a_all, [w_v], bias_v)[0]
     q, k, v = [s.reshape(wide, part_width) for s in (q, k, v)]
-    context = order.step(attend, q, k, v).reshape(TEAM, rows, part_width)
-    o_far = send_far(forward([context], [w_o], style="bare", pick=(1, 2), hold=[g_all[1]]))
+    context = order.step(attend, q, k, v, hold=[g_all[1]]).reshape(TEAM, rows, part_width)
+    if outer == 2:
+        down_pair = jnp.stack([down_weight, outer_pass(pin(down_weight, k))])[None]
+        w_down = [[depth_gather(pin(down_pair, context))]]
+    else:
+        w_down = [[lax.all_gather(down_weight, SPREAD, axis=0, tiled=True)]]
+    o_far = send_far(forward([context], [w_o], style="bare", pick=(1, 2)))
     o_near = forward([context], [w_o], style="bare", pick=(0, 2))
     w_up = [both_halves(block_up[0], context)]
     *o_parts, o_across = join_near(o_near, o_far)

time: 863 us -> 851 us (0.986)
  waiting for transfers between devices: 273 us -> 257 us
    ppermute x8, waiting for transfers between devices: 16.7 us -> 4.24 us  [shift_pass(): return lax.ppermute(a, axis, [(i, (i + step) % size) for i in range(size)])]
    unnamed x200 -> x213, local copies, waits for them, and re-layouts: 63 us -> 61.5 us
  transfers between devices with their start and end apart: 76 -> 76, of which waited for: 31 -> 29; matrix products, arithmetic and copies ran while one was open for 6% -> 6% of each run, Pallas kernels for 46% -> 46%
where the time goes in v4:
time: 851 us; the launch traced here: 841 us
  Pallas kernels  393 us (46%)
  waiting for transfers between devices  257 us (30%)
  local copies, waits for them, and re-layouts  85.7 us (10%)
  starting transfers between devices  53.9 us (6%)
  matrix products  21.2 us (2%)
  between operations  15.7 us (2%)
  other arithmetic  14.5 us (2%)
    pallas_call x44, Pallas kernels, kernel_call(): pl.pallas_call(run, grid_spec=pltpu.PrefetchScalarGridSpec(num_scalar_pre...  393 us
    ppermute x12, waiting for transfers between devices, outer_pass(): lax.ppermute(a, 'outer', [(o, order[(p + 1) % outer]) for p, o in enumera...  170 us
    ppermute x42, waiting for transfers between devices, team_swap(): return lax.ppermute(a, 'team', [(i, i ^ flip) for i in range(TEAM)])  81.1 us
    unnamed x213, local copies, waits for them, and re-layouts  61.5 us
    ppermute x42, starting transfers between devices, team_swap(): return lax.ppermute(a, 'team', [(i, i ^ flip) for i in range(TEAM)])  27.1 us
  transfers between devices with their start and end apart: 76, of which 29 were waited for; matrix products, arithmetic and copies ran while one was open for 6% of the time, Pallas kernels for 46%

profile of v4, /device:TPU:0, one launch (start us, length us, event | category | flops | bytes accessed | tf_op | source)
XLA Modules:
  0.0 841.4 jit_solution(9948305287119097628)
XLA Ops:
  19.1 8.1 collective-permute-done.8
  27.2 10.1 %collective-permute-done.9 = bf16[64,3584]{1,0:T(8,128)(2,1)} collective-permute-done((bf16[64,3584]{1,0:T(8,128)(2,1)S(1)}, bf16[64,3584]{1,0:T(8,128)(2,1)}, u32[]{:S(2)}, u32[]{:S(2)}) %collective-permute-start.9) | collective-permute-done | bytes 458784 | tf_op jit(solution)/shard_map/ppermute | solution.py:33
  72.8 24.3 %collective-permute-done.12 = bf16[1,256,2048]{2,1,0:T(8,128)(2,1)S(1)} collective-permute-done((bf16[1,256,2048]{2,1,0:T(8,128)(2,1)}, bf16[1,256,2048]{2,1,0:T(8,128)(2,1)S(1)}, u32[]{:S(2)}, u32[]{:S(2)}) %collective-permute-start.12) | collective-permute-done | bytes 1048608 | tf_op jit(solution)/shard_map/ppermute | solution.py:43
  97.1 21.0 %collective-permute-done.11.refs_1_.refs_6_.refs_3_ = bf16[1,4,4,64,512]{4,3,2,1,0:T(8,128)(2,1)S(1)} collective-permute-done((bf16[1,4,4,64,512]{4,3,2,1,0:T(8,128)(2,1)}, bf16[1,4,4,64,512]{4,3,2,1,0:T(8,128)(2,1)S(1)}, u32[]{:S(2)}, u32[]{:S(2)}) %collective-permute-start.11) | collective-permute-done | bytes 1048608 | tf_op jit(solution)/shard_map/ppermute | solution.py:43
  119.4 5.1 fusion.7.refs_4_
  131.8 8.4 %shard_map.323.refs_8_.refs_1_ = bf16[4,512,512]{2,1,0:T(8,128)(2,1)S(1)} custom-call(s32[1]{0:T(128)} %bitcast.5.refs_0_, bf16[512,2048]{1,0:T(8,128)(2,1)} %copy-done.3, bf16[512,2048]{1,0:T(8,128)(2,1)} %copy-done, bf16[512,2048]{1,0:T(8,128)(2,1)} %collective-permute-done.13.refs_3_, bf16[512,2048]{1,0:T(8,128)(2,1)} %collective-permute-done.14.refs_4_, ...), custom_call_target="tpu_custom_call" | custom-call | flops 4294967 | bytes 12582 | tf_op jit(solution)/shard_map/pallas_call | solution.py:171
  143.2 10.4 %collective-permute-done.15.refs_6_.refs_5_ = bf16[1,4,4,64,512]{4,3,2,1,0:T(8,128)(2,1)} collective-permute-done((bf16[1,4,4,64,512]{4,3,2,1,0:T(8,128)(2,1)}, bf16[1,4,4,64,512]{4,3,2,1,0:T(8,128)(2,1)}, u32[]{:S(2)}, u32[]{:S(2)}) %collective-permute-start.15) | collective-permute-done | bytes 1048608 | tf_op jit(solution)/shard_map/ppermute | solution.py:43
  153.6 8.6 %shard_map.324.refs_8_ = bf16[4,512,512]{2,1,0:T(8,128)(2,1)S(1)} custom-call(s32[1]{0:T(128)} %bitcast.5.refs_0_, bf16[512,2048]{1,0:T(8,128)(2,1)} %copy-done.3, bf16[512,2048]{1,0:T(8,128)(2,1)} %copy-done, bf16[512,2048]{1,0:T(8,128)(2,1)} %collective-permute-done.13.refs_3_, bf16[512,2048]{1,0:T(8,128)(2,1)} %collective-permute-done.14.refs_4_, ...), custom_call_target="tpu_custom_call" | custom-call | flops 4294967 | bytes 12582 | tf_op jit(solution)/shard_map/pallas_call | solution.py:171
  164.2 11.9 %collective-permute-done.16.refs_6_.refs_7_ = bf16[1,4,4,64,512]{4,3,2,1,0:T(8,128)(2,1)} collective-permute-done((bf16[1,4,4,64,512]{4,3,2,1,0:T(8,128)(2,1)}, bf16[1,4,4,64,512]{4,3,2,1,0:T(8,128)(2,1)}, u32[]{:S(2)}, u32[]{:S(2)}) %collective-permute-start.16) | collective-permute-done | bytes 1048608 | tf_op jit(solution)/shard_map/ppermute | solution.py:43
  176.1 8.7 %shard_map.326.refs_3_ = bf16[4,512,512]{2,1,0:T(8,128)(2,1)S(1)} custom-call(s32[1]{0:T(128)} %bitcast.5.refs_0_, bf16[512,2048]{1,0:T(8,128)(2,1)} %copy-done.3, bf16[512,2048]{1,0:T(8,128)(2,1)} %copy-done, bf16[512,2048]{1,0:T(8,128)(2,1)} %collective-permute-done.13.refs_3_, bf16[512,2048]{1,0:T(8,128)(2,1)} %collective-permute-done.14.refs_4_, ...), custom_call_target="tpu_custom_call" | custom-call | flops 4294967 | bytes 12582 | tf_op jit(solution)/shard_map/pallas_call | solution.py:171
  186.1 14.0 %shard_map.328.refs_4_ = bf16[2048,512]{1,0:T(8,128)(2,1)S(1)} custom-call(bf16[2048,512]{1,0:T(8,128)(2,1)S(1)} %bitcast.144, bf16[2048,512]{1,0:T(8,128)(2,1)} %bitcast.148, bf16[2048,512]{1,0:T(8,128)(2,1)} %bitcast.151, bf16[4,512,512]{2,1,0:T(8,128)(2,1)} %copy-done.17, bf16[512,2048]{1,0:T(8,128)(2,1)} %collective-permute-done.17.refs_4_.refs_3_.refs_2_), custom_call_target="tpu_custom_call" | custom-call | flops 4294967 | bytes 8388 | tf_op jit(solution)/shard_map/pallas_call | solution.py:171
  202.5 7.9 shard_map.329
  211.3 7.6 shard_map.330
  225.4 33.5 %collective-permute-done.21.refs_8_.refs_6_.refs_3_ = bf16[1,4,4,64,1024]{4,3,2,1,0:T(8,128)(2,1)} collective-permute-done((bf16[1,4,4,64,1024]{4,3,2,1,0:T(8,128)(2,1)}, bf16[1,4,4,64,1024]{4,3,2,1,0:T(8,128)(2,1)}, u32[]{:S(2)}, u32[]{:S(2)}) %collective-permute-start.21) | collective-permute-done | bytes 2097184 | tf_op jit(solution)/shard_map/ppermute | solution.py:43
  258.8 12.8 %collective-permute-done.20.refs_3_ = bf16[512,2048]{1,0:T(8,128)(2,1)} collective-permute-done((bf16[512,2048]{1,0:T(8,128)(2,1)S(1)}, bf16[512,2048]{1,0:T(8,128)(2,1)}, u32[]{:S(2)}, u32[]{:S(2)}) %collective-permute-start.20) | collective-permute-done | bytes 2097184 | tf_op jit(solution)/shard_map/ppermute | solution.py:33
  273.2 6.1 shard_map.333
  283.9 44.1 %collective-permute-done.23.refs_1_.refs_8_.refs_5_ = bf16[1,4,4,64,1024]{4,3,2,1,0:T(8,128)(2,1)S(1)} collective-permute-done((bf16[1,4,4,64,1024]{4,3,2,1,0:T(8,128)(2,1)S(1)}, bf16[1,4,4,64,1024]{4,3,2,1,0:T(8,128)(2,1)S(1)}, u32[]{:S(2)}, u32[]{:S(2)}) %collective-permute-start.23) | collective-permute-done | bytes 2097184 | tf_op jit(solution)/shard_map/ppermute | solution.py:43
  334.0 30.1 %shard_map.336 = (bf16[4,512,2048]{2,1,0:T(8,128)(2,1)}, bf16[4,512,2048]{2,1,0:T(8,128)(2,1)}) custom-call(s32[1]{0:T(128)} %bitcast.5.refs_0_, bf16[512,2048]{1,0:T(8,128)(2,1)S(1)} %get-tuple-element.53.refs_1_.refs_10_, bf16[512,2048]{1,0:T(8,128)(2,1)} %shard_map.335.refs_2_, bf16[512,2048]{1,0:T(8,128)(2,1)} %collective-permute-done.24.refs_3_, ...), custom_call_target="tpu_custom_call" | custom-call | flops 17179868 | bytes 25165 | tf_op jit(solution)/shard_map/pallas_call | solution.py:171
  364.1 14.9 %shard_map.339.refs_6_ = bf16[2048,1024]{1,0:T(8,128)(2,1)} custom-call(s32[1]{0:T(128)} %bitcast.5.refs_0_, bf16[4,512,2048]{2,1,0:T(8,128)(2,1)} %get-tuple-element.54.refs_1_, bf16[512,2048]{1,0:T(8,128)(2,1)} %shard_map.327.refs_2_.refs_1_, bf16[512,2048]{1,0:T(8,128)(2,1)} %collective-permute-done.17.refs_4_.refs_3_.refs_2_, ...), custom_call_target="tpu_custom_call" | custom-call | flops 8589934 | bytes 16777 | tf_op jit(solution)/shard_map/pallas_call | solution.py:171
  379.4 15.0 %shard_map.340.refs_8_ = bf16[2048,1024]{1,0:T(8,128)(2,1)} custom-call(s32[1]{0:T(128)} %bitcast.5.refs_0_, bf16[4,512,2048]{2,1,0:T(8,128)(2,1)} %get-tuple-element.54.refs_1_, bf16[512,2048]{1,0:T(8,128)(2,1)} %shard_map.327.refs_2_.refs_1_, bf16[512,2048]{1,0:T(8,128)(2,1)} %collective-permute-done.17.refs_4_.refs_3_.refs_2_, ...), custom_call_target="tpu_custom_call" | custom-call | flops 8589934 | bytes 16777 | tf_op jit(solution)/shard_map/pallas_call | solution.py:171
  394.5 25.8 %shard_map.341 = (bf16[4,512,2048]{2,1,0:T(8,128)(2,1)}, f32[1,2048]{1,0:T(1,128)S(1)}) custom-call(s32[1]{0:T(128)} %bitcast.5.refs_0_, bf16[512,2048]{1,0:T(8,128)(2,1)} %shard_map.327.refs_2_.refs_1_, bf16[512,2048]{1,0:T(8,128)(2,1)} %collective-permute-done.17.refs_4_.refs_3_.refs_2_, bf16[512,2048]{1,0:T(8,128)(2,1)} %collective-permute-done.27.refs_4_.refs_3_, ...), custom_call_target="tpu_custom_call" | custom-call | flops 17179868 | bytes 25165 | tf_op jit(solution)/shard_map/pallas_call | solution.py:171
  420.3 15.1 %shard_map.342 = (bf16[512,2048]{1,0:T(8,128)(2,1)S(1)}, bf16[512,2048]{1,0:T(8,128)(2,1)}) custom-call(s32[1]{0:T(128)} %bitcast.5.refs_0_, bf16[4,512,2048]{2,1,0:T(8,128)(2,1)} %get-tuple-element.56.refs_1_.refs_5_, bf16[1,4,4,64,1024]{4,3,2,1,0:T(8,128)(2,1)} %shard_map.332.refs_5_.refs_2_, ...), custom_call_target="tpu_custom_call" | custom-call | flops 8589934 | bytes 12582 | tf_op jit(solution)/shard_map/pallas_call | solution.py:171
  437.5 14.5 %shard_map.343 = (bf16[512,2048]{1,0:T(8,128)(2,1)S(1)}, bf16[512,2048]{1,0:T(8,128)(2,1)S(1)}) custom-call(s32[1]{0:T(128)} %bitcast.5.refs_0_, bf16[4,512,2048]{2,1,0:T(8,128)(2,1)} %get-tuple-element.56.refs_1_.refs_5_, bf16[1,4,4,64,1024]{4,3,2,1,0:T(8,128)(2,1)} %shard_map.332.refs_5_.refs_2_, ...), custom_call_target="tpu_custom_call" | custom-call | flops 8589934 | bytes 12582 | tf_op jit(solution)/shard_map/pallas_call | solution.py:171
  455.4 8.3 shard_map.345.refs_6_
  465.1 7.5 shard_map.346.refs_6_
  473.9 7.4 shard_map.347.refs_6_
  482.7 7.4 shard_map.348.refs_6_
  491.5 9.9 %collective-permute-done.31.refs_2_ = bf16[512,2048]{1,0:T(8,128)(2,1)S(1)} collective-permute-done((bf16[512,2048]{1,0:T(8,128)(2,1)S(1)}, bf16[512,2048]{1,0:T(8,128)(2,1)S(1)}, u32[]{:S(2)}, u32[]{:S(2)}) %collective-permute-start.31) | collective-permute-done | bytes 2097184 | tf_op jit(solution)/shard_map/ppermute | solution.py:33
  502.8 8.4 %shard_map.349 = (f32[512,2048]{1,0:T(8,128)}, bf16[512,2048]{1,0:T(8,128)(2,1)}, f32[4,2048]{1,0:T(4,128)S(1)}) custom-call(bf16[512,2048]{1,0:T(8,128)(2,1)S(1)} %get-tuple-element.59.refs_0_, bf16[512,2048]{1,0:T(8,128)(2,1)} %copy-done.78, bf16[512,2048]{1,0:T(8,128)(2,1)} %copy-done.79, f32[512,2048]{1,0:T(8,128)} %get-tuple-element.52.refs_3_.refs_0_, ...), custom_call_target="tpu_custom_call" | custom-call | flops 20971 | bytes 16777 | tf_op jit(solution)/shard_map/pallas_call | solution.py:171
  513.8 13.7 %shard_map.350 = (bf16[512,2048]{1,0:T(8,128)(2,1)}, bf16[512,2048]{1,0:T(8,128)(2,1)S(1)}) custom-call(s32[1]{0:T(128)} %bitcast.5.refs_0_, bf16[4,512,2048]{2,1,0:T(8,128)(2,1)} %get-tuple-element.54.refs_1_, bf16[4,2,256,2048]{3,2,1,0:T(8,128)(2,1)} %all-gather.20.cloned.1.call-done.refs_5_.refs_6_.refs_2_.refs_3_, ...), custom_call_target="tpu_custom_call" | custom-call | flops 8589934 | bytes 16777 | tf_op jit(solution)/shard_map/pallas_call | solution.py:171
  528.9 13.4 %shard_map.351 = (bf16[512,2048]{1,0:T(8,128)(2,1)S(1)}, bf16[512,2048]{1,0:T(8,128)(2,1)S(1)}) custom-call(s32[1]{0:T(128)} %bitcast.5.refs_0_, bf16[4,512,2048]{2,1,0:T(8,128)(2,1)} %get-tuple-element.54.refs_1_, bf16[4,2,256,2048]{3,2,1,0:T(8,128)(2,1)} %all-gather.20.cloned.1.call-done.refs_5_.refs_6_.refs_2_.refs_3_, ...), custom_call_target="tpu_custom_call" | custom-call | flops 8589934 | bytes 16777 | tf_op jit(solution)/shard_map/pallas_call | solution.py:171
  544.9 13.3 %collective-permute-done.36.refs_0_ = bf16[512,2048]{1,0:T(8,128)(2,1)S(1)} collective-permute-done((bf16[512,2048]{1,0:T(8,128)(2,1)}, bf16[512,2048]{1,0:T(8,128)(2,1)S(1)}, u32[]{:S(2)}, u32[]{:S(2)}) %collective-permute-start.36) | collective-permute-done | bytes 2097184 | tf_op jit(solution)/shard_map/ppermute | solution.py:33
  559.6 5.3 shard_map.353.refs_5_
  566.4 5.3 shard_map.354.refs_2_
  588.2 18.8 %shard_map.357 = (bf16[1024,1536]{1,0:T(8,128)(2,1)}, f32[1,1536]{1,0:T(1,128)S(1)}) custom-call(bf16[2048,512]{1,0:T(8,128)(2,1)S(1)} %bitcast.145, bf16[2048,512]{1,0:T(8,128)(2,1)S(1)} %bitcast.150, bf16[2048,512]{1,0:T(8,128)(2,1)} %bitcast.152, bf16[1024,512]{1,0:T(8,128)(2,1)S(1)} %bitcast.166, bf16[512,2048]{1,0:T(8,128)(2,1)} %shard_map.356.refs_4_), custom_call_target="tpu_custom_call" | custom-call | flops 5368709 | bytes 7340 | tf_op jit(solution)/shard_map/pallas_call | solution.py:171
  607.0 12.2 %shard_map.358 = (bf16[512,2048]{1,0:T(8,128)(2,1)}, bf16[512,2048]{1,0:T(8,128)(2,1)}) custom-call(s32[1]{0:T(128)} %bitcast.5.refs_0_, bf16[2,512,1536]{2,1,0:T(8,128)(2,1)} %bitcast.177, bf16[1,4,4,64,512]{4,3,2,1,0:T(8,128)(2,1)S(1)} %bitcast.169, bf16[1,4,4,64,512]{4,3,2,1,0:T(8,128)(2,1)S(1)} %copy-done.34, bf16[1,4,4,64,512]{4,3,2,1,0:T(8,128)(2,1)S(1)} %bitcast.173, ...), custom_call_target="tpu_custom_call" | custom-call | flops 6442450 | bytes 9437 | tf_op jit(solution)/shard_map/pallas_call | solution.py:171
  619.1 7.8 collective-permute-done.39
  632.4 6.6 shard_map.360.refs_6_
  641.9 5.6 shard_map.361.refs_4_.refs_1_
  653.6 18.7 %shard_map.362 = (bf16[1024,1536]{1,0:T(8,128)(2,1)}, f32[1,1536]{1,0:T(1,128)S(1)}) custom-call(bf16[2048,512]{1,0:T(8,128)(2,1)S(1)} %bitcast.146, bf16[2048,512]{1,0:T(8,128)(2,1)} %bitcast.149, bf16[2048,512]{1,0:T(8,128)(2,1)} %bitcast.153, bf16[1024,512]{1,0:T(8,128)(2,1)S(1)} %bitcast.165, bf16[256,2048]{1,0:T(8,128)(2,1)S(1)} %copy-done.40, ...), custom_call_target="tpu_custom_call" | custom-call | flops 5368709 | bytes 7340 | tf_op jit(solution)/shard_map/pallas_call | solution.py:171
  675.0 12.5 %shard_map.364 = (bf16[512,2048]{1,0:T(8,128)(2,1)}, bf16[512,2048]{1,0:T(8,128)(2,1)}) custom-call(s32[1]{0:T(128)} %bitcast.5.refs_0_, bf16[2,512,1536]{2,1,0:T(8,128)(2,1)} %bitcast.182, bf16[1,4,4,64,512]{4,3,2,1,0:T(8,128)(2,1)S(1)} %bitcast.170, bf16[1,4,4,64,512]{4,3,2,1,0:T(8,128)(2,1)S(1)} %copy-done.34, bf16[1,4,4,64,512]{4,3,2,1,0:T(8,128)(2,1)S(1)} %bitcast.174, ...), custom_call_target="tpu_custom_call" | custom-call | flops 6442450 | bytes 9437 | tf_op jit(solution)/shard_map/pallas_call | solution.py:171
  705.0 8.5 %shard_map.367.refs_7_ = bf16[1,4,4,64,1024]{4,3,2,1,0:T(8,128)(2,1)} custom-call(s32[1]{0:T(128)} %bitcast.5.refs_0_, bf16[512,2048]{1,0:T(8,128)(2,1)S(1)} %copy-done.5, bf16[512,2048]{1,0:T(8,128)(2,1)} %copy-done, bf16[512,2048]{1,0:T(8,128)(2,1)} %collective-permute-done.13.refs_3_, bf16[512,2048]{1,0:T(8,128)(2,1)} %collective-permute-done.14.refs_4_, ...), custom_call_target="tpu_custom_call" | custom-call | flops 4294967 | bytes 10485 | tf_op jit(solution)/shard_map/pallas_call | solution.py:171
  719.4 6.3 collective-permute-done.42
  731.2 7.9 shard_map.370.refs_5_
  749.8 8.2 shard_map.372
  759.4 10.8 %collective-permute-done.55 = bf16[1,4,4,64,1024]{4,3,2,1,0:T(8,128)(2,1)} collective-permute-done((bf16[1,4,4,64,1024]{4,3,2,1,0:T(8,128)(2,1)}, bf16[1,4,4,64,1024]{4,3,2,1,0:T(8,128)(2,1)}, u32[]{:S(2)}, u32[]{:S(2)}) %collective-permute-start.55) | collective-permute-done | bytes 2097184 | tf_op jit(solution)/shard_map/ppermute | solution.py:43
  786.9 4.7 collective-permute-done.59
  803.7 6.8 bitcast_select_fusion
  (507 shorter events, 232.3 us)
Async XLA Ops:
  7.2 60.8 %all-gather.8.cloned.1.call-start = ((), (), s32[]{:S(2)}) async-start(), calls=%async_computation.7 | async-start | bytes 1310720 | tf_op jit(solution)/shard_map/all_gather | solution.py:690
  7.9 63.4 %all-gather.10.cloned.1.call-start = ((), (), s32[]{:S(2)}) async-start(), calls=%async_computation.8 | async-start | bytes 1310720 | tf_op jit(solution)/shard_map/all_gather | solution.py:690
  13.8 13.4 %collective-permute-start.8 = (bf16[64,3584]{1,0:T(8,128)(2,1)S(1)}, bf16[64,3584]{1,0:T(8,128)(2,1)}, u32[]{:S(2)}, u32[]{:S(2)}) collective-permute-start(bf16[64,3584]{1,0:T(8,128)(2,1)S(1)} %pad_maximum_fusion.5), channel_id=1, source_target_pairs={{0,12},{4,8},{8,4},{12,0},{1,13},{5,9},{9,5},{13,1},{2,14},{6,10},... | collective-permute-start | bytes 1376264 | tf_op jit(solution)/shard_map/ppermute | solution.py:33
  16.9 20.4 %collective-permute-start.9 = (bf16[64,3584]{1,0:T(8,128)(2,1)S(1)}, bf16[64,3584]{1,0:T(8,128)(2,1)}, u32[]{:S(2)}, u32[]{:S(2)}) collective-permute-start(bf16[64,3584]{1,0:T(8,128)(2,1)S(1)} %pad_maximum_fusion.6), channel_id=1, source_target_pairs={{0,8},{4,12},{8,0},{12,4},{1,9},{5,13},{9,1},{13,5},{2,10},{6,14},... | collective-permute-start | bytes 1376264 | tf_op jit(solution)/shard_map/ppermute | solution.py:33
  18.3 19.0 %collective-permute-start.10 = (bf16[64,3584]{1,0:T(8,128)(2,1)S(1)}, bf16[64,3584]{1,0:T(8,128)(2,1)}, u32[]{:S(2)}, u32[]{:S(2)}) collective-permute-start(bf16[64,3584]{1,0:T(8,128)(2,1)S(1)} %pad_maximum_fusion.7), channel_id=1, source_target_pairs={{0,4},{4,0},{8,12},{12,8},{1,5},{5,1},{9,13},{13,9},{2,6},{6,2},{1... | collective-permute-start | bytes 1376264 | tf_op jit(solution)/shard_map/ppermute | solution.py:33
  39.8 87.5 %all-gather.12.cloned.1.call-start = ((), (), s32[]{:S(2)}) async-start(), calls=%async_computation.9 | async-start | bytes 1310720 | tf_op jit(solution)/shard_map/all_gather | solution.py:690
  40.5 99.8 %all-gather.14.cloned.1.call-start = ((), (), s32[]{:S(2)}) async-start(), calls=%async_computation.10 | async-start | bytes 1310720 | tf_op jit(solution)/shard_map/all_gather | solution.py:690
  41.1 169.4 %all-gather.16.cloned.1.call-start = ((), (), s32[]{:S(2)}) async-start(), calls=%async_computation.11 | async-start | bytes 2621440 | tf_op jit(solution)/shard_map/all_gather | solution.py:690
  53.9 225.4 %all-gather.18.cloned.1.call-start = ((), (), s32[]{:S(2)}) async-start(), calls=%async_computation.12 | async-start | bytes 2621440 | tf_op jit(solution)/shard_map/all_gather | solution.py:690
  69.3 48.8 %collective-permute-start.7 = (bf16[512,2048]{1,0:T(8,128)(2,1)}, bf16[512,2048]{1,0:T(8,128)(2,1)S(1)}, u32[]{:S(2)}, u32[]{:S(2)}) collective-permute-start(bf16[512,2048]{1,0:T(8,128)(2,1)} %copy-done.3), channel_id=1, source_target_pairs={{0,8},{4,12},{8,0},{12,4},{1,9},{5,13},{9,1},{13,5},{2,10},{6,14},... | collective-permute-start | bytes 6291464 | tf_op jit(solution)/shard_map/ppermute | solution.py:33
  70.8 26.3 %collective-permute-start.12 = (bf16[1,256,2048]{2,1,0:T(8,128)(2,1)}, bf16[1,256,2048]{2,1,0:T(8,128)(2,1)S(1)}, u32[]{:S(2)}, u32[]{:S(2)}) collective-permute-start(bf16[1,256,2048]{2,1,0:T(8,128)(2,1)} %bitcast.6.refs_1_), channel_id=1, source_target_pairs={{0,16},{16,0},{1,17},{17,1},{2,18},{18,2},{3,19},{19,3},{4,20},{20... | collective-permute-start | bytes 3145736 | tf_op jit(solution)/shard_map/ppermute | solution.py:43
  71.3 46.8 %collective-permute-start.11 = (bf16[1,4,4,64,512]{4,3,2,1,0:T(8,128)(2,1)}, bf16[1,4,4,64,512]{4,3,2,1,0:T(8,128)(2,1)S(1)}, u32[]{:S(2)}, u32[]{:S(2)}) collective-permute-start(bf16[1,4,4,64,512]{4,3,2,1,0:T(8,128)(2,1)} %bitcast.167), channel_id=1, source_target_pairs={{0,16},{16,0},{1,17},{17,1},{2,18},{18,2},{3,19},{19,3},{4,20},{20... | collective-permute-start | bytes 3145736 | tf_op jit(solution)/shard_map/ppermute | solution.py:43
  72.8 56.5 %collective-permute-start.13 = (bf16[512,2048]{1,0:T(8,128)(2,1)}, bf16[512,2048]{1,0:T(8,128)(2,1)}, u32[]{:S(2)}, u32[]{:S(2)}) collective-permute-start(bf16[512,2048]{1,0:T(8,128)(2,1)} %copy-done.3), channel_id=1, source_target_pairs={{0,4},{4,0},{8,12},{12,8},{1,5},{5,1},{9,13},{13,9},{2,6},{6,2},{1... | collective-permute-start | bytes 6291464 | tf_op jit(solution)/shard_map/ppermute | solution.py:33
  119.1 275.4 %all-gather.20.cloned.1.call-start = ((), (), s32[]{:S(2)}) async-start(), calls=%async_computation.13 | async-start | bytes 10485760 | tf_op jit(solution)/shard_map/all_gather | solution.py:690
  127.3 26.3 %collective-permute-start.15 = (bf16[1,4,4,64,512]{4,3,2,1,0:T(8,128)(2,1)}, bf16[1,4,4,64,512]{4,3,2,1,0:T(8,128)(2,1)}, u32[]{:S(2)}, u32[]{:S(2)}) collective-permute-start(bf16[1,4,4,64,512]{4,3,2,1,0:T(8,128)(2,1)} %bitcast.171), channel_id=1, source_target_pairs={{0,16},{16,0},{1,17},{17,1},{2,18},{18,2},{3,19},{19,3},{4,20},{20... | collective-permute-start | bytes 3145736 | tf_op jit(solution)/shard_map/ppermute | solution.py:43
  127.8 58.3 %collective-permute-start.17 = (bf16[512,2048]{1,0:T(8,128)(2,1)}, bf16[512,2048]{1,0:T(8,128)(2,1)}, u32[]{:S(2)}, u32[]{:S(2)}) collective-permute-start(bf16[512,2048]{1,0:T(8,128)(2,1)} %shard_map.327.refs_2_.refs_1_), channel_id=1, source_target_pairs={{0,8},{4,12},{8,0},{12,4},{1,9},{5,13},{9,1},{13,5},{2,10},{6,14},... | collective-permute-start | bytes 6291464 | tf_op jit(solution)/shard_map/ppermute | solution.py:33
  141.6 34.5 %collective-permute-start.16 = (bf16[1,4,4,64,512]{4,3,2,1,0:T(8,128)(2,1)}, bf16[1,4,4,64,512]{4,3,2,1,0:T(8,128)(2,1)}, u32[]{:S(2)}, u32[]{:S(2)}) collective-permute-start(bf16[1,4,4,64,512]{4,3,2,1,0:T(8,128)(2,1)} %shard_map.325.refs_5_.refs_6_), channel_id=1, source_target_pairs={{0,16},{16,0},{1,17},{17,1},{2,18},{18,2},{3,19},{19,3},{4,20},{20... | collective-permute-start | bytes 3145736 | tf_op jit(solution)/shard_map/ppermute | solution.py:43
  163.6 36.5 %collective-permute-start.26 = (bf16[256,2048]{1,0:T(8,128)(2,1)S(1)}, bf16[256,2048]{1,0:T(8,128)(2,1)S(1)}, u32[]{:S(2)}, u32[]{:S(2)}) collective-permute-start(bf16[256,2048]{1,0:T(8,128)(2,1)S(1)} %shard_map.337), channel_id=1, source_target_pairs={{0,16},{16,0},{1,17},{17,1},{2,18},{18,2},{3,19},{19,3},{4,20},{20... | collective-permute-start | bytes 3145736 | tf_op jit(solution)/shard_map/ppermute | solution.py:43
  202.2 310.5 %reduce-scatter.8.cloned.1.call-start = ((), (), s32[]{:S(2)}) async-start(), calls=%async_computation.14 | async-start | bytes 4718592 | tf_op jit(solution)/shard_map/reduce_scatter | solution.py:846
  210.5 48.4 %collective-permute-start.21 = (bf16[1,4,4,64,1024]{4,3,2,1,0:T(8,128)(2,1)}, bf16[1,4,4,64,1024]{4,3,2,1,0:T(8,128)(2,1)}, u32[]{:S(2)}, u32[]{:S(2)}) collective-permute-start(bf16[1,4,4,64,1024]{4,3,2,1,0:T(8,128)(2,1)} %shard_map.332.refs_5_.refs_2_), channel_id=1, source_target_pairs={{0,16},{16,0},{1,17},{17,1},{2,18},{18,2},{3,19},{19,3},{4,20},{20... | collective-permute-start | bytes 6291464 | tf_op jit(solution)/shard_map/ppermute | solution.py:43
  211.1 47.7 %collective-permute-start.18 = (bf16[512,2048]{1,0:T(8,128)(2,1)}, bf16[512,2048]{1,0:T(8,128)(2,1)}, u32[]{:S(2)}, u32[]{:S(2)}) collective-permute-start(bf16[512,2048]{1,0:T(8,128)(2,1)} %get-tuple-element.50), channel_id=1, source_target_pairs={{0,4},{4,0},{8,12},{12,8},{1,5},{5,1},{9,13},{13,9},{2,6},{6,2},{1... | collective-permute-start | bytes 6291464 | tf_op jit(solution)/shard_map/ppermute | solution.py:33
  223.5 48.1 %collective-permute-start.20 = (bf16[512,2048]{1,0:T(8,128)(2,1)S(1)}, bf16[512,2048]{1,0:T(8,128)(2,1)}, u32[]{:S(2)}, u32[]{:S(2)}) collective-permute-start(bf16[512,2048]{1,0:T(8,128)(2,1)S(1)} %shard_map.331.refs_7_), channel_id=1, source_target_pairs={{0,8},{4,12},{8,0},{12,4},{1,9},{5,13},{9,1},{13,5},{2,10},{6,14},... | collective-permute-start | bytes 6291464 | tf_op jit(solution)/shard_map/ppermute | solution.py:33
  281.0 47.1 %collective-permute-start.23 = (bf16[1,4,4,64,1024]{4,3,2,1,0:T(8,128)(2,1)S(1)}, bf16[1,4,4,64,1024]{4,3,2,1,0:T(8,128)(2,1)S(1)}, u32[]{:S(2)}, u32[]{:S(2)}) collective-permute-start(bf16[1,4,4,64,1024]{4,3,2,1,0:T(8,128)(2,1)S(1)} %shard_map.334.refs_7_.refs_4_), channel_id=1, source_target_pairs={{0,16},{16,0},{1,17},{17,1},{2,18},{18,2},{3,19},{19,3},{4,20},{20... | collective-permute-start | bytes 6291464 | tf_op jit(solution)/shard_map/ppermute | solution.py:43
  282.4 47.1 %collective-permute-start.22 = (bf16[512,2048]{1,0:T(8,128)(2,1)S(1)}, bf16[512,2048]{1,0:T(8,128)(2,1)}, u32[]{:S(2)}, u32[]{:S(2)}) collective-permute-start(bf16[512,2048]{1,0:T(8,128)(2,1)S(1)} %get-tuple-element.53.refs_1_.refs_10_), channel_id=1, source_target_pairs={{0,8},{4,12},{8,0},{12,4},{1,9},{5,13},{9,1},{13,5},{2,10},{6,14},... | collective-permute-start | bytes 6291464 | tf_op jit(solution)/shard_map/ppermute | solution.py:33
  283.9 46.2 %collective-permute-start.24 = (bf16[512,2048]{1,0:T(8,128)(2,1)S(1)}, bf16[512,2048]{1,0:T(8,128)(2,1)}, u32[]{:S(2)}, u32[]{:S(2)}) collective-permute-start(bf16[512,2048]{1,0:T(8,128)(2,1)S(1)} %get-tuple-element.53.refs_1_.refs_10_), channel_id=1, source_target_pairs={{0,4},{4,0},{8,12},{12,8},{1,5},{5,1},{9,13},{13,9},{2,6},{6,2},{1... | collective-permute-start | bytes 6291464 | tf_op jit(solution)/shard_map/ppermute | solution.py:33
  329.5 34.6 %collective-permute-start.27 = (bf16[512,2048]{1,0:T(8,128)(2,1)}, bf16[512,2048]{1,0:T(8,128)(2,1)}, u32[]{:S(2)}, u32[]{:S(2)}) collective-permute-start(bf16[512,2048]{1,0:T(8,128)(2,1)} %shard_map.327.refs_2_.refs_1_), channel_id=1, source_target_pairs={{0,4},{4,0},{8,12},{12,8},{1,5},{5,1},{9,13},{13,9},{2,6},{6,2},{1... | collective-permute-start | bytes 6291464 | tf_op jit(solution)/shard_map/ppermute | solution.py:33
  330.0 34.1 %collective-permute-start.28 = (bf16[512,2048]{1,0:T(8,128)(2,1)}, bf16[512,2048]{1,0:T(8,128)(2,1)}, u32[]{:S(2)}, u32[]{:S(2)}) collective-permute-start(bf16[512,2048]{1,0:T(8,128)(2,1)} %collective-permute-done.17.refs_4_.refs_3_.refs_2_), channel_id=1, source_target_pairs={{0,4},{4,0},{8,12},{12,8},{1,5},{5,1},{9,13},{13,9},{2,6},{6,2},{1... | collective-permute-start | bytes 6291464 | tf_op jit(solution)/shard_map/ppermute | solution.py:33
  379.0 193.7 %reduce-scatter.10.cloned.1.call-start = ((), (), s32[]{:S(2)}) async-start(), calls=%async_computation.15 | async-start | bytes 4718592 | tf_op jit(solution)/shard_map/reduce_scatter | solution.py:846
  436.7 15.3 %collective-permute-start.30 = (bf16[512,2048]{1,0:T(8,128)(2,1)}, bf16[512,2048]{1,0:T(8,128)(2,1)}, u32[]{:S(2)}, u32[]{:S(2)}) collective-permute-start(bf16[512,2048]{1,0:T(8,128)(2,1)} %get-tuple-element.58.refs_6_), channel_id=1, source_target_pairs={{0,4},{4,0},{8,12},{12,8},{1,5},{5,1},{9,13},{13,9},{2,6},{6,2},{1... | collective-permute-start | bytes 6291464 | tf_op jit(solution)/shard_map/ppermute | solution.py:33
  436.8 211.7 %reduce-scatter.12.cloned.1.call-start = ((), (), s32[]{:S(2)}) async-start(), calls=%async_computation.16 | async-start | bytes 2621440 | tf_op jit(solution)/shard_map/reduce_scatter | solution.py:827
  437.0 54.5 %collective-permute-start.29 = (bf16[512,2048]{1,0:T(8,128)(2,1)}, bf16[512,2048]{1,0:T(8,128)(2,1)S(1)}, u32[]{:S(2)}, u32[]{:S(2)}) collective-permute-start(bf16[512,2048]{1,0:T(8,128)(2,1)} %copy-done.73), channel_id=1, source_target_pairs={{0,4},{4,0},{8,12},{12,8},{1,5},{5,1},{9,13},{13,9},{2,6},{6,2},{1... | collective-permute-start | bytes 6291464 | tf_op jit(solution)/shard_map/ppermute | solution.py:33
  453.8 47.6 %collective-permute-start.31 = (bf16[512,2048]{1,0:T(8,128)(2,1)S(1)}, bf16[512,2048]{1,0:T(8,128)(2,1)S(1)}, u32[]{:S(2)}, u32[]{:S(2)}) collective-permute-start(bf16[512,2048]{1,0:T(8,128)(2,1)S(1)} %shard_map.344.refs_6_), channel_id=1, source_target_pairs={{0,8},{4,12},{8,0},{12,4},{1,9},{5,13},{9,1},{13,5},{2,10},{6,14},... | collective-permute-start | bytes 6291464 | tf_op jit(solution)/shard_map/ppermute | solution.py:33
  463.7 81.2 %collective-permute-start.34 = (bf16[1,4,4,64,1024]{4,3,2,1,0:T(8,128)(2,1)}, bf16[1,4,4,64,1024]{4,3,2,1,0:T(8,128)(2,1)}, u32[]{:S(2)}, u32[]{:S(2)}) collective-permute-start(bf16[1,4,4,64,1024]{4,3,2,1,0:T(8,128)(2,1)} %shard_map.345.refs_6_), channel_id=1, source_target_pairs={{0,16},{16,0},{1,17},{17,1},{2,18},{18,2},{3,19},{19,3},{4,20},{20... | collective-permute-start | bytes 6291464 | tf_op jit(solution)/shard_map/ppermute | solution.py:43
  511.2 47.0 %collective-permute-start.36 = (bf16[512,2048]{1,0:T(8,128)(2,1)}, bf16[512,2048]{1,0:T(8,128)(2,1)S(1)}, u32[]{:S(2)}, u32[]{:S(2)}) collective-permute-start(bf16[512,2048]{1,0:T(8,128)(2,1)} %get-tuple-element.67.refs_1_.refs_2_), channel_id=1, source_target_pairs={{0,8},{4,12},{8,0},{12,4},{1,9},{5,13},{9,1},{13,5},{2,10},{6,14},... | collective-permute-start | bytes 6291464 | tf_op jit(solution)/shard_map/ppermute | solution.py:33
  512.8 52.2 %collective-permute-start.35 = (bf16[512,2048]{1,0:T(8,128)(2,1)}, bf16[512,2048]{1,0:T(8,128)(2,1)}, u32[]{:S(2)}, u32[]{:S(2)}) collective-permute-start(bf16[512,2048]{1,0:T(8,128)(2,1)} %get-tuple-element.67.refs_1_.refs_2_), channel_id=1, source_target_pairs={{0,4},{4,0},{8,12},{12,8},{1,5},{5,1},{9,13},{13,9},{2,6},{6,2},{1... | collective-permute-start | bytes 6291464 | tf_op jit(solution)/shard_map/ppermute | solution.py:33
  578.5 113.7 %reduce-scatter.14.cloned.1.call-start = ((), (), s32[]{:S(2)}) async-start(), calls=%async_computation.17 | async-start | bytes 2621440 | tf_op jit(solution)/shard_map/reduce_scatter | solution.py:827
  578.7 48.3 %collective-permute-start.39 = (bf16[1,4,4,64,1024]{4,3,2,1,0:T(8,128)(2,1)}, bf16[1,4,4,64,1024]{4,3,2,1,0:T(8,128)(2,1)S(1)}, u32[]{:S(2)}, u32[]{:S(2)}) collective-permute-start(bf16[1,4,4,64,1024]{4,3,2,1,0:T(8,128)(2,1)} %copy-done.49), channel_id=1, source_target_pairs={{0,16},{16,0},{1,17},{17,1},{2,18},{18,2},{3,19},{19,3},{4,20},{20... | collective-permute-start | bytes 6291464 | tf_op jit(solution)/shard_map/ppermute | solution.py:43
  630.8 71.6 %reduce-scatter.16.cloned.1.call-start = ((), (), s32[]{:S(2)}) async-start(), calls=%async_computation.18 | async-start | bytes 1310720 | tf_op jit(solution)/shard_map/reduce_scatter | solution.py:827
  639.0 33.3 %collective-permute-start.40 = (bf16[256,2048]{1,0:T(8,128)(2,1)}, bf16[256,2048]{1,0:T(8,128)(2,1)}, u32[]{:S(2)}, u32[]{:S(2)}) collective-permute-start(bf16[256,2048]{1,0:T(8,128)(2,1)} %shard_map.360.refs_6_), channel_id=1, source_target_pairs={{0,16},{16,0},{1,17},{17,1},{2,18},{18,2},{3,19},{19,3},{4,20},{20... | collective-permute-start | bytes 3145736 | tf_op jit(solution)/shard_map/ppermute | solution.py:43
  640.4 47.2 %collective-permute-start.38 = (bf16[512,2048]{1,0:T(8,128)(2,1)}, bf16[512,2048]{1,0:T(8,128)(2,1)}, u32[]{:S(2)}, u32[]{:S(2)}) collective-permute-start(bf16[512,2048]{1,0:T(8,128)(2,1)} %shard_map.356.refs_4_), channel_id=1, source_target_pairs={{0,8},{4,12},{8,0},{12,4},{1,9},{5,13},{9,1},{13,5},{2,10},{6,14},... | collective-permute-start | bytes 6291464 | tf_op jit(solution)/shard_map/ppermute | solution.py:33
  641.9 45.7 %collective-permute-start.41 = (bf16[512,2048]{1,0:T(8,128)(2,1)}, bf16[512,2048]{1,0:T(8,128)(2,1)}, u32[]{:S(2)}, u32[]{:S(2)}) collective-permute-start(bf16[512,2048]{1,0:T(8,128)(2,1)} %get-tuple-element.70.refs_2_), channel_id=1, source_target_pairs={{0,4},{4,0},{8,12},{12,8},{1,5},{5,1},{9,13},{13,9},{2,6},{6,2},{1... | collective-permute-start | bytes 6291464 | tf_op jit(solution)/shard_map/ppermute | solution.py:33
  675.0 136.4 %reduce-scatter.18.cloned.1.call-start = ((), (), s32[]{:S(2)}) async-start(), calls=%async_computation.19 | async-start | bytes 1310720 | tf_op jit(solution)/shard_map/reduce_scatter | solution.py:827
  699.6 26.1 %collective-permute-start.42 = (bf16[1,4,4,64,512]{4,3,2,1,0:T(8,128)(2,1)S(1)}, bf16[1,4,4,64,512]{4,3,2,1,0:T(8,128)(2,1)}, u32[]{:S(2)}, u32[]{:S(2)}) collective-permute-start(bf16[1,4,4,64,512]{4,3,2,1,0:T(8,128)(2,1)S(1)} %shard_map.366.refs_7_), channel_id=1, source_target_pairs={{0,16},{16,0},{1,17},{17,1},{2,18},{18,2},{3,19},{19,3},{4,20},{20... | collective-permute-start | bytes 3145736 | tf_op jit(solution)/shard_map/ppermute | solution.py:43
  700.4 40.1 %collective-permute-start.32 = (bf16[512,2048]{1,0:T(8,128)(2,1)}, bf16[512,2048]{1,0:T(8,128)(2,1)}, u32[]{:S(2)}, u32[]{:S(2)}) collective-permute-start(bf16[512,2048]{1,0:T(8,128)(2,1)} %get-tuple-element.65), channel_id=1, source_target_pairs={{0,4},{4,0},{8,12},{12,8},{1,5},{5,1},{9,13},{13,9},{2,6},{6,2},{1... | collective-permute-start | bytes 6291464 | tf_op jit(solution)/shard_map/ppermute | solution.py:33
  700.7 49.2 %collective-permute-start.43 = (bf16[512,2048]{1,0:T(8,128)(2,1)}, bf16[512,2048]{1,0:T(8,128)(2,1)}, u32[]{:S(2)}, u32[]{:S(2)}) collective-permute-start(bf16[512,2048]{1,0:T(8,128)(2,1)} %get-tuple-element.75), channel_id=1, source_target_pairs={{0,4},{4,0},{8,12},{12,8},{1,5},{5,1},{9,13},{13,9},{2,6},{6,2},{1... | collective-permute-start | bytes 6291464 | tf_op jit(solution)/shard_map/ppermute | solution.py:33
  700.9 48.9 %collective-permute-start.44 = (bf16[512,2048]{1,0:T(8,128)(2,1)}, bf16[512,2048]{1,0:T(8,128)(2,1)}, u32[]{:S(2)}, u32[]{:S(2)}) collective-permute-start(bf16[512,2048]{1,0:T(8,128)(2,1)} %shard_map.365.refs_7_), channel_id=1, source_target_pairs={{0,8},{4,12},{8,0},{12,4},{1,9},{5,13},{9,1},{13,5},{2,10},{6,14},... | collective-permute-start | bytes 6291464 | tf_op jit(solution)/shard_map/ppermute | solution.py:33
  713.5 56.7 %collective-permute-start.55 = (bf16[1,4,4,64,1024]{4,3,2,1,0:T(8,128)(2,1)}, bf16[1,4,4,64,1024]{4,3,2,1,0:T(8,128)(2,1)}, u32[]{:S(2)}, u32[]{:S(2)}) collective-permute-start(bf16[1,4,4,64,1024]{4,3,2,1,0:T(8,128)(2,1)} %shard_map.367.refs_7_), channel_id=1, source_target_pairs={{0,16},{16,0},{1,17},{17,1},{2,18},{18,2},{3,19},{19,3},{4,20},{20... | collective-permute-start | bytes 6291464 | tf_op jit(solution)/shard_map/ppermute | solution.py:43
  729.4 89.9 %reduce-scatter.20.cloned.1.call-start = ((), (), s32[]{:S(2)}) async-start(), calls=%async_computation.20 | async-start | bytes 2621440 | tf_op jit(solution)/shard_map/reduce_scatter | solution.py:827
  (130 other events, 775.8 us)
Sparse Core Ops, SparseCore 0:
  9.6 30.5 all-gather.7
  42.4 27.4 all-gather.9
  72.1 27.4 all-gather.11
  101.5 27.4 all-gather.13
  131.0 45.4 all-gather.15
  178.4 44.6 all-gather.17
  224.7 148.3 all-gather.19
  379.1 86.6 reduce-scatter.7
  469.9 96.7 reduce-scatter.9
  578.7 42.7 reduce-scatter.11
  630.9 42.7 reduce-scatter.13
  675.9 26.4 reduce-scatter.15
  729.5 25.0 reduce-scatter.17
  774.6 40.7 reduce-scatter.19

commit v5 on v4

--- a/solution.py
+++ b/solution.py
@@ -789,10 +789,10 @@
     a_own = pin(a_own, block_o)
     a_across = team_swap(a_own, 2)
     w_o = flatten(both_halves(block_o))
-    a_across = pin(a_across, w_q[1], w_o[1])
+    g_rows = pack(cotangent)
+    a_across = pin(a_across, w_q[1], w_o[1], g_rows)
     a_all = [a_own, a_across, team_swap(a_own, 1), team_swap(a_across, 1)]
     block_up = [stored(depth_gather(columns(up_deal, i, 2))) for i in range(2)]
-    g_rows = pack(cotangent)
     g_all = team_gather(pin(g_rows, a_all[1]))
 
     wide = TEAM * rows
@@ -846,7 +846,6 @@
         return lax.psum_scatter(grad, SPREAD, scatter_dimension=0, tiled=True)
 
     grad_down = [settle_whole(weight_grad([active], g_all, None, cut=(0, 1, 2)))]
-    grad_down.append(settle_whole(weight_grad([active], g_all, None, cut=(1, 2, 2))))
     d_inner, sum_inner = back(g_all, w_down, style="slope", slope=slope)
     n_far = send_far(back([d_inner], w_up, style="bare", pick=(1, 2)))
     n_near = back([d_inner], w_up, style="bare", pick=(0, 2))
@@ -854,17 +853,19 @@
     up_sent = [
         send_away(weight_grad(b_all, [d_inner], 1, spread=spread, cut=(i, i + 1, 2))) for i in range(2)
     ]
-    up_mine = [weight_grad(b_all, [d_inner], 0, spread=spread, cut=(i, i + 1, 2)) for i in range(2)]
+    down_late = weight_grad([active], g_all, None, cut=(1, 2, 2))
     d_hidden, d_out, sums2 = by_rows(
         functools.partial(norm_back_kernel, 3), n_parts + [hidden, g_rows], [gain2], [F32, BF], sums=4
     )
+    grad_down.append(settle_whole(pin(down_late, d_out)))
     y_far = send_far(forward([active], w_down, style="bare", pick=(1, 2), hold=[grad_down[0]]))
     y_near = forward([active], w_down, style="bare", pick=(0, 2))
-    d_out_all = team_gather(d_out, up_sent[0], y_near[1])
+    up_mine = [weight_grad(b_all, [d_inner], 0, spread=spread, cut=(i, i + 1, 2)) for i in range(2)]
+    d_out_all = team_gather(d_out, up_sent[0], up_mine[1])
 
     (d_near,) = back(d_out_all[:2], [w_o])
     (d_far,) = back(d_out_all[2:], [w_o])
-    grad_up = [settle(up_sent[0], up_mine[0], hold=[grad_down[1]])]
+    grad_up = [settle(up_sent[0], up_mine[0])]
     *y_parts, y_across = join_near(y_near, y_far)
     q_far, sum_far = order.step(attend_back, q, k, v, d_far.reshape(2 * rows, -1), 2 * rows // SLOT)
     q_far = q_far.reshape(2, rows, -1)
@@ -872,19 +873,19 @@
     grad_up.append(settle(up_sent[1], up_mine[1]))
     o_sent = send_away(weight_grad([context], d_out_all, 1))
     o_mine = weight_grad([context], d_out_all, 0)
-    q_near, sum_near = order.step(attend_back, q, k, v, d_near.reshape(2 * rows, -1), 0, hold=[grad_up[0]])
+    q_near, sum_near = order.step(attend_back, q, k, v, d_near.reshape(2 * rows, -1), 0, hold=[grad_down[1]])
     q_near = q_near.reshape(2, rows, -1)
     grad_o = settle(o_sent, o_mine)
     a_near = back([q_near], [w_q, w_k, w_v], style="bare")
-    a_parts = join_near(a_near, a_far, hold=[y_parts[2]])[:3]
+    a_parts = join_near(a_near, a_far, hold=[y_parts[2], grad_up[0]])[:3]
     parts = ((0, 1, 3), (1, 3, 3))
     d_both = [q_near, q_far]
     qkv_sent = [
-        send_away(weight_grad(a_all, d_both, 1, spread=spread, cut=parts[0], hold=[grad_up[1]])),
-        send_away(weight_grad(a_all, d_both, 1, spread=spread, cut=parts[1], hold=[grad_o])),
+        send_away(weight_grad(a_all, d_both, 1, spread=spread, cut=parts[0])),
+        send_away(weight_grad(a_all, d_both, 1, spread=spread, cut=parts[1], hold=[grad_up[1]])),
     ]
     grad_q = settle(qkv_sent[0], weight_grad(a_all, d_both, 0, spread=spread, cut=parts[0]))
-    kv_mine = weight_grad(a_all, d_both, 0, spread=spread, cut=parts[1])
+    kv_mine = weight_grad(a_all, d_both, 0, spread=spread, cut=parts[1], hold=[grad_o])
     (y_rows,) = by_rows(functools.partial(join_kernel, 4), [hidden] + y_parts, [bias_down], [BF])
     layer_out = unpack(y_rows, tokens)
     _, d_input, sums1 = by_rows(

time: 851 us -> 853 us (level)
    all_gather x7, waiting for transfers between devices: 0.05 us -> 16.9 us  [depth_gather(): return lax.all_gather(a, 'fsdp', axis=0, tiled=True)]
    ppermute x42, waiting for transfers between devices: 81.1 us -> 71.6 us  [team_swap(): return lax.ppermute(a, 'team', [(i, i ^ flip) for i in range(TEAM)])]
    unnamed x213 -> x205, local copies, waits for them, and re-layouts: 61.5 us -> 59.1 us
  transfers between devices with their start and end apart: 76 -> 76, of which waited for: 29 -> 31; matrix products, arithmetic and copies ran while one was open for 6% -> 6% of each run, Pallas kernels for 46% -> 46%
where the time goes in v5:
time: 853 us; the launch traced here: 845 us
  Pallas kernels  391 us (46%)
  waiting for transfers between devices  261 us (31%)
  local copies, waits for them, and re-layouts  88.6 us (10%)
  starting transfers between devices  52.8 us (6%)
  matrix products  22 us (3%)
  between operations  15.7 us (2%)
  other arithmetic  14.5 us (2%)
    pallas_call x44, Pallas kernels, kernel_call(): pl.pallas_call(run, grid_spec=pltpu.PrefetchScalarGridSpec(num_scalar_pre...  391 us
    ppermute x12, waiting for transfers between devices, outer_pass(): lax.ppermute(a, 'outer', [(o, order[(p + 1) % outer]) for p, o in enumera...  169 us
    ppermute x42, waiting for transfers between devices, team_swap(): return lax.ppermute(a, 'team', [(i, i ^ flip) for i in range(TEAM)])  71.6 us
    unnamed x205, local copies, waits for them, and re-layouts  59.1 us
    ppermute x42, starting transfers between devices, team_swap(): return lax.ppermute(a, 'team', [(i, i ^ flip) for i in range(TEAM)])  25.9 us
  transfers between devices with their start and end apart: 76, of which 31 were waited for; matrix products, arithmetic and copies ran while one was open for 6% of the time, Pallas kernels for 46%

profile of v5, /device:TPU:0, one launch (start us, length us, event | category | flops | bytes accessed | tf_op | source)
XLA Modules:
  0.0 845.5 jit_solution(1971368587438441061)
XLA Ops:
  22.2 9.5 %collective-permute-done.8 = bf16[64,3584]{1,0:T(8,128)(2,1)} collective-permute-done((bf16[64,3584]{1,0:T(8,128)(2,1)S(1)}, bf16[64,3584]{1,0:T(8,128)(2,1)}, u32[]{:S(2)}, u32[]{:S(2)}) %collective-permute-start.8) | collective-permute-done | bytes 458784 | tf_op jit(solution)/shard_map/ppermute | solution.py:33
  31.7 10.0 %collective-permute-done.9 = bf16[64,3584]{1,0:T(8,128)(2,1)} collective-permute-done((bf16[64,3584]{1,0:T(8,128)(2,1)S(1)}, bf16[64,3584]{1,0:T(8,128)(2,1)}, u32[]{:S(2)}, u32[]{:S(2)}) %collective-permute-start.9) | collective-permute-done | bytes 458784 | tf_op jit(solution)/shard_map/ppermute | solution.py:33
  72.9 8.0 all-gather.10.cloned.1.call-done
  82.5 5.9 fusion.7.refs_3_.refs_4_
  88.5 10.2 %collective-permute-done.12 = bf16[1,256,2048]{2,1,0:T(8,128)(2,1)S(1)} collective-permute-done((bf16[1,256,2048]{2,1,0:T(8,128)(2,1)}, bf16[1,256,2048]{2,1,0:T(8,128)(2,1)S(1)}, u32[]{:S(2)}, u32[]{:S(2)}) %collective-permute-start.12) | collective-permute-done | bytes 1048608 | tf_op jit(solution)/shard_map/ppermute | solution.py:43
  98.6 21.7 %collective-permute-done.11.refs_1_.refs_6_.refs_3_ = bf16[1,4,4,64,512]{4,3,2,1,0:T(8,128)(2,1)S(1)} collective-permute-done((bf16[1,4,4,64,512]{4,3,2,1,0:T(8,128)(2,1)}, bf16[1,4,4,64,512]{4,3,2,1,0:T(8,128)(2,1)S(1)}, u32[]{:S(2)}, u32[]{:S(2)}) %collective-permute-start.11) | collective-permute-done | bytes 1048608 | tf_op jit(solution)/shard_map/ppermute | solution.py:43
  129.8 8.5 %shard_map.323.refs_8_.refs_1_ = bf16[4,512,512]{2,1,0:T(8,128)(2,1)S(1)} custom-call(s32[1]{0:T(128)} %bitcast.5.refs_0_, bf16[512,2048]{1,0:T(8,128)(2,1)} %shard_map.321.refs_1_, bf16[512,2048]{1,0:T(8,128)(2,1)} %copy-done, bf16[512,2048]{1,0:T(8,128)(2,1)} %collective-permute-done.13.refs_3_, bf16[512,2048]{1,0:T(8,128)(2,1)} %collective-permute-done.14.refs_4_, ...), custom_call_target="tpu_custom_call" | custom-call | flops 4294967 | bytes 12582 | tf_op jit(solution)/shard_map/pallas_call | solution.py:171
  141.7 9.9 %collective-permute-done.15.refs_6_.refs_5_ = bf16[1,4,4,64,512]{4,3,2,1,0:T(8,128)(2,1)} collective-permute-done((bf16[1,4,4,64,512]{4,3,2,1,0:T(8,128)(2,1)}, bf16[1,4,4,64,512]{4,3,2,1,0:T(8,128)(2,1)}, u32[]{:S(2)}, u32[]{:S(2)}) %collective-permute-start.15) | collective-permute-done | bytes 1048608 | tf_op jit(solution)/shard_map/ppermute | solution.py:43
  151.6 8.6 %shard_map.324.refs_8_ = bf16[4,512,512]{2,1,0:T(8,128)(2,1)S(1)} custom-call(s32[1]{0:T(128)} %bitcast.5.refs_0_, bf16[512,2048]{1,0:T(8,128)(2,1)} %shard_map.321.refs_1_, bf16[512,2048]{1,0:T(8,128)(2,1)} %copy-done, bf16[512,2048]{1,0:T(8,128)(2,1)} %collective-permute-done.13.refs_3_, bf16[512,2048]{1,0:T(8,128)(2,1)} %collective-permute-done.14.refs_4_, ...), custom_call_target="tpu_custom_call" | custom-call | flops 4294967 | bytes 12582 | tf_op jit(solution)/shard_map/pallas_call | solution.py:171
  162.2 11.9 %collective-permute-done.16.refs_6_.refs_7_ = bf16[1,4,4,64,512]{4,3,2,1,0:T(8,128)(2,1)} collective-permute-done((bf16[1,4,4,64,512]{4,3,2,1,0:T(8,128)(2,1)}, bf16[1,4,4,64,512]{4,3,2,1,0:T(8,128)(2,1)}, u32[]{:S(2)}, u32[]{:S(2)}) %collective-permute-start.16) | collective-permute-done | bytes 1048608 | tf_op jit(solution)/shard_map/ppermute | solution.py:43
  174.1 8.7 %shard_map.326.refs_3_ = bf16[4,512,512]{2,1,0:T(8,128)(2,1)S(1)} custom-call(s32[1]{0:T(128)} %bitcast.5.refs_0_, bf16[512,2048]{1,0:T(8,128)(2,1)} %shard_map.321.refs_1_, bf16[512,2048]{1,0:T(8,128)(2,1)} %copy-done, bf16[512,2048]{1,0:T(8,128)(2,1)} %collective-permute-done.13.refs_3_, bf16[512,2048]{1,0:T(8,128)(2,1)} %collective-permute-done.14.refs_4_, ...), custom_call_target="tpu_custom_call" | custom-call | flops 4294967 | bytes 12582 | tf_op jit(solution)/shard_map/pallas_call | solution.py:171
  184.2 14.0 %shard_map.328.refs_4_ = bf16[2048,512]{1,0:T(8,128)(2,1)S(1)} custom-call(bf16[2048,512]{1,0:T(8,128)(2,1)S(1)} %bitcast.144, bf16[2048,512]{1,0:T(8,128)(2,1)} %bitcast.148, bf16[2048,512]{1,0:T(8,128)(2,1)} %bitcast.151, bf16[4,512,512]{2,1,0:T(8,128)(2,1)} %copy-done.12, bf16[512,2048]{1,0:T(8,128)(2,1)} %collective-permute-done.17.refs_4_.refs_3_.refs_2_), custom_call_target="tpu_custom_call" | custom-call | flops 4294967 | bytes 8388 | tf_op jit(solution)/shard_map/pallas_call | solution.py:171
  200.6 7.9 shard_map.329
  209.2 7.6 shard_map.330
  223.4 33.5 %collective-permute-done.21.refs_8_.refs_6_.refs_3_ = bf16[1,4,4,64,1024]{4,3,2,1,0:T(8,128)(2,1)} collective-permute-done((bf16[1,4,4,64,1024]{4,3,2,1,0:T(8,128)(2,1)}, bf16[1,4,4,64,1024]{4,3,2,1,0:T(8,128)(2,1)}, u32[]{:S(2)}, u32[]{:S(2)}) %collective-permute-start.21) | collective-permute-done | bytes 2097184 | tf_op jit(solution)/shard_map/ppermute | solution.py:43
  256.9 12.7 %collective-permute-done.20.refs_3_ = bf16[512,2048]{1,0:T(8,128)(2,1)} collective-permute-done((bf16[512,2048]{1,0:T(8,128)(2,1)S(1)}, bf16[512,2048]{1,0:T(8,128)(2,1)}, u32[]{:S(2)}, u32[]{:S(2)}) %collective-permute-start.20) | collective-permute-done | bytes 2097184 | tf_op jit(solution)/shard_map/ppermute | solution.py:33
  271.2 6.1 shard_map.333
  282.0 44.1 %collective-permute-done.23.refs_1_.refs_8_.refs_5_ = bf16[1,4,4,64,1024]{4,3,2,1,0:T(8,128)(2,1)S(1)} collective-permute-done((bf16[1,4,4,64,1024]{4,3,2,1,0:T(8,128)(2,1)S(1)}, bf16[1,4,4,64,1024]{4,3,2,1,0:T(8,128)(2,1)S(1)}, u32[]{:S(2)}, u32[]{:S(2)}) %collective-permute-start.23) | collective-permute-done | bytes 2097184 | tf_op jit(solution)/shard_map/ppermute | solution.py:43
  332.0 30.1 %shard_map.336 = (bf16[4,512,2048]{2,1,0:T(8,128)(2,1)}, bf16[4,512,2048]{2,1,0:T(8,128)(2,1)}) custom-call(s32[1]{0:T(128)} %bitcast.5.refs_0_, bf16[512,2048]{1,0:T(8,128)(2,1)S(1)} %get-tuple-element.53.refs_1_.refs_10_, bf16[512,2048]{1,0:T(8,128)(2,1)} %shard_map.335.refs_2_, bf16[512,2048]{1,0:T(8,128)(2,1)} %collective-permute-done.24.refs_3_, ...), custom_call_target="tpu_custom_call" | custom-call | flops 17179868 | bytes 25165 | tf_op jit(solution)/shard_map/pallas_call | solution.py:171
  362.1 14.9 %shard_map.339.refs_8_ = bf16[2048,1024]{1,0:T(8,128)(2,1)} custom-call(s32[1]{0:T(128)} %bitcast.5.refs_0_, bf16[4,512,2048]{2,1,0:T(8,128)(2,1)} %get-tuple-element.54.refs_1_, bf16[512,2048]{1,0:T(8,128)(2,1)} %shard_map.327.refs_2_.refs_1_, bf16[512,2048]{1,0:T(8,128)(2,1)} %collective-permute-done.17.refs_4_.refs_3_.refs_2_, ...), custom_call_target="tpu_custom_call" | custom-call | flops 8589934 | bytes 16777 | tf_op jit(solution)/shard_map/pallas_call | solution.py:171
  377.3 6.9 all-gather.20.cloned.1.call-done.refs_5_.refs_6_.refs_2_.refs_3_
  384.2 25.6 %shard_map.340 = (bf16[4,512,2048]{2,1,0:T(8,128)(2,1)}, f32[1,2048]{1,0:T(1,128)S(1)}) custom-call(s32[1]{0:T(128)} %bitcast.5.refs_0_, bf16[512,2048]{1,0:T(8,128)(2,1)} %shard_map.327.refs_2_.refs_1_, bf16[512,2048]{1,0:T(8,128)(2,1)} %collective-permute-done.17.refs_4_.refs_3_.refs_2_, bf16[512,2048]{1,0:T(8,128)(2,1)} %collective-permute-done.27.refs_4_.refs_3_, ...), custom_call_target="tpu_custom_call" | custom-call | flops 17179868 | bytes 25165 | tf_op jit(solution)/shard_map/pallas_call | solution.py:171
  409.8 14.7 %shard_map.341 = (bf16[512,2048]{1,0:T(8,128)(2,1)S(1)}, bf16[512,2048]{1,0:T(8,128)(2,1)S(1)}) custom-call(s32[1]{0:T(128)} %bitcast.5.refs_0_, bf16[4,512,2048]{2,1,0:T(8,128)(2,1)} %get-tuple-element.56.refs_1_.refs_5_, bf16[1,4,4,64,1024]{4,3,2,1,0:T(8,128)(2,1)} %shard_map.332.refs_5_.refs_2_, ...), custom_call_target="tpu_custom_call" | custom-call | flops 8589934 | bytes 12582 | tf_op jit(solution)/shard_map/pallas_call | solution.py:171
  425.9 14.5 %shard_map.342 = (bf16[512,2048]{1,0:T(8,128)(2,1)S(1)}, bf16[512,2048]{1,0:T(8,128)(2,1)S(1)}) custom-call(s32[1]{0:T(128)} %bitcast.5.refs_0_, bf16[4,512,2048]{2,1,0:T(8,128)(2,1)} %get-tuple-element.56.refs_1_.refs_5_, bf16[1,4,4,64,1024]{4,3,2,1,0:T(8,128)(2,1)} %shard_map.332.refs_5_.refs_2_, ...), custom_call_target="tpu_custom_call" | custom-call | flops 8589934 | bytes 12582 | tf_op jit(solution)/shard_map/pallas_call | solution.py:171
  445.1 7.5 shard_map.344.refs_6_
  454.0 7.5 shard_map.345.refs_6_
  462.9 15.2 %shard_map.346.refs_6_.refs_0_ = bf16[2048,1024]{1,0:T(8,128)(2,1)} custom-call(s32[1]{0:T(128)} %bitcast.5.refs_0_, bf16[4,512,2048]{2,1,0:T(8,128)(2,1)} %get-tuple-element.54.refs_1_, bf16[512,2048]{1,0:T(8,128)(2,1)} %shard_map.327.refs_2_.refs_1_, bf16[512,2048]{1,0:T(8,128)(2,1)} %collective-permute-done.17.refs_4_.refs_3_.refs_2_, ...), custom_call_target="tpu_custom_call" | custom-call | flops 8589934 | bytes 16777 | tf_op jit(solution)/shard_map/pallas_call | solution.py:171
  478.0 13.2 %collective-permute-done.31.refs_2_ = bf16[512,2048]{1,0:T(8,128)(2,1)S(1)} collective-permute-done((bf16[512,2048]{1,0:T(8,128)(2,1)S(1)}, bf16[512,2048]{1,0:T(8,128)(2,1)S(1)}, u32[]{:S(2)}, u32[]{:S(2)}) %collective-permute-start.31) | collective-permute-done | bytes 2097184 | tf_op jit(solution)/shard_map/ppermute | solution.py:33
  492.6 8.0 shard_map.347
  506.0 14.4 %shard_map.348 = (bf16[512,2048]{1,0:T(8,128)(2,1)}, bf16[512,2048]{1,0:T(8,128)(2,1)S(1)}) custom-call(s32[1]{0:T(128)} %bitcast.5.refs_0_, bf16[4,512,2048]{2,1,0:T(8,128)(2,1)} %get-tuple-element.54.refs_1_, bf16[4,2,256,2048]{3,2,1,0:T(8,128)(2,1)} %all-gather.20.cloned.1.call-done.refs_5_.refs_6_.refs_2_.refs_3_, ...), custom_call_target="tpu_custom_call" | custom-call | flops 8589934 | bytes 16777 | tf_op jit(solution)/shard_map/pallas_call | solution.py:171
  521.8 13.2 %shard_map.349 = (bf16[512,2048]{1,0:T(8,128)(2,1)S(1)}, bf16[512,2048]{1,0:T(8,128)(2,1)S(1)}) custom-call(s32[1]{0:T(128)} %bitcast.5.refs_0_, bf16[4,512,2048]{2,1,0:T(8,128)(2,1)} %get-tuple-element.54.refs_1_, bf16[4,2,256,2048]{3,2,1,0:T(8,128)(2,1)} %all-gather.20.cloned.1.call-done.refs_5_.refs_6_.refs_2_.refs_3_, ...), custom_call_target="tpu_custom_call" | custom-call | flops 8589934 | bytes 16777 | tf_op jit(solution)/shard_map/pallas_call | solution.py:171
  537.7 7.4 shard_map.350.refs_6_
  546.5 7.5 shard_map.351.refs_2_.refs_5_
  555.3 14.4 %collective-permute-done.34.refs_1_ = bf16[1,4,4,64,1024]{4,3,2,1,0:T(8,128)(2,1)} collective-permute-done((bf16[1,4,4,64,1024]{4,3,2,1,0:T(8,128)(2,1)}, bf16[1,4,4,64,1024]{4,3,2,1,0:T(8,128)(2,1)}, u32[]{:S(2)}, u32[]{:S(2)}) %collective-permute-start.34) | collective-permute-done | bytes 2097184 | tf_op jit(solution)/shard_map/ppermute | solution.py:43
  575.8 5.3 shard_map.354.refs_2_
  596.3 18.8 %shard_map.357 = (bf16[1024,1536]{1,0:T(8,128)(2,1)}, f32[1,1536]{1,0:T(1,128)S(1)}) custom-call(bf16[2048,512]{1,0:T(8,128)(2,1)S(1)} %bitcast.145, bf16[2048,512]{1,0:T(8,128)(2,1)S(1)} %bitcast.150, bf16[2048,512]{1,0:T(8,128)(2,1)} %bitcast.152, bf16[1024,512]{1,0:T(8,128)(2,1)S(1)} %bitcast.165, bf16[512,2048]{1,0:T(8,128)(2,1)} %copy-done.48), custom_call_target="tpu_custom_call" | custom-call | flops 5368709 | bytes 7340 | tf_op jit(solution)/shard_map/pallas_call | solution.py:171
  615.1 12.1 %shard_map.358 = (bf16[512,2048]{1,0:T(8,128)(2,1)}, bf16[512,2048]{1,0:T(8,128)(2,1)}) custom-call(s32[1]{0:T(128)} %bitcast.5.refs_0_, bf16[2,512,1536]{2,1,0:T(8,128)(2,1)} %bitcast.176, bf16[1,4,4,64,512]{4,3,2,1,0:T(8,128)(2,1)S(1)} %bitcast.168, bf16[1,4,4,64,512]{4,3,2,1,0:T(8,128)(2,1)S(1)} %copy-done.28, bf16[1,4,4,64,512]{4,3,2,1,0:T(8,128)(2,1)S(1)} %bitcast.172, ...), custom_call_target="tpu_custom_call" | custom-call | flops 6442450 | bytes 9437 | tf_op jit(solution)/shard_map/pallas_call | solution.py:171
  627.2 6.8 collective-permute-done.39
  641.4 6.2 shard_map.360.refs_6_
  649.1 5.5 shard_map.361.refs_4_.refs_1_
  660.7 18.7 %shard_map.363 = (bf16[1024,1536]{1,0:T(8,128)(2,1)}, f32[1,1536]{1,0:T(1,128)S(1)}) custom-call(bf16[2048,512]{1,0:T(8,128)(2,1)S(1)} %bitcast.146, bf16[2048,512]{1,0:T(8,128)(2,1)} %bitcast.149, bf16[2048,512]{1,0:T(8,128)(2,1)} %bitcast.153, bf16[1024,512]{1,0:T(8,128)(2,1)S(1)} %bitcast.164, bf16[256,2048]{1,0:T(8,128)(2,1)S(1)} %copy-done.32, ...), custom_call_target="tpu_custom_call" | custom-call | flops 5368709 | bytes 7340 | tf_op jit(solution)/shard_map/pallas_call | solution.py:171
  682.1 12.2 %shard_map.365 = (bf16[512,2048]{1,0:T(8,128)(2,1)}, bf16[512,2048]{1,0:T(8,128)(2,1)}) custom-call(s32[1]{0:T(128)} %bitcast.5.refs_0_, bf16[2,512,1536]{2,1,0:T(8,128)(2,1)} %bitcast.181, bf16[1,4,4,64,512]{4,3,2,1,0:T(8,128)(2,1)S(1)} %bitcast.169, bf16[1,4,4,64,512]{4,3,2,1,0:T(8,128)(2,1)S(1)} %copy-done.28, bf16[1,4,4,64,512]{4,3,2,1,0:T(8,128)(2,1)S(1)} %bitcast.173, ...), custom_call_target="tpu_custom_call" | custom-call | flops 6442450 | bytes 9437 | tf_op jit(solution)/shard_map/pallas_call | solution.py:171
  708.8 8.7 %shard_map.368.refs_7_ = bf16[1,4,4,64,1024]{4,3,2,1,0:T(8,128)(2,1)} custom-call(s32[1]{0:T(128)} %bitcast.5.refs_0_, bf16[512,2048]{1,0:T(8,128)(2,1)} %shard_map.321.refs_1_, bf16[512,2048]{1,0:T(8,128)(2,1)} %copy-done, bf16[512,2048]{1,0:T(8,128)(2,1)} %collective-permute-done.13.refs_3_, bf16[512,2048]{1,0:T(8,128)(2,1)} %collective-permute-done.14.refs_4_, ...), custom_call_target="tpu_custom_call" | custom-call | flops 4294967 | bytes 10485 | tf_op jit(solution)/shard_map/pallas_call | solution.py:171
  723.4 8.1 collective-permute-done.42
  737.8 8.3 shard_map.371.refs_5_
  756.8 8.2 shard_map.373
  766.4 8.4 collective-permute-done.55
  807.3 6.8 bitcast_select_fusion
  (500 shorter events, 241.5 us)
Async XLA Ops:
  7.2 64.6 %all-gather.8.cloned.1.call-start = ((), (), s32[]{:S(2)}) async-start(), calls=%async_computation.7 | async-start | bytes 1310720 | tf_op jit(solution)/shard_map/all_gather | solution.py:690
  18.0 13.7 %collective-permute-start.8 = (bf16[64,3584]{1,0:T(8,128)(2,1)S(1)}, bf16[64,3584]{1,0:T(8,128)(2,1)}, u32[]{:S(2)}, u32[]{:S(2)}) collective-permute-start(bf16[64,3584]{1,0:T(8,128)(2,1)S(1)} %pad_maximum_fusion.5), channel_id=1, source_target_pairs={{0,12},{4,8},{8,4},{12,0},{1,13},{5,9},{9,5},{13,1},{2,14},{6,10},... | collective-permute-start | bytes 1376264 | tf_op jit(solution)/shard_map/ppermute | solution.py:33
  21.4 20.4 %collective-permute-start.9 = (bf16[64,3584]{1,0:T(8,128)(2,1)S(1)}, bf16[64,3584]{1,0:T(8,128)(2,1)}, u32[]{:S(2)}, u32[]{:S(2)}) collective-permute-start(bf16[64,3584]{1,0:T(8,128)(2,1)S(1)} %pad_maximum_fusion.6), channel_id=1, source_target_pairs={{0,8},{4,12},{8,0},{12,4},{1,9},{5,13},{9,1},{13,5},{2,10},{6,14},... | collective-permute-start | bytes 1376264 | tf_op jit(solution)/shard_map/ppermute | solution.py:33
  21.5 59.5 %all-gather.10.cloned.1.call-start = ((), (), s32[]{:S(2)}) async-start(), calls=%async_computation.8 | async-start | bytes 1310720 | tf_op jit(solution)/shard_map/all_gather | solution.py:690
  44.2 81.0 %all-gather.12.cloned.1.call-start = ((), (), s32[]{:S(2)}) async-start(), calls=%async_computation.9 | async-start | bytes 1310720 | tf_op jit(solution)/shard_map/all_gather | solution.py:690
  45.0 95.2 %all-gather.14.cloned.1.call-start = ((), (), s32[]{:S(2)}) async-start(), calls=%async_computation.10 | async-start | bytes 1310720 | tf_op jit(solution)/shard_map/all_gather | solution.py:690
  45.5 163.0 %all-gather.16.cloned.1.call-start = ((), (), s32[]{:S(2)}) async-start(), calls=%async_computation.11 | async-start | bytes 2621440 | tf_op jit(solution)/shard_map/all_gather | solution.py:690
  56.5 220.9 %all-gather.18.cloned.1.call-start = ((), (), s32[]{:S(2)}) async-start(), calls=%async_computation.12 | async-start | bytes 2621440 | tf_op jit(solution)/shard_map/all_gather | solution.py:690
  71.8 48.6 %collective-permute-start.7 = (bf16[512,2048]{1,0:T(8,128)(2,1)}, bf16[512,2048]{1,0:T(8,128)(2,1)S(1)}, u32[]{:S(2)}, u32[]{:S(2)}) collective-permute-start(bf16[512,2048]{1,0:T(8,128)(2,1)} %shard_map.321.refs_1_), channel_id=1, source_target_pairs={{0,8},{4,12},{8,0},{12,4},{1,9},{5,13},{9,1},{13,5},{2,10},{6,14},... | collective-permute-start | bytes 6291464 | tf_op jit(solution)/shard_map/ppermute | solution.py:33
  72.4 26.2 %collective-permute-start.12 = (bf16[1,256,2048]{2,1,0:T(8,128)(2,1)}, bf16[1,256,2048]{2,1,0:T(8,128)(2,1)S(1)}, u32[]{:S(2)}, u32[]{:S(2)}) collective-permute-start(bf16[1,256,2048]{2,1,0:T(8,128)(2,1)} %bitcast.6.refs_1_), channel_id=1, source_target_pairs={{0,16},{16,0},{1,17},{17,1},{2,18},{18,2},{3,19},{19,3},{4,20},{20... | collective-permute-start | bytes 3145736 | tf_op jit(solution)/shard_map/ppermute | solution.py:43
  81.0 39.4 %collective-permute-start.11 = (bf16[1,4,4,64,512]{4,3,2,1,0:T(8,128)(2,1)}, bf16[1,4,4,64,512]{4,3,2,1,0:T(8,128)(2,1)S(1)}, u32[]{:S(2)}, u32[]{:S(2)}) collective-permute-start(bf16[1,4,4,64,512]{4,3,2,1,0:T(8,128)(2,1)} %bitcast.166), channel_id=1, source_target_pairs={{0,16},{16,0},{1,17},{17,1},{2,18},{18,2},{3,19},{19,3},{4,20},{20... | collective-permute-start | bytes 3145736 | tf_op jit(solution)/shard_map/ppermute | solution.py:43
  88.5 38.9 %collective-permute-start.13 = (bf16[512,2048]{1,0:T(8,128)(2,1)}, bf16[512,2048]{1,0:T(8,128)(2,1)}, u32[]{:S(2)}, u32[]{:S(2)}) collective-permute-start(bf16[512,2048]{1,0:T(8,128)(2,1)} %shard_map.321.refs_1_), channel_id=1, source_target_pairs={{0,4},{4,0},{8,12},{12,8},{1,5},{5,1},{9,13},{13,9},{2,6},{6,2},{1... | collective-permute-start | bytes 6291464 | tf_op jit(solution)/shard_map/ppermute | solution.py:33
  121.4 262.9 %all-gather.20.cloned.1.call-start = ((), (), s32[]{:S(2)}) async-start(), calls=%async_computation.13 | async-start | bytes 10485760 | tf_op jit(solution)/shard_map/all_gather | solution.py:690
  125.2 26.4 %collective-permute-start.15 = (bf16[1,4,4,64,512]{4,3,2,1,0:T(8,128)(2,1)}, bf16[1,4,4,64,512]{4,3,2,1,0:T(8,128)(2,1)}, u32[]{:S(2)}, u32[]{:S(2)}) collective-permute-start(bf16[1,4,4,64,512]{4,3,2,1,0:T(8,128)(2,1)} %bitcast.170), channel_id=1, source_target_pairs={{0,16},{16,0},{1,17},{17,1},{2,18},{18,2},{3,19},{19,3},{4,20},{20... | collective-permute-start | bytes 3145736 | tf_op jit(solution)/shard_map/ppermute | solution.py:43
  125.8 58.4 %collective-permute-start.17 = (bf16[512,2048]{1,0:T(8,128)(2,1)}, bf16[512,2048]{1,0:T(8,128)(2,1)}, u32[]{:S(2)}, u32[]{:S(2)}) collective-permute-start(bf16[512,2048]{1,0:T(8,128)(2,1)} %shard_map.327.refs_2_.refs_1_), channel_id=1, source_target_pairs={{0,8},{4,12},{8,0},{12,4},{1,9},{5,13},{9,1},{13,5},{2,10},{6,14},... | collective-permute-start | bytes 6291464 | tf_op jit(solution)/shard_map/ppermute | solution.py:33
  140.1 34.0 %collective-permute-start.16 = (bf16[1,4,4,64,512]{4,3,2,1,0:T(8,128)(2,1)}, bf16[1,4,4,64,512]{4,3,2,1,0:T(8,128)(2,1)}, u32[]{:S(2)}, u32[]{:S(2)}) collective-permute-start(bf16[1,4,4,64,512]{4,3,2,1,0:T(8,128)(2,1)} %shard_map.325.refs_5_.refs_6_), channel_id=1, source_target_pairs={{0,16},{16,0},{1,17},{17,1},{2,18},{18,2},{3,19},{19,3},{4,20},{20... | collective-permute-start | bytes 3145736 | tf_op jit(solution)/shard_map/ppermute | solution.py:43
  161.6 36.7 %collective-permute-start.26 = (bf16[256,2048]{1,0:T(8,128)(2,1)S(1)}, bf16[256,2048]{1,0:T(8,128)(2,1)S(1)}, u32[]{:S(2)}, u32[]{:S(2)}) collective-permute-start(bf16[256,2048]{1,0:T(8,128)(2,1)S(1)} %shard_map.337), channel_id=1, source_target_pairs={{0,16},{16,0},{1,17},{17,1},{2,18},{18,2},{3,19},{19,3},{4,20},{20... | collective-permute-start | bytes 3145736 | tf_op jit(solution)/shard_map/ppermute | solution.py:43
  200.3 304.7 %reduce-scatter.8.cloned.1.call-start = ((), (), s32[]{:S(2)}) async-start(), calls=%async_computation.14 | async-start | bytes 4718592 | tf_op jit(solution)/shard_map/reduce_scatter | solution.py:846
  208.5 48.4 %collective-permute-start.21 = (bf16[1,4,4,64,1024]{4,3,2,1,0:T(8,128)(2,1)}, bf16[1,4,4,64,1024]{4,3,2,1,0:T(8,128)(2,1)}, u32[]{:S(2)}, u32[]{:S(2)}) collective-permute-start(bf16[1,4,4,64,1024]{4,3,2,1,0:T(8,128)(2,1)} %shard_map.332.refs_5_.refs_2_), channel_id=1, source_target_pairs={{0,16},{16,0},{1,17},{17,1},{2,18},{18,2},{3,19},{19,3},{4,20},{20... | collective-permute-start | bytes 6291464 | tf_op jit(solution)/shard_map/ppermute | solution.py:43
  209.1 47.8 %collective-permute-start.18 = (bf16[512,2048]{1,0:T(8,128)(2,1)}, bf16[512,2048]{1,0:T(8,128)(2,1)}, u32[]{:S(2)}, u32[]{:S(2)}) collective-permute-start(bf16[512,2048]{1,0:T(8,128)(2,1)} %get-tuple-element.50), channel_id=1, source_target_pairs={{0,4},{4,0},{8,12},{12,8},{1,5},{5,1},{9,13},{13,9},{2,6},{6,2},{1... | collective-permute-start | bytes 6291464 | tf_op jit(solution)/shard_map/ppermute | solution.py:33
  221.6 48.1 %collective-permute-start.20 = (bf16[512,2048]{1,0:T(8,128)(2,1)S(1)}, bf16[512,2048]{1,0:T(8,128)(2,1)}, u32[]{:S(2)}, u32[]{:S(2)}) collective-permute-start(bf16[512,2048]{1,0:T(8,128)(2,1)S(1)} %shard_map.331.refs_7_), channel_id=1, source_target_pairs={{0,8},{4,12},{8,0},{12,4},{1,9},{5,13},{9,1},{13,5},{2,10},{6,14},... | collective-permute-start | bytes 6291464 | tf_op jit(solution)/shard_map/ppermute | solution.py:33
  279.0 47.1 %collective-permute-start.23 = (bf16[1,4,4,64,1024]{4,3,2,1,0:T(8,128)(2,1)S(1)}, bf16[1,4,4,64,1024]{4,3,2,1,0:T(8,128)(2,1)S(1)}, u32[]{:S(2)}, u32[]{:S(2)}) collective-permute-start(bf16[1,4,4,64,1024]{4,3,2,1,0:T(8,128)(2,1)S(1)} %shard_map.334.refs_7_.refs_4_), channel_id=1, source_target_pairs={{0,16},{16,0},{1,17},{17,1},{2,18},{18,2},{3,19},{19,3},{4,20},{20... | collective-permute-start | bytes 6291464 | tf_op jit(solution)/shard_map/ppermute | solution.py:43
  280.5 47.0 %collective-permute-start.22 = (bf16[512,2048]{1,0:T(8,128)(2,1)S(1)}, bf16[512,2048]{1,0:T(8,128)(2,1)}, u32[]{:S(2)}, u32[]{:S(2)}) collective-permute-start(bf16[512,2048]{1,0:T(8,128)(2,1)S(1)} %get-tuple-element.53.refs_1_.refs_10_), channel_id=1, source_target_pairs={{0,8},{4,12},{8,0},{12,4},{1,9},{5,13},{9,1},{13,5},{2,10},{6,14},... | collective-permute-start | bytes 6291464 | tf_op jit(solution)/shard_map/ppermute | solution.py:33
  282.0 46.1 %collective-permute-start.24 = (bf16[512,2048]{1,0:T(8,128)(2,1)S(1)}, bf16[512,2048]{1,0:T(8,128)(2,1)}, u32[]{:S(2)}, u32[]{:S(2)}) collective-permute-start(bf16[512,2048]{1,0:T(8,128)(2,1)S(1)} %get-tuple-element.53.refs_1_.refs_10_), channel_id=1, source_target_pairs={{0,4},{4,0},{8,12},{12,8},{1,5},{5,1},{9,13},{13,9},{2,6},{6,2},{1... | collective-permute-start | bytes 6291464 | tf_op jit(solution)/shard_map/ppermute | solution.py:33
  327.5 34.6 %collective-permute-start.27 = (bf16[512,2048]{1,0:T(8,128)(2,1)}, bf16[512,2048]{1,0:T(8,128)(2,1)}, u32[]{:S(2)}, u32[]{:S(2)}) collective-permute-start(bf16[512,2048]{1,0:T(8,128)(2,1)} %shard_map.327.refs_2_.refs_1_), channel_id=1, source_target_pairs={{0,4},{4,0},{8,12},{12,8},{1,5},{5,1},{9,13},{13,9},{2,6},{6,2},{1... | collective-permute-start | bytes 6291464 | tf_op jit(solution)/shard_map/ppermute | solution.py:33
  328.0 34.1 %collective-permute-start.28 = (bf16[512,2048]{1,0:T(8,128)(2,1)}, bf16[512,2048]{1,0:T(8,128)(2,1)}, u32[]{:S(2)}, u32[]{:S(2)}) collective-permute-start(bf16[512,2048]{1,0:T(8,128)(2,1)} %collective-permute-done.17.refs_4_.refs_3_.refs_2_), channel_id=1, source_target_pairs={{0,4},{4,0},{8,12},{12,8},{1,5},{5,1},{9,13},{13,9},{2,6},{6,2},{1... | collective-permute-start | bytes 6291464 | tf_op jit(solution)/shard_map/ppermute | solution.py:33
  377.0 278.6 %reduce-scatter.10.cloned.1.call-start = ((), (), s32[]{:S(2)}) async-start(), calls=%async_computation.15 | async-start | bytes 4718592 | tf_op jit(solution)/shard_map/reduce_scatter | solution.py:846
  424.5 15.9 %collective-permute-start.30 = (bf16[512,2048]{1,0:T(8,128)(2,1)S(1)}, bf16[512,2048]{1,0:T(8,128)(2,1)S(1)}, u32[]{:S(2)}, u32[]{:S(2)}) collective-permute-start(bf16[512,2048]{1,0:T(8,128)(2,1)S(1)} %get-tuple-element.58.refs_6_), channel_id=1, source_target_pairs={{0,4},{4,0},{8,12},{12,8},{1,5},{5,1},{9,13},{13,9},{2,6},{6,2},{1... | collective-permute-start | bytes 6291464 | tf_op jit(solution)/shard_map/ppermute | solution.py:33
  424.6 53.4 %collective-permute-start.29 = (bf16[512,2048]{1,0:T(8,128)(2,1)S(1)}, bf16[512,2048]{1,0:T(8,128)(2,1)}, u32[]{:S(2)}, u32[]{:S(2)}) collective-permute-start(bf16[512,2048]{1,0:T(8,128)(2,1)S(1)} %get-tuple-element.60), channel_id=1, source_target_pairs={{0,4},{4,0},{8,12},{12,8},{1,5},{5,1},{9,13},{13,9},{2,6},{6,2},{1... | collective-permute-start | bytes 6291464 | tf_op jit(solution)/shard_map/ppermute | solution.py:33
  443.6 47.6 %collective-permute-start.31 = (bf16[512,2048]{1,0:T(8,128)(2,1)S(1)}, bf16[512,2048]{1,0:T(8,128)(2,1)S(1)}, u32[]{:S(2)}, u32[]{:S(2)}) collective-permute-start(bf16[512,2048]{1,0:T(8,128)(2,1)S(1)} %shard_map.343.refs_6_), channel_id=1, source_target_pairs={{0,8},{4,12},{8,0},{12,4},{1,9},{5,13},{9,1},{13,5},{2,10},{6,14},... | collective-permute-start | bytes 6291464 | tf_op jit(solution)/shard_map/ppermute | solution.py:33
  502.0 192.3 %reduce-scatter.12.cloned.1.call-start = ((), (), s32[]{:S(2)}) async-start(), calls=%async_computation.16 | async-start | bytes 2621440 | tf_op jit(solution)/shard_map/reduce_scatter | solution.py:827
  502.1 67.6 %collective-permute-start.34 = (bf16[1,4,4,64,1024]{4,3,2,1,0:T(8,128)(2,1)}, bf16[1,4,4,64,1024]{4,3,2,1,0:T(8,128)(2,1)}, u32[]{:S(2)}, u32[]{:S(2)}) collective-permute-start(bf16[1,4,4,64,1024]{4,3,2,1,0:T(8,128)(2,1)} %copy-done.42), channel_id=1, source_target_pairs={{0,16},{16,0},{1,17},{17,1},{2,18},{18,2},{3,19},{19,3},{4,20},{20... | collective-permute-start | bytes 6291464 | tf_op jit(solution)/shard_map/ppermute | solution.py:43
  503.6 66.1 %collective-permute-start.36 = (bf16[512,2048]{1,0:T(8,128)(2,1)}, bf16[512,2048]{1,0:T(8,128)(2,1)}, u32[]{:S(2)}, u32[]{:S(2)}) collective-permute-start(bf16[512,2048]{1,0:T(8,128)(2,1)} %copy-done.13), channel_id=1, source_target_pairs={{0,8},{4,12},{8,0},{12,4},{1,9},{5,13},{9,1},{13,5},{2,10},{6,14},... | collective-permute-start | bytes 6291464 | tf_op jit(solution)/shard_map/ppermute | solution.py:33
  505.0 69.4 %collective-permute-start.35 = (bf16[512,2048]{1,0:T(8,128)(2,1)}, bf16[512,2048]{1,0:T(8,128)(2,1)}, u32[]{:S(2)}, u32[]{:S(2)}) collective-permute-start(bf16[512,2048]{1,0:T(8,128)(2,1)} %copy-done.13), channel_id=1, source_target_pairs={{0,4},{4,0},{8,12},{12,8},{1,5},{5,1},{9,13},{13,9},{2,6},{6,2},{1... | collective-permute-start | bytes 6291464 | tf_op jit(solution)/shard_map/ppermute | solution.py:33
  585.4 122.4 %reduce-scatter.14.cloned.1.call-start = ((), (), s32[]{:S(2)}) async-start(), calls=%async_computation.17 | async-start | bytes 2621440 | tf_op jit(solution)/shard_map/reduce_scatter | solution.py:827
  586.0 48.0 %collective-permute-start.39 = (bf16[1,4,4,64,1024]{4,3,2,1,0:T(8,128)(2,1)}, bf16[1,4,4,64,1024]{4,3,2,1,0:T(8,128)(2,1)S(1)}, u32[]{:S(2)}, u32[]{:S(2)}) collective-permute-start(bf16[1,4,4,64,1024]{4,3,2,1,0:T(8,128)(2,1)} %copy-done.41), channel_id=1, source_target_pairs={{0,16},{16,0},{1,17},{17,1},{2,18},{18,2},{3,19},{19,3},{4,20},{20... | collective-permute-start | bytes 6291464 | tf_op jit(solution)/shard_map/ppermute | solution.py:43
  638.0 98.9 %reduce-scatter.16.cloned.1.call-start = ((), (), s32[]{:S(2)}) async-start(), calls=%async_computation.18 | async-start | bytes 1310720 | tf_op jit(solution)/shard_map/reduce_scatter | solution.py:827
  638.0 56.3 %collective-permute-start.41 = (bf16[512,2048]{1,0:T(8,128)(2,1)}, bf16[512,2048]{1,0:T(8,128)(2,1)}, u32[]{:S(2)}, u32[]{:S(2)}) collective-permute-start(bf16[512,2048]{1,0:T(8,128)(2,1)} %get-tuple-element.70.refs_2_), channel_id=1, source_target_pairs={{0,4},{4,0},{8,12},{12,8},{1,5},{5,1},{9,13},{13,9},{2,6},{6,2},{1... | collective-permute-start | bytes 6291464 | tf_op jit(solution)/shard_map/ppermute | solution.py:33
  638.1 56.2 %collective-permute-start.38 = (bf16[512,2048]{1,0:T(8,128)(2,1)}, bf16[512,2048]{1,0:T(8,128)(2,1)}, u32[]{:S(2)}, u32[]{:S(2)}) collective-permute-start(bf16[512,2048]{1,0:T(8,128)(2,1)} %copy-done.48), channel_id=1, source_target_pairs={{0,8},{4,12},{8,0},{12,4},{1,9},{5,13},{9,1},{13,5},{2,10},{6,14},... | collective-permute-start | bytes 6291464 | tf_op jit(solution)/shard_map/ppermute | solution.py:33
  647.6 31.8 %collective-permute-start.40 = (bf16[256,2048]{1,0:T(8,128)(2,1)}, bf16[256,2048]{1,0:T(8,128)(2,1)}, u32[]{:S(2)}, u32[]{:S(2)}) collective-permute-start(bf16[256,2048]{1,0:T(8,128)(2,1)} %shard_map.360.refs_6_), channel_id=1, source_target_pairs={{0,16},{16,0},{1,17},{17,1},{2,18},{18,2},{3,19},{19,3},{4,20},{20... | collective-permute-start | bytes 3145736 | tf_op jit(solution)/shard_map/ppermute | solution.py:43
  682.0 132.9 %reduce-scatter.18.cloned.1.call-start = ((), (), s32[]{:S(2)}) async-start(), calls=%async_computation.19 | async-start | bytes 1310720 | tf_op jit(solution)/shard_map/reduce_scatter | solution.py:827
  705.2 26.3 %collective-permute-start.42 = (bf16[1,4,4,64,512]{4,3,2,1,0:T(8,128)(2,1)S(1)}, bf16[1,4,4,64,512]{4,3,2,1,0:T(8,128)(2,1)}, u32[]{:S(2)}, u32[]{:S(2)}) collective-permute-start(bf16[1,4,4,64,512]{4,3,2,1,0:T(8,128)(2,1)S(1)} %shard_map.367.refs_7_), channel_id=1, source_target_pairs={{0,16},{16,0},{1,17},{17,1},{2,18},{18,2},{3,19},{19,3},{4,20},{20... | collective-permute-start | bytes 3145736 | tf_op jit(solution)/shard_map/ppermute | solution.py:43
  705.9 41.5 %collective-permute-start.32 = (bf16[512,2048]{1,0:T(8,128)(2,1)}, bf16[512,2048]{1,0:T(8,128)(2,1)}, u32[]{:S(2)}, u32[]{:S(2)}) collective-permute-start(bf16[512,2048]{1,0:T(8,128)(2,1)} %get-tuple-element.65), channel_id=1, source_target_pairs={{0,4},{4,0},{8,12},{12,8},{1,5},{5,1},{9,13},{13,9},{2,6},{6,2},{1... | collective-permute-start | bytes 6291464 | tf_op jit(solution)/shard_map/ppermute | solution.py:33
  705.9 50.9 %collective-permute-start.43 = (bf16[512,2048]{1,0:T(8,128)(2,1)}, bf16[512,2048]{1,0:T(8,128)(2,1)}, u32[]{:S(2)}, u32[]{:S(2)}) collective-permute-start(bf16[512,2048]{1,0:T(8,128)(2,1)} %get-tuple-element.75), channel_id=1, source_target_pairs={{0,4},{4,0},{8,12},{12,8},{1,5},{5,1},{9,13},{13,9},{2,6},{6,2},{1... | collective-permute-start | bytes 6291464 | tf_op jit(solution)/shard_map/ppermute | solution.py:33
  706.4 50.4 %collective-permute-start.44 = (bf16[512,2048]{1,0:T(8,128)(2,1)}, bf16[512,2048]{1,0:T(8,128)(2,1)}, u32[]{:S(2)}, u32[]{:S(2)}) collective-permute-start(bf16[512,2048]{1,0:T(8,128)(2,1)} %copy-done.44), channel_id=1, source_target_pairs={{0,8},{4,12},{8,0},{12,4},{1,9},{5,13},{9,1},{13,5},{2,10},{6,14},... | collective-permute-start | bytes 6291464 | tf_op jit(solution)/shard_map/ppermute | solution.py:33
  717.5 57.3 %collective-permute-start.55 = (bf16[1,4,4,64,1024]{4,3,2,1,0:T(8,128)(2,1)}, bf16[1,4,4,64,1024]{4,3,2,1,0:T(8,128)(2,1)}, u32[]{:S(2)}, u32[]{:S(2)}) collective-permute-start(bf16[1,4,4,64,1024]{4,3,2,1,0:T(8,128)(2,1)} %shard_map.368.refs_7_), channel_id=1, source_target_pairs={{0,16},{16,0},{1,17},{17,1},{2,18},{18,2},{3,19},{19,3},{4,20},{20... | collective-permute-start | bytes 6291464 | tf_op jit(solution)/shard_map/ppermute | solution.py:43
  735.0 87.7 %reduce-scatter.20.cloned.1.call-start = ((), (), s32[]{:S(2)}) async-start(), calls=%async_computation.20 | async-start | bytes 2621440 | tf_op jit(solution)/shard_map/reduce_scatter | solution.py:827
  781.3 14.0 %collective-permute-start.60 = (bf16[64,2048]{1,0:T(8,128)(2,1)}, bf16[64,2048]{1,0:T(8,128)(2,1)S(1)}, u32[]{:S(2)}, u32[]{:S(2)}) collective-permute-start(bf16[64,2048]{1,0:T(8,128)(2,1)} %get-tuple-element.105), channel_id=1, source_target_pairs={{0,8},{4,12},{8,0},{12,4},{1,9},{5,13},{9,1},{13,5},{2,10},{6,14},... | collective-permute-start | bytes 786440 | tf_op jit(solution)/shard_map/ppermute | solution.py:33
  (126 other events, 692.2 us)
Sparse Core Ops, SparseCore 0:
  21.6 29.7 all-gather.7
  53.6 27.3 all-gather.9
  83.1 27.4 all-gather.11
  112.7 27.4 all-gather.13
  142.1 45.4 all-gather.15
  189.6 44.6 all-gather.17
  235.8 148.3 all-gather.19
  388.4 86.1 reduce-scatter.7
  502.1 99.4 reduce-scatter.9
  603.7 42.5 reduce-scatter.11
  648.7 43.1 reduce-scatter.13
  694.1 26.4 reduce-scatter.15
  735.2 25.4 reduce-scatter.17
  779.3 42.4 reduce-scatter.19

commit v6 on v4

--- a/solution.py
+++ b/solution.py
@@ -789,10 +789,10 @@
     a_own = pin(a_own, block_o)
     a_across = team_swap(a_own, 2)
     w_o = flatten(both_halves(block_o))
-    a_across = pin(a_across, w_q[1], w_o[1])
+    g_rows = pack(cotangent)
+    a_across = pin(a_across, w_q[1], w_o[1], g_rows)
     a_all = [a_own, a_across, team_swap(a_own, 1), team_swap(a_across, 1)]
     block_up = [stored(depth_gather(columns(up_deal, i, 2))) for i in range(2)]
-    g_rows = pack(cotangent)
     g_all = team_gather(pin(g_rows, a_all[1]))
 
     wide = TEAM * rows

time: 851 us -> 842 us (0.989)
    unnamed x213 -> x201, local copies, waits for them, and re-layouts: 61.5 us -> 58.1 us
  transfers between devices with their start and end apart: 76 -> 76, of which waited for: 29 -> 31; matrix products, arithmetic and copies ran while one was open for 6% -> 7% of each run, Pallas kernels for 46% -> 47%
where the time goes in v6:
time: 842 us; the launch traced here: 835 us
  Pallas kernels  394 us (47%)
  waiting for transfers between devices  253 us (30%)
  local copies, waits for them, and re-layouts  82.3 us (10%)
  starting transfers between devices  53.5 us (6%)
  matrix products  22 us (3%)
  between operations  15.7 us (2%)
  other arithmetic  14.5 us (2%)
    pallas_call x44, Pallas kernels, kernel_call(): pl.pallas_call(run, grid_spec=pltpu.PrefetchScalarGridSpec(num_scalar_pre...  394 us
    ppermute x12, waiting for transfers between devices, outer_pass(): lax.ppermute(a, 'outer', [(o, order[(p + 1) % outer]) for p, o in enumera...  164 us
    ppermute x42, waiting for transfers between devices, team_swap(): return lax.ppermute(a, 'team', [(i, i ^ flip) for i in range(TEAM)])  81.7 us
    unnamed x201, local copies, waits for them, and re-layouts  58.1 us
    ppermute x42, starting transfers between devices, team_swap(): return lax.ppermute(a, 'team', [(i, i ^ flip) for i in range(TEAM)])  27.1 us
  transfers between devices with their start and end apart: 76, of which 31 were waited for; matrix products, arithmetic and copies ran while one was open for 7% of the time, Pallas kernels for 47%

profile of v6, /device:TPU:0, one launch (start us, length us, event | category | flops | bytes accessed | tf_op | source)
XLA Modules:
  0.0 834.6 jit_solution(69672201166778887)
XLA Ops:
  19.1 8.1 collective-permute-done.8
  27.2 10.1 %collective-permute-done.9 = bf16[64,3584]{1,0:T(8,128)(2,1)} collective-permute-done((bf16[64,3584]{1,0:T(8,128)(2,1)S(1)}, bf16[64,3584]{1,0:T(8,128)(2,1)}, u32[]{:S(2)}, u32[]{:S(2)}) %collective-permute-start.9) | collective-permute-done | bytes 458784 | tf_op jit(solution)/shard_map/ppermute | solution.py:33
  71.6 5.9 fusion.7.refs_3_.refs_4_
  77.5 18.3 %collective-permute-done.12 = bf16[1,256,2048]{2,1,0:T(8,128)(2,1)S(1)} collective-permute-done((bf16[1,256,2048]{2,1,0:T(8,128)(2,1)}, bf16[1,256,2048]{2,1,0:T(8,128)(2,1)S(1)}, u32[]{:S(2)}, u32[]{:S(2)}) %collective-permute-start.12) | collective-permute-done | bytes 1048608 | tf_op jit(solution)/shard_map/ppermute | solution.py:43
  95.8 21.0 %collective-permute-done.11.refs_1_.refs_6_.refs_3_ = bf16[1,4,4,64,512]{4,3,2,1,0:T(8,128)(2,1)S(1)} collective-permute-done((bf16[1,4,4,64,512]{4,3,2,1,0:T(8,128)(2,1)}, bf16[1,4,4,64,512]{4,3,2,1,0:T(8,128)(2,1)S(1)}, u32[]{:S(2)}, u32[]{:S(2)}) %collective-permute-start.11) | collective-permute-done | bytes 1048608 | tf_op jit(solution)/shard_map/ppermute | solution.py:43
  126.4 8.4 %shard_map.323.refs_8_.refs_1_ = bf16[4,512,512]{2,1,0:T(8,128)(2,1)S(1)} custom-call(s32[1]{0:T(128)} %bitcast.5.refs_0_, bf16[512,2048]{1,0:T(8,128)(2,1)} %shard_map.321.refs_1_, bf16[512,2048]{1,0:T(8,128)(2,1)} %copy-done, bf16[512,2048]{1,0:T(8,128)(2,1)} %collective-permute-done.13.refs_3_, bf16[512,2048]{1,0:T(8,128)(2,1)} %collective-permute-done.14.refs_4_, ...), custom_call_target="tpu_custom_call" | custom-call | flops 4294967 | bytes 12582 | tf_op jit(solution)/shard_map/pallas_call | solution.py:171
  137.8 10.4 %collective-permute-done.15.refs_6_.refs_5_ = bf16[1,4,4,64,512]{4,3,2,1,0:T(8,128)(2,1)} collective-permute-done((bf16[1,4,4,64,512]{4,3,2,1,0:T(8,128)(2,1)}, bf16[1,4,4,64,512]{4,3,2,1,0:T(8,128)(2,1)}, u32[]{:S(2)}, u32[]{:S(2)}) %collective-permute-start.15) | collective-permute-done | bytes 1048608 | tf_op jit(solution)/shard_map/ppermute | solution.py:43
  148.2 8.6 %shard_map.324.refs_8_ = bf16[4,512,512]{2,1,0:T(8,128)(2,1)S(1)} custom-call(s32[1]{0:T(128)} %bitcast.5.refs_0_, bf16[512,2048]{1,0:T(8,128)(2,1)} %shard_map.321.refs_1_, bf16[512,2048]{1,0:T(8,128)(2,1)} %copy-done, bf16[512,2048]{1,0:T(8,128)(2,1)} %collective-permute-done.13.refs_3_, bf16[512,2048]{1,0:T(8,128)(2,1)} %collective-permute-done.14.refs_4_, ...), custom_call_target="tpu_custom_call" | custom-call | flops 4294967 | bytes 12582 | tf_op jit(solution)/shard_map/pallas_call | solution.py:171
  158.8 11.9 %collective-permute-done.16.refs_6_.refs_7_ = bf16[1,4,4,64,512]{4,3,2,1,0:T(8,128)(2,1)} collective-permute-done((bf16[1,4,4,64,512]{4,3,2,1,0:T(8,128)(2,1)}, bf16[1,4,4,64,512]{4,3,2,1,0:T(8,128)(2,1)}, u32[]{:S(2)}, u32[]{:S(2)}) %collective-permute-start.16) | collective-permute-done | bytes 1048608 | tf_op jit(solution)/shard_map/ppermute | solution.py:43
  170.7 8.7 %shard_map.326.refs_3_ = bf16[4,512,512]{2,1,0:T(8,128)(2,1)S(1)} custom-call(s32[1]{0:T(128)} %bitcast.5.refs_0_, bf16[512,2048]{1,0:T(8,128)(2,1)} %shard_map.321.refs_1_, bf16[512,2048]{1,0:T(8,128)(2,1)} %copy-done, bf16[512,2048]{1,0:T(8,128)(2,1)} %collective-permute-done.13.refs_3_, bf16[512,2048]{1,0:T(8,128)(2,1)} %collective-permute-done.14.refs_4_, ...), custom_call_target="tpu_custom_call" | custom-call | flops 4294967 | bytes 12582 | tf_op jit(solution)/shard_map/pallas_call | solution.py:171
  180.7 14.0 %shard_map.328.refs_4_ = bf16[2048,512]{1,0:T(8,128)(2,1)S(1)} custom-call(bf16[2048,512]{1,0:T(8,128)(2,1)S(1)} %bitcast.144, bf16[2048,512]{1,0:T(8,128)(2,1)} %bitcast.148, bf16[2048,512]{1,0:T(8,128)(2,1)} %bitcast.151, bf16[4,512,512]{2,1,0:T(8,128)(2,1)} %copy-done.12, bf16[512,2048]{1,0:T(8,128)(2,1)} %collective-permute-done.17.refs_4_.refs_3_.refs_2_), custom_call_target="tpu_custom_call" | custom-call | flops 4294967 | bytes 8388 | tf_op jit(solution)/shard_map/pallas_call | solution.py:171
  197.2 7.9 shard_map.329
  206.0 7.6 shard_map.330
  220.1 33.5 %collective-permute-done.21.refs_8_.refs_6_.refs_3_ = bf16[1,4,4,64,1024]{4,3,2,1,0:T(8,128)(2,1)} collective-permute-done((bf16[1,4,4,64,1024]{4,3,2,1,0:T(8,128)(2,1)}, bf16[1,4,4,64,1024]{4,3,2,1,0:T(8,128)(2,1)}, u32[]{:S(2)}, u32[]{:S(2)}) %collective-permute-start.21) | collective-permute-done | bytes 2097184 | tf_op jit(solution)/shard_map/ppermute | solution.py:43
  253.6 12.8 %collective-permute-done.20.refs_3_ = bf16[512,2048]{1,0:T(8,128)(2,1)} collective-permute-done((bf16[512,2048]{1,0:T(8,128)(2,1)S(1)}, bf16[512,2048]{1,0:T(8,128)(2,1)}, u32[]{:S(2)}, u32[]{:S(2)}) %collective-permute-start.20) | collective-permute-done | bytes 2097184 | tf_op jit(solution)/shard_map/ppermute | solution.py:33
  268.0 6.1 shard_map.333
  278.7 44.1 %collective-permute-done.23.refs_1_.refs_8_.refs_5_ = bf16[1,4,4,64,1024]{4,3,2,1,0:T(8,128)(2,1)S(1)} collective-permute-done((bf16[1,4,4,64,1024]{4,3,2,1,0:T(8,128)(2,1)S(1)}, bf16[1,4,4,64,1024]{4,3,2,1,0:T(8,128)(2,1)S(1)}, u32[]{:S(2)}, u32[]{:S(2)}) %collective-permute-start.23) | collective-permute-done | bytes 2097184 | tf_op jit(solution)/shard_map/ppermute | solution.py:43
  328.7 30.1 %shard_map.336 = (bf16[4,512,2048]{2,1,0:T(8,128)(2,1)}, bf16[4,512,2048]{2,1,0:T(8,128)(2,1)}) custom-call(s32[1]{0:T(128)} %bitcast.5.refs_0_, bf16[512,2048]{1,0:T(8,128)(2,1)S(1)} %get-tuple-element.53.refs_1_.refs_10_, bf16[512,2048]{1,0:T(8,128)(2,1)} %shard_map.335.refs_2_, bf16[512,2048]{1,0:T(8,128)(2,1)} %collective-permute-done.24.refs_3_, ...), custom_call_target="tpu_custom_call" | custom-call | flops 17179868 | bytes 25165 | tf_op jit(solution)/shard_map/pallas_call | solution.py:171
  358.9 14.9 %shard_map.339.refs_6_ = bf16[2048,1024]{1,0:T(8,128)(2,1)} custom-call(s32[1]{0:T(128)} %bitcast.5.refs_0_, bf16[4,512,2048]{2,1,0:T(8,128)(2,1)} %get-tuple-element.54.refs_1_, bf16[512,2048]{1,0:T(8,128)(2,1)} %shard_map.327.refs_2_.refs_1_, bf16[512,2048]{1,0:T(8,128)(2,1)} %collective-permute-done.17.refs_4_.refs_3_.refs_2_, ...), custom_call_target="tpu_custom_call" | custom-call | flops 8589934 | bytes 16777 | tf_op jit(solution)/shard_map/pallas_call | solution.py:171
  373.9 15.0 %shard_map.340.refs_8_ = bf16[2048,1024]{1,0:T(8,128)(2,1)} custom-call(s32[1]{0:T(128)} %bitcast.5.refs_0_, bf16[4,512,2048]{2,1,0:T(8,128)(2,1)} %get-tuple-element.54.refs_1_, bf16[512,2048]{1,0:T(8,128)(2,1)} %shard_map.327.refs_2_.refs_1_, bf16[512,2048]{1,0:T(8,128)(2,1)} %collective-permute-done.17.refs_4_.refs_3_.refs_2_, ...), custom_call_target="tpu_custom_call" | custom-call | flops 8589934 | bytes 16777 | tf_op jit(solution)/shard_map/pallas_call | solution.py:171
  388.9 25.7 %shard_map.341 = (bf16[4,512,2048]{2,1,0:T(8,128)(2,1)}, f32[1,2048]{1,0:T(1,128)S(1)}) custom-call(s32[1]{0:T(128)} %bitcast.5.refs_0_, bf16[512,2048]{1,0:T(8,128)(2,1)} %shard_map.327.refs_2_.refs_1_, bf16[512,2048]{1,0:T(8,128)(2,1)} %collective-permute-done.17.refs_4_.refs_3_.refs_2_, bf16[512,2048]{1,0:T(8,128)(2,1)} %collective-permute-done.27.refs_4_.refs_3_, ...), custom_call_target="tpu_custom_call" | custom-call | flops 17179868 | bytes 25165 | tf_op jit(solution)/shard_map/pallas_call | solution.py:171
  414.7 15.0 %shard_map.342 = (bf16[512,2048]{1,0:T(8,128)(2,1)S(1)}, bf16[512,2048]{1,0:T(8,128)(2,1)}) custom-call(s32[1]{0:T(128)} %bitcast.5.refs_0_, bf16[4,512,2048]{2,1,0:T(8,128)(2,1)} %get-tuple-element.56.refs_1_.refs_5_, bf16[1,4,4,64,1024]{4,3,2,1,0:T(8,128)(2,1)} %shard_map.332.refs_5_.refs_2_, ...), custom_call_target="tpu_custom_call" | custom-call | flops 8589934 | bytes 12582 | tf_op jit(solution)/shard_map/pallas_call | solution.py:171
  431.8 14.4 %shard_map.343 = (bf16[512,2048]{1,0:T(8,128)(2,1)S(1)}, bf16[512,2048]{1,0:T(8,128)(2,1)S(1)}) custom-call(s32[1]{0:T(128)} %bitcast.5.refs_0_, bf16[4,512,2048]{2,1,0:T(8,128)(2,1)} %get-tuple-element.56.refs_1_.refs_5_, bf16[1,4,4,64,1024]{4,3,2,1,0:T(8,128)(2,1)} %shard_map.332.refs_5_.refs_2_, ...), custom_call_target="tpu_custom_call" | custom-call | flops 8589934 | bytes 12582 | tf_op jit(solution)/shard_map/pallas_call | solution.py:171
  449.6 8.3 shard_map.345.refs_6_
  459.4 7.5 shard_map.346.refs_6_
  468.2 7.4 shard_map.347.refs_6_
  477.0 7.4 shard_map.348.refs_6_
  485.8 10.2 %collective-permute-done.31.refs_2_ = bf16[512,2048]{1,0:T(8,128)(2,1)S(1)} collective-permute-done((bf16[512,2048]{1,0:T(8,128)(2,1)S(1)}, bf16[512,2048]{1,0:T(8,128)(2,1)S(1)}, u32[]{:S(2)}, u32[]{:S(2)}) %collective-permute-start.31) | collective-permute-done | bytes 2097184 | tf_op jit(solution)/shard_map/ppermute | solution.py:33
  497.3 8.5 %shard_map.349 = (f32[512,2048]{1,0:T(8,128)}, bf16[512,2048]{1,0:T(8,128)(2,1)}, f32[4,2048]{1,0:T(4,128)S(1)}) custom-call(bf16[512,2048]{1,0:T(8,128)(2,1)S(1)} %get-tuple-element.59.refs_0_, bf16[512,2048]{1,0:T(8,128)(2,1)} %copy-done.72, bf16[512,2048]{1,0:T(8,128)(2,1)} %copy-done.73, f32[512,2048]{1,0:T(8,128)} %get-tuple-element.52.refs_3_.refs_0_, ...), custom_call_target="tpu_custom_call" | custom-call | flops 20971 | bytes 16777 | tf_op jit(solution)/shard_map/pallas_call | solution.py:171
  508.3 13.7 %shard_map.350 = (bf16[512,2048]{1,0:T(8,128)(2,1)}, bf16[512,2048]{1,0:T(8,128)(2,1)S(1)}) custom-call(s32[1]{0:T(128)} %bitcast.5.refs_0_, bf16[4,512,2048]{2,1,0:T(8,128)(2,1)} %get-tuple-element.54.refs_1_, bf16[4,2,256,2048]{3,2,1,0:T(8,128)(2,1)} %all-gather.20.cloned.1.call-done.refs_5_.refs_6_.refs_2_.refs_3_, ...), custom_call_target="tpu_custom_call" | custom-call | flops 8589934 | bytes 16777 | tf_op jit(solution)/shard_map/pallas_call | solution.py:171
  523.4 13.4 %shard_map.351 = (bf16[512,2048]{1,0:T(8,128)(2,1)S(1)}, bf16[512,2048]{1,0:T(8,128)(2,1)S(1)}) custom-call(s32[1]{0:T(128)} %bitcast.5.refs_0_, bf16[4,512,2048]{2,1,0:T(8,128)(2,1)} %get-tuple-element.54.refs_1_, bf16[4,2,256,2048]{3,2,1,0:T(8,128)(2,1)} %all-gather.20.cloned.1.call-done.refs_5_.refs_6_.refs_2_.refs_3_, ...), custom_call_target="tpu_custom_call" | custom-call | flops 8589934 | bytes 16777 | tf_op jit(solution)/shard_map/pallas_call | solution.py:171
  539.4 13.7 %collective-permute-done.36.refs_0_ = bf16[512,2048]{1,0:T(8,128)(2,1)S(1)} collective-permute-done((bf16[512,2048]{1,0:T(8,128)(2,1)}, bf16[512,2048]{1,0:T(8,128)(2,1)S(1)}, u32[]{:S(2)}, u32[]{:S(2)}) %collective-permute-start.36) | collective-permute-done | bytes 2097184 | tf_op jit(solution)/shard_map/ppermute | solution.py:33
  554.5 5.3 shard_map.353.refs_5_
  561.2 5.3 shard_map.354.refs_2_
  583.0 18.8 %shard_map.357 = (bf16[1024,1536]{1,0:T(8,128)(2,1)}, f32[1,1536]{1,0:T(1,128)S(1)}) custom-call(bf16[2048,512]{1,0:T(8,128)(2,1)S(1)} %bitcast.145, bf16[2048,512]{1,0:T(8,128)(2,1)S(1)} %bitcast.150, bf16[2048,512]{1,0:T(8,128)(2,1)} %bitcast.152, bf16[1024,512]{1,0:T(8,128)(2,1)S(1)} %bitcast.166, bf16[512,2048]{1,0:T(8,128)(2,1)} %shard_map.356.refs_4_), custom_call_target="tpu_custom_call" | custom-call | flops 5368709 | bytes 7340 | tf_op jit(solution)/shard_map/pallas_call | solution.py:171
  601.8 12.1 %shard_map.358 = (bf16[512,2048]{1,0:T(8,128)(2,1)}, bf16[512,2048]{1,0:T(8,128)(2,1)}) custom-call(s32[1]{0:T(128)} %bitcast.5.refs_0_, bf16[2,512,1536]{2,1,0:T(8,128)(2,1)} %bitcast.177, bf16[1,4,4,64,512]{4,3,2,1,0:T(8,128)(2,1)S(1)} %bitcast.169, bf16[1,4,4,64,512]{4,3,2,1,0:T(8,128)(2,1)S(1)} %copy-done.29, bf16[1,4,4,64,512]{4,3,2,1,0:T(8,128)(2,1)S(1)} %bitcast.173, ...), custom_call_target="tpu_custom_call" | custom-call | flops 6442450 | bytes 9437 | tf_op jit(solution)/shard_map/pallas_call | solution.py:171
  613.9 7.8 collective-permute-done.39
  627.2 6.5 shard_map.360.refs_6_
  636.7 5.5 shard_map.361.refs_4_.refs_1_
  648.3 18.7 %shard_map.362 = (bf16[1024,1536]{1,0:T(8,128)(2,1)}, f32[1,1536]{1,0:T(1,128)S(1)}) custom-call(bf16[2048,512]{1,0:T(8,128)(2,1)S(1)} %bitcast.146, bf16[2048,512]{1,0:T(8,128)(2,1)} %bitcast.149, bf16[2048,512]{1,0:T(8,128)(2,1)} %bitcast.153, bf16[1024,512]{1,0:T(8,128)(2,1)S(1)} %bitcast.165, bf16[256,2048]{1,0:T(8,128)(2,1)S(1)} %copy-done.35, ...), custom_call_target="tpu_custom_call" | custom-call | flops 5368709 | bytes 7340 | tf_op jit(solution)/shard_map/pallas_call | solution.py:171
  669.8 12.5 %shard_map.364 = (bf16[512,2048]{1,0:T(8,128)(2,1)}, bf16[512,2048]{1,0:T(8,128)(2,1)}) custom-call(s32[1]{0:T(128)} %bitcast.5.refs_0_, bf16[2,512,1536]{2,1,0:T(8,128)(2,1)} %bitcast.182, bf16[1,4,4,64,512]{4,3,2,1,0:T(8,128)(2,1)S(1)} %bitcast.170, bf16[1,4,4,64,512]{4,3,2,1,0:T(8,128)(2,1)S(1)} %copy-done.29, bf16[1,4,4,64,512]{4,3,2,1,0:T(8,128)(2,1)S(1)} %bitcast.174, ...), custom_call_target="tpu_custom_call" | custom-call | flops 6442450 | bytes 9437 | tf_op jit(solution)/shard_map/pallas_call | solution.py:171
  688.1 4.9 shard_map.366.refs_7_
  697.7 8.7 %shard_map.367.refs_7_ = bf16[1,4,4,64,1024]{4,3,2,1,0:T(8,128)(2,1)} custom-call(s32[1]{0:T(128)} %bitcast.5.refs_0_, bf16[512,2048]{1,0:T(8,128)(2,1)} %shard_map.321.refs_1_, bf16[512,2048]{1,0:T(8,128)(2,1)} %copy-done, bf16[512,2048]{1,0:T(8,128)(2,1)} %collective-permute-done.13.refs_3_, bf16[512,2048]{1,0:T(8,128)(2,1)} %collective-permute-done.14.refs_4_, ...), custom_call_target="tpu_custom_call" | custom-call | flops 4294967 | bytes 10485 | tf_op jit(solution)/shard_map/pallas_call | solution.py:171
  712.7 6.5 collective-permute-done.42
  724.5 8.3 shard_map.370.refs_5_
  743.6 8.2 shard_map.372
  753.1 10.5 %collective-permute-done.55 = bf16[1,4,4,64,1024]{4,3,2,1,0:T(8,128)(2,1)} collective-permute-done((bf16[1,4,4,64,1024]{4,3,2,1,0:T(8,128)(2,1)}, bf16[1,4,4,64,1024]{4,3,2,1,0:T(8,128)(2,1)}, u32[]{:S(2)}, u32[]{:S(2)}) %collective-permute-start.55) | collective-permute-done | bytes 2097184 | tf_op jit(solution)/shard_map/ppermute | solution.py:43
  797.0 6.8 bitcast_select_fusion
  (495 shorter events, 229.8 us)
Async XLA Ops:
  7.2 60.8 %all-gather.8.cloned.1.call-start = ((), (), s32[]{:S(2)}) async-start(), calls=%async_computation.7 | async-start | bytes 1310720 | tf_op jit(solution)/shard_map/all_gather | solution.py:690
  7.9 62.1 %all-gather.10.cloned.1.call-start = ((), (), s32[]{:S(2)}) async-start(), calls=%async_computation.8 | async-start | bytes 1310720 | tf_op jit(solution)/shard_map/all_gather | solution.py:690
  13.8 13.4 %collective-permute-start.8 = (bf16[64,3584]{1,0:T(8,128)(2,1)S(1)}, bf16[64,3584]{1,0:T(8,128)(2,1)}, u32[]{:S(2)}, u32[]{:S(2)}) collective-permute-start(bf16[64,3584]{1,0:T(8,128)(2,1)S(1)} %pad_maximum_fusion.5), channel_id=1, source_target_pairs={{0,12},{4,8},{8,4},{12,0},{1,13},{5,9},{9,5},{13,1},{2,14},{6,10},... | collective-permute-start | bytes 1376264 | tf_op jit(solution)/shard_map/ppermute | solution.py:33
  16.9 20.4 %collective-permute-start.9 = (bf16[64,3584]{1,0:T(8,128)(2,1)S(1)}, bf16[64,3584]{1,0:T(8,128)(2,1)}, u32[]{:S(2)}, u32[]{:S(2)}) collective-permute-start(bf16[64,3584]{1,0:T(8,128)(2,1)S(1)} %pad_maximum_fusion.6), channel_id=1, source_target_pairs={{0,8},{4,12},{8,0},{12,4},{1,9},{5,13},{9,1},{13,5},{2,10},{6,14},... | collective-permute-start | bytes 1376264 | tf_op jit(solution)/shard_map/ppermute | solution.py:33
  18.3 19.0 %collective-permute-start.10 = (bf16[64,3584]{1,0:T(8,128)(2,1)S(1)}, bf16[64,3584]{1,0:T(8,128)(2,1)}, u32[]{:S(2)}, u32[]{:S(2)}) collective-permute-start(bf16[64,3584]{1,0:T(8,128)(2,1)S(1)} %pad_maximum_fusion.7), channel_id=1, source_target_pairs={{0,4},{4,0},{8,12},{12,8},{1,5},{5,1},{9,13},{13,9},{2,6},{6,2},{1... | collective-permute-start | bytes 1376264 | tf_op jit(solution)/shard_map/ppermute | solution.py:33
  39.8 82.1 %all-gather.12.cloned.1.call-start = ((), (), s32[]{:S(2)}) async-start(), calls=%async_computation.9 | async-start | bytes 1310720 | tf_op jit(solution)/shard_map/all_gather | solution.py:690
  40.5 94.3 %all-gather.14.cloned.1.call-start = ((), (), s32[]{:S(2)}) async-start(), calls=%async_computation.10 | async-start | bytes 1310720 | tf_op jit(solution)/shard_map/all_gather | solution.py:690
  41.1 164.1 %all-gather.16.cloned.1.call-start = ((), (), s32[]{:S(2)}) async-start(), calls=%async_computation.11 | async-start | bytes 2621440 | tf_op jit(solution)/shard_map/all_gather | solution.py:690
  53.9 220.1 %all-gather.18.cloned.1.call-start = ((), (), s32[]{:S(2)}) async-start(), calls=%async_computation.12 | async-start | bytes 2621440 | tf_op jit(solution)/shard_map/all_gather | solution.py:690
  68.0 48.8 %collective-permute-start.7 = (bf16[512,2048]{1,0:T(8,128)(2,1)}, bf16[512,2048]{1,0:T(8,128)(2,1)S(1)}, u32[]{:S(2)}, u32[]{:S(2)}) collective-permute-start(bf16[512,2048]{1,0:T(8,128)(2,1)} %shard_map.321.refs_1_), channel_id=1, source_target_pairs={{0,8},{4,12},{8,0},{12,4},{1,9},{5,13},{9,1},{13,5},{2,10},{6,14},... | collective-permute-start | bytes 6291464 | tf_op jit(solution)/shard_map/ppermute | solution.py:33
  69.5 26.3 %collective-permute-start.12 = (bf16[1,256,2048]{2,1,0:T(8,128)(2,1)}, bf16[1,256,2048]{2,1,0:T(8,128)(2,1)S(1)}, u32[]{:S(2)}, u32[]{:S(2)}) collective-permute-start(bf16[1,256,2048]{2,1,0:T(8,128)(2,1)} %bitcast.6.refs_1_), channel_id=1, source_target_pairs={{0,16},{16,0},{1,17},{17,1},{2,18},{18,2},{3,19},{19,3},{4,20},{20... | collective-permute-start | bytes 3145736 | tf_op jit(solution)/shard_map/ppermute | solution.py:43
  70.0 46.8 %collective-permute-start.11 = (bf16[1,4,4,64,512]{4,3,2,1,0:T(8,128)(2,1)}, bf16[1,4,4,64,512]{4,3,2,1,0:T(8,128)(2,1)S(1)}, u32[]{:S(2)}, u32[]{:S(2)}) collective-permute-start(bf16[1,4,4,64,512]{4,3,2,1,0:T(8,128)(2,1)} %bitcast.167), channel_id=1, source_target_pairs={{0,16},{16,0},{1,17},{17,1},{2,18},{18,2},{3,19},{19,3},{4,20},{20... | collective-permute-start | bytes 3145736 | tf_op jit(solution)/shard_map/ppermute | solution.py:43
  77.5 46.4 %collective-permute-start.13 = (bf16[512,2048]{1,0:T(8,128)(2,1)}, bf16[512,2048]{1,0:T(8,128)(2,1)}, u32[]{:S(2)}, u32[]{:S(2)}) collective-permute-start(bf16[512,2048]{1,0:T(8,128)(2,1)} %shard_map.321.refs_1_), channel_id=1, source_target_pairs={{0,4},{4,0},{8,12},{12,8},{1,5},{5,1},{9,13},{13,9},{2,6},{6,2},{1... | collective-permute-start | bytes 6291464 | tf_op jit(solution)/shard_map/ppermute | solution.py:33
  117.8 271.1 %all-gather.20.cloned.1.call-start = ((), (), s32[]{:S(2)}) async-start(), calls=%async_computation.13 | async-start | bytes 10485760 | tf_op jit(solution)/shard_map/all_gather | solution.py:690
  121.8 26.4 %collective-permute-start.15 = (bf16[1,4,4,64,512]{4,3,2,1,0:T(8,128)(2,1)}, bf16[1,4,4,64,512]{4,3,2,1,0:T(8,128)(2,1)}, u32[]{:S(2)}, u32[]{:S(2)}) collective-permute-start(bf16[1,4,4,64,512]{4,3,2,1,0:T(8,128)(2,1)} %bitcast.171), channel_id=1, source_target_pairs={{0,16},{16,0},{1,17},{17,1},{2,18},{18,2},{3,19},{19,3},{4,20},{20... | collective-permute-start | bytes 3145736 | tf_op jit(solution)/shard_map/ppermute | solution.py:43
  122.3 58.3 %collective-permute-start.17 = (bf16[512,2048]{1,0:T(8,128)(2,1)}, bf16[512,2048]{1,0:T(8,128)(2,1)}, u32[]{:S(2)}, u32[]{:S(2)}) collective-permute-start(bf16[512,2048]{1,0:T(8,128)(2,1)} %shard_map.327.refs_2_.refs_1_), channel_id=1, source_target_pairs={{0,8},{4,12},{8,0},{12,4},{1,9},{5,13},{9,1},{13,5},{2,10},{6,14},... | collective-permute-start | bytes 6291464 | tf_op jit(solution)/shard_map/ppermute | solution.py:33
  136.2 34.5 %collective-permute-start.16 = (bf16[1,4,4,64,512]{4,3,2,1,0:T(8,128)(2,1)}, bf16[1,4,4,64,512]{4,3,2,1,0:T(8,128)(2,1)}, u32[]{:S(2)}, u32[]{:S(2)}) collective-permute-start(bf16[1,4,4,64,512]{4,3,2,1,0:T(8,128)(2,1)} %shard_map.325.refs_5_.refs_6_), channel_id=1, source_target_pairs={{0,16},{16,0},{1,17},{17,1},{2,18},{18,2},{3,19},{19,3},{4,20},{20... | collective-permute-start | bytes 3145736 | tf_op jit(solution)/shard_map/ppermute | solution.py:43
  158.2 36.5 %collective-permute-start.26 = (bf16[256,2048]{1,0:T(8,128)(2,1)S(1)}, bf16[256,2048]{1,0:T(8,128)(2,1)S(1)}, u32[]{:S(2)}, u32[]{:S(2)}) collective-permute-start(bf16[256,2048]{1,0:T(8,128)(2,1)S(1)} %shard_map.337), channel_id=1, source_target_pairs={{0,16},{16,0},{1,17},{17,1},{2,18},{18,2},{3,19},{19,3},{4,20},{20... | collective-permute-start | bytes 3145736 | tf_op jit(solution)/shard_map/ppermute | solution.py:43
  196.8 310.5 %reduce-scatter.8.cloned.1.call-start = ((), (), s32[]{:S(2)}) async-start(), calls=%async_computation.14 | async-start | bytes 4718592 | tf_op jit(solution)/shard_map/reduce_scatter | solution.py:846
  205.2 48.4 %collective-permute-start.21 = (bf16[1,4,4,64,1024]{4,3,2,1,0:T(8,128)(2,1)}, bf16[1,4,4,64,1024]{4,3,2,1,0:T(8,128)(2,1)}, u32[]{:S(2)}, u32[]{:S(2)}) collective-permute-start(bf16[1,4,4,64,1024]{4,3,2,1,0:T(8,128)(2,1)} %shard_map.332.refs_5_.refs_2_), channel_id=1, source_target_pairs={{0,16},{16,0},{1,17},{17,1},{2,18},{18,2},{3,19},{19,3},{4,20},{20... | collective-permute-start | bytes 6291464 | tf_op jit(solution)/shard_map/ppermute | solution.py:43
  205.8 47.7 %collective-permute-start.18 = (bf16[512,2048]{1,0:T(8,128)(2,1)}, bf16[512,2048]{1,0:T(8,128)(2,1)}, u32[]{:S(2)}, u32[]{:S(2)}) collective-permute-start(bf16[512,2048]{1,0:T(8,128)(2,1)} %get-tuple-element.50), channel_id=1, source_target_pairs={{0,4},{4,0},{8,12},{12,8},{1,5},{5,1},{9,13},{13,9},{2,6},{6,2},{1... | collective-permute-start | bytes 6291464 | tf_op jit(solution)/shard_map/ppermute | solution.py:33
  218.3 48.1 %collective-permute-start.20 = (bf16[512,2048]{1,0:T(8,128)(2,1)S(1)}, bf16[512,2048]{1,0:T(8,128)(2,1)}, u32[]{:S(2)}, u32[]{:S(2)}) collective-permute-start(bf16[512,2048]{1,0:T(8,128)(2,1)S(1)} %shard_map.331.refs_7_), channel_id=1, source_target_pairs={{0,8},{4,12},{8,0},{12,4},{1,9},{5,13},{9,1},{13,5},{2,10},{6,14},... | collective-permute-start | bytes 6291464 | tf_op jit(solution)/shard_map/ppermute | solution.py:33
  275.7 47.1 %collective-permute-start.23 = (bf16[1,4,4,64,1024]{4,3,2,1,0:T(8,128)(2,1)S(1)}, bf16[1,4,4,64,1024]{4,3,2,1,0:T(8,128)(2,1)S(1)}, u32[]{:S(2)}, u32[]{:S(2)}) collective-permute-start(bf16[1,4,4,64,1024]{4,3,2,1,0:T(8,128)(2,1)S(1)} %shard_map.334.refs_7_.refs_4_), channel_id=1, source_target_pairs={{0,16},{16,0},{1,17},{17,1},{2,18},{18,2},{3,19},{19,3},{4,20},{20... | collective-permute-start | bytes 6291464 | tf_op jit(solution)/shard_map/ppermute | solution.py:43
  277.2 47.1 %collective-permute-start.22 = (bf16[512,2048]{1,0:T(8,128)(2,1)S(1)}, bf16[512,2048]{1,0:T(8,128)(2,1)}, u32[]{:S(2)}, u32[]{:S(2)}) collective-permute-start(bf16[512,2048]{1,0:T(8,128)(2,1)S(1)} %get-tuple-element.53.refs_1_.refs_10_), channel_id=1, source_target_pairs={{0,8},{4,12},{8,0},{12,4},{1,9},{5,13},{9,1},{13,5},{2,10},{6,14},... | collective-permute-start | bytes 6291464 | tf_op jit(solution)/shard_map/ppermute | solution.py:33
  278.7 46.2 %collective-permute-start.24 = (bf16[512,2048]{1,0:T(8,128)(2,1)S(1)}, bf16[512,2048]{1,0:T(8,128)(2,1)}, u32[]{:S(2)}, u32[]{:S(2)}) collective-permute-start(bf16[512,2048]{1,0:T(8,128)(2,1)S(1)} %get-tuple-element.53.refs_1_.refs_10_), channel_id=1, source_target_pairs={{0,4},{4,0},{8,12},{12,8},{1,5},{5,1},{9,13},{13,9},{2,6},{6,2},{1... | collective-permute-start | bytes 6291464 | tf_op jit(solution)/shard_map/ppermute | solution.py:33
  324.2 34.6 %collective-permute-start.27 = (bf16[512,2048]{1,0:T(8,128)(2,1)}, bf16[512,2048]{1,0:T(8,128)(2,1)}, u32[]{:S(2)}, u32[]{:S(2)}) collective-permute-start(bf16[512,2048]{1,0:T(8,128)(2,1)} %shard_map.327.refs_2_.refs_1_), channel_id=1, source_target_pairs={{0,4},{4,0},{8,12},{12,8},{1,5},{5,1},{9,13},{13,9},{2,6},{6,2},{1... | collective-permute-start | bytes 6291464 | tf_op jit(solution)/shard_map/ppermute | solution.py:33
  324.8 34.1 %collective-permute-start.28 = (bf16[512,2048]{1,0:T(8,128)(2,1)}, bf16[512,2048]{1,0:T(8,128)(2,1)}, u32[]{:S(2)}, u32[]{:S(2)}) collective-permute-start(bf16[512,2048]{1,0:T(8,128)(2,1)} %collective-permute-done.17.refs_4_.refs_3_.refs_2_), channel_id=1, source_target_pairs={{0,4},{4,0},{8,12},{12,8},{1,5},{5,1},{9,13},{13,9},{2,6},{6,2},{1... | collective-permute-start | bytes 6291464 | tf_op jit(solution)/shard_map/ppermute | solution.py:33
  373.8 193.6 %reduce-scatter.10.cloned.1.call-start = ((), (), s32[]{:S(2)}) async-start(), calls=%async_computation.15 | async-start | bytes 4718592 | tf_op jit(solution)/shard_map/reduce_scatter | solution.py:846
  431.0 15.3 %collective-permute-start.30 = (bf16[512,2048]{1,0:T(8,128)(2,1)}, bf16[512,2048]{1,0:T(8,128)(2,1)}, u32[]{:S(2)}, u32[]{:S(2)}) collective-permute-start(bf16[512,2048]{1,0:T(8,128)(2,1)} %get-tuple-element.58.refs_6_), channel_id=1, source_target_pairs={{0,4},{4,0},{8,12},{12,8},{1,5},{5,1},{9,13},{13,9},{2,6},{6,2},{1... | collective-permute-start | bytes 6291464 | tf_op jit(solution)/shard_map/ppermute | solution.py:33
  431.3 212.0 %reduce-scatter.12.cloned.1.call-start = ((), (), s32[]{:S(2)}) async-start(), calls=%async_computation.16 | async-start | bytes 2621440 | tf_op jit(solution)/shard_map/reduce_scatter | solution.py:827
  431.5 54.3 %collective-permute-start.29 = (bf16[512,2048]{1,0:T(8,128)(2,1)}, bf16[512,2048]{1,0:T(8,128)(2,1)S(1)}, u32[]{:S(2)}, u32[]{:S(2)}) collective-permute-start(bf16[512,2048]{1,0:T(8,128)(2,1)} %copy-done.68), channel_id=1, source_target_pairs={{0,4},{4,0},{8,12},{12,8},{1,5},{5,1},{9,13},{13,9},{2,6},{6,2},{1... | collective-permute-start | bytes 6291464 | tf_op jit(solution)/shard_map/ppermute | solution.py:33
  448.1 47.9 %collective-permute-start.31 = (bf16[512,2048]{1,0:T(8,128)(2,1)S(1)}, bf16[512,2048]{1,0:T(8,128)(2,1)S(1)}, u32[]{:S(2)}, u32[]{:S(2)}) collective-permute-start(bf16[512,2048]{1,0:T(8,128)(2,1)S(1)} %shard_map.344.refs_6_), channel_id=1, source_target_pairs={{0,8},{4,12},{8,0},{12,4},{1,9},{5,13},{9,1},{13,5},{2,10},{6,14},... | collective-permute-start | bytes 6291464 | tf_op jit(solution)/shard_map/ppermute | solution.py:33
  458.0 81.4 %collective-permute-start.34 = (bf16[1,4,4,64,1024]{4,3,2,1,0:T(8,128)(2,1)}, bf16[1,4,4,64,1024]{4,3,2,1,0:T(8,128)(2,1)}, u32[]{:S(2)}, u32[]{:S(2)}) collective-permute-start(bf16[1,4,4,64,1024]{4,3,2,1,0:T(8,128)(2,1)} %shard_map.345.refs_6_), channel_id=1, source_target_pairs={{0,16},{16,0},{1,17},{17,1},{2,18},{18,2},{3,19},{19,3},{4,20},{20... | collective-permute-start | bytes 6291464 | tf_op jit(solution)/shard_map/ppermute | solution.py:43
  505.8 47.3 %collective-permute-start.36 = (bf16[512,2048]{1,0:T(8,128)(2,1)}, bf16[512,2048]{1,0:T(8,128)(2,1)S(1)}, u32[]{:S(2)}, u32[]{:S(2)}) collective-permute-start(bf16[512,2048]{1,0:T(8,128)(2,1)} %get-tuple-element.67.refs_1_.refs_2_), channel_id=1, source_target_pairs={{0,8},{4,12},{8,0},{12,4},{1,9},{5,13},{9,1},{13,5},{2,10},{6,14},... | collective-permute-start | bytes 6291464 | tf_op jit(solution)/shard_map/ppermute | solution.py:33
  507.3 52.5 %collective-permute-start.35 = (bf16[512,2048]{1,0:T(8,128)(2,1)}, bf16[512,2048]{1,0:T(8,128)(2,1)}, u32[]{:S(2)}, u32[]{:S(2)}) collective-permute-start(bf16[512,2048]{1,0:T(8,128)(2,1)} %get-tuple-element.67.refs_1_.refs_2_), channel_id=1, source_target_pairs={{0,4},{4,0},{8,12},{12,8},{1,5},{5,1},{9,13},{13,9},{2,6},{6,2},{1... | collective-permute-start | bytes 6291464 | tf_op jit(solution)/shard_map/ppermute | solution.py:33
  573.4 113.7 %reduce-scatter.14.cloned.1.call-start = ((), (), s32[]{:S(2)}) async-start(), calls=%async_computation.17 | async-start | bytes 2621440 | tf_op jit(solution)/shard_map/reduce_scatter | solution.py:827
  573.5 48.3 %collective-permute-start.39 = (bf16[1,4,4,64,1024]{4,3,2,1,0:T(8,128)(2,1)}, bf16[1,4,4,64,1024]{4,3,2,1,0:T(8,128)(2,1)S(1)}, u32[]{:S(2)}, u32[]{:S(2)}) collective-permute-start(bf16[1,4,4,64,1024]{4,3,2,1,0:T(8,128)(2,1)} %copy-done.44), channel_id=1, source_target_pairs={{0,16},{16,0},{1,17},{17,1},{2,18},{18,2},{3,19},{19,3},{4,20},{20... | collective-permute-start | bytes 6291464 | tf_op jit(solution)/shard_map/ppermute | solution.py:43
  625.6 71.1 %reduce-scatter.16.cloned.1.call-start = ((), (), s32[]{:S(2)}) async-start(), calls=%async_computation.18 | async-start | bytes 1310720 | tf_op jit(solution)/shard_map/reduce_scatter | solution.py:827
  633.7 33.4 %collective-permute-start.40 = (bf16[256,2048]{1,0:T(8,128)(2,1)}, bf16[256,2048]{1,0:T(8,128)(2,1)}, u32[]{:S(2)}, u32[]{:S(2)}) collective-permute-start(bf16[256,2048]{1,0:T(8,128)(2,1)} %shard_map.360.refs_6_), channel_id=1, source_target_pairs={{0,16},{16,0},{1,17},{17,1},{2,18},{18,2},{3,19},{19,3},{4,20},{20... | collective-permute-start | bytes 3145736 | tf_op jit(solution)/shard_map/ppermute | solution.py:43
  635.2 47.3 %collective-permute-start.38 = (bf16[512,2048]{1,0:T(8,128)(2,1)}, bf16[512,2048]{1,0:T(8,128)(2,1)}, u32[]{:S(2)}, u32[]{:S(2)}) collective-permute-start(bf16[512,2048]{1,0:T(8,128)(2,1)} %shard_map.356.refs_4_), channel_id=1, source_target_pairs={{0,8},{4,12},{8,0},{12,4},{1,9},{5,13},{9,1},{13,5},{2,10},{6,14},... | collective-permute-start | bytes 6291464 | tf_op jit(solution)/shard_map/ppermute | solution.py:33
  636.7 45.8 %collective-permute-start.41 = (bf16[512,2048]{1,0:T(8,128)(2,1)}, bf16[512,2048]{1,0:T(8,128)(2,1)}, u32[]{:S(2)}, u32[]{:S(2)}) collective-permute-start(bf16[512,2048]{1,0:T(8,128)(2,1)} %get-tuple-element.70.refs_2_), channel_id=1, source_target_pairs={{0,4},{4,0},{8,12},{12,8},{1,5},{5,1},{9,13},{13,9},{2,6},{6,2},{1... | collective-permute-start | bytes 6291464 | tf_op jit(solution)/shard_map/ppermute | solution.py:33
  669.8 134.9 %reduce-scatter.18.cloned.1.call-start = ((), (), s32[]{:S(2)}) async-start(), calls=%async_computation.19 | async-start | bytes 1310720 | tf_op jit(solution)/shard_map/reduce_scatter | solution.py:827
  693.1 26.1 %collective-permute-start.42 = (bf16[1,4,4,64,512]{4,3,2,1,0:T(8,128)(2,1)S(1)}, bf16[1,4,4,64,512]{4,3,2,1,0:T(8,128)(2,1)}, u32[]{:S(2)}, u32[]{:S(2)}) collective-permute-start(bf16[1,4,4,64,512]{4,3,2,1,0:T(8,128)(2,1)S(1)} %shard_map.366.refs_7_), channel_id=1, source_target_pairs={{0,16},{16,0},{1,17},{17,1},{2,18},{18,2},{3,19},{19,3},{4,20},{20... | collective-permute-start | bytes 3145736 | tf_op jit(solution)/shard_map/ppermute | solution.py:43
  693.7 40.4 %collective-permute-start.32 = (bf16[512,2048]{1,0:T(8,128)(2,1)}, bf16[512,2048]{1,0:T(8,128)(2,1)}, u32[]{:S(2)}, u32[]{:S(2)}) collective-permute-start(bf16[512,2048]{1,0:T(8,128)(2,1)} %get-tuple-element.65), channel_id=1, source_target_pairs={{0,4},{4,0},{8,12},{12,8},{1,5},{5,1},{9,13},{13,9},{2,6},{6,2},{1... | collective-permute-start | bytes 6291464 | tf_op jit(solution)/shard_map/ppermute | solution.py:33
  693.9 49.6 %collective-permute-start.43 = (bf16[512,2048]{1,0:T(8,128)(2,1)}, bf16[512,2048]{1,0:T(8,128)(2,1)}, u32[]{:S(2)}, u32[]{:S(2)}) collective-permute-start(bf16[512,2048]{1,0:T(8,128)(2,1)} %get-tuple-element.75), channel_id=1, source_target_pairs={{0,4},{4,0},{8,12},{12,8},{1,5},{5,1},{9,13},{13,9},{2,6},{6,2},{1... | collective-permute-start | bytes 6291464 | tf_op jit(solution)/shard_map/ppermute | solution.py:33
  694.2 49.3 %collective-permute-start.44 = (bf16[512,2048]{1,0:T(8,128)(2,1)}, bf16[512,2048]{1,0:T(8,128)(2,1)}, u32[]{:S(2)}, u32[]{:S(2)}) collective-permute-start(bf16[512,2048]{1,0:T(8,128)(2,1)} %shard_map.365.refs_7_), channel_id=1, source_target_pairs={{0,8},{4,12},{8,0},{12,4},{1,9},{5,13},{9,1},{13,5},{2,10},{6,14},... | collective-permute-start | bytes 6291464 | tf_op jit(solution)/shard_map/ppermute | solution.py:33
  706.3 57.2 %collective-permute-start.55 = (bf16[1,4,4,64,1024]{4,3,2,1,0:T(8,128)(2,1)}, bf16[1,4,4,64,1024]{4,3,2,1,0:T(8,128)(2,1)}, u32[]{:S(2)}, u32[]{:S(2)}) collective-permute-start(bf16[1,4,4,64,1024]{4,3,2,1,0:T(8,128)(2,1)} %shard_map.367.refs_7_), channel_id=1, source_target_pairs={{0,16},{16,0},{1,17},{17,1},{2,18},{18,2},{3,19},{19,3},{4,20},{20... | collective-permute-start | bytes 6291464 | tf_op jit(solution)/shard_map/ppermute | solution.py:43
  722.8 89.8 %reduce-scatter.20.cloned.1.call-start = ((), (), s32[]{:S(2)}) async-start(), calls=%async_computation.20 | async-start | bytes 2621440 | tf_op jit(solution)/shard_map/reduce_scatter | solution.py:827
  (124 other events, 656.1 us)
Sparse Core Ops, SparseCore 0:
  9.6 30.5 all-gather.7
  42.4 27.4 all-gather.9
  72.1 27.4 all-gather.11
  101.5 27.4 all-gather.13
  131.0 45.4 all-gather.15
  178.4 44.6 all-gather.17
  224.7 148.3 all-gather.19
  377.3 86.1 reduce-scatter.7
  467.5 93.3 reduce-scatter.9
  573.5 42.3 reduce-scatter.11
  625.8 42.3 reduce-scatter.13
  670.3 26.3 reduce-scatter.15
  722.9 24.6 reduce-scatter.17
  768.1 40.6 reduce-scatter.19

commit v7 on v6

--- a/solution.py
+++ b/solution.py
@@ -869,9 +869,9 @@
     q_far, sum_far = order.step(attend_back, q, k, v, d_far.reshape(2 * rows, -1), 2 * rows // SLOT)
     q_far = q_far.reshape(2, rows, -1)
     a_far = send_far(back([q_far], [w_q, w_k, w_v], style="bare"))
-    grad_up.append(settle(up_sent[1], up_mine[1]))
     o_sent = send_away(weight_grad([context], d_out_all, 1))
     o_mine = weight_grad([context], d_out_all, 0)
+    grad_up.append(settle(up_sent[1], up_mine[1]))
     q_near, sum_near = order.step(attend_back, q, k, v, d_near.reshape(2 * rows, -1), 0, hold=[grad_up[0]])
     q_near = q_near.reshape(2, rows, -1)
     grad_o = settle(o_sent, o_mine)

time: 842 us -> 841 us (level)
    ppermute x12, waiting for transfers between devices: 164 us -> 148 us  [outer_pass(): lax.ppermute(a, 'outer', [(o, order[(p + 1) % outer]) for p, o in enumera...]
    ppermute x42, waiting for transfers between devices: 81.7 us -> 90.3 us  [team_swap(): return lax.ppermute(a, 'team', [(i, i ^ flip) for i in range(TEAM)])]
  transfers between devices with their start and end apart: 76 -> 76, of which waited for: 31 -> 29; matrix products, arithmetic and copies ran while one was open for 7% -> 7% of each run, Pallas kernels for 47% -> 47%
where the time goes in v7:
time: 841 us; the launch traced here: 834 us
  Pallas kernels  394 us (47%)
  waiting for transfers between devices  253 us (30%)
  local copies, waits for them, and re-layouts  81.2 us (10%)
  starting transfers between devices  53.6 us (6%)
  matrix products  22 us (3%)
  between operations  15.7 us (2%)
  other arithmetic  14.5 us (2%)
    pallas_call x44, Pallas kernels, kernel_call(): pl.pallas_call(run, grid_spec=pltpu.PrefetchScalarGridSpec(num_scalar_pre...  394 us
    ppermute x12, waiting for transfers between devices, outer_pass(): lax.ppermute(a, 'outer', [(o, order[(p + 1) % outer]) for p, o in enumera...  148 us
    ppermute x42, waiting for transfers between devices, team_swap(): return lax.ppermute(a, 'team', [(i, i ^ flip) for i in range(TEAM)])  90.3 us
    unnamed x201, local copies, waits for them, and re-layouts  57 us
    ppermute x42, starting transfers between devices, team_swap(): return lax.ppermute(a, 'team', [(i, i ^ flip) for i in range(TEAM)])  27.1 us
  transfers between devices with their start and end apart: 76, of which 29 were waited for; matrix products, arithmetic and copies ran while one was open for 7% of the time, Pallas kernels for 47%

profile of v7, /device:TPU:0, one launch (start us, length us, event | category | flops | bytes accessed | tf_op | source)
XLA Modules:
  0.0 833.8 jit_solution(7343793655903030911)
XLA Ops:
  19.1 8.1 collective-permute-done.8
  27.2 10.1 %collective-permute-done.9 = bf16[64,3584]{1,0:T(8,128)(2,1)} collective-permute-done((bf16[64,3584]{1,0:T(8,128)(2,1)S(1)}, bf16[64,3584]{1,0:T(8,128)(2,1)}, u32[]{:S(2)}, u32[]{:S(2)}) %collective-permute-start.9) | collective-permute-done | bytes 458784 | tf_op jit(solution)/shard_map/ppermute | solution.py:33
  71.6 5.9 fusion.7.refs_3_.refs_4_
  77.5 18.3 %collective-permute-done.12 = bf16[1,256,2048]{2,1,0:T(8,128)(2,1)S(1)} collective-permute-done((bf16[1,256,2048]{2,1,0:T(8,128)(2,1)}, bf16[1,256,2048]{2,1,0:T(8,128)(2,1)S(1)}, u32[]{:S(2)}, u32[]{:S(2)}) %collective-permute-start.12) | collective-permute-done | bytes 1048608 | tf_op jit(solution)/shard_map/ppermute | solution.py:43
  95.8 21.0 %collective-permute-done.11.refs_1_.refs_6_.refs_3_ = bf16[1,4,4,64,512]{4,3,2,1,0:T(8,128)(2,1)S(1)} collective-permute-done((bf16[1,4,4,64,512]{4,3,2,1,0:T(8,128)(2,1)}, bf16[1,4,4,64,512]{4,3,2,1,0:T(8,128)(2,1)S(1)}, u32[]{:S(2)}, u32[]{:S(2)}) %collective-permute-start.11) | collective-permute-done | bytes 1048608 | tf_op jit(solution)/shard_map/ppermute | solution.py:43
  126.4 8.4 %shard_map.323.refs_8_.refs_1_ = bf16[4,512,512]{2,1,0:T(8,128)(2,1)S(1)} custom-call(s32[1]{0:T(128)} %bitcast.5.refs_0_, bf16[512,2048]{1,0:T(8,128)(2,1)} %shard_map.321.refs_1_, bf16[512,2048]{1,0:T(8,128)(2,1)} %copy-done, bf16[512,2048]{1,0:T(8,128)(2,1)} %collective-permute-done.13.refs_3_, bf16[512,2048]{1,0:T(8,128)(2,1)} %collective-permute-done.14.refs_4_, ...), custom_call_target="tpu_custom_call" | custom-call | flops 4294967 | bytes 12582 | tf_op jit(solution)/shard_map/pallas_call | solution.py:171
  137.7 10.5 %collective-permute-done.15.refs_6_.refs_5_ = bf16[1,4,4,64,512]{4,3,2,1,0:T(8,128)(2,1)} collective-permute-done((bf16[1,4,4,64,512]{4,3,2,1,0:T(8,128)(2,1)}, bf16[1,4,4,64,512]{4,3,2,1,0:T(8,128)(2,1)}, u32[]{:S(2)}, u32[]{:S(2)}) %collective-permute-start.15) | collective-permute-done | bytes 1048608 | tf_op jit(solution)/shard_map/ppermute | solution.py:43
  148.2 8.6 %shard_map.324.refs_8_ = bf16[4,512,512]{2,1,0:T(8,128)(2,1)S(1)} custom-call(s32[1]{0:T(128)} %bitcast.5.refs_0_, bf16[512,2048]{1,0:T(8,128)(2,1)} %shard_map.321.refs_1_, bf16[512,2048]{1,0:T(8,128)(2,1)} %copy-done, bf16[512,2048]{1,0:T(8,128)(2,1)} %collective-permute-done.13.refs_3_, bf16[512,2048]{1,0:T(8,128)(2,1)} %collective-permute-done.14.refs_4_, ...), custom_call_target="tpu_custom_call" | custom-call | flops 4294967 | bytes 12582 | tf_op jit(solution)/shard_map/pallas_call | solution.py:171
  158.8 11.9 %collective-permute-done.16.refs_6_.refs_7_ = bf16[1,4,4,64,512]{4,3,2,1,0:T(8,128)(2,1)} collective-permute-done((bf16[1,4,4,64,512]{4,3,2,1,0:T(8,128)(2,1)}, bf16[1,4,4,64,512]{4,3,2,1,0:T(8,128)(2,1)}, u32[]{:S(2)}, u32[]{:S(2)}) %collective-permute-start.16) | collective-permute-done | bytes 1048608 | tf_op jit(solution)/shard_map/ppermute | solution.py:43
  170.7 8.7 %shard_map.326.refs_3_ = bf16[4,512,512]{2,1,0:T(8,128)(2,1)S(1)} custom-call(s32[1]{0:T(128)} %bitcast.5.refs_0_, bf16[512,2048]{1,0:T(8,128)(2,1)} %shard_map.321.refs_1_, bf16[512,2048]{1,0:T(8,128)(2,1)} %copy-done, bf16[512,2048]{1,0:T(8,128)(2,1)} %collective-permute-done.13.refs_3_, bf16[512,2048]{1,0:T(8,128)(2,1)} %collective-permute-done.14.refs_4_, ...), custom_call_target="tpu_custom_call" | custom-call | flops 4294967 | bytes 12582 | tf_op jit(solution)/shard_map/pallas_call | solution.py:171
  180.7 14.0 %shard_map.328.refs_4_ = bf16[2048,512]{1,0:T(8,128)(2,1)S(1)} custom-call(bf16[2048,512]{1,0:T(8,128)(2,1)S(1)} %bitcast.144, bf16[2048,512]{1,0:T(8,128)(2,1)} %bitcast.148, bf16[2048,512]{1,0:T(8,128)(2,1)} %bitcast.151, bf16[4,512,512]{2,1,0:T(8,128)(2,1)} %copy-done.12, bf16[512,2048]{1,0:T(8,128)(2,1)} %collective-permute-done.17.refs_4_.refs_3_.refs_2_), custom_call_target="tpu_custom_call" | custom-call | flops 4294967 | bytes 8388 | tf_op jit(solution)/shard_map/pallas_call | solution.py:171
  197.3 7.9 shard_map.329
  206.1 7.6 shard_map.330
  220.2 33.5 %collective-permute-done.21.refs_8_.refs_6_.refs_3_ = bf16[1,4,4,64,1024]{4,3,2,1,0:T(8,128)(2,1)} collective-permute-done((bf16[1,4,4,64,1024]{4,3,2,1,0:T(8,128)(2,1)}, bf16[1,4,4,64,1024]{4,3,2,1,0:T(8,128)(2,1)}, u32[]{:S(2)}, u32[]{:S(2)}) %collective-permute-start.21) | collective-permute-done | bytes 2097184 | tf_op jit(solution)/shard_map/ppermute | solution.py:43
  253.6 12.8 %collective-permute-done.20.refs_3_ = bf16[512,2048]{1,0:T(8,128)(2,1)} collective-permute-done((bf16[512,2048]{1,0:T(8,128)(2,1)S(1)}, bf16[512,2048]{1,0:T(8,128)(2,1)}, u32[]{:S(2)}, u32[]{:S(2)}) %collective-permute-start.20) | collective-permute-done | bytes 2097184 | tf_op jit(solution)/shard_map/ppermute | solution.py:33
  268.0 6.1 shard_map.333
  278.7 44.1 %collective-permute-done.23.refs_1_.refs_8_.refs_5_ = bf16[1,4,4,64,1024]{4,3,2,1,0:T(8,128)(2,1)S(1)} collective-permute-done((bf16[1,4,4,64,1024]{4,3,2,1,0:T(8,128)(2,1)S(1)}, bf16[1,4,4,64,1024]{4,3,2,1,0:T(8,128)(2,1)S(1)}, u32[]{:S(2)}, u32[]{:S(2)}) %collective-permute-start.23) | collective-permute-done | bytes 2097184 | tf_op jit(solution)/shard_map/ppermute | solution.py:43
  328.8 30.1 %shard_map.336 = (bf16[4,512,2048]{2,1,0:T(8,128)(2,1)}, bf16[4,512,2048]{2,1,0:T(8,128)(2,1)}) custom-call(s32[1]{0:T(128)} %bitcast.5.refs_0_, bf16[512,2048]{1,0:T(8,128)(2,1)S(1)} %get-tuple-element.53.refs_1_.refs_10_, bf16[512,2048]{1,0:T(8,128)(2,1)} %shard_map.335.refs_2_, bf16[512,2048]{1,0:T(8,128)(2,1)} %collective-permute-done.24.refs_3_, ...), custom_call_target="tpu_custom_call" | custom-call | flops 17179868 | bytes 25165 | tf_op jit(solution)/shard_map/pallas_call | solution.py:171
  359.0 14.9 %shard_map.339.refs_6_ = bf16[2048,1024]{1,0:T(8,128)(2,1)} custom-call(s32[1]{0:T(128)} %bitcast.5.refs_0_, bf16[4,512,2048]{2,1,0:T(8,128)(2,1)} %get-tuple-element.54.refs_1_, bf16[512,2048]{1,0:T(8,128)(2,1)} %shard_map.327.refs_2_.refs_1_, bf16[512,2048]{1,0:T(8,128)(2,1)} %collective-permute-done.17.refs_4_.refs_3_.refs_2_, ...), custom_call_target="tpu_custom_call" | custom-call | flops 8589934 | bytes 16777 | tf_op jit(solution)/shard_map/pallas_call | solution.py:171
  373.9 15.0 %shard_map.340.refs_8_ = bf16[2048,1024]{1,0:T(8,128)(2,1)} custom-call(s32[1]{0:T(128)} %bitcast.5.refs_0_, bf16[4,512,2048]{2,1,0:T(8,128)(2,1)} %get-tuple-element.54.refs_1_, bf16[512,2048]{1,0:T(8,128)(2,1)} %shard_map.327.refs_2_.refs_1_, bf16[512,2048]{1,0:T(8,128)(2,1)} %collective-permute-done.17.refs_4_.refs_3_.refs_2_, ...), custom_call_target="tpu_custom_call" | custom-call | flops 8589934 | bytes 16777 | tf_op jit(solution)/shard_map/pallas_call | solution.py:171
  389.0 25.7 %shard_map.341 = (bf16[4,512,2048]{2,1,0:T(8,128)(2,1)}, f32[1,2048]{1,0:T(1,128)S(1)}) custom-call(s32[1]{0:T(128)} %bitcast.5.refs_0_, bf16[512,2048]{1,0:T(8,128)(2,1)} %shard_map.327.refs_2_.refs_1_, bf16[512,2048]{1,0:T(8,128)(2,1)} %collective-permute-done.17.refs_4_.refs_3_.refs_2_, bf16[512,2048]{1,0:T(8,128)(2,1)} %collective-permute-done.27.refs_4_.refs_3_, ...), custom_call_target="tpu_custom_call" | custom-call | flops 17179868 | bytes 25165 | tf_op jit(solution)/shard_map/pallas_call | solution.py:171
  414.7 15.0 %shard_map.342 = (bf16[512,2048]{1,0:T(8,128)(2,1)S(1)}, bf16[512,2048]{1,0:T(8,128)(2,1)}) custom-call(s32[1]{0:T(128)} %bitcast.5.refs_0_, bf16[4,512,2048]{2,1,0:T(8,128)(2,1)} %get-tuple-element.56.refs_1_.refs_5_, bf16[1,4,4,64,1024]{4,3,2,1,0:T(8,128)(2,1)} %shard_map.332.refs_5_.refs_2_, ...), custom_call_target="tpu_custom_call" | custom-call | flops 8589934 | bytes 12582 | tf_op jit(solution)/shard_map/pallas_call | solution.py:171
  431.9 14.4 %shard_map.343 = (bf16[512,2048]{1,0:T(8,128)(2,1)S(1)}, bf16[512,2048]{1,0:T(8,128)(2,1)S(1)}) custom-call(s32[1]{0:T(128)} %bitcast.5.refs_0_, bf16[4,512,2048]{2,1,0:T(8,128)(2,1)} %get-tuple-element.56.refs_1_.refs_5_, bf16[1,4,4,64,1024]{4,3,2,1,0:T(8,128)(2,1)} %shard_map.332.refs_5_.refs_2_, ...), custom_call_target="tpu_custom_call" | custom-call | flops 8589934 | bytes 12582 | tf_op jit(solution)/shard_map/pallas_call | solution.py:171
  449.7 8.3 shard_map.345.refs_6_
  459.5 8.3 %shard_map.346.refs_6_ = bf16[1,4,4,64,1024]{4,3,2,1,0:T(8,128)(2,1)} custom-call(s32[1]{0:T(128)} %bitcast.5.refs_0_, bf16[512,2048]{1,0:T(8,128)(2,1)S(1)} %get-tuple-element.53.refs_1_.refs_10_, bf16[512,2048]{1,0:T(8,128)(2,1)} %shard_map.335.refs_2_, bf16[512,2048]{1,0:T(8,128)(2,1)} %collective-permute-done.24.refs_3_, ...), custom_call_target="tpu_custom_call" | custom-call | flops 4294967 | bytes 10485 | tf_op jit(solution)/shard_map/pallas_call | solution.py:171
  467.8 7.4 shard_map.347.refs_6_
  476.6 7.4 shard_map.348.refs_6_
  485.4 10.7 %collective-permute-done.31.refs_2_ = bf16[512,2048]{1,0:T(8,128)(2,1)S(1)} collective-permute-done((bf16[512,2048]{1,0:T(8,128)(2,1)S(1)}, bf16[512,2048]{1,0:T(8,128)(2,1)S(1)}, u32[]{:S(2)}, u32[]{:S(2)}) %collective-permute-start.31) | collective-permute-done | bytes 2097184 | tf_op jit(solution)/shard_map/ppermute | solution.py:33
  497.4 8.5 %shard_map.349 = (f32[512,2048]{1,0:T(8,128)}, bf16[512,2048]{1,0:T(8,128)(2,1)}, f32[4,2048]{1,0:T(4,128)S(1)}) custom-call(bf16[512,2048]{1,0:T(8,128)(2,1)S(1)} %get-tuple-element.59.refs_0_, bf16[512,2048]{1,0:T(8,128)(2,1)} %copy-done.72, bf16[512,2048]{1,0:T(8,128)(2,1)} %copy-done.73, f32[512,2048]{1,0:T(8,128)} %get-tuple-element.52.refs_3_.refs_0_, ...), custom_call_target="tpu_custom_call" | custom-call | flops 20971 | bytes 16777 | tf_op jit(solution)/shard_map/pallas_call | solution.py:171
  508.4 13.7 %shard_map.350 = (bf16[512,2048]{1,0:T(8,128)(2,1)}, bf16[512,2048]{1,0:T(8,128)(2,1)S(1)}) custom-call(s32[1]{0:T(128)} %bitcast.5.refs_0_, bf16[4,512,2048]{2,1,0:T(8,128)(2,1)} %get-tuple-element.54.refs_1_, bf16[4,2,256,2048]{3,2,1,0:T(8,128)(2,1)} %all-gather.20.cloned.1.call-done.refs_5_.refs_6_.refs_2_.refs_3_, ...), custom_call_target="tpu_custom_call" | custom-call | flops 8589934 | bytes 16777 | tf_op jit(solution)/shard_map/pallas_call | solution.py:171
  523.5 13.4 %shard_map.351 = (bf16[512,2048]{1,0:T(8,128)(2,1)S(1)}, bf16[512,2048]{1,0:T(8,128)(2,1)S(1)}) custom-call(s32[1]{0:T(128)} %bitcast.5.refs_0_, bf16[4,512,2048]{2,1,0:T(8,128)(2,1)} %get-tuple-element.54.refs_1_, bf16[4,2,256,2048]{3,2,1,0:T(8,128)(2,1)} %all-gather.20.cloned.1.call-done.refs_5_.refs_6_.refs_2_.refs_3_, ...), custom_call_target="tpu_custom_call" | custom-call | flops 8589934 | bytes 16777 | tf_op jit(solution)/shard_map/pallas_call | solution.py:171
  539.6 13.7 %collective-permute-done.36.refs_0_ = bf16[512,2048]{1,0:T(8,128)(2,1)S(1)} collective-permute-done((bf16[512,2048]{1,0:T(8,128)(2,1)}, bf16[512,2048]{1,0:T(8,128)(2,1)S(1)}, u32[]{:S(2)}, u32[]{:S(2)}) %collective-permute-start.36) | collective-permute-done | bytes 2097184 | tf_op jit(solution)/shard_map/ppermute | solution.py:33
  554.6 5.3 shard_map.353.refs_5_
  561.3 5.3 shard_map.354.refs_2_
  585.8 18.8 %shard_map.357 = (bf16[1024,1536]{1,0:T(8,128)(2,1)}, f32[1,1536]{1,0:T(1,128)S(1)}) custom-call(bf16[2048,512]{1,0:T(8,128)(2,1)S(1)} %bitcast.145, bf16[2048,512]{1,0:T(8,128)(2,1)S(1)} %bitcast.149, bf16[2048,512]{1,0:T(8,128)(2,1)} %bitcast.152, bf16[1024,512]{1,0:T(8,128)(2,1)S(1)} %bitcast.165, bf16[512,2048]{1,0:T(8,128)(2,1)} %copy-done.45), custom_call_target="tpu_custom_call" | custom-call | flops 5368709 | bytes 7340 | tf_op jit(solution)/shard_map/pallas_call | solution.py:171
  604.6 12.2 %shard_map.358 = (bf16[512,2048]{1,0:T(8,128)(2,1)}, bf16[512,2048]{1,0:T(8,128)(2,1)}) custom-call(s32[1]{0:T(128)} %bitcast.5.refs_0_, bf16[2,512,1536]{2,1,0:T(8,128)(2,1)} %bitcast.176, bf16[1,4,4,64,512]{4,3,2,1,0:T(8,128)(2,1)S(1)} %bitcast.168, bf16[1,4,4,64,512]{4,3,2,1,0:T(8,128)(2,1)S(1)} %copy-done.28, bf16[1,4,4,64,512]{4,3,2,1,0:T(8,128)(2,1)S(1)} %bitcast.172, ...), custom_call_target="tpu_custom_call" | custom-call | flops 6442450 | bytes 9437 | tf_op jit(solution)/shard_map/pallas_call | solution.py:171
  616.8 5.5 shard_map.359.refs_6_
  622.4 5.9 shard_map.360.refs_2_.refs_1_
  640.5 18.7 %shard_map.362 = (bf16[1024,1536]{1,0:T(8,128)(2,1)}, f32[1,1536]{1,0:T(1,128)S(1)}) custom-call(bf16[2048,512]{1,0:T(8,128)(2,1)S(1)} %bitcast.146, bf16[2048,512]{1,0:T(8,128)(2,1)S(1)} %bitcast.150, bf16[2048,512]{1,0:T(8,128)(2,1)} %bitcast.153, bf16[1024,512]{1,0:T(8,128)(2,1)S(1)} %bitcast.164, bf16[1,4,4,64,1024]{4,3,2,1,0:T(8,128)(2,1)} %bitcast.162, ...), custom_call_target="tpu_custom_call" | custom-call | flops 5368709 | bytes 7340 | tf_op jit(solution)/shard_map/pallas_call | solution.py:171
  661.9 12.6 %shard_map.364 = (bf16[512,2048]{1,0:T(8,128)(2,1)}, bf16[512,2048]{1,0:T(8,128)(2,1)}) custom-call(s32[1]{0:T(128)} %bitcast.5.refs_0_, bf16[2,512,1536]{2,1,0:T(8,128)(2,1)} %bitcast.181, bf16[1,4,4,64,512]{4,3,2,1,0:T(8,128)(2,1)S(1)} %bitcast.169, bf16[1,4,4,64,512]{4,3,2,1,0:T(8,128)(2,1)S(1)} %copy-done.28, bf16[1,4,4,64,512]{4,3,2,1,0:T(8,128)(2,1)S(1)} %bitcast.173, ...), custom_call_target="tpu_custom_call" | custom-call | flops 6442450 | bytes 9437 | tf_op jit(solution)/shard_map/pallas_call | solution.py:171
  674.5 8.0 collective-permute-done.38.refs_3_
  688.1 4.9 shard_map.366.refs_7_
  695.7 8.4 %reduce-scatter.16.cloned.1.call-done.refs_8_ = bf16[64,2048]{1,0:T(8,128)(2,1)} async-done(((bf16[256,2048]{1,0:T(8,128)(2,1)}), bf16[64,2048]{1,0:T(8,128)(2,1)}) %reduce-scatter.16.cloned.1.call-update) | async-done | bytes 262160 | tf_op jit(solution)/shard_map/reduce_scatter | solution.py:827
  705.0 8.6 %shard_map.367.refs_7_ = bf16[1,4,4,64,1024]{4,3,2,1,0:T(8,128)(2,1)} custom-call(s32[1]{0:T(128)} %bitcast.5.refs_0_, bf16[512,2048]{1,0:T(8,128)(2,1)} %shard_map.321.refs_1_, bf16[512,2048]{1,0:T(8,128)(2,1)} %copy-done, bf16[512,2048]{1,0:T(8,128)(2,1)} %collective-permute-done.13.refs_3_, bf16[512,2048]{1,0:T(8,128)(2,1)} %collective-permute-done.14.refs_4_, ...), custom_call_target="tpu_custom_call" | custom-call | flops 4294967 | bytes 10485 | tf_op jit(solution)/shard_map/pallas_call | solution.py:171
  725.4 8.3 shard_map.370.refs_5_
  744.4 8.3 shard_map.372
  753.9 8.4 %collective-permute-done.55 = bf16[1,4,4,64,1024]{4,3,2,1,0:T(8,128)(2,1)} collective-permute-done((bf16[1,4,4,64,1024]{4,3,2,1,0:T(8,128)(2,1)}, bf16[1,4,4,64,1024]{4,3,2,1,0:T(8,128)(2,1)}, u32[]{:S(2)}, u32[]{:S(2)}) %collective-permute-start.55) | collective-permute-done | bytes 2097184 | tf_op jit(solution)/shard_map/ppermute | solution.py:43
  795.9 6.8 bitcast_select_fusion
  (495 shorter events, 228.1 us)
Async XLA Ops:
  7.2 60.8 %all-gather.8.cloned.1.call-start = ((), (), s32[]{:S(2)}) async-start(), calls=%async_computation.7 | async-start | bytes 1310720 | tf_op jit(solution)/shard_map/all_gather | solution.py:690
  7.9 62.1 %all-gather.10.cloned.1.call-start = ((), (), s32[]{:S(2)}) async-start(), calls=%async_computation.8 | async-start | bytes 1310720 | tf_op jit(solution)/shard_map/all_gather | solution.py:690
  13.8 13.4 %collective-permute-start.8 = (bf16[64,3584]{1,0:T(8,128)(2,1)S(1)}, bf16[64,3584]{1,0:T(8,128)(2,1)}, u32[]{:S(2)}, u32[]{:S(2)}) collective-permute-start(bf16[64,3584]{1,0:T(8,128)(2,1)S(1)} %pad_maximum_fusion.5), channel_id=1, source_target_pairs={{0,12},{4,8},{8,4},{12,0},{1,13},{5,9},{9,5},{13,1},{2,14},{6,10},... | collective-permute-start | bytes 1376264 | tf_op jit(solution)/shard_map/ppermute | solution.py:33
  16.9 20.4 %collective-permute-start.9 = (bf16[64,3584]{1,0:T(8,128)(2,1)S(1)}, bf16[64,3584]{1,0:T(8,128)(2,1)}, u32[]{:S(2)}, u32[]{:S(2)}) collective-permute-start(bf16[64,3584]{1,0:T(8,128)(2,1)S(1)} %pad_maximum_fusion.6), channel_id=1, source_target_pairs={{0,8},{4,12},{8,0},{12,4},{1,9},{5,13},{9,1},{13,5},{2,10},{6,14},... | collective-permute-start | bytes 1376264 | tf_op jit(solution)/shard_map/ppermute | solution.py:33
  18.3 19.0 %collective-permute-start.10 = (bf16[64,3584]{1,0:T(8,128)(2,1)S(1)}, bf16[64,3584]{1,0:T(8,128)(2,1)}, u32[]{:S(2)}, u32[]{:S(2)}) collective-permute-start(bf16[64,3584]{1,0:T(8,128)(2,1)S(1)} %pad_maximum_fusion.7), channel_id=1, source_target_pairs={{0,4},{4,0},{8,12},{12,8},{1,5},{5,1},{9,13},{13,9},{2,6},{6,2},{1... | collective-permute-start | bytes 1376264 | tf_op jit(solution)/shard_map/ppermute | solution.py:33
  39.8 82.1 %all-gather.12.cloned.1.call-start = ((), (), s32[]{:S(2)}) async-start(), calls=%async_computation.9 | async-start | bytes 1310720 | tf_op jit(solution)/shard_map/all_gather | solution.py:690
  40.5 94.3 %all-gather.14.cloned.1.call-start = ((), (), s32[]{:S(2)}) async-start(), calls=%async_computation.10 | async-start | bytes 1310720 | tf_op jit(solution)/shard_map/all_gather | solution.py:690
  41.1 164.2 %all-gather.16.cloned.1.call-start = ((), (), s32[]{:S(2)}) async-start(), calls=%async_computation.11 | async-start | bytes 2621440 | tf_op jit(solution)/shard_map/all_gather | solution.py:690
  53.9 220.2 %all-gather.18.cloned.1.call-start = ((), (), s32[]{:S(2)}) async-start(), calls=%async_computation.12 | async-start | bytes 2621440 | tf_op jit(solution)/shard_map/all_gather | solution.py:690
  68.0 48.8 %collective-permute-start.7 = (bf16[512,2048]{1,0:T(8,128)(2,1)}, bf16[512,2048]{1,0:T(8,128)(2,1)S(1)}, u32[]{:S(2)}, u32[]{:S(2)}) collective-permute-start(bf16[512,2048]{1,0:T(8,128)(2,1)} %shard_map.321.refs_1_), channel_id=1, source_target_pairs={{0,8},{4,12},{8,0},{12,4},{1,9},{5,13},{9,1},{13,5},{2,10},{6,14},... | collective-permute-start | bytes 6291464 | tf_op jit(solution)/shard_map/ppermute | solution.py:33
  69.5 26.3 %collective-permute-start.12 = (bf16[1,256,2048]{2,1,0:T(8,128)(2,1)}, bf16[1,256,2048]{2,1,0:T(8,128)(2,1)S(1)}, u32[]{:S(2)}, u32[]{:S(2)}) collective-permute-start(bf16[1,256,2048]{2,1,0:T(8,128)(2,1)} %bitcast.6.refs_1_), channel_id=1, source_target_pairs={{0,16},{16,0},{1,17},{17,1},{2,18},{18,2},{3,19},{19,3},{4,20},{20... | collective-permute-start | bytes 3145736 | tf_op jit(solution)/shard_map/ppermute | solution.py:43
  70.0 46.8 %collective-permute-start.11 = (bf16[1,4,4,64,512]{4,3,2,1,0:T(8,128)(2,1)}, bf16[1,4,4,64,512]{4,3,2,1,0:T(8,128)(2,1)S(1)}, u32[]{:S(2)}, u32[]{:S(2)}) collective-permute-start(bf16[1,4,4,64,512]{4,3,2,1,0:T(8,128)(2,1)} %bitcast.166), channel_id=1, source_target_pairs={{0,16},{16,0},{1,17},{17,1},{2,18},{18,2},{3,19},{19,3},{4,20},{20... | collective-permute-start | bytes 3145736 | tf_op jit(solution)/shard_map/ppermute | solution.py:43
  77.5 46.4 %collective-permute-start.13 = (bf16[512,2048]{1,0:T(8,128)(2,1)}, bf16[512,2048]{1,0:T(8,128)(2,1)}, u32[]{:S(2)}, u32[]{:S(2)}) collective-permute-start(bf16[512,2048]{1,0:T(8,128)(2,1)} %shard_map.321.refs_1_), channel_id=1, source_target_pairs={{0,4},{4,0},{8,12},{12,8},{1,5},{5,1},{9,13},{13,9},{2,6},{6,2},{1... | collective-permute-start | bytes 6291464 | tf_op jit(solution)/shard_map/ppermute | solution.py:33
  117.8 271.2 %all-gather.20.cloned.1.call-start = ((), (), s32[]{:S(2)}) async-start(), calls=%async_computation.13 | async-start | bytes 10485760 | tf_op jit(solution)/shard_map/all_gather | solution.py:690
  121.8 26.4 %collective-permute-start.15 = (bf16[1,4,4,64,512]{4,3,2,1,0:T(8,128)(2,1)}, bf16[1,4,4,64,512]{4,3,2,1,0:T(8,128)(2,1)}, u32[]{:S(2)}, u32[]{:S(2)}) collective-permute-start(bf16[1,4,4,64,512]{4,3,2,1,0:T(8,128)(2,1)} %bitcast.170), channel_id=1, source_target_pairs={{0,16},{16,0},{1,17},{17,1},{2,18},{18,2},{3,19},{19,3},{4,20},{20... | collective-permute-start | bytes 3145736 | tf_op jit(solution)/shard_map/ppermute | solution.py:43
  122.3 58.4 %collective-permute-start.17 = (bf16[512,2048]{1,0:T(8,128)(2,1)}, bf16[512,2048]{1,0:T(8,128)(2,1)}, u32[]{:S(2)}, u32[]{:S(2)}) collective-permute-start(bf16[512,2048]{1,0:T(8,128)(2,1)} %shard_map.327.refs_2_.refs_1_), channel_id=1, source_target_pairs={{0,8},{4,12},{8,0},{12,4},{1,9},{5,13},{9,1},{13,5},{2,10},{6,14},... | collective-permute-start | bytes 6291464 | tf_op jit(solution)/shard_map/ppermute | solution.py:33
  136.1 34.5 %collective-permute-start.16 = (bf16[1,4,4,64,512]{4,3,2,1,0:T(8,128)(2,1)}, bf16[1,4,4,64,512]{4,3,2,1,0:T(8,128)(2,1)}, u32[]{:S(2)}, u32[]{:S(2)}) collective-permute-start(bf16[1,4,4,64,512]{4,3,2,1,0:T(8,128)(2,1)} %shard_map.325.refs_5_.refs_6_), channel_id=1, source_target_pairs={{0,16},{16,0},{1,17},{17,1},{2,18},{18,2},{3,19},{19,3},{4,20},{20... | collective-permute-start | bytes 3145736 | tf_op jit(solution)/shard_map/ppermute | solution.py:43
  158.2 36.6 %collective-permute-start.26 = (bf16[256,2048]{1,0:T(8,128)(2,1)S(1)}, bf16[256,2048]{1,0:T(8,128)(2,1)S(1)}, u32[]{:S(2)}, u32[]{:S(2)}) collective-permute-start(bf16[256,2048]{1,0:T(8,128)(2,1)S(1)} %shard_map.337), channel_id=1, source_target_pairs={{0,16},{16,0},{1,17},{17,1},{2,18},{18,2},{3,19},{19,3},{4,20},{20... | collective-permute-start | bytes 3145736 | tf_op jit(solution)/shard_map/ppermute | solution.py:43
  196.9 310.5 %reduce-scatter.8.cloned.1.call-start = ((), (), s32[]{:S(2)}) async-start(), calls=%async_computation.14 | async-start | bytes 4718592 | tf_op jit(solution)/shard_map/reduce_scatter | solution.py:846
  205.3 48.4 %collective-permute-start.21 = (bf16[1,4,4,64,1024]{4,3,2,1,0:T(8,128)(2,1)}, bf16[1,4,4,64,1024]{4,3,2,1,0:T(8,128)(2,1)}, u32[]{:S(2)}, u32[]{:S(2)}) collective-permute-start(bf16[1,4,4,64,1024]{4,3,2,1,0:T(8,128)(2,1)} %shard_map.332.refs_5_.refs_2_), channel_id=1, source_target_pairs={{0,16},{16,0},{1,17},{17,1},{2,18},{18,2},{3,19},{19,3},{4,20},{20... | collective-permute-start | bytes 6291464 | tf_op jit(solution)/shard_map/ppermute | solution.py:43
  205.9 47.7 %collective-permute-start.18 = (bf16[512,2048]{1,0:T(8,128)(2,1)}, bf16[512,2048]{1,0:T(8,128)(2,1)}, u32[]{:S(2)}, u32[]{:S(2)}) collective-permute-start(bf16[512,2048]{1,0:T(8,128)(2,1)} %get-tuple-element.50), channel_id=1, source_target_pairs={{0,4},{4,0},{8,12},{12,8},{1,5},{5,1},{9,13},{13,9},{2,6},{6,2},{1... | collective-permute-start | bytes 6291464 | tf_op jit(solution)/shard_map/ppermute | solution.py:33
  218.3 48.1 %collective-permute-start.20 = (bf16[512,2048]{1,0:T(8,128)(2,1)S(1)}, bf16[512,2048]{1,0:T(8,128)(2,1)}, u32[]{:S(2)}, u32[]{:S(2)}) collective-permute-start(bf16[512,2048]{1,0:T(8,128)(2,1)S(1)} %shard_map.331.refs_7_), channel_id=1, source_target_pairs={{0,8},{4,12},{8,0},{12,4},{1,9},{5,13},{9,1},{13,5},{2,10},{6,14},... | collective-permute-start | bytes 6291464 | tf_op jit(solution)/shard_map/ppermute | solution.py:33
  275.7 47.1 %collective-permute-start.23 = (bf16[1,4,4,64,1024]{4,3,2,1,0:T(8,128)(2,1)S(1)}, bf16[1,4,4,64,1024]{4,3,2,1,0:T(8,128)(2,1)S(1)}, u32[]{:S(2)}, u32[]{:S(2)}) collective-permute-start(bf16[1,4,4,64,1024]{4,3,2,1,0:T(8,128)(2,1)S(1)} %shard_map.334.refs_7_.refs_4_), channel_id=1, source_target_pairs={{0,16},{16,0},{1,17},{17,1},{2,18},{18,2},{3,19},{19,3},{4,20},{20... | collective-permute-start | bytes 6291464 | tf_op jit(solution)/shard_map/ppermute | solution.py:43
  277.2 47.1 %collective-permute-start.22 = (bf16[512,2048]{1,0:T(8,128)(2,1)S(1)}, bf16[512,2048]{1,0:T(8,128)(2,1)}, u32[]{:S(2)}, u32[]{:S(2)}) collective-permute-start(bf16[512,2048]{1,0:T(8,128)(2,1)S(1)} %get-tuple-element.53.refs_1_.refs_10_), channel_id=1, source_target_pairs={{0,8},{4,12},{8,0},{12,4},{1,9},{5,13},{9,1},{13,5},{2,10},{6,14},... | collective-permute-start | bytes 6291464 | tf_op jit(solution)/shard_map/ppermute | solution.py:33
  278.7 46.1 %collective-permute-start.24 = (bf16[512,2048]{1,0:T(8,128)(2,1)S(1)}, bf16[512,2048]{1,0:T(8,128)(2,1)}, u32[]{:S(2)}, u32[]{:S(2)}) collective-permute-start(bf16[512,2048]{1,0:T(8,128)(2,1)S(1)} %get-tuple-element.53.refs_1_.refs_10_), channel_id=1, source_target_pairs={{0,4},{4,0},{8,12},{12,8},{1,5},{5,1},{9,13},{13,9},{2,6},{6,2},{1... | collective-permute-start | bytes 6291464 | tf_op jit(solution)/shard_map/ppermute | solution.py:33
  324.3 34.6 %collective-permute-start.27 = (bf16[512,2048]{1,0:T(8,128)(2,1)}, bf16[512,2048]{1,0:T(8,128)(2,1)}, u32[]{:S(2)}, u32[]{:S(2)}) collective-permute-start(bf16[512,2048]{1,0:T(8,128)(2,1)} %shard_map.327.refs_2_.refs_1_), channel_id=1, source_target_pairs={{0,4},{4,0},{8,12},{12,8},{1,5},{5,1},{9,13},{13,9},{2,6},{6,2},{1... | collective-permute-start | bytes 6291464 | tf_op jit(solution)/shard_map/ppermute | solution.py:33
  324.8 34.1 %collective-permute-start.28 = (bf16[512,2048]{1,0:T(8,128)(2,1)}, bf16[512,2048]{1,0:T(8,128)(2,1)}, u32[]{:S(2)}, u32[]{:S(2)}) collective-permute-start(bf16[512,2048]{1,0:T(8,128)(2,1)} %collective-permute-done.17.refs_4_.refs_3_.refs_2_), channel_id=1, source_target_pairs={{0,4},{4,0},{8,12},{12,8},{1,5},{5,1},{9,13},{13,9},{2,6},{6,2},{1... | collective-permute-start | bytes 6291464 | tf_op jit(solution)/shard_map/ppermute | solution.py:33
  373.9 193.7 %reduce-scatter.10.cloned.1.call-start = ((), (), s32[]{:S(2)}) async-start(), calls=%async_computation.15 | async-start | bytes 4718592 | tf_op jit(solution)/shard_map/reduce_scatter | solution.py:846
  431.1 15.2 %collective-permute-start.30 = (bf16[512,2048]{1,0:T(8,128)(2,1)}, bf16[512,2048]{1,0:T(8,128)(2,1)}, u32[]{:S(2)}, u32[]{:S(2)}) collective-permute-start(bf16[512,2048]{1,0:T(8,128)(2,1)} %get-tuple-element.58.refs_6_), channel_id=1, source_target_pairs={{0,4},{4,0},{8,12},{12,8},{1,5},{5,1},{9,13},{13,9},{2,6},{6,2},{1... | collective-permute-start | bytes 6291464 | tf_op jit(solution)/shard_map/ppermute | solution.py:33
  431.3 205.1 %reduce-scatter.12.cloned.1.call-start = ((), (), s32[]{:S(2)}) async-start(), calls=%async_computation.16 | async-start | bytes 2621440 | tf_op jit(solution)/shard_map/reduce_scatter | solution.py:827
  431.5 53.8 %collective-permute-start.29 = (bf16[512,2048]{1,0:T(8,128)(2,1)}, bf16[512,2048]{1,0:T(8,128)(2,1)S(1)}, u32[]{:S(2)}, u32[]{:S(2)}) collective-permute-start(bf16[512,2048]{1,0:T(8,128)(2,1)} %copy-done.68), channel_id=1, source_target_pairs={{0,4},{4,0},{8,12},{12,8},{1,5},{5,1},{9,13},{13,9},{2,6},{6,2},{1... | collective-permute-start | bytes 6291464 | tf_op jit(solution)/shard_map/ppermute | solution.py:33
  448.1 47.9 %collective-permute-start.31 = (bf16[512,2048]{1,0:T(8,128)(2,1)S(1)}, bf16[512,2048]{1,0:T(8,128)(2,1)S(1)}, u32[]{:S(2)}, u32[]{:S(2)}) collective-permute-start(bf16[512,2048]{1,0:T(8,128)(2,1)S(1)} %shard_map.344.refs_6_), channel_id=1, source_target_pairs={{0,8},{4,12},{8,0},{12,4},{1,9},{5,13},{9,1},{13,5},{2,10},{6,14},... | collective-permute-start | bytes 6291464 | tf_op jit(solution)/shard_map/ppermute | solution.py:33
  458.1 81.5 %collective-permute-start.34 = (bf16[1,4,4,64,1024]{4,3,2,1,0:T(8,128)(2,1)}, bf16[1,4,4,64,1024]{4,3,2,1,0:T(8,128)(2,1)}, u32[]{:S(2)}, u32[]{:S(2)}) collective-permute-start(bf16[1,4,4,64,1024]{4,3,2,1,0:T(8,128)(2,1)} %shard_map.345.refs_6_), channel_id=1, source_target_pairs={{0,16},{16,0},{1,17},{17,1},{2,18},{18,2},{3,19},{19,3},{4,20},{20... | collective-permute-start | bytes 6291464 | tf_op jit(solution)/shard_map/ppermute | solution.py:43
  505.9 47.4 %collective-permute-start.36 = (bf16[512,2048]{1,0:T(8,128)(2,1)}, bf16[512,2048]{1,0:T(8,128)(2,1)S(1)}, u32[]{:S(2)}, u32[]{:S(2)}) collective-permute-start(bf16[512,2048]{1,0:T(8,128)(2,1)} %get-tuple-element.67.refs_1_.refs_2_), channel_id=1, source_target_pairs={{0,8},{4,12},{8,0},{12,4},{1,9},{5,13},{9,1},{13,5},{2,10},{6,14},... | collective-permute-start | bytes 6291464 | tf_op jit(solution)/shard_map/ppermute | solution.py:33
  507.3 52.6 %collective-permute-start.35 = (bf16[512,2048]{1,0:T(8,128)(2,1)}, bf16[512,2048]{1,0:T(8,128)(2,1)}, u32[]{:S(2)}, u32[]{:S(2)}) collective-permute-start(bf16[512,2048]{1,0:T(8,128)(2,1)} %get-tuple-element.67.refs_1_.refs_2_), channel_id=1, source_target_pairs={{0,4},{4,0},{8,12},{12,8},{1,5},{5,1},{9,13},{13,9},{2,6},{6,2},{1... | collective-permute-start | bytes 6291464 | tf_op jit(solution)/shard_map/ppermute | solution.py:33
  573.4 113.6 %reduce-scatter.14.cloned.1.call-start = ((), (), s32[]{:S(2)}) async-start(), calls=%async_computation.17 | async-start | bytes 2621440 | tf_op jit(solution)/shard_map/reduce_scatter | solution.py:827
  575.0 53.3 %collective-permute-start.39 = (bf16[1,4,4,64,1024]{4,3,2,1,0:T(8,128)(2,1)}, bf16[1,4,4,64,1024]{4,3,2,1,0:T(8,128)(2,1)S(1)}, u32[]{:S(2)}, u32[]{:S(2)}) collective-permute-start(bf16[1,4,4,64,1024]{4,3,2,1,0:T(8,128)(2,1)} %shard_map.346.refs_6_), channel_id=1, source_target_pairs={{0,16},{16,0},{1,17},{17,1},{2,18},{18,2},{3,19},{19,3},{4,20},{20... | collective-permute-start | bytes 6291464 | tf_op jit(solution)/shard_map/ppermute | solution.py:43
  633.2 70.9 %reduce-scatter.16.cloned.1.call-start = ((), (), s32[]{:S(2)}) async-start(), calls=%async_computation.18 | async-start | bytes 1310720 | tf_op jit(solution)/shard_map/reduce_scatter | solution.py:827
  633.2 25.9 %collective-permute-start.40 = (bf16[256,2048]{1,0:T(8,128)(2,1)}, bf16[256,2048]{1,0:T(8,128)(2,1)}, u32[]{:S(2)}, u32[]{:S(2)}) collective-permute-start(bf16[256,2048]{1,0:T(8,128)(2,1)} %copy-done.48), channel_id=1, source_target_pairs={{0,16},{16,0},{1,17},{17,1},{2,18},{18,2},{3,19},{19,3},{4,20},{20... | collective-permute-start | bytes 3145736 | tf_op jit(solution)/shard_map/ppermute | solution.py:43
  634.7 47.8 %collective-permute-start.38 = (bf16[512,2048]{1,0:T(8,128)(2,1)}, bf16[512,2048]{1,0:T(8,128)(2,1)}, u32[]{:S(2)}, u32[]{:S(2)}) collective-permute-start(bf16[512,2048]{1,0:T(8,128)(2,1)} %copy-done.45), channel_id=1, source_target_pairs={{0,8},{4,12},{8,0},{12,4},{1,9},{5,13},{9,1},{13,5},{2,10},{6,14},... | collective-permute-start | bytes 6291464 | tf_op jit(solution)/shard_map/ppermute | solution.py:33
  636.4 46.1 %collective-permute-start.41 = (bf16[512,2048]{1,0:T(8,128)(2,1)}, bf16[512,2048]{1,0:T(8,128)(2,1)}, u32[]{:S(2)}, u32[]{:S(2)}) collective-permute-start(bf16[512,2048]{1,0:T(8,128)(2,1)} %get-tuple-element.70.refs_6_), channel_id=1, source_target_pairs={{0,4},{4,0},{8,12},{12,8},{1,5},{5,1},{9,13},{13,9},{2,6},{6,2},{1... | collective-permute-start | bytes 6291464 | tf_op jit(solution)/shard_map/ppermute | solution.py:33
  661.8 141.7 %reduce-scatter.18.cloned.1.call-start = ((), (), s32[]{:S(2)}) async-start(), calls=%async_computation.19 | async-start | bytes 1310720 | tf_op jit(solution)/shard_map/reduce_scatter | solution.py:827
  693.1 27.0 %collective-permute-start.42 = (bf16[1,4,4,64,512]{4,3,2,1,0:T(8,128)(2,1)S(1)}, bf16[1,4,4,64,512]{4,3,2,1,0:T(8,128)(2,1)}, u32[]{:S(2)}, u32[]{:S(2)}) collective-permute-start(bf16[1,4,4,64,512]{4,3,2,1,0:T(8,128)(2,1)S(1)} %shard_map.366.refs_7_), channel_id=1, source_target_pairs={{0,16},{16,0},{1,17},{17,1},{2,18},{18,2},{3,19},{19,3},{4,20},{20... | collective-permute-start | bytes 3145736 | tf_op jit(solution)/shard_map/ppermute | solution.py:43
  693.8 41.2 %collective-permute-start.32 = (bf16[512,2048]{1,0:T(8,128)(2,1)}, bf16[512,2048]{1,0:T(8,128)(2,1)}, u32[]{:S(2)}, u32[]{:S(2)}) collective-permute-start(bf16[512,2048]{1,0:T(8,128)(2,1)} %get-tuple-element.65), channel_id=1, source_target_pairs={{0,4},{4,0},{8,12},{12,8},{1,5},{5,1},{9,13},{13,9},{2,6},{6,2},{1... | collective-permute-start | bytes 6291464 | tf_op jit(solution)/shard_map/ppermute | solution.py:33
  693.8 50.5 %collective-permute-start.43 = (bf16[512,2048]{1,0:T(8,128)(2,1)}, bf16[512,2048]{1,0:T(8,128)(2,1)}, u32[]{:S(2)}, u32[]{:S(2)}) collective-permute-start(bf16[512,2048]{1,0:T(8,128)(2,1)} %get-tuple-element.75), channel_id=1, source_target_pairs={{0,4},{4,0},{8,12},{12,8},{1,5},{5,1},{9,13},{13,9},{2,6},{6,2},{1... | collective-permute-start | bytes 6291464 | tf_op jit(solution)/shard_map/ppermute | solution.py:33
  694.3 50.0 %collective-permute-start.44 = (bf16[512,2048]{1,0:T(8,128)(2,1)}, bf16[512,2048]{1,0:T(8,128)(2,1)}, u32[]{:S(2)}, u32[]{:S(2)}) collective-permute-start(bf16[512,2048]{1,0:T(8,128)(2,1)} %shard_map.365.refs_7_), channel_id=1, source_target_pairs={{0,8},{4,12},{8,0},{12,4},{1,9},{5,13},{9,1},{13,5},{2,10},{6,14},... | collective-permute-start | bytes 6291464 | tf_op jit(solution)/shard_map/ppermute | solution.py:33
  713.7 48.7 %collective-permute-start.55 = (bf16[1,4,4,64,1024]{4,3,2,1,0:T(8,128)(2,1)}, bf16[1,4,4,64,1024]{4,3,2,1,0:T(8,128)(2,1)}, u32[]{:S(2)}, u32[]{:S(2)}) collective-permute-start(bf16[1,4,4,64,1024]{4,3,2,1,0:T(8,128)(2,1)} %shard_map.367.refs_7_), channel_id=1, source_target_pairs={{0,16},{16,0},{1,17},{17,1},{2,18},{18,2},{3,19},{19,3},{4,20},{20... | collective-permute-start | bytes 6291464 | tf_op jit(solution)/shard_map/ppermute | solution.py:43
  723.6 88.0 %reduce-scatter.20.cloned.1.call-start = ((), (), s32[]{:S(2)}) async-start(), calls=%async_computation.20 | async-start | bytes 2621440 | tf_op jit(solution)/shard_map/reduce_scatter | solution.py:827
  (124 other events, 674.6 us)
Sparse Core Ops, SparseCore 0:
  9.6 30.5 all-gather.7
  42.4 27.4 all-gather.9
  72.1 27.4 all-gather.11
  101.5 27.4 all-gather.13
  131.0 45.4 all-gather.15
  178.4 44.5 all-gather.17
  224.6 148.4 all-gather.19
  377.4 86.1 reduce-scatter.7
  467.6 93.3 reduce-scatter.9
  573.6 42.1 reduce-scatter.11
  633.3 42.1 reduce-scatter.13
  677.7 26.3 reduce-scatter.15
  723.7 24.8 reduce-scatter.17
  766.8 41.7 reduce-scatter.19
